TPU v7x, 128 devices: a whole 4x4x4 slice. The times are simulated.
128 devices in a mesh: tp: 4 (over z_lo, core), worker: 32 (over z_hi, y, x).
Axes of the slice: x: 4, y: 4, z: 4 (z_hi: 2, z_lo: 2; z = z_hi * 2 + z_lo), core: 2. Of those that a mesh axis runs over, the one named last changes fastest.
Arguments:
- queries: bfloat16 [12288, 2560], P('worker', 'tp'), may hold values from -6 to 6
- keys: bfloat16 [12288, 2560], P('worker', 'tp'), may hold values from -6 to 6
- values: bfloat16 [12288, 2560], P('worker', 'tp'), may hold values from -32 to 32
- out_grad: bfloat16 [12288, 5120], P('worker', 'tp'), may hold values from -24 to 24
- segments: int32 [12288], P('worker'), may hold values from 0 to 3, as said below
- drift: bfloat16 [32, 2560, 5120], P('worker', 'tp'), may hold values from -3 to 3
- master: float32 [2560, 5120], P(('tp', 'worker')), may hold values from -4 to 4
- momentum: float32 [2560, 5120], P(('tp', 'worker')), may hold values from -1.5 to 1.5
Outputs:
- new_params: bfloat16 [2560, 5120], P('tp')
- new_master: float32 [2560, 5120], P(('tp', 'worker'))
- new_momentum: float32 [2560, 5120], P(('tp', 'worker'))
Inputs may be any that keep to these rules, and one draw needn't show every extreme that they name: `segments`: within each worker's 384 tokens the document id starts at 0, never falls and ends at 3.
All inputs are finite; a program needn't handle non-finite values.
Results may differ from a plain program's by a relative error of at most 0.0065.
Values may be sent and summed in bfloat16 or wider, within the bound.
No kernel may reach another device: no remote copies, remote signals or barrier semaphores. Data moves between devices by JAX's collectives and lax.ppermute only.
A program may use at most 128 MiB of HBM per device.

v0:
```python
import math

import jax
import jax.numpy as jnp
from jax import lax
from jax.sharding import PartitionSpec as P

HD = 128


inner_rate = 0.8
outer_rate = 0.7
outer_mu = 0.9
neg_big = -1e30


def head_context(query_head, key_head, value_head, allowed):
    scores = jnp.dot(query_head, key_head.T, preferred_element_type=jnp.float32) * (
        1.0 / math.sqrt(HD)
    )
    scores = jnp.where(allowed, scores, neg_big)
    row_max = jnp.max(scores, axis=1, keepdims=True)
    exp_scores = jnp.exp(scores - row_max)
    weights = (exp_scores / jnp.sum(exp_scores, axis=1, keepdims=True)).astype(jnp.bfloat16)
    return jnp.dot(weights, value_head, preferred_element_type=jnp.float32).astype(jnp.bfloat16)


def per_device(queries, keys, values, out_grad, segments, drift, master, momentum):
    own_drift = drift[0]
    tokens_here = queries.shape[0]
    heads_here = queries.shape[1] // HD
    position = jnp.arange(tokens_here, dtype=jnp.int32)
    allowed = (position[None, :] <= position[:, None]) & (segments[None, :] == segments[:, None])

    def one_head(head_index):
        first = head_index * HD
        return head_context(
            lax.dynamic_slice_in_dim(queries, first, HD, 1),
            lax.dynamic_slice_in_dim(keys, first, HD, 1),
            lax.dynamic_slice_in_dim(values, first, HD, 1),
            allowed,
        )

    context = lax.map(one_head, jnp.arange(heads_here, dtype=jnp.int32))
    piece = lax.all_gather(out_grad, "tp", axis=1, tiled=True)
    block = lax.dot_general(
        context, piece, (((1,), (0,)), ((), ())), preferred_element_type=jnp.float32
    )
    gradient = block.reshape(heads_here * HD, piece.shape[1])
    entries = gradient.shape[0] * lax.axis_size("tp") * gradient.shape[1]
    squares = lax.psum(jnp.sum(gradient * gradient), "tp")
    rms_value = jnp.sqrt(squares / entries + 1e-06)
    update = (inner_rate * gradient / rms_value).astype(jnp.bfloat16)
    worker_term = own_drift.astype(jnp.float32) + update.astype(jnp.float32)
    summed = lax.psum_scatter(worker_term, "worker", scatter_dimension=0, tiled=True)
    mean_delta = summed / lax.axis_size("worker")
    new_momentum = outer_mu * momentum + mean_delta
    new_master = master - outer_rate * (mean_delta + outer_mu * new_momentum)
    new_params = lax.all_gather(new_master.astype(jnp.bfloat16), "worker", axis=0, tiled=True)
    return (new_params, new_master, new_momentum)


def solution(mesh):
    placed = (
        P("worker", "tp"),
        P("worker", "tp"),
        P("worker", "tp"),
        P("worker", "tp"),
        P("worker"),
        P("worker", "tp", None),
        P(("tp", "worker"), None),
        P(("tp", "worker"), None),
    )
    return jax.shard_map(
        per_device,
        mesh=mesh,
        in_specs=placed,
        out_specs=(P("tp", None), P(("tp", "worker"), None), P(("tp", "worker"), None)),
        check_vma=False,
    )
```

profile of v0, /device:TPU:32, one launch (start us, length us, event | category | flops | bytes accessed | tf_op | source)
XLA Modules:
  0.0 468.9 jit_solution(37543501295261735)
XLA Ops:
  7.2 0.0 all-gather.4.cloned.1.call-start
  7.2 0.7 all-gather.4.cloned.1.call-update
  7.9 0.0 all-gather.6.cloned.1.call-start
  8.0 19.1 %while.11 = (s32[]{:T(128)}, bf16[5,384,128]{2,1,0:T(8,128)(2,1)S(1)}, s32[5]{0:T(128)S(1)}, bf16[384,640]{1,0:T(8,128)(2,1)}, bf16[384,640]{1,0:T(8,128)(2,1)},...) while((s32[]{:T(128)}, ...), condition=%wide.region_3.4_spmd.clone, body=%wide.region_0.3_spmd.clone.sunk | while | flops 77167872 | bytes 2177195 | solution.py:44
  8.0 0.6 dynamic_slice.34
  9.2 1.2 fusion.24
  10.4 0.1 fusion.25
  10.6 1.2 fusion.26
  11.8 0.6 dynamic_slice.34
  13.0 1.2 fusion.24
  14.3 0.1 fusion.25
  14.4 1.2 fusion.26
  15.6 0.6 dynamic_slice.34
  16.9 1.2 fusion.24
  18.1 0.1 fusion.25
  18.2 1.2 fusion.26
  19.4 0.6 dynamic_slice.34
  20.7 1.3 fusion.24
  21.9 0.1 fusion.25
  22.1 1.2 fusion.26
  23.3 0.6 dynamic_slice.34
  24.5 1.2 fusion.24
  25.8 0.1 fusion.25
  25.9 1.2 fusion.26
  27.1 27.2 %all-gather.4.cloned.1.call-done = bf16[384,5120]{1,0:T(8,128)(2,1)} async-done(((bf16[384,1280]{1,0:T(8,128)(2,1)}), bf16[384,5120]{1,0:T(8,128)(2,1)}) %all-gather.4.cloned.1.call-update) | async-done | bytes 3932176 | tf_op jit(solution)/shard_map/all_gather | solution.py:45
  54.3 11.0 %multiply_reduce_fusion = (f32[]{:T(128)}, f32[5,128,5120]{2,1,0:T(8,128)}) fusion(bf16[5,384,128]{2,1,0:T(8,128)(2,1)S(1)} %get-tuple-element.40, bf16[384,5120]{1,0:T(8,128)(2,1)} %all-gather.4.cloned.1.call-done), kind=kOutput, calls=%fused_computation.20 | convolution fusion | flops 2523136000 | bytes 17530884 | tf_op jit(solution)/shard_map/dot_general | solution.py:46
  65.3 8.4 %psum.7 = f32[]{:T(128)} all-reduce(f32[]{:T(128)} %get-tuple-element.77), channel_id=1, replica_groups=mesh['tp'=4,'worker'=32] {'tp'}, use_global_device_ids=true, to_apply=%region_5.6 | all-reduce | flops 1 | bytes 8 | tf_op jit(solution)/shard_map/psum | solution.py:51
  74.4 9.2 %divide_convert_fusion.2 = bf16[5,128,5120]{2,1,0:T(8,128)(2,1)} fusion(f32[5,128,5120]{2,1,0:T(8,128)} %get-tuple-element.78, f32[]{:T(128)S(6)} %sqrt.3), kind=kLoop, calls=%fused_computation.19 | loop fusion | flops 9830400 | bytes 19660804 | tf_op jit(solution)/shard_map/convert_element_type | solution.py:53
  83.6 11.8 %convert_add_fusion = f32[640,5120]{1,0:T(8,128)} fusion(bf16[5,128,5120]{2,1,0:T(8,128)(2,1)} %divide_convert_fusion.2, bf16[1,640,5120]{2,1,0:T(8,128)(2,1)} %param.15), kind=kLoop, calls=%fused_computation.18 | loop fusion | flops 9830400 | bytes 26214400 | tf_op jit(solution)/shard_map/add | solution.py:54
  95.5 0.0 copy-start.5
  95.5 180.3 %fusion.2 = f32[24,5120]{1,0:T(8,128)S(1)} fusion(f32[640,5120]{1,0:T(8,128)} %convert_add_fusion), kind=kCustom, calls=%all-reduce-scatter | all-reduce-scatter fusion | flops 3932161 | bytes 13599232
  275.8 0.0 copy-start
  275.8 1.3 collective-permute-start.5
  277.1 1.3 collective-permute-start
  278.4 5.5 %collective-permute-start.1 = (f32[24,5120]{1,0:T(8,128)S(1)}, f32[24,5120]{1,0:T(8,128)S(1)}, u32[]{:S(2)}, u32[]{:S(2)}) collective-permute-start(f32[24,5120]{1,0:T(8,128)S(1)} %fusion.2), channel_id=1, source_target_pairs={{0,2},{1,3},{2,4},{3,5},{4,6},{5,7},{6,8},{7,9},{8,10},{9,11},{10,... | collective-permute-start | bytes 1474568
  283.9 3.6 collective-permute-start.2
  287.5 8.2 %collective-permute-start.3 = (f32[24,5120]{1,0:T(8,128)S(1)}, f32[24,5120]{1,0:T(8,128)S(1)}, u32[]{:S(2)}, u32[]{:S(2)}) collective-permute-start(f32[24,5120]{1,0:T(8,128)S(1)} %fusion.2), channel_id=1, source_target_pairs={{0,4},{1,5},{2,6},{3,7},{4,8},{5,9},{6,10},{7,11},{8,12},{9,13},{1... | collective-permute-start | bytes 1474568
  295.8 0.0 collective-permute-done.5
  295.8 2.1 collective-permute-start.4
  297.8 0.0 copy-done.5
  297.8 0.6 dynamic-slice.4
  299.1 0.0 collective-permute-done
  299.1 0.0 copy-start.1
  299.1 2.3 collective-permute-done.1
  301.4 0.0 copy-start.2
  301.4 0.0 collective-permute-done.2
  301.4 0.0 copy-start.3
  301.4 29.7 %collective-permute-done.3 = f32[24,5120]{1,0:T(8,128)S(1)} collective-permute-done((f32[24,5120]{1,0:T(8,128)S(1)}, f32[24,5120]{1,0:T(8,128)S(1)}, u32[]{:S(2)}, u32[]{:S(2)}) %collective-permute-start.3) | collective-permute-done | bytes 491552
  331.1 0.0 copy-done
  331.1 0.0 copy-done.1
  331.1 0.0 copy-done.2
  331.1 0.0 copy-done.3
  331.1 0.0 copy-start.4
  331.1 0.8 copy-done.4
  331.9 0.0 collective-permute-done.4
  331.9 12.5 %concatenate = f32[148,5120]{1,0:T(8,128)S(1)} concatenate(f32[4,5120]{1,0:T(4,128)S(1)} %collective-permute-done.5, f32[24,5120]{1,0:T(8,128)} %collective-permute-done.4, f32[24,5120]{1,0:T(8,128)} %copy-done.4, f32[24,5120]{1,0:T(8,128)} %copy-done.3, f32[24,5120]{1,0:T(8,128)} %copy-done.2, f32[24,5120]{1,0:T(8,128)} %copy-done.1, f32[24,5120]{1,0:T(8,128)} %copy-done), dimensions={0} | concatenate | bytes 6062080
  344.4 2.3 convert_bitcast_fusion
  346.7 0.0 all-gather.6.cloned.1.call-update
  346.8 106.7 %all-gather.6.cloned.1.call-done = bf16[32,20,5120]{2,1,0:T(8,128)(2,1)} async-done(((bf16[1,20,5120]{2,1,0:T(8,128)(2,1)}), bf16[32,20,5120]{2,1,0:T(8,128)(2,1)}) %all-gather.6.cloned.1.call-update) | async-done | bytes 6553616 | tf_op jit(solution)/shard_map/all_gather | solution.py:59
  453.5 8.6 %reshape.25 = bf16[640,5120]{1,0:T(8,128)(2,1)} reshape(bf16[32,20,5120]{2,1,0:T(8,128)(2,1)} %all-gather.6.cloned.1.call-done) | data formatting | bytes 13107200
  (3 shorter events, 0.0 us)
Async XLA Ops:
  7.2 47.2 %all-gather.4.cloned.1.call-start = ((), (), s32[]{:S(2)}) async-start(), calls=%async_computation | async-start | bytes 4915200 | tf_op jit(solution)/shard_map/all_gather | solution.py:45
  7.9 445.6 %all-gather.6.cloned.1.call-start = ((), (), s32[]{:S(2)}) async-start(), calls=%async_computation.1 | async-start | bytes 8110080 | tf_op jit(solution)/shard_map/all_gather | solution.py:59
  95.5 202.4 %copy-start.5 = (u32[128]{0:T(128)S(1)}, u32[128]{0:T(128)}, u32[]{:S(2)}) copy-start(u32[128]{0:T(128)} %constant.46) | copy-start | bytes 1540
  275.8 55.4 %copy-start = (f32[24,5120]{1,0:T(8,128)}, f32[24,5120]{1,0:T(8,128)S(1)}, u32[]{:S(2)}) copy-start(f32[24,5120]{1,0:T(8,128)S(1)} %fusion.2) | copy-start | bytes 1474564
  275.8 20.0 %collective-permute-start.5 = (f32[4,5120]{1,0:T(4,128)S(1)}, f32[4,5120]{1,0:T(4,128)S(1)}, u32[]{:S(2)}, u32[]{:S(2)}) collective-permute-start(f32[4,5120]{1,0:T(4,128)S(1)} %slice), channel_id=1, source_target_pairs={{0,6},{1,7},{2,8},{3,9},{4,10},{5,11},{6,12},{7,13},{8,14},{9,15},... | collective-permute-start | bytes 245768
  277.1 22.0 %collective-permute-start = (f32[24,5120]{1,0:T(8,128)S(1)}, f32[24,5120]{1,0:T(8,128)S(1)}, u32[]{:S(2)}, u32[]{:S(2)}) collective-permute-start(f32[24,5120]{1,0:T(8,128)S(1)} %fusion.2), channel_id=1, source_target_pairs={{0,1},{1,2},{2,3},{3,4},{4,5},{5,6},{6,7},{7,8},{8,9},{9,10},{10,1... | collective-permute-start | bytes 1474568
  278.4 23.0 %collective-permute-start.1 = (f32[24,5120]{1,0:T(8,128)S(1)}, f32[24,5120]{1,0:T(8,128)S(1)}, u32[]{:S(2)}, u32[]{:S(2)}) collective-permute-start(f32[24,5120]{1,0:T(8,128)S(1)} %fusion.2), channel_id=1, source_target_pairs={{0,2},{1,3},{2,4},{3,5},{4,6},{5,7},{6,8},{7,9},{8,10},{9,11},{10,... | collective-permute-start | bytes 1474568
  283.9 17.5 %collective-permute-start.2 = (f32[24,5120]{1,0:T(8,128)S(1)}, f32[24,5120]{1,0:T(8,128)S(1)}, u32[]{:S(2)}, u32[]{:S(2)}) collective-permute-start(f32[24,5120]{1,0:T(8,128)S(1)} %fusion.2), channel_id=1, source_target_pairs={{0,3},{1,4},{2,5},{3,6},{4,7},{5,8},{6,9},{7,10},{8,11},{9,12},{10... | collective-permute-start | bytes 1474568
  287.5 43.6 %collective-permute-start.3 = (f32[24,5120]{1,0:T(8,128)S(1)}, f32[24,5120]{1,0:T(8,128)S(1)}, u32[]{:S(2)}, u32[]{:S(2)}) collective-permute-start(f32[24,5120]{1,0:T(8,128)S(1)} %fusion.2), channel_id=1, source_target_pairs={{0,4},{1,5},{2,6},{3,7},{4,8},{5,9},{6,10},{7,11},{8,12},{9,13},{1... | collective-permute-start | bytes 1474568
  295.8 36.1 %collective-permute-start.4 = (f32[24,5120]{1,0:T(8,128)S(1)}, f32[24,5120]{1,0:T(8,128)}, u32[]{:S(2)}, u32[]{:S(2)}) collective-permute-start(f32[24,5120]{1,0:T(8,128)S(1)} %fusion.2), channel_id=1, source_target_pairs={{0,5},{1,6},{2,7},{3,8},{4,9},{5,10},{6,11},{7,12},{8,13},{9,14},{... | collective-permute-start | bytes 1474568
  299.1 32.0 %copy-start.1 = (f32[24,5120]{1,0:T(8,128)}, f32[24,5120]{1,0:T(8,128)S(1)}, u32[]{:S(2)}) copy-start(f32[24,5120]{1,0:T(8,128)S(1)} %collective-permute-done) | copy-start | bytes 1474564
  301.4 29.7 %copy-start.2 = (f32[24,5120]{1,0:T(8,128)}, f32[24,5120]{1,0:T(8,128)S(1)}, u32[]{:S(2)}) copy-start(f32[24,5120]{1,0:T(8,128)S(1)} %collective-permute-done.1) | copy-start | bytes 1474564
  301.4 29.7 %copy-start.3 = (f32[24,5120]{1,0:T(8,128)}, f32[24,5120]{1,0:T(8,128)S(1)}, u32[]{:S(2)}) copy-start(f32[24,5120]{1,0:T(8,128)S(1)} %collective-permute-done.2) | copy-start | bytes 1474564
  331.1 0.8 copy-start.4
Sparse Core Ops, SparseCore 0:
  9.7 44.6 all-gather.3
  346.9 106.5 all-gather.5
where the time goes:
time: 472 us; the launch traced here: 469 us
  blocking collectives  189 us (40%)
  waiting for transfers between devices  167 us (35%)
  local copies, waits for them, and re-layouts  25.4 us (5%)
  other arithmetic  24.1 us (5%)
  matrix products  23.2 us (5%)
  starting transfers between devices  22.1 us (5%)
  between operations  15.5 us (3%)
    unnamed x1, blocking collectives  180 us
    all_gather x1, waiting for transfers between devices, per_device(): lax.all_gather(new_master.astype(jnp.bfloat16), 'worker', axis=0, tiled=T...  107 us
    unnamed x8, waiting for transfers between devices  32.7 us
    all_gather x1, waiting for transfers between devices, per_device(): piece = lax.all_gather(out_grad, 'tp', axis=1, tiled=True)  27.2 us
    unnamed x16, local copies, waits for them, and re-layouts  22.5 us
    unnamed x6, starting transfers between devices  22 us
    add x1, other arithmetic, per_device(): worker_term = own_drift.astype(jnp.float32) + update.astype(jnp.float32)  11.8 us
    dot_general x1, matrix products, per_device(): lax.dot_general(context, piece, (((1,), (0,)), ((), ())), preferred_eleme...  11 us
  transfers between devices with their start and end apart: 8, of which 4 were waited for; matrix products, arithmetic and copies ran while one was open for 3% of the time, Pallas kernels for 0%

commit v1 on v0

v1 whole, which is shorter than its diff:
```python
import math

import jax
import jax.numpy as jnp
from jax import lax
from jax.experimental import pallas as pl
from jax.experimental.pallas import tpu as pltpu
from jax.sharding import PartitionSpec as P

HD = 128
NX, NY, NZ = 4, 4, 2
TILE_R = 80
HALF_C = 640

inner_rate = 0.8
outer_rate = 0.7
outer_mu = 0.9
neg_big = -1e30
bf16 = jnp.bfloat16
f32 = jnp.float32
VMEM_LIMIT = 60 << 20


def worker_of(zh, y, x):
    return (zh % NZ) * NX * NY + (y % NY) * NX + (x % NX)


def move(value, axis, step):
    pairs = []
    for zh in range(NZ):
        for y in range(NY):
            for x in range(NX):
                to = {
                    "x": worker_of(zh, y, x + step),
                    "y": worker_of(zh, y + step, x),
                    "z": worker_of(zh + step, y, x),
                }[axis]
                pairs.append((worker_of(zh, y, x), to))
    return lax.ppermute(value, "worker", pairs)


def swap_tp(value, bit):
    return lax.ppermute(value, "tp", [(t, t ^ bit) for t in range(4)])


def attention_body(q_ref, k_ref, v_ref, seg_row_ref, seg_col_ref, ct_ref, gram_ref):
    tokens, width = q_ref.shape
    scale = 1.0 / math.sqrt(HD)
    blocks = tokens // HD
    for h in range(width // HD):
        cols = slice(h * HD, (h + 1) * HD)
        for b in range(blocks):
            queries = slice(b * HD, (b + 1) * HD)
            seen = (b + 1) * HD
            scores = lax.dot_general(
                k_ref[:seen, cols], q_ref[queries, cols], (((1,), (1,)), ((), ())),
                preferred_element_type=f32,
            ) * scale
            key_at = lax.broadcasted_iota(jnp.int32, (seen, HD), 0)
            query_at = lax.broadcasted_iota(jnp.int32, (seen, HD), 1) + b * HD
            allowed = (key_at <= query_at) & (seg_col_ref[:seen, :] == seg_row_ref[:, queries])
            scores = jnp.where(allowed, scores, neg_big)
            exp_scores = jnp.exp(scores - jnp.max(scores, axis=0, keepdims=True))
            total = jnp.sum(exp_scores, axis=0, keepdims=True)
            weights = (exp_scores * (1.0 / total)).astype(bf16)
            ct_ref[cols, queries] = lax.dot_general(
                v_ref[:seen, cols], weights, (((0,), (0,)), ((), ())),
                preferred_element_type=f32,
            ).astype(bf16)
    gram_ref[...] = lax.dot_general(
        ct_ref[...], ct_ref[...], (((0,), (0,)), ((), ())), preferred_element_type=f32
    )


def attention(queries, keys, values, segments):
    tokens, width = queries.shape
    return pl.pallas_call(
        attention_body,
        out_shape=(
            jax.ShapeDtypeStruct((width, tokens), bf16),
            jax.ShapeDtypeStruct((tokens, tokens), f32),
        ),
        compiler_params=pltpu.CompilerParams(vmem_limit_bytes=VMEM_LIMIT),
        name="attention",
    )(queries, keys, values, segments.reshape(1, tokens), segments.reshape(tokens, 1))


def column_of(tp, half, quarter):
    first = (tp ^ (2 * half) ^ (quarter // 2)) * (2 * HALF_C) + (quarter % 2) * HALF_C
    return pl.multiple_of(first, HALF_C)


def row_of(zh, y, j, ky):
    return pl.multiple_of((zh ^ j) * (NY * TILE_R) + ((y + ky) % NY) * TILE_R, TILE_R)


SEND_ORDER = (2, 1, 3, 0)


def pseudo_body(at_ref, scale_ref, ct_ref, g0_ref, g1_ref, g2_ref, g3_ref, drift_ref, *rest):
    outs, (drift_buf, rows_buf, sems) = rest[:14], rest[14:]
    x, y, zh, tp = at_ref[0], at_ref[1], at_ref[2], at_ref[3]
    scale = scale_ref[0]
    a_out, b_out = outs[:7], outs[7:]

    def copy(slot, k, half):
        return pltpu.make_async_copy(
            drift_ref.at[0, :, pl.ds(column_of(tp, half, (x + k) % NX), HALF_C)],
            drift_buf.at[slot], sems.at[slot],
        )

    steps = [(k, half) for k in SEND_ORDER for half in range(2)]
    for slot, (k, half) in enumerate(steps):
        copy(slot, k, half).start()
    for j in range(2):
        for ky in range(NY):
            first = (j * NY + ky) * TILE_R
            rows_buf[first:first + TILE_R, :] = ct_ref[pl.ds(row_of(zh, y, j, ky), TILE_R), :]

    def store(group, block, index, half, value):
        cols = slice(half * HALF_C, (half + 1) * HALF_C)
        if block == 0:
            group[0][index, :, cols] = value
        else:
            group[1 + 2 * (block - 1) + index // 2][index % 2, :, cols] = value

    for slot, (k, half) in enumerate(steps):
        quarter = (x + k) % NX
        cols = pl.ds(pl.multiple_of((quarter % 2) * HALF_C, HALF_C), HALF_C)
        near, far = (g0_ref, g1_ref) if half == 0 else (g2_ref, g3_ref)
        piece = jnp.where(quarter >= 2, far[:, cols], near[:, cols])
        copy(slot, k, half).wait()
        for j in range(2):
            rows = slice(j * NY * TILE_R, (j + 1) * NY * TILE_R)
            block = jnp.dot(rows_buf[rows, :], piece, preferred_element_type=f32)
            for ky in range(NY):
                own = drift_buf[slot, pl.ds(row_of(zh, y, j, ky), TILE_R), :]
                value = block[ky * TILE_R:(ky + 1) * TILE_R] * scale + own.astype(f32)
                value = value.astype(bf16)
                if j == 0:
                    store(a_out, k, ky, half, value)
                else:
                    store(b_out, ky, k, half, value)


def pseudo_gradient(at, scale, ct, pieces, drift):
    whole = jax.ShapeDtypeStruct((4, TILE_R, 2 * HALF_C), bf16)
    part = jax.ShapeDtypeStruct((2, TILE_R, 2 * HALF_C), bf16)
    vmem = pl.BlockSpec(memory_space=pltpu.VMEM)
    smem = pl.BlockSpec(memory_space=pltpu.SMEM)
    return pl.pallas_call(
        pseudo_body,
        out_shape=((whole,) + (part,) * 6) * 2,
        in_specs=[smem, smem] + [vmem] * 5 + [pl.BlockSpec(memory_space=pl.ANY)],
        out_specs=(vmem,) * 14,
        scratch_shapes=[
            pltpu.VMEM((8, 2 * NY * TILE_R, HALF_C), bf16),
            pltpu.VMEM(ct.shape, bf16),
            pltpu.SemaphoreType.DMA((8,)),
        ],
        compiler_params=pltpu.CompilerParams(vmem_limit_bytes=VMEM_LIMIT),
        name="pseudo_gradient",
    )(at, scale, ct, *pieces, drift)


def base_body(at_ref, master_ref, momentum_ref, base_ref):
    tp = at_ref[3]
    for quarter in range(NX):
        for half in range(2):
            cols = pl.ds(column_of(tp, half, quarter), HALF_C)
            base_ref[quarter, :, half * HALF_C:(half + 1) * HALF_C] = (
                master_ref[:, cols] - (outer_rate * outer_mu * outer_mu) * momentum_ref[:, cols]
            )


def base_rows(at, master, momentum):
    vmem = pl.BlockSpec(memory_space=pltpu.VMEM)
    return pl.pallas_call(
        base_body,
        out_shape=jax.ShapeDtypeStruct((NX, master.shape[0], 2 * HALF_C), f32),
        in_specs=[pl.BlockSpec(memory_space=pltpu.SMEM), vmem, vmem],
        out_specs=vmem,
        name="base_rows",
    )(at, master, momentum)


def outer_body(at_ref, master_ref, momentum_ref, mean_ref, new_master_ref, new_momentum_ref):
    x, tp = at_ref[0], at_ref[3]
    for quarter in range(NX):
        for half in range(2):
            cols = pl.ds(column_of(tp, half, quarter), HALF_C)
            mean = mean_ref[(quarter - x + NX) % NX, :, half * HALF_C:(half + 1) * HALF_C]
            new = outer_mu * momentum_ref[:, cols] + mean
            new_momentum_ref[:, cols] = new
            new_master_ref[:, cols] = master_ref[:, cols] - outer_rate * (mean + outer_mu * new)


def outer_rows(at, master, momentum, mean):
    vmem = pl.BlockSpec(memory_space=pltpu.VMEM)
    out = jax.ShapeDtypeStruct(master.shape, f32)
    return pl.pallas_call(
        outer_body,
        out_shape=(out, out),
        in_specs=[pl.BlockSpec(memory_space=pltpu.SMEM), vmem, vmem, vmem],
        out_specs=(vmem, vmem),
        name="outer_rows",
    )(at, master, momentum, mean)


def place_body(at_ref, *rest):
    tiles, out_ref, sems = rest[:-2], rest[-2], rest[-1]
    x, y, zh, tp = at_ref[0], at_ref[1], at_ref[2], at_ref[3]
    copies = []
    for n, (where, (j, ky, kx)) in enumerate(TILES):
        ref, index = where
        for half in range(2):
            cols = slice(half * HALF_C, (half + 1) * HALF_C)
            source = tiles[ref].at[:, cols] if index is None else tiles[ref].at[index, :, cols]
            copies.append(pltpu.make_async_copy(
                source,
                out_ref.at[pl.ds(row_of(zh, y, j, ky), TILE_R),
                           pl.ds(column_of(tp, half, (x + kx) % NX), HALF_C)],
                sems.at[2 * n + half],
            ))
    for one in copies:
        one.start()
    for one in copies:
        one.wait()


def tile_list():
    found = []
    for j in range(2):
        base = 10 * j
        for small in range(4):
            found.append(((base + small, None), (j, small, 0) if j == 0 else (j, 0, small)))
        for large in range(1, 4):
            for small in range(4):
                operand = base + 4 + 2 * (large - 1) + small // 2
                place = (j, small, large) if j == 0 else (j, large, small)
                found.append(((operand, small % 2), place))
    return found


TILES = tile_list()


def place(at, tiles, rows, width):
    hbm = pl.BlockSpec(memory_space=pl.ANY)
    return pl.pallas_call(
        place_body,
        out_shape=jax.ShapeDtypeStruct((rows, width), bf16),
        in_specs=[pl.BlockSpec(memory_space=pltpu.SMEM)] + [hbm] * len(tiles),
        out_specs=hbm,
        scratch_shapes=[pltpu.SemaphoreType.DMA((2 * len(TILES),))],
        name="place",
    )(at, *tiles)


def add(*terms):
    total = terms[0].astype(f32)
    for term in terms[1:]:
        total = total + term.astype(f32)
    return total


def reduce_route(blocks, first, second):
    own, one_a, one_b, two_a, two_b, three_a, three_b = blocks
    via_a = move(two_a, first, 1)
    via_b = move(two_b, first, -1)
    got_1b = move(one_b, first, 1)
    got_3a = move(three_a, first, -1)
    got_1a = move(add(one_a, via_a).astype(bf16), first, 1)
    got_3b = move(add(three_b, via_b).astype(bf16), first, -1)
    tiles = []
    for k in range(4):
        up, down = (got_1a, got_3a) if k < 2 else (got_1b, got_3b)
        tiles.append(add(own[k], up[k % 2], down[k % 2]))
    two = move(tiles[2].astype(bf16), second, 2)
    one = move(tiles[1].astype(bf16), second, 1)
    three = move(tiles[3].astype(bf16), second, -1)
    return add(tiles[0], one, three, two)


def gather_route(tile, first, second):
    one = move(tile, first, -1)
    three = move(tile, first, 1)
    two = move(tile, first, -2)
    half_a = jnp.stack([tile, one])
    half_b = jnp.stack([two, three])
    a1 = move(half_a, second, -1)
    b3 = move(half_b, second, 1)
    b1 = move(half_b, second, -1)
    a3 = move(half_a, second, 1)
    a2 = move(a1, second, -1)
    b2 = move(b3, second, 1)
    return [tile, one, two, three, a1, b1, a2, b2, a3, b3]


def per_device(queries, keys, values, out_grad, segments, drift, master, momentum):
    tp = lax.axis_index("tp")
    worker = lax.axis_index("worker")
    x, y, zh = worker % NX, (worker // NX) % NY, worker // (NX * NY)
    at = jnp.stack([x, y, zh, tp]).astype(jnp.int32)
    tokens = queries.shape[0]
    entries = queries.shape[1] * lax.axis_size("tp") * drift.shape[2]

    gram = lax.dot_general(out_grad, out_grad, (((1,), (1,)), ((), ())), preferred_element_type=f32)
    side = (tp % 2) * (tokens // 2)
    other = (tokens // 2) - side
    mine = lax.dynamic_slice_in_dim(gram, side, tokens // 2, 0)
    mine = mine + swap_tp(lax.dynamic_slice_in_dim(gram, other, tokens // 2, 0), 1)
    mine = mine + swap_tp(mine, 2)
    theirs = swap_tp(mine, 1)

    partner = swap_tp(out_grad, 1)
    across = swap_tp(out_grad, 2)
    across_partner = swap_tp(across, 1)

    base = base_rows(at, master, momentum)
    base_got = jnp.stack(
        [lax.dynamic_index_in_dim(base, x, 0, False)]
        + [move(lax.dynamic_index_in_dim(base, (x + k) % NX, 0, False), "x", k) for k in (1, 2, 3)]
    )
    base_tile = jnp.concatenate(
        [lax.dynamic_index_in_dim(base_got, (x - g + NX) % NX, 0, False) for g in range(NX)], axis=0
    )

    ct, own_gram = attention(queries, keys, values, segments)
    squares = jnp.sum(lax.dynamic_slice_in_dim(own_gram, side, tokens // 2, 0) * mine)
    squares = squares + jnp.sum(lax.dynamic_slice_in_dim(own_gram, other, tokens // 2, 0) * theirs)
    squares = lax.psum(squares, "tp")
    scale = (inner_rate / jnp.sqrt(squares / entries + 1e-06)).reshape(1)

    sends = pseudo_gradient(at, scale, ct, (out_grad, partner, across, across_partner), drift)
    here = reduce_route(sends[:7], "x", "y")
    there = reduce_route(sends[7:], "y", "x")
    summed = add(here, move(there.astype(bf16), "z", 1))
    mean = summed / lax.axis_size("worker")

    tile = (base_tile - (outer_rate * (1.0 + outer_mu)) * mean).astype(bf16)
    opposite = move(tile, "z", 1)
    tiles = gather_route(tile, "y", "x") + gather_route(opposite, "x", "y")

    def rows_for(k):
        return lax.dynamic_slice_in_dim(mean, ((x + k) % NX) * master.shape[0], master.shape[0], 0)

    means = jnp.stack([rows_for(0)] + [move(rows_for(NX - k), "x", -k) for k in (1, 2, 3)])
    new_master, new_momentum = outer_rows(at, master, momentum, means)
    new_params = place(at, tiles, drift.shape[1], drift.shape[2])
    return (new_params, new_master, new_momentum)


def solution(mesh):
    placed = (
        P("worker", "tp"),
        P("worker", "tp"),
        P("worker", "tp"),
        P("worker", "tp"),
        P("worker"),
        P("worker", "tp", None),
        P(("tp", "worker"), None),
        P(("tp", "worker"), None),
    )
    return jax.shard_map(
        per_device,
        mesh=mesh,
        in_specs=placed,
        out_specs=(P("tp", None), P(("tp", "worker"), None), P(("tp", "worker"), None)),
        check_vma=False,
    )
```

time: 472 us -> 424 us (0.90)
  Pallas kernels: 0 us -> 222 us
  blocking collectives: 189 us -> 6.67 us
  waiting for transfers between devices: 167 us -> 109 us
  starting transfers between devices: 22.1 us -> 65.9 us
  matrix products: 23.2 us -> 2.18 us
  local copies, waits for them, and re-layouts: 25.4 us -> 4.91 us
  other arithmetic: 24.1 us -> 9.9 us
  between operations: 15.5 us -> 3.21 us
    pallas_call x0 -> x5, Pallas kernels: none -> 222 us  [the longest x1 201 us: place(): pl.pallas_call(place_body, out_shape=jax.ShapeDtypeStruct((rows, width),...]
    unnamed x1 -> x0, blocking collectives: 180 us -> none
    all_gather x2 -> x0, waiting for transfers between devices: 134 us -> none  [the longest x1 107 us: per_device(): lax.all_gather(new_master.astype(jnp.bfloat16), 'worker', axis=0, tiled=T...]
    ppermute x0 -> x50, waiting for transfers between devices: none -> 109 us  [the longest x44 79.9 us: move(): return lax.ppermute(value, 'worker', pairs)]
    ppermute x0 -> x50, starting transfers between devices: none -> 65.9 us  [the longest x44 64.8 us: move(): return lax.ppermute(value, 'worker', pairs)]
    unnamed x8 -> x0, waiting for transfers between devices: 32.7 us -> none
    unnamed x6 -> x0, starting transfers between devices: 22 us -> none
    unnamed x16 -> x38, local copies, waits for them, and re-layouts: 22.5 us -> 1.32 us
  transfers between devices with their start and end apart: 8 -> 50, of which waited for: 4 -> 23; matrix products, arithmetic and copies ran while one was open for 3% -> 4% of each run, Pallas kernels for 0% -> 2%
where the time goes in v1:
time: 424 us
  Pallas kernels  222 us (52%)
  waiting for transfers between devices  109 us (26%)
  starting transfers between devices  65.9 us (16%)
  other arithmetic  9.9 us (2%)
  blocking collectives  6.67 us (2%)
  local copies, waits for them, and re-layouts  4.91 us (1%)
    pallas_call x1, Pallas kernels, place(): pl.pallas_call(place_body, out_shape=jax.ShapeDtypeStruct((rows, width),...  201 us
    ppermute x44, waiting for transfers between devices, move(): return lax.ppermute(value, 'worker', pairs)  79.9 us
    ppermute x44, starting transfers between devices, move(): return lax.ppermute(value, 'worker', pairs)  64.8 us
    ppermute x6, waiting for transfers between devices, swap_tp(): return lax.ppermute(value, 'tp', [(t, t ^ bit) for t in range(4)])  29.2 us
    pallas_call x1, Pallas kernels, pseudo_gradient(): pl.pallas_call(pseudo_body, out_shape=((whole,) + (part,) * 6) * 2, in_sp...  11.2 us
  transfers between devices with their start and end apart: 50, of which 23 were waited for; matrix products, arithmetic and copies ran while one was open for 4% of the time, Pallas kernels for 2%

profile of v1, /device:TPU:32, one launch (start us, length us, event | category | flops | bytes accessed | tf_op | source)
XLA Modules:
  0.0 423.5 jit_solution(9262481696668803962)
XLA Ops:
  0.7 2.2 fusion.14
  2.9 0.7 constant_dynamic-slice_fusion.3
  4.2 20.2 %collective-permute-done.7.g2_ref = bf16[384,1280]{1,0:T(8,128)(2,1)S(1)} collective-permute-done((bf16[384,1280]{1,0:T(8,128)(2,1)}, bf16[384,1280]{1,0:T(8,128)(2,1)S(1)}, u32[]{:S(2)}, u32[]{:S(2)}) %collective-permute-start.7) | collective-permute-done | bytes 983072 | tf_op jit(solution)/shard_map/ppermute | solution.py:43
  24.4 1.2 dynamic-slice_add_fusion
  26.0 8.9 %collective-permute-done.4 = f32[192,384]{1,0:T(8,128)S(1)} collective-permute-done((f32[192,384]{1,0:T(8,128)S(1)}, f32[192,384]{1,0:T(8,128)S(1)}, u32[]{:S(2)}, u32[]{:S(2)}) %collective-permute-start.4) | collective-permute-done | bytes 294944 | tf_op jit(solution)/shard_map/ppermute | solution.py:43
  35.1 1.2 reshape.61.seg_row_ref
  36.3 1.5 reshape.64.seg_col_ref
  37.8 5.0 %attention.1 = (bf16[640,384]{1,0:T(8,128)(2,1)}, f32[384,384]{1,0:T(8,128)}) custom-call(bf16[384,640]{1,0:T(8,128)(2,1)} %q_ref.1, bf16[384,640]{1,0:T(8,128)(2,1)} %k_ref.1, bf16[384,640]{1,0:T(8,128)(2,1)} %v_ref.1, s32[1,384]{1,0:T(1,128)} %reshape.61.seg_row_ref, s32[384,1]{1,0:T(8,128)} %reshape.64.seg_col_ref), custom_call_target="tpu_custom_call" | custom-call | tf_op jit(solution)/shard_map/attention/pallas_call | solution.py:77
  43.5 1.7 multiply_reduce_fusion
  46.4 2.0 base_rows.1
  48.4 6.7 %psum.7 = f32[]{:T(128)} all-reduce(f32[]{:T(128)S(6)} %add.232), channel_id=1, replica_groups=mesh['tp'=4,'worker'=32] {'tp'}, use_global_device_ids=true, to_apply=%region_2.3 | all-reduce | flops 1 | bytes 8 | tf_op jit(solution)/shard_map/psum | solution.py:332
  55.8 0.9 copy-done.3
  57.1 11.2 %pseudo_gradient.1 = (bf16[4,80,1280]{2,1,0:T(8,128)(2,1)}, bf16[2,80,1280]{2,1,0:T(8,128)(2,1)}, bf16[2,80,1280]{2,1,0:T(8,128)(2,1)}, bf16[2,80,1280]{2,1,0:T(...) custom-call(s32[4]{0:T(128)} %pad_add_fusion.at_ref, ...), custom_call_target="tpu_custom_call" | custom-call | tf_op jit(solution)/shard_map/pseudo_gradient/pallas_call | solution.py:151
  68.4 3.1 collective-permute-start.23
  71.5 2.8 collective-permute-start.2
  74.3 0.8 collective-permute-start.1
  75.1 0.9 collective-permute-start
  76.0 2.9 collective-permute-done.2
  79.0 2.4 collective-permute-done.1
  81.4 1.3 collective-permute-done
  82.8 3.2 collective-permute-start.20
  86.5 1.5 collective-permute-start.13
  88.0 1.1 add_convert_fusion
  89.1 14.2 %collective-permute-done.18 = bf16[2,80,1280]{2,1,0:T(8,128)(2,1)S(1)} collective-permute-done((bf16[2,80,1280]{2,1,0:T(8,128)(2,1)}, bf16[2,80,1280]{2,1,0:T(8,128)(2,1)S(1)}, u32[]{:S(2)}, u32[]{:S(2)}) %collective-permute-start.18) | collective-permute-done | bytes 409632 | tf_op jit(solution)/shard_map/ppermute | solution.py:39
  103.4 1.1 add_convert_fusion.1
  104.5 1.1 add_convert_fusion.2
  105.6 8.6 %collective-permute-done.9 = bf16[2,80,1280]{2,1,0:T(8,128)(2,1)S(1)} collective-permute-done((bf16[2,80,1280]{2,1,0:T(8,128)(2,1)}, bf16[2,80,1280]{2,1,0:T(8,128)(2,1)S(1)}, u32[]{:S(2)}, u32[]{:S(2)}) %collective-permute-start.9) | collective-permute-done | bytes 409632 | tf_op jit(solution)/shard_map/ppermute | solution.py:39
  114.3 1.1 add_convert_fusion.3
  115.6 2.0 collective-permute-start.10
  117.6 6.5 %collective-permute-done.19 = bf16[2,80,1280]{2,1,0:T(8,128)(2,1)S(1)} collective-permute-done((bf16[2,80,1280]{2,1,0:T(8,128)(2,1)S(1)}, bf16[2,80,1280]{2,1,0:T(8,128)(2,1)S(1)}, u32[]{:S(2)}, u32[]{:S(2)}) %collective-permute-start.19) | collective-permute-done | bytes 409632 | tf_op jit(solution)/shard_map/ppermute | solution.py:39
  124.4 2.0 collective-permute-start.25
  126.4 1.7 collective-permute-done.11
  128.1 8.8 %collective-permute-done.15 = bf16[2,80,1280]{2,1,0:T(8,128)(2,1)S(1)} collective-permute-done((bf16[2,80,1280]{2,1,0:T(8,128)(2,1)S(1)}, bf16[2,80,1280]{2,1,0:T(8,128)(2,1)S(1)}, u32[]{:S(2)}, u32[]{:S(2)}) %collective-permute-start.15) | collective-permute-done | bytes 409632 | tf_op jit(solution)/shard_map/ppermute | solution.py:39
  137.1 1.2 collective-permute-start.17
  138.3 2.2 collective-permute-start.16
  140.5 0.8 collective-permute-start.12
  142.0 3.0 collective-permute-start.27
  145.0 2.2 collective-permute-done.16
  147.4 1.9 collective-permute-done.27
  149.6 3.0 collective-permute-start.28
  153.6 2.9 collective-permute-start.37
  156.6 1.5 collective-permute-start.49
  158.2 1.8 collective-permute-start.31
  160.0 0.9 collective-permute-done.37.rest_10_
  160.9 2.6 collective-permute-start.38
  163.7 1.4 collective-permute-start.39
  165.1 9.4 %collective-permute-done.38.rest_11_ = bf16[80,1280]{1,0:T(8,128)(2,1)S(1)} collective-permute-done((bf16[80,1280]{1,0:T(8,128)(2,1)S(1)}, bf16[80,1280]{1,0:T(8,128)(2,1)S(1)}, u32[]{:S(2)}, u32[]{:S(2)}) %collective-permute-start.38) | collective-permute-done | bytes 204832 | tf_op jit(solution)/shard_map/ppermute | solution.py:39
  174.6 4.2 collective-permute-start.48
  178.8 3.7 collective-permute-done.40.rest_13_
  182.5 4.5 %collective-permute-start.47 = (f32[20,1280]{1,0:T(8,128)S(1)}, f32[20,1280]{1,0:T(8,128)S(1)}, u32[]{:S(2)}, u32[]{:S(2)}) collective-permute-start(f32[20,1280]{1,0:T(8,128)S(1)} %get-tuple-element.60), channel_id=1, source_target_pairs={{0,3},{1,0},{2,1},{3,2},{4,7},{5,4},{6,5},{7,6},{8,11},{9,8},{10,9... | collective-permute-start | bytes 307208 | tf_op jit(solution)/shard_map/ppermute | solution.py:39
  187.6 3.1 collective-permute-start.36
  190.7 0.8 collective-permute-done.47
  191.5 3.4 collective-permute-start.41
  195.0 2.0 collective-permute-start.44
  196.9 2.5 collective-permute-start.46
  199.5 4.6 %collective-permute-done.36.rest_8_ = bf16[2,80,1280]{2,1,0:T(8,128)(2,1)S(1)} collective-permute-done((bf16[2,80,1280]{2,1,0:T(8,128)(2,1)S(1)}, bf16[2,80,1280]{2,1,0:T(8,128)(2,1)S(1)}, u32[]{:S(2)}, u32[]{:S(2)}) %collective-permute-start.36) | collective-permute-done | bytes 409632 | tf_op jit(solution)/shard_map/ppermute | solution.py:39
  204.1 2.0 collective-permute-start.33
  206.1 3.0 collective-permute-done.42.rest_15_
  209.1 3.7 collective-permute-start.43
  212.9 0.8 pad_maximum_fusion.1.mean_ref
  213.7 2.4 outer_rows.1
  216.1 2.5 collective-permute-done.43.rest_16_
  218.6 3.7 collective-permute-done.45.rest_17_
  222.4 200.9 %place.1 = bf16[640,5120]{1,0:T(8,128)(2,1)} custom-call(s32[4]{0:T(128)} %pad_add_fusion.at_ref, bf16[80,1280]{1,0:T(8,128)(2,1)} %copy-done.1, bf16[80,1280]{1,0:T(8,128)(2,1)} %copy-done.5, bf16[80,1280]{1,0:T(8,128)(2,1)} %copy-done.6, bf16[80,1280]{1,0:T(8,128)(2,1)} %copy-done.7, bf16[2,80,1280]{2,1,0:T(8,128)(2,1)} %copy-done.14, ...), custom_call_target="tpu_custom_call" | custom-call | tf_op jit(solution)/shard_map/place/pallas_call | solution.py:250
  (106 shorter events, 7.1 us)
Async XLA Ops:
  0.6 23.8 %collective-permute-start.7 = (bf16[384,1280]{1,0:T(8,128)(2,1)}, bf16[384,1280]{1,0:T(8,128)(2,1)S(1)}, u32[]{:S(2)}, u32[]{:S(2)}) collective-permute-start(bf16[384,1280]{1,0:T(8,128)(2,1)} %g0_ref.1), channel_id=1, source_target_pairs={{0,64},{32,96},{64,0},{96,32},{1,65},{33,97},{65,1},{97,33},{2,66}... | collective-permute-start | bytes 2949128 | tf_op jit(solution)/shard_map/ppermute | solution.py:43
  3.7 20.7 %collective-permute-start.3 = (f32[192,384]{1,0:T(8,128)}, f32[192,384]{1,0:T(8,128)}, u32[]{:S(2)}, u32[]{:S(2)}) collective-permute-start(f32[192,384]{1,0:T(8,128)} %constant_dynamic-slice_fusion.3), channel_id=1, source_target_pairs={{0,32},{32,0},{64,96},{96,64},{1,33},{33,1},{65,97},{97,65},{2,34}... | collective-permute-start | bytes 884744 | tf_op jit(solution)/shard_map/ppermute | solution.py:43
  3.7 52.1 %collective-permute-start.6 = (bf16[384,1280]{1,0:T(8,128)(2,1)}, bf16[384,1280]{1,0:T(8,128)(2,1)S(1)}, u32[]{:S(2)}, u32[]{:S(2)}) collective-permute-start(bf16[384,1280]{1,0:T(8,128)(2,1)} %g0_ref.1), channel_id=1, source_target_pairs={{0,32},{32,0},{64,96},{96,64},{1,33},{33,1},{65,97},{97,65},{2,34}... | collective-permute-start | bytes 2949128 | tf_op jit(solution)/shard_map/ppermute | solution.py:43
  24.4 31.4 %copy-start.2 = (bf16[384,1280]{1,0:T(8,128)(2,1)}, bf16[384,1280]{1,0:T(8,128)(2,1)S(1)}, u32[]{:S(2)}) copy-start(bf16[384,1280]{1,0:T(8,128)(2,1)S(1)} %collective-permute-done.7.g2_ref) | copy-start | bytes 2949124
  24.4 31.4 %collective-permute-start.8 = (bf16[384,1280]{1,0:T(8,128)(2,1)S(1)}, bf16[384,1280]{1,0:T(8,128)(2,1)S(1)}, u32[]{:S(2)}, u32[]{:S(2)}) collective-permute-start(bf16[384,1280]{1,0:T(8,128)(2,1)S(1)} %collective-permute-done.7.g2_ref), channel_id=1, source_target_pairs={{0,32},{32,0},{64,96},{96,64},{1,33},{33,1},{65,97},{97,65},{2,34}... | collective-permute-start | bytes 2949128 | tf_op jit(solution)/shard_map/ppermute | solution.py:43
  25.6 9.3 %collective-permute-start.4 = (f32[192,384]{1,0:T(8,128)S(1)}, f32[192,384]{1,0:T(8,128)S(1)}, u32[]{:S(2)}, u32[]{:S(2)}) collective-permute-start(f32[192,384]{1,0:T(8,128)S(1)} %dynamic-slice_add_fusion), channel_id=1, source_target_pairs={{0,64},{32,96},{64,0},{96,32},{1,65},{33,97},{65,1},{97,33},{2,66}... | collective-permute-start | bytes 884744 | tf_op jit(solution)/shard_map/ppermute | solution.py:43
  35.0 8.5 %collective-permute-start.5 = (f32[192,384]{1,0:T(8,128)S(1)}, f32[192,384]{1,0:T(8,128)S(1)}, u32[]{:S(2)}, u32[]{:S(2)}) collective-permute-start(f32[192,384]{1,0:T(8,128)S(1)} %add.231), channel_id=1, source_target_pairs={{0,32},{32,0},{64,96},{96,64},{1,33},{33,1},{65,97},{97,65},{2,34}... | collective-permute-start | bytes 884744 | tf_op jit(solution)/shard_map/ppermute | solution.py:43
  68.3 55.7 %copy-start.13 = (bf16[4,80,1280]{2,1,0:T(8,128)(2,1)S(1)}, bf16[4,80,1280]{2,1,0:T(8,128)(2,1)}, u32[]{:S(2)}) copy-start(bf16[4,80,1280]{2,1,0:T(8,128)(2,1)} %get-tuple-element.30) | copy-start | bytes 2457604
  68.3 68.5 %copy-start.12 = (bf16[4,80,1280]{2,1,0:T(8,128)(2,1)S(1)}, bf16[4,80,1280]{2,1,0:T(8,128)(2,1)}, u32[]{:S(2)}) copy-start(bf16[4,80,1280]{2,1,0:T(8,128)(2,1)} %get-tuple-element.23) | copy-start | bytes 2457604
  68.4 18.2 %collective-permute-start.23 = (bf16[2,80,1280]{2,1,0:T(8,128)(2,1)}, bf16[2,80,1280]{2,1,0:T(8,128)(2,1)S(1)}, u32[]{:S(2)}, u32[]{:S(2)}) collective-permute-start(bf16[2,80,1280]{2,1,0:T(8,128)(2,1)} %get-tuple-element.36), channel_id=1, source_target_pairs={{0,12},{1,13},{2,14},{3,15},{4,0},{5,1},{6,2},{7,3},{8,4},{9,5},{1... | collective-permute-start | bytes 1228808 | tf_op jit(solution)/shard_map/ppermute | solution.py:39
  71.5 7.4 %collective-permute-start.2 = (f32[20,1280]{1,0:T(8,128)S(1)}, f32[20,1280]{1,0:T(8,128)S(1)}, u32[]{:S(2)}, u32[]{:S(2)}) collective-permute-start(f32[20,1280]{1,0:T(8,128)S(1)} %get-tuple-element.54), channel_id=1, source_target_pairs={{0,3},{1,0},{2,1},{3,2},{4,7},{5,4},{6,5},{7,6},{8,11},{9,8},{10,9... | collective-permute-start | bytes 307208 | tf_op jit(solution)/shard_map/ppermute | solution.py:39
  74.3 7.0 %collective-permute-start.1 = (f32[20,1280]{1,0:T(8,128)S(1)}, f32[20,1280]{1,0:T(8,128)S(1)}, u32[]{:S(2)}, u32[]{:S(2)}) collective-permute-start(f32[20,1280]{1,0:T(8,128)S(1)} %get-tuple-element.55), channel_id=1, source_target_pairs={{0,2},{1,3},{2,0},{3,1},{4,6},{5,7},{6,4},{7,5},{8,10},{9,11},{10,... | collective-permute-start | bytes 307208 | tf_op jit(solution)/shard_map/ppermute | solution.py:39
  75.1 7.5 %collective-permute-start = (f32[20,1280]{1,0:T(8,128)S(1)}, f32[20,1280]{1,0:T(8,128)S(1)}, u32[]{:S(2)}, u32[]{:S(2)}) collective-permute-start(f32[20,1280]{1,0:T(8,128)S(1)} %get-tuple-element.56), channel_id=1, source_target_pairs={{0,1},{1,2},{2,3},{3,0},{4,5},{5,6},{6,7},{7,4},{8,9},{9,10},{10,1... | collective-permute-start | bytes 307208 | tf_op jit(solution)/shard_map/ppermute | solution.py:39
  82.7 32.7 %collective-permute-start.22 = (bf16[2,80,1280]{2,1,0:T(8,128)(2,1)}, bf16[2,80,1280]{2,1,0:T(8,128)(2,1)S(1)}, u32[]{:S(2)}, u32[]{:S(2)}) collective-permute-start(bf16[2,80,1280]{2,1,0:T(8,128)(2,1)} %get-tuple-element.34), channel_id=1, source_target_pairs={{0,4},{1,5},{2,6},{3,7},{4,8},{5,9},{6,10},{7,11},{8,12},{9,13},{1... | collective-permute-start | bytes 1228808 | tf_op jit(solution)/shard_map/ppermute | solution.py:39
  82.8 32.7 %collective-permute-start.20 = (bf16[2,80,1280]{2,1,0:T(8,128)(2,1)}, bf16[2,80,1280]{2,1,0:T(8,128)(2,1)S(1)}, u32[]{:S(2)}, u32[]{:S(2)}) collective-permute-start(bf16[2,80,1280]{2,1,0:T(8,128)(2,1)} %get-tuple-element.33), channel_id=1, source_target_pairs={{0,12},{1,13},{2,14},{3,15},{4,0},{5,1},{6,2},{7,3},{8,4},{9,5},{1... | collective-permute-start | bytes 1228808 | tf_op jit(solution)/shard_map/ppermute | solution.py:39
  86.0 17.4 %collective-permute-start.18 = (bf16[2,80,1280]{2,1,0:T(8,128)(2,1)}, bf16[2,80,1280]{2,1,0:T(8,128)(2,1)S(1)}, u32[]{:S(2)}, u32[]{:S(2)}) collective-permute-start(bf16[2,80,1280]{2,1,0:T(8,128)(2,1)} %get-tuple-element.32), channel_id=1, source_target_pairs={{0,4},{1,5},{2,6},{3,7},{4,8},{5,9},{6,10},{7,11},{8,12},{9,13},{1... | collective-permute-start | bytes 1228808 | tf_op jit(solution)/shard_map/ppermute | solution.py:39
  86.0 18.5 %collective-permute-start.14 = (bf16[2,80,1280]{2,1,0:T(8,128)(2,1)}, bf16[2,80,1280]{2,1,0:T(8,128)(2,1)S(1)}, u32[]{:S(2)}, u32[]{:S(2)}) collective-permute-start(bf16[2,80,1280]{2,1,0:T(8,128)(2,1)} %get-tuple-element.29), channel_id=1, source_target_pairs={{0,3},{1,0},{2,1},{3,2},{4,7},{5,4},{6,5},{7,6},{8,11},{9,8},{10,9... | collective-permute-start | bytes 1228808 | tf_op jit(solution)/shard_map/ppermute | solution.py:39
  86.5 37.8 %collective-permute-start.13 = (bf16[2,80,1280]{2,1,0:T(8,128)(2,1)}, bf16[2,80,1280]{2,1,0:T(8,128)(2,1)S(1)}, u32[]{:S(2)}, u32[]{:S(2)}) collective-permute-start(bf16[2,80,1280]{2,1,0:T(8,128)(2,1)} %get-tuple-element.27), channel_id=1, source_target_pairs={{0,1},{1,2},{2,3},{3,0},{4,5},{5,6},{6,7},{7,4},{8,9},{9,10},{10,1... | collective-permute-start | bytes 1228808 | tf_op jit(solution)/shard_map/ppermute | solution.py:39
  103.3 10.9 %collective-permute-start.9 = (bf16[2,80,1280]{2,1,0:T(8,128)(2,1)}, bf16[2,80,1280]{2,1,0:T(8,128)(2,1)S(1)}, u32[]{:S(2)}, u32[]{:S(2)}) collective-permute-start(bf16[2,80,1280]{2,1,0:T(8,128)(2,1)} %get-tuple-element.25), channel_id=1, source_target_pairs={{0,1},{1,2},{2,3},{3,0},{4,5},{5,6},{6,7},{7,4},{8,9},{9,10},{10,1... | collective-permute-start | bytes 1228808 | tf_op jit(solution)/shard_map/ppermute | solution.py:39
  104.5 11.1 %collective-permute-start.24 = (bf16[2,80,1280]{2,1,0:T(8,128)(2,1)S(1)}, bf16[2,80,1280]{2,1,0:T(8,128)(2,1)S(1)}, u32[]{:S(2)}, u32[]{:S(2)}) collective-permute-start(bf16[2,80,1280]{2,1,0:T(8,128)(2,1)S(1)} %add_convert_fusion), channel_id=1, source_target_pairs={{0,12},{1,13},{2,14},{3,15},{4,0},{5,1},{6,2},{7,3},{8,4},{9,5},{1... | collective-permute-start | bytes 1228808 | tf_op jit(solution)/shard_map/ppermute | solution.py:39
  114.3 9.8 %collective-permute-start.19 = (bf16[2,80,1280]{2,1,0:T(8,128)(2,1)S(1)}, bf16[2,80,1280]{2,1,0:T(8,128)(2,1)S(1)}, u32[]{:S(2)}, u32[]{:S(2)}) collective-permute-start(bf16[2,80,1280]{2,1,0:T(8,128)(2,1)S(1)} %add_convert_fusion.1), channel_id=1, source_target_pairs={{0,4},{1,5},{2,6},{3,7},{4,8},{5,9},{6,10},{7,11},{8,12},{9,13},{1... | collective-permute-start | bytes 1228808 | tf_op jit(solution)/shard_map/ppermute | solution.py:39
  115.4 12.7 %collective-permute-start.11 = (bf16[2,80,1280]{2,1,0:T(8,128)(2,1)}, bf16[2,80,1280]{2,1,0:T(8,128)(2,1)S(1)}, u32[]{:S(2)}, u32[]{:S(2)}) collective-permute-start(bf16[2,80,1280]{2,1,0:T(8,128)(2,1)} %get-tuple-element.26), channel_id=1, source_target_pairs={{0,3},{1,0},{2,1},{3,2},{4,7},{5,4},{6,5},{7,6},{8,11},{9,8},{10,9... | collective-permute-start | bytes 1228808 | tf_op jit(solution)/shard_map/ppermute | solution.py:39
  115.5 21.4 %collective-permute-start.15 = (bf16[2,80,1280]{2,1,0:T(8,128)(2,1)S(1)}, bf16[2,80,1280]{2,1,0:T(8,128)(2,1)S(1)}, u32[]{:S(2)}, u32[]{:S(2)}) collective-permute-start(bf16[2,80,1280]{2,1,0:T(8,128)(2,1)S(1)} %add_convert_fusion.2), channel_id=1, source_target_pairs={{0,3},{1,0},{2,1},{3,2},{4,7},{5,4},{6,5},{7,6},{8,11},{9,8},{10,9... | collective-permute-start | bytes 1228808 | tf_op jit(solution)/shard_map/ppermute | solution.py:39
  115.6 21.3 %collective-permute-start.10 = (bf16[2,80,1280]{2,1,0:T(8,128)(2,1)S(1)}, bf16[2,80,1280]{2,1,0:T(8,128)(2,1)S(1)}, u32[]{:S(2)}, u32[]{:S(2)}) collective-permute-start(bf16[2,80,1280]{2,1,0:T(8,128)(2,1)S(1)} %add_convert_fusion.3), channel_id=1, source_target_pairs={{0,1},{1,2},{2,3},{3,0},{4,5},{5,6},{6,7},{7,4},{8,9},{9,10},{10,1... | collective-permute-start | bytes 1228808 | tf_op jit(solution)/shard_map/ppermute | solution.py:39
  124.3 16.2 %collective-permute-start.26 = (bf16[80,1280]{1,0:T(8,128)(2,1)S(1)}, bf16[80,1280]{1,0:T(8,128)(2,1)S(1)}, u32[]{:S(2)}, u32[]{:S(2)}) collective-permute-start(bf16[80,1280]{1,0:T(8,128)(2,1)S(1)} %get-tuple-element.46), channel_id=1, source_target_pairs={{0,2},{1,3},{2,0},{3,1},{4,6},{5,7},{6,4},{7,5},{8,10},{9,11},{10,... | collective-permute-start | bytes 614408 | tf_op jit(solution)/shard_map/ppermute | solution.py:39
  124.4 17.5 %collective-permute-start.25 = (bf16[80,1280]{1,0:T(8,128)(2,1)S(1)}, bf16[80,1280]{1,0:T(8,128)(2,1)S(1)}, u32[]{:S(2)}, u32[]{:S(2)}) collective-permute-start(bf16[80,1280]{1,0:T(8,128)(2,1)S(1)} %get-tuple-element.45), channel_id=1, source_target_pairs={{0,3},{1,0},{2,1},{3,2},{4,7},{5,4},{6,5},{7,6},{8,11},{9,8},{10,9... | collective-permute-start | bytes 614408 | tf_op jit(solution)/shard_map/ppermute | solution.py:39
  128.1 13.8 %collective-permute-start.21 = (bf16[80,1280]{1,0:T(8,128)(2,1)S(1)}, bf16[80,1280]{1,0:T(8,128)(2,1)S(1)}, u32[]{:S(2)}, u32[]{:S(2)}) collective-permute-start(bf16[80,1280]{1,0:T(8,128)(2,1)S(1)} %get-tuple-element.48), channel_id=1, source_target_pairs={{0,1},{1,2},{2,3},{3,0},{4,5},{5,6},{6,7},{7,4},{8,9},{9,10},{10,1... | collective-permute-start | bytes 614408 | tf_op jit(solution)/shard_map/ppermute | solution.py:39
  137.1 8.0 %collective-permute-start.17 = (bf16[80,1280]{1,0:T(8,128)(2,1)S(1)}, bf16[80,1280]{1,0:T(8,128)(2,1)S(1)}, u32[]{:S(2)}, u32[]{:S(2)}) collective-permute-start(bf16[80,1280]{1,0:T(8,128)(2,1)S(1)} %get-tuple-element.44), channel_id=1, source_target_pairs={{0,8},{1,9},{2,10},{3,11},{4,12},{5,13},{6,14},{7,15},{8,0},{9,1},... | collective-permute-start | bytes 614408 | tf_op jit(solution)/shard_map/ppermute | solution.py:39
  138.3 9.0 %collective-permute-start.16 = (bf16[80,1280]{1,0:T(8,128)(2,1)S(1)}, bf16[80,1280]{1,0:T(8,128)(2,1)S(1)}, u32[]{:S(2)}, u32[]{:S(2)}) collective-permute-start(bf16[80,1280]{1,0:T(8,128)(2,1)S(1)} %get-tuple-element.43), channel_id=1, source_target_pairs={{0,12},{1,13},{2,14},{3,15},{4,0},{5,1},{6,2},{7,3},{8,4},{9,5},{1... | collective-permute-start | bytes 614408 | tf_op jit(solution)/shard_map/ppermute | solution.py:39
  140.5 7.0 %collective-permute-start.12 = (bf16[80,1280]{1,0:T(8,128)(2,1)S(1)}, bf16[80,1280]{1,0:T(8,128)(2,1)S(1)}, u32[]{:S(2)}, u32[]{:S(2)}) collective-permute-start(bf16[80,1280]{1,0:T(8,128)(2,1)S(1)} %get-tuple-element.47), channel_id=1, source_target_pairs={{0,4},{1,5},{2,6},{3,7},{4,8},{5,9},{6,10},{7,11},{8,12},{9,13},{1... | collective-permute-start | bytes 614408 | tf_op jit(solution)/shard_map/ppermute | solution.py:39
  142.0 7.3 %collective-permute-start.27 = (bf16[80,1280]{1,0:T(8,128)(2,1)S(1)}, bf16[80,1280]{1,0:T(8,128)(2,1)S(1)}, u32[]{:S(2)}, u32[]{:S(2)}) collective-permute-start(bf16[80,1280]{1,0:T(8,128)(2,1)S(1)} %fusion.3), channel_id=1, source_target_pairs={{0,16},{1,17},{2,18},{3,19},{4,20},{5,21},{6,22},{7,23},{8,24},{9,... | collective-permute-start | bytes 614408 | tf_op jit(solution)/shard_map/ppermute | solution.py:39
  149.6 72.7 %copy-start.1 = (bf16[80,1280]{1,0:T(8,128)(2,1)}, bf16[80,1280]{1,0:T(8,128)(2,1)S(1)}, u32[]{:S(2)}) copy-start(bf16[80,1280]{1,0:T(8,128)(2,1)S(1)} %fusion.rest_0_) | copy-start | bytes 614404
  149.6 8.5 %collective-permute-start.28 = (bf16[80,1280]{1,0:T(8,128)(2,1)S(1)}, bf16[80,1280]{1,0:T(8,128)(2,1)S(1)}, u32[]{:S(2)}, u32[]{:S(2)}) collective-permute-start(bf16[80,1280]{1,0:T(8,128)(2,1)S(1)} %fusion.rest_0_), channel_id=1, source_target_pairs={{0,12},{1,13},{2,14},{3,15},{4,0},{5,1},{6,2},{7,3},{8,4},{9,5},{1... | collective-permute-start | bytes 614408 | tf_op jit(solution)/shard_map/ppermute | solution.py:39
  152.7 10.8 %collective-permute-start.29 = (bf16[80,1280]{1,0:T(8,128)(2,1)S(1)}, bf16[80,1280]{1,0:T(8,128)(2,1)S(1)}, u32[]{:S(2)}, u32[]{:S(2)}) collective-permute-start(bf16[80,1280]{1,0:T(8,128)(2,1)S(1)} %fusion.rest_0_), channel_id=1, source_target_pairs={{0,8},{1,9},{2,10},{3,11},{4,12},{5,13},{6,14},{7,15},{8,0},{9,1},... | collective-permute-start | bytes 614408 | tf_op jit(solution)/shard_map/ppermute | solution.py:39
  153.2 10.2 %collective-permute-start.30 = (bf16[80,1280]{1,0:T(8,128)(2,1)S(1)}, bf16[80,1280]{1,0:T(8,128)(2,1)S(1)}, u32[]{:S(2)}, u32[]{:S(2)}) collective-permute-start(bf16[80,1280]{1,0:T(8,128)(2,1)S(1)} %fusion.rest_0_), channel_id=1, source_target_pairs={{0,4},{1,5},{2,6},{3,7},{4,8},{5,9},{6,10},{7,11},{8,12},{9,13},{1... | collective-permute-start | bytes 614408 | tf_op jit(solution)/shard_map/ppermute | solution.py:39
  153.6 7.3 %collective-permute-start.37 = (bf16[80,1280]{1,0:T(8,128)(2,1)S(1)}, bf16[80,1280]{1,0:T(8,128)(2,1)S(1)}, u32[]{:S(2)}, u32[]{:S(2)}) collective-permute-start(bf16[80,1280]{1,0:T(8,128)(2,1)S(1)} %fusion.rest_0_), channel_id=1, source_target_pairs={{0,16},{1,17},{2,18},{3,19},{4,20},{5,21},{6,22},{7,23},{8,24},{9,... | collective-permute-start | bytes 614408 | tf_op jit(solution)/shard_map/ppermute | solution.py:39
  156.6 30.5 %collective-permute-start.49 = (f32[20,1280]{1,0:T(8,128)S(1)}, f32[20,1280]{1,0:T(8,128)S(1)}, u32[]{:S(2)}, u32[]{:S(2)}) collective-permute-start(f32[20,1280]{1,0:T(8,128)S(1)} %get-tuple-element.58), channel_id=1, source_target_pairs={{0,1},{1,2},{2,3},{3,0},{4,5},{5,6},{6,7},{7,4},{8,9},{9,10},{10,1... | collective-permute-start | bytes 307208 | tf_op jit(solution)/shard_map/ppermute | solution.py:39
  158.1 64.2 %copy-start.5 = (bf16[80,1280]{1,0:T(8,128)(2,1)}, bf16[80,1280]{1,0:T(8,128)(2,1)S(1)}, u32[]{:S(2)}) copy-start(bf16[80,1280]{1,0:T(8,128)(2,1)S(1)} %collective-permute-done.28.rest_1_) | copy-start | bytes 614404
  158.2 36.7 %collective-permute-start.31 = (bf16[2,80,1280]{2,1,0:T(8,128)(2,1)S(1)}, bf16[2,80,1280]{2,1,0:T(8,128)(2,1)S(1)}, u32[]{:S(2)}, u32[]{:S(2)}) collective-permute-start(bf16[2,80,1280]{2,1,0:T(8,128)(2,1)S(1)} %pad_maximum_fusion.2), channel_id=1, source_target_pairs={{0,3},{1,0},{2,1},{3,2},{4,7},{5,4},{6,5},{7,6},{8,11},{9,8},{10,9... | collective-permute-start | bytes 1228808 | tf_op jit(solution)/shard_map/ppermute | solution.py:39
  160.9 61.5 %copy-start.8 = (bf16[80,1280]{1,0:T(8,128)(2,1)}, bf16[80,1280]{1,0:T(8,128)(2,1)S(1)}, u32[]{:S(2)}) copy-start(bf16[80,1280]{1,0:T(8,128)(2,1)S(1)} %collective-permute-done.37.rest_10_) | copy-start | bytes 614404
  160.9 13.7 %collective-permute-start.38 = (bf16[80,1280]{1,0:T(8,128)(2,1)S(1)}, bf16[80,1280]{1,0:T(8,128)(2,1)S(1)}, u32[]{:S(2)}, u32[]{:S(2)}) collective-permute-start(bf16[80,1280]{1,0:T(8,128)(2,1)S(1)} %collective-permute-done.37.rest_10_), channel_id=1, source_target_pairs={{0,3},{1,0},{2,1},{3,2},{4,7},{5,4},{6,5},{7,6},{8,11},{9,8},{10,9... | collective-permute-start | bytes 614408 | tf_op jit(solution)/shard_map/ppermute | solution.py:39
  163.5 58.9 %copy-start.6 = (bf16[80,1280]{1,0:T(8,128)(2,1)}, bf16[80,1280]{1,0:T(8,128)(2,1)S(1)}, u32[]{:S(2)}) copy-start(bf16[80,1280]{1,0:T(8,128)(2,1)S(1)} %collective-permute-done.29.rest_2_) | copy-start | bytes 614404
  163.5 58.9 %copy-start.7 = (bf16[80,1280]{1,0:T(8,128)(2,1)}, bf16[80,1280]{1,0:T(8,128)(2,1)S(1)}, u32[]{:S(2)}) copy-start(bf16[80,1280]{1,0:T(8,128)(2,1)S(1)} %collective-permute-done.30.rest_3_) | copy-start | bytes 614404
  163.5 31.4 %collective-permute-start.32 = (bf16[2,80,1280]{2,1,0:T(8,128)(2,1)S(1)}, bf16[2,80,1280]{2,1,0:T(8,128)(2,1)S(1)}, u32[]{:S(2)}, u32[]{:S(2)}) collective-permute-start(bf16[2,80,1280]{2,1,0:T(8,128)(2,1)S(1)} %pad_maximum_fusion.3), channel_id=1, source_target_pairs={{0,3},{1,0},{2,1},{3,2},{4,7},{5,4},{6,5},{7,6},{8,11},{9,8},{10,9... | collective-permute-start | bytes 1228808 | tf_op jit(solution)/shard_map/ppermute | solution.py:39
  163.7 10.9 %collective-permute-start.39 = (bf16[80,1280]{1,0:T(8,128)(2,1)S(1)}, bf16[80,1280]{1,0:T(8,128)(2,1)S(1)}, u32[]{:S(2)}, u32[]{:S(2)}) collective-permute-start(bf16[80,1280]{1,0:T(8,128)(2,1)S(1)} %collective-permute-done.37.rest_10_), channel_id=1, source_target_pairs={{0,2},{1,3},{2,0},{3,1},{4,6},{5,7},{6,4},{7,5},{8,10},{9,11},{10,... | collective-permute-start | bytes 614408 | tf_op jit(solution)/shard_map/ppermute | solution.py:39
  174.5 47.8 %copy-start.9 = (bf16[80,1280]{1,0:T(8,128)(2,1)}, bf16[80,1280]{1,0:T(8,128)(2,1)S(1)}, u32[]{:S(2)}) copy-start(bf16[80,1280]{1,0:T(8,128)(2,1)S(1)} %collective-permute-done.38.rest_11_) | copy-start | bytes 614404
  174.5 8.0 %collective-permute-start.40 = (bf16[80,1280]{1,0:T(8,128)(2,1)S(1)}, bf16[80,1280]{1,0:T(8,128)(2,1)S(1)}, u32[]{:S(2)}, u32[]{:S(2)}) collective-permute-start(bf16[80,1280]{1,0:T(8,128)(2,1)S(1)} %collective-permute-done.37.rest_10_), channel_id=1, source_target_pairs={{0,1},{1,2},{2,3},{3,0},{4,5},{5,6},{6,7},{7,4},{8,9},{9,10},{10,1... | collective-permute-start | bytes 614408 | tf_op jit(solution)/shard_map/ppermute | solution.py:39
  174.6 47.8 %copy-start.10 = (bf16[80,1280]{1,0:T(8,128)(2,1)}, bf16[80,1280]{1,0:T(8,128)(2,1)S(1)}, u32[]{:S(2)}) copy-start(bf16[80,1280]{1,0:T(8,128)(2,1)S(1)} %collective-permute-done.39.rest_12_) | copy-start | bytes 614404
  174.6 13.0 %collective-permute-start.48 = (f32[20,1280]{1,0:T(8,128)S(1)}, f32[20,1280]{1,0:T(8,128)S(1)}, u32[]{:S(2)}, u32[]{:S(2)}) collective-permute-start(f32[20,1280]{1,0:T(8,128)S(1)} %get-tuple-element.59), channel_id=1, source_target_pairs={{0,2},{1,3},{2,0},{3,1},{4,6},{5,7},{6,4},{7,5},{8,10},{9,11},{10,... | collective-permute-start | bytes 307208 | tf_op jit(solution)/shard_map/ppermute | solution.py:39
  182.5 39.9 %copy-start.11 = (bf16[80,1280]{1,0:T(8,128)(2,1)}, bf16[80,1280]{1,0:T(8,128)(2,1)S(1)}, u32[]{:S(2)}) copy-start(bf16[80,1280]{1,0:T(8,128)(2,1)S(1)} %collective-permute-done.40.rest_13_) | copy-start | bytes 614404
  182.5 8.9 %collective-permute-start.47 = (f32[20,1280]{1,0:T(8,128)S(1)}, f32[20,1280]{1,0:T(8,128)S(1)}, u32[]{:S(2)}, u32[]{:S(2)}) collective-permute-start(f32[20,1280]{1,0:T(8,128)S(1)} %get-tuple-element.60), channel_id=1, source_target_pairs={{0,3},{1,0},{2,1},{3,2},{4,7},{5,4},{6,5},{7,6},{8,11},{9,8},{10,9... | collective-permute-start | bytes 307208 | tf_op jit(solution)/shard_map/ppermute | solution.py:39
  187.1 9.9 %collective-permute-start.34 = (bf16[2,80,1280]{2,1,0:T(8,128)(2,1)S(1)}, bf16[2,80,1280]{2,1,0:T(8,128)(2,1)S(1)}, u32[]{:S(2)}, u32[]{:S(2)}) collective-permute-start(bf16[2,80,1280]{2,1,0:T(8,128)(2,1)S(1)} %pad_maximum_fusion.3), channel_id=1, source_target_pairs={{0,1},{1,2},{2,3},{3,0},{4,5},{5,6},{6,7},{7,4},{8,9},{9,10},{10,1... | collective-permute-start | bytes 1228808 | tf_op jit(solution)/shard_map/ppermute | solution.py:39
  187.6 16.4 %collective-permute-start.36 = (bf16[2,80,1280]{2,1,0:T(8,128)(2,1)S(1)}, bf16[2,80,1280]{2,1,0:T(8,128)(2,1)S(1)}, u32[]{:S(2)}, u32[]{:S(2)}) collective-permute-start(bf16[2,80,1280]{2,1,0:T(8,128)(2,1)S(1)} %pad_maximum_fusion.2), channel_id=1, source_target_pairs={{0,1},{1,2},{2,3},{3,0},{4,5},{5,6},{6,7},{7,4},{8,9},{9,10},{10,1... | collective-permute-start | bytes 1228808 | tf_op jit(solution)/shard_map/ppermute | solution.py:39
  191.5 14.7 %collective-permute-start.41 = (bf16[2,80,1280]{2,1,0:T(8,128)(2,1)S(1)}, bf16[2,80,1280]{2,1,0:T(8,128)(2,1)}, u32[]{:S(2)}, u32[]{:S(2)}) collective-permute-start(bf16[2,80,1280]{2,1,0:T(8,128)(2,1)S(1)} %pad_maximum_fusion.4), channel_id=1, source_target_pairs={{0,12},{1,13},{2,14},{3,15},{4,0},{5,1},{6,2},{7,3},{8,4},{9,5},{1... | collective-permute-start | bytes 1228808 | tf_op jit(solution)/shard_map/ppermute | solution.py:39
  194.9 27.5 %copy-start.14 = (bf16[2,80,1280]{2,1,0:T(8,128)(2,1)}, bf16[2,80,1280]{2,1,0:T(8,128)(2,1)S(1)}, u32[]{:S(2)}) copy-start(bf16[2,80,1280]{2,1,0:T(8,128)(2,1)S(1)} %collective-permute-done.31.rest_4_) | copy-start | bytes 1228804
  194.9 14.2 %collective-permute-start.42 = (bf16[2,80,1280]{2,1,0:T(8,128)(2,1)S(1)}, bf16[2,80,1280]{2,1,0:T(8,128)(2,1)S(1)}, u32[]{:S(2)}, u32[]{:S(2)}) collective-permute-start(bf16[2,80,1280]{2,1,0:T(8,128)(2,1)S(1)} %pad_maximum_fusion.5), channel_id=1, source_target_pairs={{0,12},{1,13},{2,14},{3,15},{4,0},{5,1},{6,2},{7,3},{8,4},{9,5},{1... | collective-permute-start | bytes 1228808 | tf_op jit(solution)/shard_map/ppermute | solution.py:39
  195.0 27.4 %copy-start.15 = (bf16[2,80,1280]{2,1,0:T(8,128)(2,1)}, bf16[2,80,1280]{2,1,0:T(8,128)(2,1)S(1)}, u32[]{:S(2)}) copy-start(bf16[2,80,1280]{2,1,0:T(8,128)(2,1)S(1)} %collective-permute-done.32.rest_5_) | copy-start | bytes 1228804
  195.0 17.9 %collective-permute-start.44 = (bf16[2,80,1280]{2,1,0:T(8,128)(2,1)S(1)}, bf16[2,80,1280]{2,1,0:T(8,128)(2,1)}, u32[]{:S(2)}, u32[]{:S(2)}) collective-permute-start(bf16[2,80,1280]{2,1,0:T(8,128)(2,1)S(1)} %pad_maximum_fusion.5), channel_id=1, source_target_pairs={{0,4},{1,5},{2,6},{3,7},{4,8},{5,9},{6,10},{7,11},{8,12},{9,13},{1... | collective-permute-start | bytes 1228808 | tf_op jit(solution)/shard_map/ppermute | solution.py:39
  196.9 25.5 %copy-start.16 = (bf16[2,80,1280]{2,1,0:T(8,128)(2,1)}, bf16[2,80,1280]{2,1,0:T(8,128)(2,1)S(1)}, u32[]{:S(2)}) copy-start(bf16[2,80,1280]{2,1,0:T(8,128)(2,1)S(1)} %collective-permute-done.34.rest_9_) | copy-start | bytes 1228804
  196.9 19.2 %collective-permute-start.46 = (bf16[2,80,1280]{2,1,0:T(8,128)(2,1)S(1)}, bf16[2,80,1280]{2,1,0:T(8,128)(2,1)}, u32[]{:S(2)}, u32[]{:S(2)}) collective-permute-start(bf16[2,80,1280]{2,1,0:T(8,128)(2,1)S(1)} %pad_maximum_fusion.4), channel_id=1, source_target_pairs={{0,4},{1,5},{2,6},{3,7},{4,8},{5,9},{6,10},{7,11},{8,12},{9,13},{1... | collective-permute-start | bytes 1228808 | tf_op jit(solution)/shard_map/ppermute | solution.py:39
  204.1 12.1 %collective-permute-start.33 = (bf16[2,80,1280]{2,1,0:T(8,128)(2,1)S(1)}, bf16[2,80,1280]{2,1,0:T(8,128)(2,1)}, u32[]{:S(2)}, u32[]{:S(2)}) collective-permute-start(bf16[2,80,1280]{2,1,0:T(8,128)(2,1)S(1)} %collective-permute-done.31.rest_4_), channel_id=1, source_target_pairs={{0,3},{1,0},{2,1},{3,2},{4,7},{5,4},{6,5},{7,6},{8,11},{9,8},{10,9... | collective-permute-start | bytes 1228808 | tf_op jit(solution)/shard_map/ppermute | solution.py:39
  206.1 10.0 %collective-permute-start.35 = (bf16[2,80,1280]{2,1,0:T(8,128)(2,1)S(1)}, bf16[2,80,1280]{2,1,0:T(8,128)(2,1)}, u32[]{:S(2)}, u32[]{:S(2)}) collective-permute-start(bf16[2,80,1280]{2,1,0:T(8,128)(2,1)S(1)} %collective-permute-done.34.rest_9_), channel_id=1, source_target_pairs={{0,1},{1,2},{2,3},{3,0},{4,5},{5,6},{6,7},{7,4},{8,9},{9,10},{10,1... | collective-permute-start | bytes 1228808 | tf_op jit(solution)/shard_map/ppermute | solution.py:39
  209.1 9.5 %collective-permute-start.43 = (bf16[2,80,1280]{2,1,0:T(8,128)(2,1)}, bf16[2,80,1280]{2,1,0:T(8,128)(2,1)}, u32[]{:S(2)}, u32[]{:S(2)}) collective-permute-start(bf16[2,80,1280]{2,1,0:T(8,128)(2,1)} %collective-permute-done.41.rest_14_), channel_id=1, source_target_pairs={{0,12},{1,13},{2,14},{3,15},{4,0},{5,1},{6,2},{7,3},{8,4},{9,5},{1... | collective-permute-start | bytes 1228808 | tf_op jit(solution)/shard_map/ppermute | solution.py:39
  212.8 9.5 %collective-permute-start.45 = (bf16[2,80,1280]{2,1,0:T(8,128)(2,1)}, bf16[2,80,1280]{2,1,0:T(8,128)(2,1)}, u32[]{:S(2)}, u32[]{:S(2)}) collective-permute-start(bf16[2,80,1280]{2,1,0:T(8,128)(2,1)} %collective-permute-done.44.rest_19_), channel_id=1, source_target_pairs={{0,4},{1,5},{2,6},{3,7},{4,8},{5,9},{6,10},{7,11},{8,12},{9,13},{1... | collective-permute-start | bytes 1228808 | tf_op jit(solution)/shard_map/ppermute | solution.py:39
  (5 other events, 37.7 us)

commit v2 on v1

v2 whole, which is shorter than its diff:
```python
import math

import jax
import jax.numpy as jnp
from jax import lax
from jax.experimental import pallas as pl
from jax.experimental.pallas import tpu as pltpu
from jax.sharding import PartitionSpec as P

HD = 128
NX, NY, NZ = 4, 4, 2
TILE_R = 80
HALF_C = 640

inner_rate = 0.8
outer_rate = 0.7
outer_mu = 0.9
neg_big = -1e30
bf16 = jnp.bfloat16
f32 = jnp.float32
VMEM_LIMIT = 60 << 20


def worker_of(zh, y, x):
    return (zh % NZ) * NX * NY + (y % NY) * NX + (x % NX)


def move(value, axis, step):
    pairs = []
    for zh in range(NZ):
        for y in range(NY):
            for x in range(NX):
                to = {
                    "x": worker_of(zh, y, x + step),
                    "y": worker_of(zh, y + step, x),
                    "z": worker_of(zh + step, y, x),
                }[axis]
                pairs.append((worker_of(zh, y, x), to))
    return lax.ppermute(value, "worker", pairs)


def swap_tp(value, bit):
    return lax.ppermute(value, "tp", [(t, t ^ bit) for t in range(4)])


def attention_body(q_ref, k_ref, v_ref, seg_row_ref, seg_col_ref, ct_ref, gram_ref):
    tokens, width = q_ref.shape
    scale = 1.0 / math.sqrt(HD)
    blocks = tokens // HD
    for h in range(width // HD):
        cols = slice(h * HD, (h + 1) * HD)
        for b in range(blocks):
            queries = slice(b * HD, (b + 1) * HD)
            seen = (b + 1) * HD
            scores = lax.dot_general(
                k_ref[:seen, cols], q_ref[queries, cols], (((1,), (1,)), ((), ())),
                preferred_element_type=f32,
            ) * scale
            key_at = lax.broadcasted_iota(jnp.int32, (seen, HD), 0)
            query_at = lax.broadcasted_iota(jnp.int32, (seen, HD), 1) + b * HD
            allowed = (key_at <= query_at) & (seg_col_ref[:seen, :] == seg_row_ref[:, queries])
            scores = jnp.where(allowed, scores, neg_big)
            exp_scores = jnp.exp(scores - jnp.max(scores, axis=0, keepdims=True))
            total = jnp.sum(exp_scores, axis=0, keepdims=True)
            weights = (exp_scores * (1.0 / total)).astype(bf16)
            ct_ref[cols, queries] = lax.dot_general(
                v_ref[:seen, cols], weights, (((0,), (0,)), ((), ())),
                preferred_element_type=f32,
            ).astype(bf16)
    gram_ref[...] = lax.dot_general(
        ct_ref[...], ct_ref[...], (((0,), (0,)), ((), ())), preferred_element_type=f32
    )


def attention(queries, keys, values, segments):
    tokens, width = queries.shape
    return pl.pallas_call(
        attention_body,
        out_shape=(
            jax.ShapeDtypeStruct((width, tokens), bf16),
            jax.ShapeDtypeStruct((tokens, tokens), f32),
        ),
        compiler_params=pltpu.CompilerParams(vmem_limit_bytes=VMEM_LIMIT),
        cost_estimate=pl.CostEstimate(
            flops=4_000_000_000, bytes_accessed=2_600_000, transcendentals=500_000
        ),
        name="attention",
    )(queries, keys, values, segments.reshape(1, tokens), segments.reshape(tokens, 1))


def column_of(tp, half, quarter):
    first = (tp ^ (2 * half) ^ (quarter // 2)) * (2 * HALF_C) + (quarter % 2) * HALF_C
    return pl.multiple_of(first, HALF_C)


def row_of(zh, y, j, ky):
    return pl.multiple_of((zh ^ j) * (NY * TILE_R) + ((y + ky) % NY) * TILE_R, TILE_R)


SEND_ORDER = (2, 1, 3, 0)


def pseudo_body(at_ref, scale_ref, ct_ref, g0_ref, g1_ref, g2_ref, g3_ref, drift_ref, *rest):
    outs, (drift_buf, g_buf, rows_buf, out_buf, drift_sems, g_sems, out_sems) = rest[:8], rest[8:]
    x, y, zh, tp = at_ref[0], at_ref[1], at_ref[2], at_ref[3]
    scale = scale_ref[0]
    steps = [(k, half) for k in SEND_ORDER for half in range(2)]

    def drift_copy(slot):
        k, half = steps[slot]
        return pltpu.make_async_copy(
            drift_ref.at[0, :, pl.ds(column_of(tp, half, (x + k) % NX), HALF_C)],
            drift_buf.at[slot], drift_sems.at[slot],
        )

    def g_copy(slot, ref):
        quarter = (x + steps[slot][0]) % NX
        return pltpu.make_async_copy(
            ref.at[:, pl.ds(pl.multiple_of((quarter % 2) * HALF_C, HALF_C), HALF_C)],
            g_buf.at[slot], g_sems.at[slot],
        )

    for slot, (k, half) in enumerate(steps):
        near, far = (g0_ref, g1_ref) if half == 0 else (g2_ref, g3_ref)
        quarter = (x + k) % NX
        pl.when(quarter < 2)(lambda slot=slot, near=near: g_copy(slot, near).start())
        pl.when(quarter >= 2)(lambda slot=slot, far=far: g_copy(slot, far).start())
        drift_copy(slot).start()
    for j in range(2):
        for ky in range(NY):
            first = (j * NY + ky) * TILE_R
            rows_buf[first:first + TILE_R, :] = ct_ref[pl.ds(row_of(zh, y, j, ky), TILE_R), :]

    copies = []
    for slot, (k, half) in enumerate(steps):
        cols = slice(half * HALF_C, (half + 1) * HALF_C)
        g_copy(slot, g0_ref).wait()
        drift_copy(slot).wait()
        for j in range(2):
            rows = slice(j * NY * TILE_R, (j + 1) * NY * TILE_R)
            block = jnp.dot(rows_buf[rows, :], g_buf[slot], preferred_element_type=f32)
            for ky in range(NY):
                own = drift_buf[slot, pl.ds(row_of(zh, y, j, ky), TILE_R), :]
                value = block[ky * TILE_R:(ky + 1) * TILE_R] * scale + own.astype(f32)
                group, index = (k, ky) if j == 0 else (4 + ky, k)
                out_buf[group, index, :, cols] = value.astype(bf16)
        if half == 1:
            made = [(k, None)] + [(4 + ky, k) for ky in range(NY)]
            for group, index in made:
                src, dst = out_buf.at[group], outs[group]
                if index is not None:
                    src, dst = src.at[index], dst.at[index]
                copies.append(pltpu.make_async_copy(src, dst, out_sems.at[len(copies)]))
                copies[-1].start()
    for one in copies:
        one.wait()


def pseudo_gradient(at, scale, ct, pieces, drift):
    block = jax.ShapeDtypeStruct((4, TILE_R, 2 * HALF_C), bf16)
    smem = pl.BlockSpec(memory_space=pltpu.SMEM)
    hbm = pl.BlockSpec(memory_space=pl.ANY)
    tokens, rows = ct.shape[1], ct.shape[0]
    return pl.pallas_call(
        pseudo_body,
        out_shape=(block,) * 8,
        in_specs=[smem, smem, pl.BlockSpec(memory_space=pltpu.VMEM)] + [hbm] * 5,
        out_specs=(hbm,) * 8,
        scratch_shapes=[
            pltpu.VMEM((8, rows, HALF_C), bf16),
            pltpu.VMEM((8, tokens, HALF_C), bf16),
            pltpu.VMEM(ct.shape, bf16),
            pltpu.VMEM((8, 4, TILE_R, 2 * HALF_C), bf16),
            pltpu.SemaphoreType.DMA((8,)),
            pltpu.SemaphoreType.DMA((8,)),
            pltpu.SemaphoreType.DMA((20,)),
        ],
        compiler_params=pltpu.CompilerParams(vmem_limit_bytes=VMEM_LIMIT),
        cost_estimate=pl.CostEstimate(
            flops=2 * rows * tokens * 5120, bytes_accessed=18_000_000, transcendentals=0
        ),
        name="pseudo_gradient",
    )(at, scale, ct, *pieces, drift)


def base_body(at_ref, master_ref, momentum_ref, base_ref):
    tp = at_ref[3]
    for quarter in range(NX):
        for half in range(2):
            cols = pl.ds(column_of(tp, half, quarter), HALF_C)
            base_ref[quarter, :, half * HALF_C:(half + 1) * HALF_C] = (
                master_ref[:, cols] - (outer_rate * outer_mu * outer_mu) * momentum_ref[:, cols]
            )


def base_rows(at, master, momentum):
    vmem = pl.BlockSpec(memory_space=pltpu.VMEM)
    return pl.pallas_call(
        base_body,
        out_shape=jax.ShapeDtypeStruct((NX, master.shape[0], 2 * HALF_C), f32),
        in_specs=[pl.BlockSpec(memory_space=pltpu.SMEM), vmem, vmem],
        out_specs=vmem,
        name="base_rows",
    )(at, master, momentum)


def outer_body(at_ref, master_ref, momentum_ref, mean_ref, new_master_ref, new_momentum_ref):
    x, tp = at_ref[0], at_ref[3]
    for quarter in range(NX):
        for half in range(2):
            cols = pl.ds(column_of(tp, half, quarter), HALF_C)
            mean = mean_ref[(quarter - x + NX) % NX, :, half * HALF_C:(half + 1) * HALF_C]
            new = outer_mu * momentum_ref[:, cols] + mean
            new_momentum_ref[:, cols] = new
            new_master_ref[:, cols] = master_ref[:, cols] - outer_rate * (mean + outer_mu * new)


def outer_rows(at, master, momentum, mean):
    vmem = pl.BlockSpec(memory_space=pltpu.VMEM)
    out = jax.ShapeDtypeStruct(master.shape, f32)
    return pl.pallas_call(
        outer_body,
        out_shape=(out, out),
        in_specs=[pl.BlockSpec(memory_space=pltpu.SMEM), vmem, vmem, vmem],
        out_specs=(vmem, vmem),
        name="outer_rows",
    )(at, master, momentum, mean)


def place_body(at_ref, *rest):
    blocks, out_ref, (stage, in_sems, out_sems) = rest[:8], rest[8], rest[9:]
    x, y, zh, tp = at_ref[0], at_ref[1], at_ref[2], at_ref[3]
    copies = []
    for j in range(2):
        for large in range(4):
            for small in range(4):
                ky, kx = (small, large) if j == 0 else (large, small)
                for half in range(2):
                    copies.append(pltpu.make_async_copy(
                        blocks[4 * j + large].at[small, :, half * HALF_C:(half + 1) * HALF_C],
                        stage.at[pl.ds(row_of(zh, y, j, ky), TILE_R),
                                 pl.ds(column_of(tp, half, (x + kx) % NX), HALF_C)],
                        in_sems.at[len(copies)],
                    ))
    for one in copies:
        one.start()
    rows = NY * TILE_R
    outs = []
    for j in range(2):
        for one in copies[32 * j:32 * (j + 1)]:
            one.wait()
        at = pl.ds(pl.multiple_of((zh ^ j) * rows, rows), rows)
        outs.append(pltpu.make_async_copy(stage.at[at], out_ref.at[at], out_sems.at[j]))
        outs[-1].start()
    for one in outs:
        one.wait()


def place(at, blocks, rows, width):
    hbm = pl.BlockSpec(memory_space=pl.ANY)
    return pl.pallas_call(
        place_body,
        out_shape=jax.ShapeDtypeStruct((rows, width), bf16),
        in_specs=[pl.BlockSpec(memory_space=pltpu.SMEM)] + [hbm] * 8,
        out_specs=hbm,
        scratch_shapes=[
            pltpu.VMEM((rows, width), bf16),
            pltpu.SemaphoreType.DMA((64,)),
            pltpu.SemaphoreType.DMA((2,)),
        ],
        compiler_params=pltpu.CompilerParams(vmem_limit_bytes=VMEM_LIMIT),
        name="place",
    )(at, *blocks)


def add(*terms):
    total = terms[0].astype(f32)
    for term in terms[1:]:
        total = total + term.astype(f32)
    return total


def ring(values, axis, sign):
    two = move(values[1], axis, 2 * sign)
    one = move(values[0], axis, sign)
    three = move(values[2], axis, -sign)
    return [one, two, three]


def reduce_blocks(blocks, axis):
    return add(blocks[0], *ring(blocks[1:], axis, 1))


def reduce_tiles(tiles, axis):
    sent = tiles.astype(bf16)
    return add(tiles[0], *ring([sent[1], sent[2], sent[3]], axis, 1))


def rounded(value):
    return lax.reduce_precision(value, 8, 7)


def per_device(queries, keys, values, out_grad, segments, drift, master, momentum):
    tp = lax.axis_index("tp")
    worker = lax.axis_index("worker")
    x, y, zh = worker % NX, (worker // NX) % NY, worker // (NX * NY)
    at = jnp.stack([x, y, zh, tp]).astype(jnp.int32)
    tokens = queries.shape[0]
    own_rows = master.shape[0]
    entries = queries.shape[1] * lax.axis_size("tp") * drift.shape[2]

    across = swap_tp(out_grad, 2)
    partner = swap_tp(out_grad, 1)

    gram = lax.dot_general(out_grad, out_grad, (((1,), (1,)), ((), ())), preferred_element_type=f32)
    side = (tp % 2) * (tokens // 2)
    other = (tokens // 2) - side
    mine = lax.dynamic_slice_in_dim(gram, side, tokens // 2, 0)
    mine = mine + swap_tp(lax.dynamic_slice_in_dim(gram, other, tokens // 2, 0), 1)
    far = swap_tp(mine, 2)

    base = base_rows(at, master, momentum)
    base_got = jnp.stack(
        [lax.dynamic_index_in_dim(base, x, 0, False)]
        + ring([lax.dynamic_index_in_dim(base, (x + k) % NX, 0, False) for k in (1, 2, 3)], "x", 1)
    )
    base_tile = jnp.concatenate(
        [lax.dynamic_index_in_dim(base_got, (x - g + NX) % NX, 0, False) for g in range(NX)], axis=0
    )
    base_tiles = jnp.stack([base_tile, move(base_tile, "z", 1)])

    ct, own_gram = attention(queries, keys, values, segments)
    far, mine, ct, own_gram = lax.optimization_barrier((far, mine, ct, own_gram))
    across, ct = lax.optimization_barrier((across, ct))
    across_partner = swap_tp(across, 1)
    mine = mine + far
    theirs = swap_tp(mine, 1)
    squares = jnp.sum(lax.dynamic_slice_in_dim(own_gram, side, tokens // 2, 0) * mine)
    squares = squares + jnp.sum(lax.dynamic_slice_in_dim(own_gram, other, tokens // 2, 0) * theirs)
    squares = jnp.full((8, 128), squares, f32)
    squares = squares + swap_tp(squares, 1)
    squares = squares + swap_tp(squares, 2)
    scale = (inner_rate / jnp.sqrt(squares[0, :1] / entries + 1e-06))

    scale, base_tiles, across_partner = lax.optimization_barrier((scale, base_tiles, across_partner))
    sends = pseudo_gradient(at, scale, ct, (out_grad, partner, across, across_partner), drift)
    here = reduce_tiles(reduce_blocks(sends[:4], "x"), "y")
    there = reduce_tiles(reduce_blocks(sends[4:], "y"), "x")
    here, there = rounded(here), rounded(there)
    crossed = move(jnp.stack([there, here]).astype(bf16), "z", 1)
    mean = (jnp.stack([here, there]) + crossed.astype(f32)) / lax.axis_size("worker")
    fresh = (base_tiles - (outer_rate * (1.0 + outer_mu)) * mean).astype(bf16)

    def mean_rows(k):
        return lax.dynamic_slice_in_dim(mean[0], ((x + k) % NX) * own_rows, own_rows, 0)

    here_got = ring([fresh[0]] * 3, "y", -1)
    there_got = ring(
        [jnp.concatenate([fresh[1], mean_rows(NX - k).astype(bf16)]) for k in (1, 2, 3)], "x", -1
    )
    means = jnp.stack([mean_rows(0)] + [got[TILE_R:].astype(f32) for got in there_got])
    here_block = jnp.stack([fresh[0]] + here_got)
    there_block = jnp.stack([fresh[1]] + [got[:TILE_R] for got in there_got])
    here_blocks = [here_block] + ring([here_block] * 3, "x", -1)
    there_blocks = [there_block] + ring([there_block] * 3, "y", -1)
    new_master, new_momentum = outer_rows(at, master, momentum, means)
    new_params = place(at, here_blocks + there_blocks, drift.shape[1], drift.shape[2])
    return (new_params, new_master, new_momentum)


def solution(mesh):
    placed = (
        P("worker", "tp"),
        P("worker", "tp"),
        P("worker", "tp"),
        P("worker", "tp"),
        P("worker"),
        P("worker", "tp", None),
        P(("tp", "worker"), None),
        P(("tp", "worker"), None),
    )
    return jax.shard_map(
        per_device,
        mesh=mesh,
        in_specs=placed,
        out_specs=(P("tp", None), P(("tp", "worker"), None), P(("tp", "worker"), None)),
        check_vma=False,
    )
```

time: 424 us -> 201 us (0.47)
  Pallas kernels: 222 us -> 25.1 us
  starting transfers between devices: 65.9 us -> 55.7 us
  waiting for transfers between devices: 109 us -> 102 us
  blocking collectives: 6.67 us -> 0 us
    pallas_call x1, Pallas kernels: 201 us -> 6.09 us  [place(): pl.pallas_call(place_body, out_shape=jax.ShapeDtypeStruct((rows, width),...]
    ppermute x6 -> x8, waiting for transfers between devices: 29.2 us -> 9.72 us  [swap_tp(): return lax.ppermute(value, 'tp', [(t, t ^ bit) for t in range(4)])]
    ppermute x44 -> x29, starting transfers between devices: 64.8 us -> 51.7 us  [move(): return lax.ppermute(value, 'worker', pairs)]
    ppermute x44 -> x29, waiting for transfers between devices: 79.9 us -> 92.7 us  [move(): return lax.ppermute(value, 'worker', pairs)]
    psum x1 -> x0, blocking collectives: 6.67 us -> none  [per_device(): squares = lax.psum(squares, 'tp')]
  transfers between devices with their start and end apart: 50 -> 37, of which waited for: 23 -> 17; matrix products, arithmetic and copies ran while one was open for 4% -> 6% of each run, Pallas kernels for 2% -> 5%
where the time goes in v2:
time: 201 us; the launch traced here: 200 us
  waiting for transfers between devices  102 us (51%)
  starting transfers between devices  55.7 us (28%)
  Pallas kernels  25.1 us (12%)
  other arithmetic  7.13 us (4%)
  local copies, waits for them, and re-layouts  4.02 us (2%)
  between operations  3.2 us (2%)
  matrix products  2.18 us (1%)
    ppermute x29, waiting for transfers between devices, move(): return lax.ppermute(value, 'worker', pairs)  92.7 us
    ppermute x29, starting transfers between devices, move(): return lax.ppermute(value, 'worker', pairs)  51.7 us
    ppermute x8, waiting for transfers between devices, swap_tp(): return lax.ppermute(value, 'tp', [(t, t ^ bit) for t in range(4)])  9.72 us
    pallas_call x1, Pallas kernels, pseudo_gradient(): pl.pallas_call(pseudo_body, out_shape=(block,) * 8, in_specs=[smem, smem,...  9.51 us
    pallas_call x1, Pallas kernels, place(): pl.pallas_call(place_body, out_shape=jax.ShapeDtypeStruct((rows, width),...  6.09 us
    pallas_call x1, Pallas kernels, attention(): pl.pallas_call(attention_body, out_shape=(jax.ShapeDtypeStruct((width, to...  5.02 us
  transfers between devices with their start and end apart: 37, of which 17 were waited for; matrix products, arithmetic and copies ran while one was open for 6% of the time, Pallas kernels for 5%

profile of v2, /device:TPU:32, one launch (start us, length us, event | category | flops | bytes accessed | tf_op | source)
XLA Modules:
  0.0 199.7 jit_solution(3184554471661782438)
XLA Ops:
  0.7 2.2 %fusion.23 = f32[384,384]{1,0:T(8,128)S(1)} fusion(bf16[384,1280]{1,0:T(8,128)(2,1)} %g0_ref.1), kind=kOutput, calls=%fused_computation.70 | convolution fusion | flops 377487360 | bytes 1572864 | tf_op jit(solution)/shard_map/dot_general | solution.py:315
  3.2 0.7 pad_add_fusion.at_ref
  3.9 2.0 %base_rows.1 = f32[4,20,1280]{2,1,0:T(8,128)} custom-call(s32[4]{0:T(128)} %pad_add_fusion.at_ref, f32[20,5120]{1,0:T(8,128)} %master_ref.3, f32[20,5120]{1,0:T(8,128)} %momentum_ref.3), custom_call_target="tpu_custom_call" | custom-call | tf_op jit(solution)/shard_map/base_rows/pallas_call | solution.py:198
  5.9 1.8 constant_dynamic-slice_fusion.1
  7.6 2.9 %collective-permute-start.7 = (f32[20,1280]{1,0:T(8,128)}, f32[20,1280]{1,0:T(8,128)S(1)}, u32[]{:S(2)}, u32[]{:S(2)}) collective-permute-start(f32[20,1280]{1,0:T(8,128)} %get-tuple-element.68), channel_id=1, source_target_pairs={{0,3},{1,0},{2,1},{3,2},{4,7},{5,4},{6,5},{7,6},{8,11},{9,8},{10,9... | collective-permute-start | bytes 307208 | tf_op jit(solution)/shard_map/ppermute | solution.py:39
  10.5 0.8 collective-permute-start.6
  11.3 0.9 collective-permute-start.5
  12.2 0.6 reshape.27.seg_row_ref
  12.8 0.8 reshape.32.seg_col_ref
  13.6 2.0 %collective-permute-start.1 = (f32[192,384]{1,0:T(8,128)S(1)}, f32[192,384]{1,0:T(8,128)S(1)}, u32[]{:S(2)}, u32[]{:S(2)}) collective-permute-start(f32[192,384]{1,0:T(8,128)S(1)} %dynamic-slice_add_fusion), channel_id=1, source_target_pairs={{0,64},{32,96},{64,0},{96,32},{1,65},{33,97},{65,1},{97,33},{2,66}... | collective-permute-start | bytes 884744 | tf_op jit(solution)/shard_map/ppermute | solution.py:43
  15.6 5.0 %attention.1 = (bf16[640,384]{1,0:T(8,128)(2,1)}, f32[384,384]{1,0:T(8,128)}) custom-call(bf16[384,640]{1,0:T(8,128)(2,1)} %q_ref.1, bf16[384,640]{1,0:T(8,128)(2,1)} %k_ref.1, bf16[384,640]{1,0:T(8,128)(2,1)} %v_ref.1, s32[1,384]{1,0:T(1,128)} %reshape.27.seg_row_ref, s32[384,1]{1,0:T(8,128)} %reshape.32.seg_col_ref), custom_call_target="tpu_custom_call" | custom-call | flops 4000000000 | bytes 2600000 | tf_op jit(solution)/shard_map/attention/pallas_call | solution.py:77
  20.8 1.1 pad_maximum_fusion.3
  21.8 8.9 %collective-permute-done.1 = f32[192,384]{1,0:T(8,128)S(1)} collective-permute-done((f32[192,384]{1,0:T(8,128)S(1)}, f32[192,384]{1,0:T(8,128)S(1)}, u32[]{:S(2)}, u32[]{:S(2)}) %collective-permute-start.1) | collective-permute-done | bytes 294944 | tf_op jit(solution)/shard_map/ppermute | solution.py:43
  31.0 3.1 %collective-permute-start.8 = (f32[80,1280]{1,0:T(8,128)S(1)}, f32[80,1280]{1,0:T(8,128)}, u32[]{:S(2)}, u32[]{:S(2)}) collective-permute-start(f32[80,1280]{1,0:T(8,128)S(1)} %pad_maximum_fusion.5), channel_id=1, source_target_pairs={{0,16},{1,17},{2,18},{3,19},{4,20},{5,21},{6,22},{7,23},{8,24},{9,... | collective-permute-start | bytes 1228808 | tf_op jit(solution)/shard_map/ppermute | solution.py:39
  34.0 0.2 collective-permute-start.10
  34.2 0.7 multiply_reduce_fusion
  36.2 0.4 collective-permute-start.3
  36.6 0.8 collective-permute-done.3
  37.4 1.0 collective-permute-start.4
  38.4 6.1 %collective-permute-done.8 = f32[80,1280]{1,0:T(8,128)} collective-permute-done((f32[80,1280]{1,0:T(8,128)S(1)}, f32[80,1280]{1,0:T(8,128)}, u32[]{:S(2)}, u32[]{:S(2)}) %collective-permute-start.8) | collective-permute-done | bytes 409632 | tf_op jit(solution)/shard_map/ppermute | solution.py:39
  44.6 1.1 pad_maximum_fusion
  45.7 0.5 slice.61
  46.9 9.5 %pseudo_gradient.1 = (bf16[4,80,1280]{2,1,0:T(8,128)(2,1)}, bf16[4,80,1280]{2,1,0:T(8,128)(2,1)}, bf16[4,80,1280]{2,1,0:T(8,128)(2,1)}, bf16[4,80,1280]{2,1,0:T(...) custom-call(s32[4]{0:T(128)} %pad_add_fusion.at_ref, ...), custom_call_target="tpu_custom_call" | custom-call | flops 2516582400 | bytes 18000000 | tf_op jit(solution)/shard_map/pseudo_gradient/pallas_call | solution.py:164
  56.4 1.6 collective-permute-start.12
  58.0 2.7 %collective-permute-start.13 = (bf16[4,80,1280]{2,1,0:T(8,128)(2,1)}, bf16[4,80,1280]{2,1,0:T(8,128)(2,1)S(1)}, u32[]{:S(2)}, u32[]{:S(2)}) collective-permute-start(bf16[4,80,1280]{2,1,0:T(8,128)(2,1)} %get-tuple-element.37), channel_id=1, source_target_pairs={{0,2},{1,3},{2,0},{3,1},{4,6},{5,7},{6,4},{7,5},{8,10},{9,11},{10,... | collective-permute-start | bytes 2457608 | tf_op jit(solution)/shard_map/ppermute | solution.py:39
  60.7 1.4 collective-permute-start.14
  62.1 1.6 collective-permute-start.18
  63.7 2.9 %collective-permute-start.19 = (bf16[4,80,1280]{2,1,0:T(8,128)(2,1)}, bf16[4,80,1280]{2,1,0:T(8,128)(2,1)S(1)}, u32[]{:S(2)}, u32[]{:S(2)}) collective-permute-start(bf16[4,80,1280]{2,1,0:T(8,128)(2,1)} %get-tuple-element.41), channel_id=1, source_target_pairs={{0,8},{1,9},{2,10},{3,11},{4,12},{5,13},{6,14},{7,15},{8,0},{9,1},... | collective-permute-start | bytes 2457608 | tf_op jit(solution)/shard_map/ppermute | solution.py:39
  66.6 11.6 %collective-permute-done.12 = bf16[4,80,1280]{2,1,0:T(8,128)(2,1)S(1)} collective-permute-done((bf16[4,80,1280]{2,1,0:T(8,128)(2,1)}, bf16[4,80,1280]{2,1,0:T(8,128)(2,1)S(1)}, u32[]{:S(2)}, u32[]{:S(2)}) %collective-permute-start.12) | collective-permute-done | bytes 819232 | tf_op jit(solution)/shard_map/ppermute | solution.py:39
  78.2 3.0 %collective-permute-start.20 = (bf16[4,80,1280]{2,1,0:T(8,128)(2,1)}, bf16[4,80,1280]{2,1,0:T(8,128)(2,1)S(1)}, u32[]{:S(2)}, u32[]{:S(2)}) collective-permute-start(bf16[4,80,1280]{2,1,0:T(8,128)(2,1)} %get-tuple-element.42), channel_id=1, source_target_pairs={{0,12},{1,13},{2,14},{3,15},{4,0},{5,1},{6,2},{7,3},{8,4},{9,5},{1... | collective-permute-start | bytes 2457608 | tf_op jit(solution)/shard_map/ppermute | solution.py:39
  81.1 15.1 %collective-permute-done.13 = bf16[4,80,1280]{2,1,0:T(8,128)(2,1)S(1)} collective-permute-done((bf16[4,80,1280]{2,1,0:T(8,128)(2,1)}, bf16[4,80,1280]{2,1,0:T(8,128)(2,1)S(1)}, u32[]{:S(2)}, u32[]{:S(2)}) %collective-permute-start.13) | collective-permute-done | bytes 819232 | tf_op jit(solution)/shard_map/ppermute | solution.py:39
  96.2 1.5 fusion.20
  97.8 1.6 collective-permute-start.15
  99.5 1.7 collective-permute-start.17
  101.2 2.0 collective-permute-start.16
  103.1 0.4 fusion.21
  103.6 1.5 collective-permute-start.21
  105.1 1.8 collective-permute-start.23
  106.9 0.6 collective-permute-done.15
  107.5 1.6 collective-permute-start.22
  109.1 1.3 collective-permute-done.16
  110.6 0.9 collective-permute-done.21
  111.5 3.1 %collective-permute-done.23 = bf16[80,1280]{1,0:T(8,128)(2,1)S(1)} collective-permute-done((bf16[80,1280]{1,0:T(8,128)(2,1)S(1)}, bf16[80,1280]{1,0:T(8,128)(2,1)S(1)}, u32[]{:S(2)}, u32[]{:S(2)}) %collective-permute-start.23) | collective-permute-done | bytes 204832 | tf_op jit(solution)/shard_map/ppermute | solution.py:39
  114.6 1.4 collective-permute-done.22
  116.2 3.0 %collective-permute-start.24 = (bf16[2,80,1280]{2,1,0:T(8,128)(2,1)S(1)}, bf16[2,80,1280]{2,1,0:T(8,128)(2,1)S(1)}, u32[]{:S(2)}, u32[]{:S(2)}) collective-permute-start(bf16[2,80,1280]{2,1,0:T(8,128)(2,1)S(1)} %pad_maximum_fusion.6), channel_id=1, source_target_pairs={{0,16},{1,17},{2,18},{3,19},{4,20},{5,21},{6,22},{7,23},{8,24},{9,... | collective-permute-start | bytes 1228808 | tf_op jit(solution)/shard_map/ppermute | solution.py:39
  119.2 8.2 %collective-permute-done.24 = bf16[2,80,1280]{2,1,0:T(8,128)(2,1)S(1)} collective-permute-done((bf16[2,80,1280]{2,1,0:T(8,128)(2,1)S(1)}, bf16[2,80,1280]{2,1,0:T(8,128)(2,1)S(1)}, u32[]{:S(2)}, u32[]{:S(2)}) %collective-permute-start.24) | collective-permute-done | bytes 409632 | tf_op jit(solution)/shard_map/ppermute | solution.py:39
  127.6 0.7 collective-permute-start.27
  128.3 1.8 collective-permute-start.26
  130.2 1.1 collective-permute-start.25
  131.4 3.5 %collective-permute-start.31 = (bf16[100,1280]{1,0:T(8,128)(2,1)S(1)}, bf16[100,1280]{1,0:T(8,128)(2,1)S(1)}, u32[]{:S(2)}, u32[]{:S(2)}) collective-permute-start(bf16[100,1280]{1,0:T(8,128)(2,1)S(1)} %get-tuple-element.78), channel_id=1, source_target_pairs={{0,3},{1,0},{2,1},{3,2},{4,7},{5,4},{6,5},{7,6},{8,11},{9,8},{10,9... | collective-permute-start | bytes 768008 | tf_op jit(solution)/shard_map/ppermute | solution.py:39
  134.9 0.5 collective-permute-start.32
  135.4 2.1 %collective-permute-done.27 = bf16[80,1280]{1,0:T(8,128)(2,1)S(1)} collective-permute-done((bf16[80,1280]{1,0:T(8,128)(2,1)S(1)}, bf16[80,1280]{1,0:T(8,128)(2,1)S(1)}, u32[]{:S(2)}, u32[]{:S(2)}) %collective-permute-start.27) | collective-permute-done | bytes 204832 | tf_op jit(solution)/shard_map/ppermute | solution.py:39
  137.6 0.6 collective-permute-start.33
  138.3 0.6 collective-permute-start.30
  138.9 3.5 %collective-permute-start.29 = (bf16[4,80,1280]{2,1,0:T(8,128)(2,1)S(1)}, bf16[4,80,1280]{2,1,0:T(8,128)(2,1)S(1)}, u32[]{:S(2)}, u32[]{:S(2)}) collective-permute-start(bf16[4,80,1280]{2,1,0:T(8,128)(2,1)S(1)} %pad_maximum_fusion.1.rest_0_), channel_id=1, source_target_pairs={{0,2},{1,3},{2,0},{3,1},{4,6},{5,7},{6,4},{7,5},{8,10},{9,11},{10,... | collective-permute-start | bytes 2457608 | tf_op jit(solution)/shard_map/ppermute | solution.py:39
  142.4 15.9 %collective-permute-done.31 = bf16[100,1280]{1,0:T(8,128)(2,1)S(1)} collective-permute-done((bf16[100,1280]{1,0:T(8,128)(2,1)S(1)}, bf16[100,1280]{1,0:T(8,128)(2,1)S(1)}, u32[]{:S(2)}, u32[]{:S(2)}) %collective-permute-start.31) | collective-permute-done | bytes 256032 | tf_op jit(solution)/shard_map/ppermute | solution.py:39
  158.4 4.2 %collective-permute-start.28 = (bf16[4,80,1280]{2,1,0:T(8,128)(2,1)S(1)}, bf16[4,80,1280]{2,1,0:T(8,128)(2,1)}, u32[]{:S(2)}, u32[]{:S(2)}) collective-permute-start(bf16[4,80,1280]{2,1,0:T(8,128)(2,1)S(1)} %pad_maximum_fusion.1.rest_0_), channel_id=1, source_target_pairs={{0,3},{1,0},{2,1},{3,2},{4,7},{5,4},{6,5},{7,6},{8,11},{9,8},{10,9... | collective-permute-start | bytes 2457608 | tf_op jit(solution)/shard_map/ppermute | solution.py:39
  162.9 0.3 collective-permute-start.35
  163.2 17.9 %collective-permute-done.30.rest_3_ = bf16[4,80,1280]{2,1,0:T(8,128)(2,1)S(1)} collective-permute-done((bf16[4,80,1280]{2,1,0:T(8,128)(2,1)S(1)}, bf16[4,80,1280]{2,1,0:T(8,128)(2,1)S(1)}, u32[]{:S(2)}, u32[]{:S(2)}) %collective-permute-start.30) | collective-permute-done | bytes 819232 | tf_op jit(solution)/shard_map/ppermute | solution.py:39
  181.0 0.8 collective-permute-start.34
  181.8 0.8 pad_maximum_fusion.4.mean_ref
  182.6 2.4 %outer_rows.1 = (f32[20,5120]{1,0:T(8,128)}, f32[20,5120]{1,0:T(8,128)}) custom-call(s32[4]{0:T(128)} %pad_add_fusion.at_ref, f32[20,5120]{1,0:T(8,128)} %master_ref.3, f32[20,5120]{1,0:T(8,128)} %momentum_ref.3, f32[4,20,1280]{2,1,0:T(8,128)} %pad_maximum_fusion.4.mean_ref), custom_call_target="tpu_custom_call" | custom-call | tf_op jit(solution)/shard_map/outer_rows/pallas_call | solution.py:221
  185.3 8.2 %collective-permute-done.34.rest_5_ = bf16[4,80,1280]{2,1,0:T(8,128)(2,1)} collective-permute-done((bf16[4,80,1280]{2,1,0:T(8,128)(2,1)S(1)}, bf16[4,80,1280]{2,1,0:T(8,128)(2,1)}, u32[]{:S(2)}, u32[]{:S(2)}) %collective-permute-start.34) | collective-permute-done | bytes 819232 | tf_op jit(solution)/shard_map/ppermute | solution.py:39
  193.5 6.1 %place.1 = bf16[640,5120]{1,0:T(8,128)(2,1)} custom-call(s32[4]{0:T(128)} %pad_add_fusion.at_ref, bf16[4,80,1280]{2,1,0:T(8,128)(2,1)} %copy-done.1, bf16[4,80,1280]{2,1,0:T(8,128)(2,1)} %collective-permute-done.28.rest_1_, bf16[4,80,1280]{2,1,0:T(8,128)(2,1)} %copy-done.5, bf16[4,80,1280]{2,1,0:T(8,128)(2,1)} %copy-done.4, bf16[4,80,1280]{2,1,0:T(8,128)(2,1)} %copy-done.2, ...), custom_call_target="tpu_custom_call" | custom-call | tf_op jit(solution)/shard_map/place/pallas_call | solution.py:261
  (73 shorter events, 2.0 us)
Async XLA Ops:
  0.6 33.4 %collective-permute-start.9 = (bf16[384,1280]{1,0:T(8,128)(2,1)}, bf16[384,1280]{1,0:T(8,128)(2,1)S(1)}, u32[]{:S(2)}, u32[]{:S(2)}) collective-permute-start(bf16[384,1280]{1,0:T(8,128)(2,1)} %g0_ref.1), channel_id=1, source_target_pairs={{0,64},{32,96},{64,0},{96,32},{1,65},{33,97},{65,1},{97,33},{2,66}... | collective-permute-start | bytes 2949128 | tf_op jit(solution)/shard_map/ppermute | solution.py:43
  2.9 9.3 %copy-start.8 = (s32[384]{0:T(512)S(1)}, s32[384]{0:T(512)}, u32[]{:S(2)}) copy-start(s32[384]{0:T(512)} %param.12) | copy-start | bytes 4612
  3.0 10.6 %collective-permute-start = (f32[192,384]{1,0:T(8,128)S(1)}, f32[192,384]{1,0:T(8,128)S(1)}, u32[]{:S(2)}, u32[]{:S(2)}) collective-permute-start(f32[192,384]{1,0:T(8,128)S(1)} %constant_dynamic-slice_fusion.2), channel_id=1, source_target_pairs={{0,32},{32,0},{64,96},{96,64},{1,33},{33,1},{65,97},{97,65},{2,34}... | collective-permute-start | bytes 884744 | tf_op jit(solution)/shard_map/ppermute | solution.py:43
  7.6 13.0 %collective-permute-start.7 = (f32[20,1280]{1,0:T(8,128)}, f32[20,1280]{1,0:T(8,128)S(1)}, u32[]{:S(2)}, u32[]{:S(2)}) collective-permute-start(f32[20,1280]{1,0:T(8,128)} %get-tuple-element.68), channel_id=1, source_target_pairs={{0,3},{1,0},{2,1},{3,2},{4,7},{5,4},{6,5},{7,6},{8,11},{9,8},{10,9... | collective-permute-start | bytes 307208 | tf_op jit(solution)/shard_map/ppermute | solution.py:39
  10.5 10.2 %collective-permute-start.6 = (f32[20,1280]{1,0:T(8,128)S(1)}, f32[20,1280]{1,0:T(8,128)}, u32[]{:S(2)}, u32[]{:S(2)}) collective-permute-start(f32[20,1280]{1,0:T(8,128)S(1)} %get-tuple-element.69), channel_id=1, source_target_pairs={{0,2},{1,3},{2,0},{3,1},{4,6},{5,7},{6,4},{7,5},{8,10},{9,11},{10,... | collective-permute-start | bytes 307208 | tf_op jit(solution)/shard_map/ppermute | solution.py:39
  11.3 9.4 %collective-permute-start.5 = (f32[20,1280]{1,0:T(8,128)S(1)}, f32[20,1280]{1,0:T(8,128)}, u32[]{:S(2)}, u32[]{:S(2)}) collective-permute-start(f32[20,1280]{1,0:T(8,128)S(1)} %get-tuple-element.70), channel_id=1, source_target_pairs={{0,1},{1,2},{2,3},{3,0},{4,5},{5,6},{6,7},{7,4},{8,9},{9,10},{10,1... | collective-permute-start | bytes 307208 | tf_op jit(solution)/shard_map/ppermute | solution.py:39
  13.6 7.0 %copy-start = (bf16[384,1280]{1,0:T(8,128)(2,1)S(1)}, bf16[384,1280]{1,0:T(8,128)(2,1)}, u32[]{:S(2)}) copy-start(bf16[384,1280]{1,0:T(8,128)(2,1)} %g0_ref.1) | copy-start | bytes 2949124
  13.6 17.1 %collective-permute-start.1 = (f32[192,384]{1,0:T(8,128)S(1)}, f32[192,384]{1,0:T(8,128)S(1)}, u32[]{:S(2)}, u32[]{:S(2)}) collective-permute-start(f32[192,384]{1,0:T(8,128)S(1)} %dynamic-slice_add_fusion), channel_id=1, source_target_pairs={{0,64},{32,96},{64,0},{96,32},{1,65},{33,97},{65,1},{97,33},{2,66}... | collective-permute-start | bytes 884744 | tf_op jit(solution)/shard_map/ppermute | solution.py:43
  20.7 26.2 %collective-permute-start.11 = (bf16[384,1280]{1,0:T(8,128)(2,1)S(1)}, bf16[384,1280]{1,0:T(8,128)(2,1)}, u32[]{:S(2)}, u32[]{:S(2)}) collective-permute-start(bf16[384,1280]{1,0:T(8,128)(2,1)S(1)} %copy-done), channel_id=1, source_target_pairs={{0,32},{32,0},{64,96},{96,64},{1,33},{33,1},{65,97},{97,65},{2,34}... | collective-permute-start | bytes 2949128 | tf_op jit(solution)/shard_map/ppermute | solution.py:43
  20.8 13.5 %copy-start.7 = (f32[384,384]{1,0:T(8,128)S(1)}, f32[384,384]{1,0:T(8,128)}, u32[]{:S(2)}) copy-start(f32[384,384]{1,0:T(8,128)} %get-tuple-element.26) | copy-start | bytes 1769476
  30.8 3.5 %collective-permute-start.2 = (f32[192,384]{1,0:T(8,128)S(1)}, f32[192,384]{1,0:T(8,128)S(1)}, u32[]{:S(2)}, u32[]{:S(2)}) collective-permute-start(f32[192,384]{1,0:T(8,128)S(1)} %add.162), channel_id=1, source_target_pairs={{0,32},{32,0},{64,96},{96,64},{1,33},{33,1},{65,97},{97,65},{2,34}... | collective-permute-start | bytes 884744 | tf_op jit(solution)/shard_map/ppermute | solution.py:43
  31.0 13.6 %collective-permute-start.8 = (f32[80,1280]{1,0:T(8,128)S(1)}, f32[80,1280]{1,0:T(8,128)}, u32[]{:S(2)}, u32[]{:S(2)}) collective-permute-start(f32[80,1280]{1,0:T(8,128)S(1)} %pad_maximum_fusion.5), channel_id=1, source_target_pairs={{0,16},{1,17},{2,18},{3,19},{4,20},{5,21},{6,22},{7,23},{8,24},{9,... | collective-permute-start | bytes 1228808 | tf_op jit(solution)/shard_map/ppermute | solution.py:39
  34.0 11.6 %copy-start.3 = (bf16[384,1280]{1,0:T(8,128)(2,1)}, bf16[384,1280]{1,0:T(8,128)(2,1)S(1)}, u32[]{:S(2)}) copy-start(bf16[384,1280]{1,0:T(8,128)(2,1)S(1)} %collective-permute-done.9.g2_ref) | copy-start | bytes 2949124
  34.0 12.8 %collective-permute-start.10 = (bf16[384,1280]{1,0:T(8,128)(2,1)S(1)}, bf16[384,1280]{1,0:T(8,128)(2,1)}, u32[]{:S(2)}, u32[]{:S(2)}) collective-permute-start(bf16[384,1280]{1,0:T(8,128)(2,1)S(1)} %collective-permute-done.9.g2_ref), channel_id=1, source_target_pairs={{0,32},{32,0},{64,96},{96,64},{1,33},{33,1},{65,97},{97,65},{2,34}... | collective-permute-start | bytes 2949128 | tf_op jit(solution)/shard_map/ppermute | solution.py:43
  36.2 1.2 collective-permute-start.3
  37.4 8.2 %collective-permute-start.4 = (f32[8,128]{1,0:T(8,128)S(1)}, f32[8,128]{1,0:T(8,128)S(1)}, u32[]{:S(2)}, u32[]{:S(2)}) collective-permute-start(f32[8,128]{1,0:T(8,128)S(1)} %broadcast_add_fusion), channel_id=1, source_target_pairs={{0,64},{32,96},{64,0},{96,32},{1,65},{33,97},{65,1},{97,33},{2,66}... | collective-permute-start | bytes 12296 | tf_op jit(solution)/shard_map/ppermute | solution.py:43
  56.4 21.8 %collective-permute-start.12 = (bf16[4,80,1280]{2,1,0:T(8,128)(2,1)}, bf16[4,80,1280]{2,1,0:T(8,128)(2,1)S(1)}, u32[]{:S(2)}, u32[]{:S(2)}) collective-permute-start(bf16[4,80,1280]{2,1,0:T(8,128)(2,1)} %get-tuple-element.36), channel_id=1, source_target_pairs={{0,1},{1,2},{2,3},{3,0},{4,5},{5,6},{6,7},{7,4},{8,9},{9,10},{10,1... | collective-permute-start | bytes 2457608 | tf_op jit(solution)/shard_map/ppermute | solution.py:39
  58.0 38.3 %collective-permute-start.13 = (bf16[4,80,1280]{2,1,0:T(8,128)(2,1)}, bf16[4,80,1280]{2,1,0:T(8,128)(2,1)S(1)}, u32[]{:S(2)}, u32[]{:S(2)}) collective-permute-start(bf16[4,80,1280]{2,1,0:T(8,128)(2,1)} %get-tuple-element.37), channel_id=1, source_target_pairs={{0,2},{1,3},{2,0},{3,1},{4,6},{5,7},{6,4},{7,5},{8,10},{9,11},{10,... | collective-permute-start | bytes 2457608 | tf_op jit(solution)/shard_map/ppermute | solution.py:39
  60.7 35.5 %collective-permute-start.14 = (bf16[4,80,1280]{2,1,0:T(8,128)(2,1)}, bf16[4,80,1280]{2,1,0:T(8,128)(2,1)S(1)}, u32[]{:S(2)}, u32[]{:S(2)}) collective-permute-start(bf16[4,80,1280]{2,1,0:T(8,128)(2,1)} %get-tuple-element.38), channel_id=1, source_target_pairs={{0,3},{1,0},{2,1},{3,2},{4,7},{5,4},{6,5},{7,6},{8,11},{9,8},{10,9... | collective-permute-start | bytes 2457608 | tf_op jit(solution)/shard_map/ppermute | solution.py:39
  62.1 39.0 %collective-permute-start.18 = (bf16[4,80,1280]{2,1,0:T(8,128)(2,1)}, bf16[4,80,1280]{2,1,0:T(8,128)(2,1)S(1)}, u32[]{:S(2)}, u32[]{:S(2)}) collective-permute-start(bf16[4,80,1280]{2,1,0:T(8,128)(2,1)} %get-tuple-element.40), channel_id=1, source_target_pairs={{0,4},{1,5},{2,6},{3,7},{4,8},{5,9},{6,10},{7,11},{8,12},{9,13},{1... | collective-permute-start | bytes 2457608 | tf_op jit(solution)/shard_map/ppermute | solution.py:39
  63.7 39.5 %collective-permute-start.19 = (bf16[4,80,1280]{2,1,0:T(8,128)(2,1)}, bf16[4,80,1280]{2,1,0:T(8,128)(2,1)S(1)}, u32[]{:S(2)}, u32[]{:S(2)}) collective-permute-start(bf16[4,80,1280]{2,1,0:T(8,128)(2,1)} %get-tuple-element.41), channel_id=1, source_target_pairs={{0,8},{1,9},{2,10},{3,11},{4,12},{5,13},{6,14},{7,15},{8,0},{9,1},... | collective-permute-start | bytes 2457608 | tf_op jit(solution)/shard_map/ppermute | solution.py:39
  78.2 25.0 %collective-permute-start.20 = (bf16[4,80,1280]{2,1,0:T(8,128)(2,1)}, bf16[4,80,1280]{2,1,0:T(8,128)(2,1)S(1)}, u32[]{:S(2)}, u32[]{:S(2)}) collective-permute-start(bf16[4,80,1280]{2,1,0:T(8,128)(2,1)} %get-tuple-element.42), channel_id=1, source_target_pairs={{0,12},{1,13},{2,14},{3,15},{4,0},{5,1},{6,2},{7,3},{8,4},{9,5},{1... | collective-permute-start | bytes 2457608 | tf_op jit(solution)/shard_map/ppermute | solution.py:39
  97.8 5.4 %copy-start.6 = (bf16[4,80,1280]{2,1,0:T(8,128)(2,1)S(1)}, bf16[4,80,1280]{2,1,0:T(8,128)(2,1)}, u32[]{:S(2)}) copy-start(bf16[4,80,1280]{2,1,0:T(8,128)(2,1)} %get-tuple-element.39) | copy-start | bytes 2457604
  97.8 9.6 %collective-permute-start.15 = (bf16[80,1280]{1,0:T(8,128)(2,1)S(1)}, bf16[80,1280]{1,0:T(8,128)(2,1)S(1)}, u32[]{:S(2)}, u32[]{:S(2)}) collective-permute-start(bf16[80,1280]{1,0:T(8,128)(2,1)S(1)} %get-tuple-element.60), channel_id=1, source_target_pairs={{0,4},{1,5},{2,6},{3,7},{4,8},{5,9},{6,10},{7,11},{8,12},{9,13},{1... | collective-permute-start | bytes 614408 | tf_op jit(solution)/shard_map/ppermute | solution.py:39
  99.5 9.6 %collective-permute-start.17 = (bf16[80,1280]{1,0:T(8,128)(2,1)S(1)}, bf16[80,1280]{1,0:T(8,128)(2,1)S(1)}, u32[]{:S(2)}, u32[]{:S(2)}) collective-permute-start(bf16[80,1280]{1,0:T(8,128)(2,1)S(1)} %get-tuple-element.61), channel_id=1, source_target_pairs={{0,12},{1,13},{2,14},{3,15},{4,0},{5,1},{6,2},{7,3},{8,4},{9,5},{1... | collective-permute-start | bytes 614408 | tf_op jit(solution)/shard_map/ppermute | solution.py:39
  101.2 9.3 %collective-permute-start.16 = (bf16[80,1280]{1,0:T(8,128)(2,1)S(1)}, bf16[80,1280]{1,0:T(8,128)(2,1)S(1)}, u32[]{:S(2)}, u32[]{:S(2)}) collective-permute-start(bf16[80,1280]{1,0:T(8,128)(2,1)S(1)} %get-tuple-element.62), channel_id=1, source_target_pairs={{0,8},{1,9},{2,10},{3,11},{4,12},{5,13},{6,14},{7,15},{8,0},{9,1},... | collective-permute-start | bytes 614408 | tf_op jit(solution)/shard_map/ppermute | solution.py:39
  103.6 7.9 %collective-permute-start.21 = (bf16[80,1280]{1,0:T(8,128)(2,1)S(1)}, bf16[80,1280]{1,0:T(8,128)(2,1)S(1)}, u32[]{:S(2)}, u32[]{:S(2)}) collective-permute-start(bf16[80,1280]{1,0:T(8,128)(2,1)S(1)} %get-tuple-element.57), channel_id=1, source_target_pairs={{0,1},{1,2},{2,3},{3,0},{4,5},{5,6},{6,7},{7,4},{8,9},{9,10},{10,1... | collective-permute-start | bytes 614408 | tf_op jit(solution)/shard_map/ppermute | solution.py:39
  105.1 9.5 %collective-permute-start.23 = (bf16[80,1280]{1,0:T(8,128)(2,1)S(1)}, bf16[80,1280]{1,0:T(8,128)(2,1)S(1)}, u32[]{:S(2)}, u32[]{:S(2)}) collective-permute-start(bf16[80,1280]{1,0:T(8,128)(2,1)S(1)} %get-tuple-element.58), channel_id=1, source_target_pairs={{0,3},{1,0},{2,1},{3,2},{4,7},{5,4},{6,5},{7,6},{8,11},{9,8},{10,9... | collective-permute-start | bytes 614408 | tf_op jit(solution)/shard_map/ppermute | solution.py:39
  107.5 8.5 %collective-permute-start.22 = (bf16[80,1280]{1,0:T(8,128)(2,1)S(1)}, bf16[80,1280]{1,0:T(8,128)(2,1)S(1)}, u32[]{:S(2)}, u32[]{:S(2)}) collective-permute-start(bf16[80,1280]{1,0:T(8,128)(2,1)S(1)} %get-tuple-element.59), channel_id=1, source_target_pairs={{0,2},{1,3},{2,0},{3,1},{4,6},{5,7},{6,4},{7,5},{8,10},{9,11},{10,... | collective-permute-start | bytes 614408 | tf_op jit(solution)/shard_map/ppermute | solution.py:39
  116.2 11.2 %collective-permute-start.24 = (bf16[2,80,1280]{2,1,0:T(8,128)(2,1)S(1)}, bf16[2,80,1280]{2,1,0:T(8,128)(2,1)S(1)}, u32[]{:S(2)}, u32[]{:S(2)}) collective-permute-start(bf16[2,80,1280]{2,1,0:T(8,128)(2,1)S(1)} %pad_maximum_fusion.6), channel_id=1, source_target_pairs={{0,16},{1,17},{2,18},{3,19},{4,20},{5,21},{6,22},{7,23},{8,24},{9,... | collective-permute-start | bytes 1228808 | tf_op jit(solution)/shard_map/ppermute | solution.py:39
  127.6 10.0 %collective-permute-start.27 = (bf16[80,1280]{1,0:T(8,128)(2,1)S(1)}, bf16[80,1280]{1,0:T(8,128)(2,1)S(1)}, u32[]{:S(2)}, u32[]{:S(2)}) collective-permute-start(bf16[80,1280]{1,0:T(8,128)(2,1)S(1)} %get-tuple-element.72), channel_id=1, source_target_pairs={{0,4},{1,5},{2,6},{3,7},{4,8},{5,9},{6,10},{7,11},{8,12},{9,13},{1... | collective-permute-start | bytes 614408 | tf_op jit(solution)/shard_map/ppermute | solution.py:39
  128.3 9.8 %collective-permute-start.26 = (bf16[80,1280]{1,0:T(8,128)(2,1)S(1)}, bf16[80,1280]{1,0:T(8,128)(2,1)S(1)}, u32[]{:S(2)}, u32[]{:S(2)}) collective-permute-start(bf16[80,1280]{1,0:T(8,128)(2,1)S(1)} %get-tuple-element.72), channel_id=1, source_target_pairs={{0,8},{1,9},{2,10},{3,11},{4,12},{5,13},{6,14},{7,15},{8,0},{9,1},... | collective-permute-start | bytes 614408 | tf_op jit(solution)/shard_map/ppermute | solution.py:39
  130.2 8.1 %collective-permute-start.25 = (bf16[80,1280]{1,0:T(8,128)(2,1)S(1)}, bf16[80,1280]{1,0:T(8,128)(2,1)S(1)}, u32[]{:S(2)}, u32[]{:S(2)}) collective-permute-start(bf16[80,1280]{1,0:T(8,128)(2,1)S(1)} %get-tuple-element.72), channel_id=1, source_target_pairs={{0,12},{1,13},{2,14},{3,15},{4,0},{5,1},{6,2},{7,3},{8,4},{9,5},{1... | collective-permute-start | bytes 614408 | tf_op jit(solution)/shard_map/ppermute | solution.py:39
  131.4 26.9 %collective-permute-start.31 = (bf16[100,1280]{1,0:T(8,128)(2,1)S(1)}, bf16[100,1280]{1,0:T(8,128)(2,1)S(1)}, u32[]{:S(2)}, u32[]{:S(2)}) collective-permute-start(bf16[100,1280]{1,0:T(8,128)(2,1)S(1)} %get-tuple-element.78), channel_id=1, source_target_pairs={{0,3},{1,0},{2,1},{3,2},{4,7},{5,4},{6,5},{7,6},{8,11},{9,8},{10,9... | collective-permute-start | bytes 768008 | tf_op jit(solution)/shard_map/ppermute | solution.py:39
  134.9 27.7 %collective-permute-start.32 = (bf16[100,1280]{1,0:T(8,128)(2,1)S(1)}, bf16[100,1280]{1,0:T(8,128)(2,1)S(1)}, u32[]{:S(2)}, u32[]{:S(2)}) collective-permute-start(bf16[100,1280]{1,0:T(8,128)(2,1)S(1)} %get-tuple-element.79), channel_id=1, source_target_pairs={{0,2},{1,3},{2,0},{3,1},{4,6},{5,7},{6,4},{7,5},{8,10},{9,11},{10,... | collective-permute-start | bytes 768008 | tf_op jit(solution)/shard_map/ppermute | solution.py:39
  137.6 25.1 %collective-permute-start.33 = (bf16[100,1280]{1,0:T(8,128)(2,1)S(1)}, bf16[100,1280]{1,0:T(8,128)(2,1)S(1)}, u32[]{:S(2)}, u32[]{:S(2)}) collective-permute-start(bf16[100,1280]{1,0:T(8,128)(2,1)S(1)} %get-tuple-element.80), channel_id=1, source_target_pairs={{0,1},{1,2},{2,3},{3,0},{4,5},{5,6},{6,7},{7,4},{8,9},{9,10},{10,1... | collective-permute-start | bytes 768008 | tf_op jit(solution)/shard_map/ppermute | solution.py:39
  138.3 43.5 %copy-start.1 = (bf16[4,80,1280]{2,1,0:T(8,128)(2,1)}, bf16[4,80,1280]{2,1,0:T(8,128)(2,1)S(1)}, u32[]{:S(2)}) copy-start(bf16[4,80,1280]{2,1,0:T(8,128)(2,1)S(1)} %pad_maximum_fusion.1.rest_0_) | copy-start | bytes 2457604
  138.3 42.7 %collective-permute-start.30 = (bf16[4,80,1280]{2,1,0:T(8,128)(2,1)S(1)}, bf16[4,80,1280]{2,1,0:T(8,128)(2,1)S(1)}, u32[]{:S(2)}, u32[]{:S(2)}) collective-permute-start(bf16[4,80,1280]{2,1,0:T(8,128)(2,1)S(1)} %pad_maximum_fusion.1.rest_0_), channel_id=1, source_target_pairs={{0,1},{1,2},{2,3},{3,0},{4,5},{5,6},{6,7},{7,4},{8,9},{9,10},{10,1... | collective-permute-start | bytes 2457608 | tf_op jit(solution)/shard_map/ppermute | solution.py:39
  138.9 46.2 %collective-permute-start.29 = (bf16[4,80,1280]{2,1,0:T(8,128)(2,1)S(1)}, bf16[4,80,1280]{2,1,0:T(8,128)(2,1)S(1)}, u32[]{:S(2)}, u32[]{:S(2)}) collective-permute-start(bf16[4,80,1280]{2,1,0:T(8,128)(2,1)S(1)} %pad_maximum_fusion.1.rest_0_), channel_id=1, source_target_pairs={{0,2},{1,3},{2,0},{3,1},{4,6},{5,7},{6,4},{7,5},{8,10},{9,11},{10,... | collective-permute-start | bytes 2457608 | tf_op jit(solution)/shard_map/ppermute | solution.py:39
  158.4 26.7 %collective-permute-start.28 = (bf16[4,80,1280]{2,1,0:T(8,128)(2,1)S(1)}, bf16[4,80,1280]{2,1,0:T(8,128)(2,1)}, u32[]{:S(2)}, u32[]{:S(2)}) collective-permute-start(bf16[4,80,1280]{2,1,0:T(8,128)(2,1)S(1)} %pad_maximum_fusion.1.rest_0_), channel_id=1, source_target_pairs={{0,3},{1,0},{2,1},{3,2},{4,7},{5,4},{6,5},{7,6},{8,11},{9,8},{10,9... | collective-permute-start | bytes 2457608 | tf_op jit(solution)/shard_map/ppermute | solution.py:39
  162.8 30.7 %copy-start.2 = (bf16[4,80,1280]{2,1,0:T(8,128)(2,1)}, bf16[4,80,1280]{2,1,0:T(8,128)(2,1)S(1)}, u32[]{:S(2)}) copy-start(bf16[4,80,1280]{2,1,0:T(8,128)(2,1)S(1)} %pad_maximum_fusion.2.rest_4_) | copy-start | bytes 2457604
  162.8 22.5 %collective-permute-start.36 = (bf16[4,80,1280]{2,1,0:T(8,128)(2,1)S(1)}, bf16[4,80,1280]{2,1,0:T(8,128)(2,1)}, u32[]{:S(2)}, u32[]{:S(2)}) collective-permute-start(bf16[4,80,1280]{2,1,0:T(8,128)(2,1)S(1)} %pad_maximum_fusion.2.rest_4_), channel_id=1, source_target_pairs={{0,4},{1,5},{2,6},{3,7},{4,8},{5,9},{6,10},{7,11},{8,12},{9,13},{1... | collective-permute-start | bytes 2457608 | tf_op jit(solution)/shard_map/ppermute | solution.py:39
  162.9 22.4 %collective-permute-start.35 = (bf16[4,80,1280]{2,1,0:T(8,128)(2,1)S(1)}, bf16[4,80,1280]{2,1,0:T(8,128)(2,1)}, u32[]{:S(2)}, u32[]{:S(2)}) collective-permute-start(bf16[4,80,1280]{2,1,0:T(8,128)(2,1)S(1)} %pad_maximum_fusion.2.rest_4_), channel_id=1, source_target_pairs={{0,8},{1,9},{2,10},{3,11},{4,12},{5,13},{6,14},{7,15},{8,0},{9,1},... | collective-permute-start | bytes 2457608 | tf_op jit(solution)/shard_map/ppermute | solution.py:39
  181.0 12.5 %copy-start.4 = (bf16[4,80,1280]{2,1,0:T(8,128)(2,1)}, bf16[4,80,1280]{2,1,0:T(8,128)(2,1)S(1)}, u32[]{:S(2)}) copy-start(bf16[4,80,1280]{2,1,0:T(8,128)(2,1)S(1)} %collective-permute-done.30.rest_3_) | copy-start | bytes 2457604
  181.0 12.4 %collective-permute-start.34 = (bf16[4,80,1280]{2,1,0:T(8,128)(2,1)S(1)}, bf16[4,80,1280]{2,1,0:T(8,128)(2,1)}, u32[]{:S(2)}, u32[]{:S(2)}) collective-permute-start(bf16[4,80,1280]{2,1,0:T(8,128)(2,1)S(1)} %pad_maximum_fusion.2.rest_4_), channel_id=1, source_target_pairs={{0,12},{1,13},{2,14},{3,15},{4,0},{5,1},{6,2},{7,3},{8,4},{9,5},{1... | collective-permute-start | bytes 2457608 | tf_op jit(solution)/shard_map/ppermute | solution.py:39
  185.1 8.4 %copy-start.5 = (bf16[4,80,1280]{2,1,0:T(8,128)(2,1)}, bf16[4,80,1280]{2,1,0:T(8,128)(2,1)S(1)}, u32[]{:S(2)}) copy-start(bf16[4,80,1280]{2,1,0:T(8,128)(2,1)S(1)} %collective-permute-done.29.rest_2_) | copy-start | bytes 2457604

commit v3 on v2

v3 whole, which is shorter than its diff:
```python
import functools
import math

import jax
import jax.numpy as jnp
from jax import lax
from jax.experimental import pallas as pl
from jax.experimental.pallas import tpu as pltpu
from jax.sharding import PartitionSpec as P

HD = 128
NX, NY, NZ = 4, 4, 2
TILE_R = 80
HALF_C = 640

inner_rate = 0.8
outer_rate = 0.7
outer_mu = 0.9
neg_big = -1e30
bf16 = jnp.bfloat16
f32 = jnp.float32
VMEM_LIMIT = 60 << 20


def worker_of(zh, y, x):
    return (zh % NZ) * NX * NY + (y % NY) * NX + (x % NX)


def move(value, axis, step):
    pairs = []
    for zh in range(NZ):
        for y in range(NY):
            for x in range(NX):
                to = {
                    "x": worker_of(zh, y, x + step),
                    "y": worker_of(zh, y + step, x),
                    "z": worker_of(zh + step, y, x),
                }[axis]
                pairs.append((worker_of(zh, y, x), to))
    return lax.ppermute(value, "worker", pairs)


def swap_tp(value, bit):
    return lax.ppermute(value, "tp", [(t, t ^ bit) for t in range(4)])


LOWER = [(i, j) for i in range(3) for j in range(i + 1)]


def cotangent_gram_body(grad_ref, gram_ref):
    for n, (i, j) in enumerate(LOWER):
        gram_ref[n] = lax.dot_general(
            grad_ref[i * HD:(i + 1) * HD, :], grad_ref[j * HD:(j + 1) * HD, :],
            (((1,), (1,)), ((), ())), preferred_element_type=f32,
        )


def cotangent_gram(grad):
    return pl.pallas_call(
        cotangent_gram_body,
        out_shape=jax.ShapeDtypeStruct((len(LOWER), HD, HD), f32),
        name="cotangent_gram",
    )(grad)


def attention_body(q_ref, k_ref, v_ref, seg_row_ref, ct_ref, gram_ref):
    tokens, width = q_ref.shape
    scale = 1.0 / math.sqrt(HD)
    blocks = tokens // HD
    seg_row = seg_row_ref[...]
    seg_col = jnp.broadcast_to(seg_row.astype(f32), (HD, tokens)).T.astype(jnp.int32)
    for h in range(width // HD):
        cols = slice(h * HD, (h + 1) * HD)
        for b in range(blocks):
            queries = slice(b * HD, (b + 1) * HD)
            seen = (b + 1) * HD
            scores = lax.dot_general(
                k_ref[:seen, cols], q_ref[queries, cols], (((1,), (1,)), ((), ())),
                preferred_element_type=f32,
            ) * scale
            key_at = lax.broadcasted_iota(jnp.int32, (seen, HD), 0)
            query_at = lax.broadcasted_iota(jnp.int32, (seen, HD), 1) + b * HD
            allowed = (key_at <= query_at) & (seg_col[:seen, :] == seg_row[:, queries])
            scores = jnp.where(allowed, scores, neg_big)
            exp_scores = jnp.exp(scores - jnp.max(scores, axis=0, keepdims=True))
            total = jnp.sum(exp_scores, axis=0, keepdims=True)
            weights = (exp_scores * (1.0 / total)).astype(bf16)
            ct_ref[cols, queries] = lax.dot_general(
                v_ref[:seen, cols], weights, (((0,), (0,)), ((), ())),
                preferred_element_type=f32,
            ).astype(bf16)
    for n, (i, j) in enumerate(LOWER):
        block = lax.dot_general(
            ct_ref[:, i * HD:(i + 1) * HD], ct_ref[:, j * HD:(j + 1) * HD],
            (((0,), (0,)), ((), ())), preferred_element_type=f32,
        )
        gram_ref[n] = block if i == j else 2.0 * block


def attention(queries, keys, values, segments):
    tokens, width = queries.shape
    return pl.pallas_call(
        attention_body,
        out_shape=(
            jax.ShapeDtypeStruct((width, tokens), bf16),
            jax.ShapeDtypeStruct((len(LOWER), HD, HD), f32),
        ),
        compiler_params=pltpu.CompilerParams(vmem_limit_bytes=VMEM_LIMIT),
        name="attention",
    )(queries, keys, values, segments.reshape(1, tokens))


def column_of(tp, half, quarter):
    first = (tp ^ (2 * half) ^ (quarter // 2)) * (2 * HALF_C) + (quarter % 2) * HALF_C
    return pl.multiple_of(first, HALF_C)


def row_of(zh, y, j, ky):
    return pl.multiple_of((zh ^ j) * (NY * TILE_R) + ((y + ky) % NY) * TILE_R, TILE_R)


K_ORDER = (2, 1, 3, 0)
UP_DOWN = ((2, 2, 1, 1), (3, 3, 2, 2))
FIRST = [[(0, n, far[n]) for n in range(4)] for far in UP_DOWN] + [
    [(1, far[n], n) for n in range(4)] for far in UP_DOWN
]
LATER = [
    [(0, n, 0) for n in range(4)], [(0, 0, 1), (0, 1, 1)], [(0, 2, 3), (0, 3, 3)],
    [(1, 0, n) for n in range(4)], [(1, 1, 0), (1, 1, 1)], [(1, 3, 2), (1, 3, 3)],
]


def pseudo_body(outputs, at_ref, scale_ref, ct_ref, g0_ref, g1_ref, g2_ref, g3_ref, drift_ref, *rest):
    outs = rest[:len(outputs)]
    drift_buf, g_buf, rows_buf, out_buf, drift_sems, g_sems, out_sems = rest[len(outputs):]
    x, y, zh, tp = at_ref[0], at_ref[1], at_ref[2], at_ref[3]
    scale = scale_ref[0]
    pieces = ((g0_ref, g1_ref), (g2_ref, g3_ref))

    def g_copy(slot, ref, k):
        return pltpu.make_async_copy(
            ref.at[:, pl.ds(pl.multiple_of(((x + k) % 2) * HALF_C, HALF_C), HALF_C)],
            g_buf.at[slot], g_sems.at[slot],
        )

    def g_start(slot, ref, k):
        g_copy(slot, ref, k).start()

    def drift_copy(slot, k, half):
        return pltpu.make_async_copy(
            drift_ref.at[0, :, pl.ds(column_of(tp, half, (x + k) % NX), HALF_C)],
            drift_buf.at[slot], drift_sems.at[slot],
        )

    steps = [(k, half) for k in K_ORDER for half in range(2)]
    for slot, (k, half) in enumerate(steps):
        for side, ref in enumerate(pieces[half]):
            pl.when(((x + k) % NX) // 2 == side)(functools.partial(g_start, slot, ref, k))
        drift_copy(slot, k, half).start()
    for j in range(2):
        for ky in range(NY):
            first = (j * NY + ky) * TILE_R
            rows_buf[first:first + TILE_R, :] = ct_ref[pl.ds(row_of(zh, y, j, ky), TILE_R), :]

    copies = []
    for slot, (k, half) in enumerate(steps):
        cols = slice(half * HALF_C, (half + 1) * HALF_C)
        g_copy(slot, g0_ref, k).wait()
        drift_copy(slot, k, half).wait()
        for j in range(2):
            rows = slice(j * NY * TILE_R, (j + 1) * NY * TILE_R)
            block = jnp.dot(rows_buf[rows, :], g_buf[slot], preferred_element_type=f32)
            for ky in range(NY):
                own = drift_buf[slot, pl.ds(row_of(zh, y, j, ky), TILE_R), :]
                value = block[ky * TILE_R:(ky + 1) * TILE_R] * scale + own.astype(f32)
                out_buf[k, j * NY + ky, :, cols] = value.astype(bf16)
        if half == 1:
            for j in range(2):
                for ky in range(NY):
                    o, index = next(
                        (o, tiles.index((j, ky, k))) for o, tiles in enumerate(outputs) if (j, ky, k) in tiles
                    )
                    copies.append(pltpu.make_async_copy(
                        out_buf.at[k, j * NY + ky], outs[o].at[index], out_sems.at[len(copies)]
                    ))
                    copies[-1].start()
    for one in copies:
        one.wait()


def pseudo_gradient(outputs, name, at, scale, ct, pieces, drift):
    smem = pl.BlockSpec(memory_space=pltpu.SMEM)
    hbm = pl.BlockSpec(memory_space=pl.ANY)
    tokens, rows = ct.shape[1], ct.shape[0]
    count = sum(len(tiles) for tiles in outputs)
    return pl.pallas_call(
        functools.partial(pseudo_body, outputs),
        out_shape=tuple(
            jax.ShapeDtypeStruct((len(tiles), TILE_R, 2 * HALF_C), bf16) for tiles in outputs
        ),
        in_specs=[smem, smem, pl.BlockSpec(memory_space=pltpu.VMEM)] + [hbm] * 5,
        out_specs=(hbm,) * len(outputs),
        scratch_shapes=[
            pltpu.VMEM((8, rows, HALF_C), bf16),
            pltpu.VMEM((8, tokens, HALF_C), bf16),
            pltpu.VMEM(ct.shape, bf16),
            pltpu.VMEM((NX, 2 * NY, TILE_R, 2 * HALF_C), bf16),
            pltpu.SemaphoreType.DMA((8,)),
            pltpu.SemaphoreType.DMA((8,)),
            pltpu.SemaphoreType.DMA((count,)),
        ],
        compiler_params=pltpu.CompilerParams(vmem_limit_bytes=VMEM_LIMIT),
        cost_estimate=pl.CostEstimate(
            flops=2 * rows * tokens * 5120, bytes_accessed=18_000_000, transcendentals=0
        ),
        name=name,
    )(at, scale, ct, *pieces, drift)


def base_body(at_ref, master_ref, momentum_ref, base_ref):
    tp = at_ref[3]
    for quarter in range(NX):
        for half in range(2):
            cols = pl.ds(column_of(tp, half, quarter), HALF_C)
            base_ref[quarter, :, half * HALF_C:(half + 1) * HALF_C] = (
                master_ref[:, cols] - (outer_rate * outer_mu * outer_mu) * momentum_ref[:, cols]
            )


def base_rows(at, master, momentum):
    vmem = pl.BlockSpec(memory_space=pltpu.VMEM)
    return pl.pallas_call(
        base_body,
        out_shape=jax.ShapeDtypeStruct((NX, master.shape[0], 2 * HALF_C), f32),
        in_specs=[pl.BlockSpec(memory_space=pltpu.SMEM), vmem, vmem],
        out_specs=vmem,
        name="base_rows",
    )(at, master, momentum)


def outer_body(at_ref, master_ref, momentum_ref, mean_ref, new_master_ref, new_momentum_ref):
    x, tp = at_ref[0], at_ref[3]
    for quarter in range(NX):
        for half in range(2):
            cols = pl.ds(column_of(tp, half, quarter), HALF_C)
            mean = mean_ref[(quarter - x + NX) % NX, :, half * HALF_C:(half + 1) * HALF_C]
            new = outer_mu * momentum_ref[:, cols] + mean
            new_momentum_ref[:, cols] = new
            new_master_ref[:, cols] = master_ref[:, cols] - outer_rate * (mean + outer_mu * new)


def outer_rows(at, master, momentum, mean):
    vmem = pl.BlockSpec(memory_space=pltpu.VMEM)
    out = jax.ShapeDtypeStruct(master.shape, f32)
    return pl.pallas_call(
        outer_body,
        out_shape=(out, out),
        in_specs=[pl.BlockSpec(memory_space=pltpu.SMEM), vmem, vmem, vmem],
        out_specs=(vmem, vmem),
        name="outer_rows",
    )(at, master, momentum, mean)


def place_body(where, at_ref, *rest):
    count = len(where)
    blocks, (out_ref, stage, in_sems, out_sems) = rest[:count], rest[-4:]
    x, y, zh, tp = at_ref[0], at_ref[1], at_ref[2], at_ref[3]
    slots = [sum(len(tiles) for tiles in where[:n]) for n in range(count)]
    loads = [
        pltpu.make_async_copy(blocks[n], stage.at[slots[n]:slots[n] + len(where[n])], in_sems.at[n])
        for n in range(count)
    ]
    for one in loads:
        one.start()
    stores = []
    for n, tiles in enumerate(where):
        loads[n].wait()
        for m, (j, ky, k) in enumerate(tiles):
            for half in range(2):
                stores.append(pltpu.make_async_copy(
                    stage.at[slots[n] + m, :, half * HALF_C:(half + 1) * HALF_C],
                    out_ref.at[pl.ds(row_of(zh, y, j, ky), TILE_R),
                               pl.ds(column_of(tp, half, (x + k) % NX), HALF_C)],
                    out_sems.at[len(stores)],
                ))
                stores[-1].start()
    for one in stores:
        one.wait()


def place(name, where, at, blocks, rows, width, so_far=None):
    hbm = pl.BlockSpec(memory_space=pl.ANY)
    count = sum(len(tiles) for tiles in where)
    operands = [at, *blocks] + ([] if so_far is None else [so_far])
    return pl.pallas_call(
        functools.partial(place_body, where),
        out_shape=jax.ShapeDtypeStruct((rows, width), bf16),
        in_specs=[pl.BlockSpec(memory_space=pltpu.SMEM)] + [hbm] * (len(operands) - 1),
        out_specs=hbm,
        scratch_shapes=[
            pltpu.VMEM((count, TILE_R, 2 * HALF_C), bf16),
            pltpu.SemaphoreType.DMA((len(where),)),
            pltpu.SemaphoreType.DMA((2 * count,)),
        ],
        input_output_aliases={} if so_far is None else {len(operands) - 1: 0},
        compiler_params=pltpu.CompilerParams(vmem_limit_bytes=VMEM_LIMIT),
        cost_estimate=pl.CostEstimate(
            flops=0, bytes_accessed=4 * count * TILE_R * 2 * HALF_C, transcendentals=0
        ),
        name=name,
    )(*operands)


def add(*terms):
    total = terms[0].astype(f32)
    for term in terms[1:]:
        total = total + term.astype(f32)
    return total


def ring(values, axis, sign):
    two = move(values[1], axis, 2 * sign)
    one = move(values[0], axis, sign)
    three = move(values[2], axis, -sign)
    return [one, two, three]


def pass_on(waves, later, axis):
    up, down = move(waves[0], axis, 1), move(waves[1], axis, -1)
    onward_up = add(later[1], up[:2]).astype(bf16)
    onward_down = add(later[2], down[2:]).astype(bf16)
    return up, down, onward_up, onward_down


def arrive(own, up, down, onward_up, onward_down, axis):
    last_up, last_down = move(onward_up, axis, 1), move(onward_down, axis, -1)
    low = add(own[:2], down[:2], last_up)
    high = add(own[2:], up[2:], last_down)
    return jnp.concatenate([low, high])


def reduce_tiles(tiles, axis):
    sent = tiles.astype(bf16)
    return add(tiles[0], *ring([sent[1], sent[2], sent[3]], axis, 1))


def per_device(queries, keys, values, out_grad, segments, drift, master, momentum):
    tp = lax.axis_index("tp")
    worker = lax.axis_index("worker")
    x, y, zh = worker % NX, (worker // NX) % NY, worker // (NX * NY)
    at = jnp.stack([x, y, zh, tp]).astype(jnp.int32)
    own_rows = master.shape[0]
    entries = queries.shape[1] * lax.axis_size("tp") * drift.shape[2]

    partner = swap_tp(out_grad, 1)

    packed = cotangent_gram(out_grad)
    side = (tp % 2) * 3
    mine = lax.dynamic_slice_in_dim(packed, side, 3, 0)
    mine = mine + swap_tp(lax.dynamic_slice_in_dim(packed, 3 - side, 3, 0), 1)
    far = swap_tp(mine, 2)

    mine, queries = lax.optimization_barrier((mine, queries))
    ct, own_gram = attention(queries, keys, values, segments)
    far, crossing = lax.optimization_barrier((far, out_grad))
    across = swap_tp(crossing, 2)
    ct, early_at = lax.optimization_barrier((ct, at))
    base = base_rows(early_at, master, momentum)
    rings = [[first + n for n in range(NX)] for first in range(0, NX * NY * NZ, NX)]
    base_tile = lax.all_to_all(base, "worker", 0, 0, axis_index_groups=rings)
    base_tile = base_tile.reshape(TILE_R, 2 * HALF_C)
    far, mine, ct, own_gram = lax.optimization_barrier((far, mine, ct, own_gram))
    mine = mine + far
    theirs = swap_tp(mine, 1)
    squares = jnp.sum(lax.dynamic_slice_in_dim(own_gram, side, 3, 0) * mine)
    squares = squares + jnp.sum(lax.dynamic_slice_in_dim(own_gram, 3 - side, 3, 0) * theirs)
    squares = jnp.full((8, 128), squares, f32)
    squares = squares + swap_tp(squares, 1)
    across, base_tile, squares = lax.optimization_barrier((across, base_tile, squares))
    across_partner = swap_tp(across, 1)
    squares = squares + swap_tp(squares, 2)
    scale = (inner_rate / jnp.sqrt(squares[0, :1] / entries + 1e-06))

    pieces = (out_grad, partner, across, across_partner)
    scale, base_tile = lax.optimization_barrier((scale, base_tile))
    sends = pseudo_gradient(FIRST + LATER, "pseudo_gradient", at, scale, ct, pieces, drift)
    waves, later = sends[:4], sends[4:]
    here, there = pass_on(waves[:2], later[:3], "x"), pass_on(waves[2:], later[3:], "y")
    there, base_tile = lax.optimization_barrier((there, base_tile))
    base_tiles = jnp.stack([base_tile, move(base_tile, "z", 1)])
    here, there = arrive(later[0], *here, "x"), arrive(later[3], *there, "y")
    here, there = reduce_tiles(here, "y"), reduce_tiles(there, "x")
    here, there = lax.reduce_precision(here, 8, 7), lax.reduce_precision(there, 8, 7)
    crossed = move(jnp.stack([there, here]).astype(bf16), "z", 1)
    means = (jnp.stack([here, there]) + crossed.astype(f32)) / lax.axis_size("worker")
    fresh = (base_tiles - (outer_rate * (1.0 + outer_mu)) * means).astype(bf16)
    mean, tile, opposite = means[0], fresh[0], fresh[1]

    def mean_rows(k):
        return lax.dynamic_slice_in_dim(mean, ((x + k) % NX) * own_rows, own_rows, 0)

    here_got = ring([tile] * 3, "y", -1)
    there_got = ring(
        [jnp.concatenate([opposite, mean_rows(NX - k).astype(bf16)]) for k in (1, 2, 3)], "x", -1
    )
    means = jnp.stack([mean_rows(0)] + [got[TILE_R:].astype(f32) for got in there_got])
    there_got = [got[:TILE_R] for got in there_got]
    here = jnp.stack([tile] + here_got)
    there = jnp.stack([opposite] + there_got)
    here, there, means = lax.optimization_barrier((here, there, means))
    here_1, here_3 = move(here, "x", -1), move(here, "x", 1)
    there_1, there_3 = move(there, "y", -1), move(there, "y", 1)
    last = [
        move(here_1[:2], "x", -1), move(here_3[2:], "x", 1),
        move(there_1[:2], "y", -1), move(there_3[2:], "y", 1),
    ]
    new_master, new_momentum = outer_rows(at, master, momentum, means)
    rows, width = drift.shape[1], drift.shape[2]
    so_far = place(
        "place_first",
        [[(0, n, k) for n in range(4)] for k in (0, 1, 3)] + [[(1, ky, n) for n in range(4)] for ky in (0, 1, 3)],
        at, [here, here_1, here_3, there, there_1, there_3], rows, width,
    )
    new_params = place(
        "place_last",
        [[(0, 0, 2), (0, 1, 2)], [(0, 2, 2), (0, 3, 2)], [(1, 2, 0), (1, 2, 1)], [(1, 2, 2), (1, 2, 3)]],
        at, last, rows, width, so_far,
    )
    return (new_params, new_master, new_momentum)


def solution(mesh):
    placed = (
        P("worker", "tp"),
        P("worker", "tp"),
        P("worker", "tp"),
        P("worker", "tp"),
        P("worker"),
        P("worker", "tp", None),
        P(("tp", "worker"), None),
        P(("tp", "worker"), None),
    )
    return jax.shard_map(
        per_device,
        mesh=mesh,
        in_specs=placed,
        out_specs=(P("tp", None), P(("tp", "worker"), None), P(("tp", "worker"), None)),
        check_vma=False,
    )
```

time: 201 us -> 181 us (0.900)
  waiting for transfers between devices: 102 us -> 74.1 us
  Pallas kernels: 25.1 us -> 29.9 us
  other arithmetic: 7.13 us -> 11 us
  local copies, waits for them, and re-layouts: 4.02 us -> 6.67 us
  matrix products: 2.18 us -> 0 us
  starting transfers between devices: 55.7 us -> 53.6 us
    ppermute x29 -> x30, waiting for transfers between devices: 92.7 us -> 57.6 us  [move(): return lax.ppermute(value, 'worker', pairs)]
    all_to_all x0 -> x1, waiting for transfers between devices: none -> 6.25 us  [per_device(): base_tile = lax.all_to_all(base, 'worker', 0, 0, axis_index_groups=rings)]
    ppermute x29 -> x30, starting transfers between devices: 51.7 us -> 46.3 us  [move(): return lax.ppermute(value, 'worker', pairs)]
    pallas_call x2 -> x4, Pallas kernels: 15.6 us -> 20.4 us  [the longest x1 9.59 us: pseudo_gradient(): pl.pallas_call(functools.partial(pseudo_body, outputs), out_shape=tuple((...]
    all_to_all x0 -> x1, starting transfers between devices: none -> 4.3 us  [per_device(): base_tile = lax.all_to_all(base, 'worker', 0, 0, axis_index_groups=rings)]
    slice x1 -> x5, local copies, waits for them, and re-layouts: 0.06 us -> 3.47 us  [the longest x1 0.89 us: per_device(): there_3[2:]]
    add x1 -> x3, other arithmetic: 0.04 us -> 2.67 us  [the longest x2 1.72 us: add(): total = total + term.astype(f32)]
    convert_element_type x3 -> x5, other arithmetic: 2.07 us -> 4.57 us  [the longest x2 2.22 us: pass_on(): onward_up = add(later[1], up[:2]).astype(bf16)]
  transfers between devices with their start and end apart: 37 -> 39, of which waited for: 17 -> 14; matrix products, arithmetic and copies ran while one was open for 6% -> 8% of each run, Pallas kernels for 5% -> 8%
where the time goes in v3:
time: 181 us; the launch traced here: 178 us
  waiting for transfers between devices  74.1 us (41%)
  starting transfers between devices  53.6 us (30%)
  Pallas kernels  29.9 us (17%)
  other arithmetic  11 us (6%)
  local copies, waits for them, and re-layouts  6.67 us (4%)
  between operations  3.12 us (2%)
    ppermute x30, waiting for transfers between devices, move(): return lax.ppermute(value, 'worker', pairs)  57.6 us
    ppermute x30, starting transfers between devices, move(): return lax.ppermute(value, 'worker', pairs)  46.3 us
    ppermute x8, waiting for transfers between devices, swap_tp(): return lax.ppermute(value, 'tp', [(t, t ^ bit) for t in range(4)])  10.2 us
    pallas_call x1, Pallas kernels, pseudo_gradient(): pl.pallas_call(functools.partial(pseudo_body, outputs), out_shape=tuple((...  9.59 us
    pallas_call x2, Pallas kernels, place(): pl.pallas_call(functools.partial(place_body, where), out_shape=jax.ShapeD...  8.15 us
    all_to_all x1, waiting for transfers between devices, per_device(): base_tile = lax.all_to_all(base, 'worker', 0, 0, axis_index_groups=rings)  6.25 us
    pallas_call x1, Pallas kernels, attention(): pl.pallas_call(attention_body, out_shape=(jax.ShapeDtypeStruct((width, to...  4.93 us
    all_to_all x1, starting transfers between devices, per_device(): base_tile = lax.all_to_all(base, 'worker', 0, 0, axis_index_groups=rings)  4.3 us
  transfers between devices with their start and end apart: 39, of which 14 were waited for; matrix products, arithmetic and copies ran while one was open for 8% of the time, Pallas kernels for 8%

profile of v3, /device:TPU:32, one launch (start us, length us, event | category | flops | bytes accessed | tf_op | source)
XLA Modules:
  0.0 178.4 jit_solution(1643322572926730203)
XLA Ops:
  0.7 2.7 %cotangent_gram.1 = f32[6,128,128]{2,1,0:T(8,128)} custom-call(bf16[384,1280]{1,0:T(8,128)(2,1)} %g0_ref.1), custom_call_target="tpu_custom_call" | custom-call | tf_op jit(solution)/shard_map/cotangent_gram/pallas_call | solution.py:59
  3.4 0.9 constant_dynamic-slice_fusion.1
  4.4 1.4 collective-permute-done
  5.8 0.9 dynamic-slice_add_fusion
  6.9 6.9 %collective-permute-done.1 = f32[3,128,128]{2,1,0:T(8,128)S(1)} collective-permute-done((f32[3,128,128]{2,1,0:T(8,128)S(1)}, f32[3,128,128]{2,1,0:T(8,128)S(1)}, u32[]{:S(2)}, u32[]{:S(2)}) %collective-permute-start.1) | collective-permute-done | bytes 196640 | tf_op jit(solution)/shard_map/ppermute | solution.py:44
  13.8 0.3 collective-permute-start.2
  14.1 1.2 reshape.27.seg_row_ref
  15.3 0.6 pad_add_fusion.at_ref
  15.9 4.9 %attention.1 = (bf16[640,384]{1,0:T(8,128)(2,1)}, f32[6,128,128]{2,1,0:T(8,128)}) custom-call(bf16[384,640]{1,0:T(8,128)(2,1)} %q_ref, bf16[384,640]{1,0:T(8,128)(2,1)} %k_ref.1, bf16[384,640]{1,0:T(8,128)(2,1)} %v_ref.1, s32[1,384]{1,0:T(1,128)} %reshape.27.seg_row_ref), custom_call_target="tpu_custom_call" | custom-call | tf_op jit(solution)/shard_map/attention/pallas_call | solution.py:102
  20.9 2.0 %base_rows.1 = f32[4,20,1280]{2,1,0:T(8,128)} custom-call(s32[4]{0:T(128)} %pad_add_fusion.at_ref, f32[20,5120]{1,0:T(8,128)} %master_ref.3, f32[20,5120]{1,0:T(8,128)} %momentum_ref.3), custom_call_target="tpu_custom_call" | custom-call | tf_op jit(solution)/shard_map/base_rows/pallas_call | solution.py:232
  23.0 4.3 %all-to-all-start = ((f32[4,20,1280]{2,1,0:T(8,128)}), f32[4,20,1280]{2,1,0:T(8,128)S(1)}, u32[]{:S(2)}, u32[]{:S(2)}) async-start(f32[4,20,1280]{2,1,0:T(8,128)} %base_rows.1), calls=%async_computation | async-start | bytes 983040 | tf_op jit(solution)/shard_map/all_to_all | solution.py:370
  27.3 1.7 multiply_reduce_fusion
  30.2 0.3 collective-permute-start.4
  30.5 0.3 collective-permute-start.6
  30.8 6.2 %all-to-all-done = f32[4,20,1280]{2,1,0:T(8,128)S(1)} async-done(((f32[4,20,1280]{2,1,0:T(8,128)}), f32[4,20,1280]{2,1,0:T(8,128)S(1)}, u32[]{:S(2)}, u32[]{:S(2)}) %all-to-all-start) | async-done | bytes 409632 | tf_op jit(solution)/shard_map/all_to_all | solution.py:370
  37.2 1.8 %collective-permute-start.5 = (f32[8,128]{1,0:T(8,128)S(1)}, f32[8,128]{1,0:T(8,128)S(1)}, u32[]{:S(2)}, u32[]{:S(2)}) collective-permute-start(f32[8,128]{1,0:T(8,128)S(1)} %broadcast_add_fusion), channel_id=1, source_target_pairs={{0,64},{32,96},{64,0},{96,32},{1,65},{33,97},{65,1},{97,33},{2,66}... | collective-permute-start | bytes 12296 | tf_op jit(solution)/shard_map/ppermute | solution.py:44
  39.1 1.9 %collective-permute-done.5 = f32[8,128]{1,0:T(8,128)S(1)} collective-permute-done((f32[8,128]{1,0:T(8,128)S(1)}, f32[8,128]{1,0:T(8,128)S(1)}, u32[]{:S(2)}, u32[]{:S(2)}) %collective-permute-start.5) | collective-permute-done | bytes 4128 | tf_op jit(solution)/shard_map/ppermute | solution.py:44
  40.9 0.5 slice.108
  42.2 9.6 %pseudo_gradient.1 = (bf16[4,80,1280]{2,1,0:T(8,128)(2,1)}, bf16[4,80,1280]{2,1,0:T(8,128)(2,1)}, bf16[4,80,1280]{2,1,0:T(8,128)(2,1)}, bf16[4,80,1280]{2,1,0:T(...) custom-call(s32[4]{0:T(128)} %pad_add_fusion.at_ref, ...), custom_call_target="tpu_custom_call" | custom-call | flops 2516582400 | bytes 18000000 | tf_op jit(solution)/shard_map/pseudo_gradient/pallas_call | solution.py:196
  51.8 3.0 %collective-permute-start.9 = (bf16[4,80,1280]{2,1,0:T(8,128)(2,1)}, bf16[4,80,1280]{2,1,0:T(8,128)(2,1)S(1)}, u32[]{:S(2)}, u32[]{:S(2)}) collective-permute-start(bf16[4,80,1280]{2,1,0:T(8,128)(2,1)} %get-tuple-element.57), channel_id=1, source_target_pairs={{0,12},{1,13},{2,14},{3,15},{4,0},{5,1},{6,2},{7,3},{8,4},{9,5},{1... | collective-permute-start | bytes 2457608 | tf_op jit(solution)/shard_map/ppermute | solution.py:40
  54.8 2.4 %collective-permute-start.11 = (bf16[4,80,1280]{2,1,0:T(8,128)(2,1)}, bf16[4,80,1280]{2,1,0:T(8,128)(2,1)S(1)}, u32[]{:S(2)}, u32[]{:S(2)}) collective-permute-start(bf16[4,80,1280]{2,1,0:T(8,128)(2,1)} %get-tuple-element.63), channel_id=1, source_target_pairs={{0,3},{1,0},{2,1},{3,2},{4,7},{5,4},{6,5},{7,6},{8,11},{9,8},{10,9... | collective-permute-start | bytes 2457608 | tf_op jit(solution)/shard_map/ppermute | solution.py:40
  57.3 14.8 %collective-permute-done.9 = bf16[4,80,1280]{2,1,0:T(8,128)(2,1)S(1)} collective-permute-done((bf16[4,80,1280]{2,1,0:T(8,128)(2,1)}, bf16[4,80,1280]{2,1,0:T(8,128)(2,1)S(1)}, u32[]{:S(2)}, u32[]{:S(2)}) %collective-permute-start.9) | collective-permute-done | bytes 819232 | tf_op jit(solution)/shard_map/ppermute | solution.py:40
  72.1 1.1 add_convert_fusion.4
  73.2 2.2 %collective-permute-done.8 = bf16[4,80,1280]{2,1,0:T(8,128)(2,1)S(1)} collective-permute-done((bf16[4,80,1280]{2,1,0:T(8,128)(2,1)}, bf16[4,80,1280]{2,1,0:T(8,128)(2,1)S(1)}, u32[]{:S(2)}, u32[]{:S(2)}) %collective-permute-start.8) | collective-permute-done | bytes 819232 | tf_op jit(solution)/shard_map/ppermute | solution.py:40
  75.4 1.1 add_convert_fusion.5
  76.6 3.2 %collective-permute-start.20 = (bf16[2,80,1280]{2,1,0:T(8,128)(2,1)S(1)}, bf16[2,80,1280]{2,1,0:T(8,128)(2,1)S(1)}, u32[]{:S(2)}, u32[]{:S(2)}) collective-permute-start(bf16[2,80,1280]{2,1,0:T(8,128)(2,1)S(1)} %add_convert_fusion.4), channel_id=1, source_target_pairs={{0,12},{1,13},{2,14},{3,15},{4,0},{5,1},{6,2},{7,3},{8,4},{9,5},{1... | collective-permute-start | bytes 1228808 | tf_op jit(solution)/shard_map/ppermute | solution.py:40
  79.8 1.1 add_convert_fusion.2
  80.9 2.6 %collective-permute-start.15 = (bf16[2,80,1280]{2,1,0:T(8,128)(2,1)S(1)}, bf16[2,80,1280]{2,1,0:T(8,128)(2,1)S(1)}, u32[]{:S(2)}, u32[]{:S(2)}) collective-permute-start(bf16[2,80,1280]{2,1,0:T(8,128)(2,1)S(1)} %add_convert_fusion.2), channel_id=1, source_target_pairs={{0,3},{1,0},{2,1},{3,2},{4,7},{5,4},{6,5},{7,6},{8,11},{9,8},{10,9... | collective-permute-start | bytes 1228808 | tf_op jit(solution)/shard_map/ppermute | solution.py:40
  83.5 1.1 add_convert_fusion.3
  84.7 3.1 %collective-permute-start.10 = (f32[80,1280]{1,0:T(8,128)S(1)}, f32[80,1280]{1,0:T(8,128)S(1)}, u32[]{:S(2)}, u32[]{:S(2)}) collective-permute-start(f32[80,1280]{1,0:T(8,128)S(1)} %reshape.28), channel_id=1, source_target_pairs={{0,16},{1,17},{2,18},{3,19},{4,20},{5,21},{6,22},{7,23},{8,24},{9,... | collective-permute-start | bytes 1228808 | tf_op jit(solution)/shard_map/ppermute | solution.py:40
  87.8 1.4 convert_add_fusion
  89.3 2.4 %collective-permute-start.21 = (bf16[80,1280]{1,0:T(8,128)(2,1)S(1)}, bf16[80,1280]{1,0:T(8,128)(2,1)S(1)}, u32[]{:S(2)}, u32[]{:S(2)}) collective-permute-start(bf16[80,1280]{1,0:T(8,128)(2,1)S(1)} %get-tuple-element.96), channel_id=1, source_target_pairs={{0,2},{1,3},{2,0},{3,1},{4,6},{5,7},{6,4},{7,5},{8,10},{9,11},{10,... | collective-permute-start | bytes 614408 | tf_op jit(solution)/shard_map/ppermute | solution.py:40
  91.6 1.2 collective-permute-start.22
  92.8 0.9 collective-permute-start.19
  93.8 7.4 %collective-permute-done.13 = bf16[2,80,1280]{2,1,0:T(8,128)(2,1)S(1)} collective-permute-done((bf16[2,80,1280]{2,1,0:T(8,128)(2,1)S(1)}, bf16[2,80,1280]{2,1,0:T(8,128)(2,1)S(1)}, u32[]{:S(2)}, u32[]{:S(2)}) %collective-permute-start.13) | collective-permute-done | bytes 409632 | tf_op jit(solution)/shard_map/ppermute | solution.py:40
  101.2 0.3 convert_add_fusion.1
  101.6 1.8 %collective-permute-start.17 = (bf16[80,1280]{1,0:T(8,128)(2,1)S(1)}, bf16[80,1280]{1,0:T(8,128)(2,1)S(1)}, u32[]{:S(2)}, u32[]{:S(2)}) collective-permute-start(bf16[80,1280]{1,0:T(8,128)(2,1)S(1)} %get-tuple-element.99), channel_id=1, source_target_pairs={{0,12},{1,13},{2,14},{3,15},{4,0},{5,1},{6,2},{7,3},{8,4},{9,5},{1... | collective-permute-start | bytes 614408 | tf_op jit(solution)/shard_map/ppermute | solution.py:40
  103.4 0.3 collective-permute-start.14
  103.9 5.0 %collective-permute-done.16 = bf16[80,1280]{1,0:T(8,128)(2,1)S(1)} collective-permute-done((bf16[80,1280]{1,0:T(8,128)(2,1)S(1)}, bf16[80,1280]{1,0:T(8,128)(2,1)S(1)}, u32[]{:S(2)}, u32[]{:S(2)}) %collective-permute-start.16) | collective-permute-done | bytes 204832 | tf_op jit(solution)/shard_map/ppermute | solution.py:40
  108.9 2.1 %collective-permute-done.14 = bf16[80,1280]{1,0:T(8,128)(2,1)S(1)} collective-permute-done((bf16[80,1280]{1,0:T(8,128)(2,1)S(1)}, bf16[80,1280]{1,0:T(8,128)(2,1)S(1)}, u32[]{:S(2)}, u32[]{:S(2)}) %collective-permute-start.14) | collective-permute-done | bytes 204832 | tf_op jit(solution)/shard_map/ppermute | solution.py:40
  111.2 3.1 %collective-permute-start.23 = (bf16[2,80,1280]{2,1,0:T(8,128)(2,1)S(1)}, bf16[2,80,1280]{2,1,0:T(8,128)(2,1)S(1)}, u32[]{:S(2)}, u32[]{:S(2)}) collective-permute-start(bf16[2,80,1280]{2,1,0:T(8,128)(2,1)S(1)} %pad_maximum_fusion.3), channel_id=1, source_target_pairs={{0,16},{1,17},{2,18},{3,19},{4,20},{5,21},{6,22},{7,23},{8,24},{9,... | collective-permute-start | bytes 1228808 | tf_op jit(solution)/shard_map/ppermute | solution.py:40
  114.3 6.5 %collective-permute-done.23 = bf16[2,80,1280]{2,1,0:T(8,128)(2,1)S(1)} collective-permute-done((bf16[2,80,1280]{2,1,0:T(8,128)(2,1)S(1)}, bf16[2,80,1280]{2,1,0:T(8,128)(2,1)S(1)}, u32[]{:S(2)}, u32[]{:S(2)}) %collective-permute-start.23) | collective-permute-done | bytes 409632 | tf_op jit(solution)/shard_map/ppermute | solution.py:40
  120.9 0.6 collective-permute-start.24
  121.6 0.6 collective-permute-start.25
  122.2 0.9 collective-permute-start.26
  123.3 4.2 %collective-permute-start.28 = (bf16[100,1280]{1,0:T(8,128)(2,1)S(1)}, bf16[100,1280]{1,0:T(8,128)(2,1)S(1)}, u32[]{:S(2)}, u32[]{:S(2)}) collective-permute-start(bf16[100,1280]{1,0:T(8,128)(2,1)S(1)} %get-tuple-element.101), channel_id=1, source_target_pairs={{0,2},{1,3},{2,0},{3,1},{4,6},{5,7},{6,4},{7,5},{8,10},{9,11},{10,... | collective-permute-start | bytes 768008 | tf_op jit(solution)/shard_map/ppermute | solution.py:40
  127.5 3.7 %collective-permute-start.27 = (bf16[100,1280]{1,0:T(8,128)(2,1)S(1)}, bf16[100,1280]{1,0:T(8,128)(2,1)S(1)}, u32[]{:S(2)}, u32[]{:S(2)}) collective-permute-start(bf16[100,1280]{1,0:T(8,128)(2,1)S(1)} %get-tuple-element.100), channel_id=1, source_target_pairs={{0,3},{1,0},{2,1},{3,2},{4,7},{5,4},{6,5},{7,6},{8,11},{9,8},{10,9... | collective-permute-start | bytes 768008 | tf_op jit(solution)/shard_map/ppermute | solution.py:40
  131.3 2.5 %collective-permute-done.29 = bf16[100,1280]{1,0:T(8,128)(2,1)S(1)} collective-permute-done((bf16[100,1280]{1,0:T(8,128)(2,1)S(1)}, bf16[100,1280]{1,0:T(8,128)(2,1)S(1)}, u32[]{:S(2)}, u32[]{:S(2)}) %collective-permute-start.29) | collective-permute-done | bytes 256032 | tf_op jit(solution)/shard_map/ppermute | solution.py:40
  133.7 3.4 %collective-permute-done.28 = bf16[100,1280]{1,0:T(8,128)(2,1)S(1)} collective-permute-done((bf16[100,1280]{1,0:T(8,128)(2,1)S(1)}, bf16[100,1280]{1,0:T(8,128)(2,1)S(1)}, u32[]{:S(2)}, u32[]{:S(2)}) %collective-permute-start.28) | collective-permute-done | bytes 256032 | tf_op jit(solution)/shard_map/ppermute | solution.py:40
  137.1 0.8 pad_maximum_fusion.2.mean_ref
  138.1 2.2 %collective-permute-start.30 = (bf16[4,80,1280]{2,1,0:T(8,128)(2,1)S(1)}, bf16[4,80,1280]{2,1,0:T(8,128)(2,1)S(1)}, u32[]{:S(2)}, u32[]{:S(2)}) collective-permute-start(bf16[4,80,1280]{2,1,0:T(8,128)(2,1)S(1)} %pad_maximum_fusion.rest_0_), channel_id=1, source_target_pairs={{0,3},{1,0},{2,1},{3,2},{4,7},{5,4},{6,5},{7,6},{8,11},{9,8},{10,9... | collective-permute-start | bytes 2457608 | tf_op jit(solution)/shard_map/ppermute | solution.py:40
  140.3 2.7 %collective-permute-start.34 = (bf16[4,80,1280]{2,1,0:T(8,128)(2,1)S(1)}, bf16[4,80,1280]{2,1,0:T(8,128)(2,1)S(1)}, u32[]{:S(2)}, u32[]{:S(2)}) collective-permute-start(bf16[4,80,1280]{2,1,0:T(8,128)(2,1)S(1)} %pad_maximum_fusion.1.rest_3_), channel_id=1, source_target_pairs={{0,12},{1,13},{2,14},{3,15},{4,0},{5,1},{6,2},{7,3},{8,4},{9,5},{1... | collective-permute-start | bytes 2457608 | tf_op jit(solution)/shard_map/ppermute | solution.py:40
  143.0 11.8 %collective-permute-done.30.rest_1_ = bf16[4,80,1280]{2,1,0:T(8,128)(2,1)S(1)} collective-permute-done((bf16[4,80,1280]{2,1,0:T(8,128)(2,1)S(1)}, bf16[4,80,1280]{2,1,0:T(8,128)(2,1)S(1)}, u32[]{:S(2)}, u32[]{:S(2)}) %collective-permute-start.30) | collective-permute-done | bytes 819232 | tf_op jit(solution)/shard_map/ppermute | solution.py:40
  154.8 0.8 slice.165
  155.6 3.2 %collective-permute-start.31 = (bf16[2,80,1280]{2,1,0:T(8,128)(2,1)}, bf16[2,80,1280]{2,1,0:T(8,128)(2,1)}, u32[]{:S(2)}, u32[]{:S(2)}) collective-permute-start(bf16[2,80,1280]{2,1,0:T(8,128)(2,1)} %slice.165), channel_id=1, source_target_pairs={{0,3},{1,0},{2,1},{3,2},{4,7},{5,4},{6,5},{7,6},{8,11},{9,8},{10,9... | collective-permute-start | bytes 1228808 | tf_op jit(solution)/shard_map/ppermute | solution.py:40
  158.9 0.8 slice.166
  159.7 0.9 slice.167
  160.6 3.9 %collective-permute-start.35 = (bf16[2,80,1280]{2,1,0:T(8,128)(2,1)}, bf16[2,80,1280]{2,1,0:T(8,128)(2,1)}, u32[]{:S(2)}, u32[]{:S(2)}) collective-permute-start(bf16[2,80,1280]{2,1,0:T(8,128)(2,1)} %slice.167), channel_id=1, source_target_pairs={{0,12},{1,13},{2,14},{3,15},{4,0},{5,1},{6,2},{7,3},{8,4},{9,5},{1... | collective-permute-start | bytes 1228808 | tf_op jit(solution)/shard_map/ppermute | solution.py:40
  164.5 0.9 slice.168
  165.4 0.2 copy-done.6
  165.6 2.4 %outer_rows.1 = (f32[20,5120]{1,0:T(8,128)}, f32[20,5120]{1,0:T(8,128)}) custom-call(s32[4]{0:T(128)} %pad_add_fusion.at_ref, f32[20,5120]{1,0:T(8,128)} %master_ref.3, f32[20,5120]{1,0:T(8,128)} %momentum_ref.3, f32[4,20,1280]{2,1,0:T(8,128)} %pad_maximum_fusion.2.mean_ref), custom_call_target="tpu_custom_call" | custom-call | tf_op jit(solution)/shard_map/outer_rows/pallas_call | solution.py:255
  168.1 5.2 %place_first.1.rest_4_ = bf16[640,5120]{1,0:T(8,128)(2,1)} custom-call(s32[4]{0:T(128)} %pad_add_fusion.at_ref, bf16[4,80,1280]{2,1,0:T(8,128)(2,1)} %copy-done.1, bf16[4,80,1280]{2,1,0:T(8,128)(2,1)} %copy-done.3, bf16[4,80,1280]{2,1,0:T(8,128)(2,1)} %copy-done.4, bf16[4,80,1280]{2,1,0:T(8,128)(2,1)} %copy-done.2, bf16[4,80,1280]{2,1,0:T(8,128)(2,1)} %copy-done.5, ...), custom_call_target="tpu_custom_call" | custom-call | bytes 9830400 | tf_op jit(solution)/shard_map/place_first/pallas_call | solution.py:295
  173.3 1.9 %collective-permute-done.37.rest_3_ = bf16[2,80,1280]{2,1,0:T(8,128)(2,1)} collective-permute-done((bf16[2,80,1280]{2,1,0:T(8,128)(2,1)}, bf16[2,80,1280]{2,1,0:T(8,128)(2,1)}, u32[]{:S(2)}, u32[]{:S(2)}) %collective-permute-start.37) | collective-permute-done | bytes 409632 | tf_op jit(solution)/shard_map/ppermute | solution.py:40
  175.2 3.0 %place_last.1 = bf16[640,5120]{1,0:T(8,128)(2,1)} custom-call(s32[4]{0:T(128)} %pad_add_fusion.at_ref, bf16[2,80,1280]{2,1,0:T(8,128)(2,1)} %collective-permute-done.31.rest_0_, bf16[2,80,1280]{2,1,0:T(8,128)(2,1)} %collective-permute-done.33.rest_1_, bf16[2,80,1280]{2,1,0:T(8,128)(2,1)} %collective-permute-done.35.rest_2_, ...), custom_call_target="tpu_custom_call", output_to_operand_aliasing={{}: (5, {})} | custom-call | bytes 3276800 | tf_op jit(solution)/shard_map/place_last/pallas_call | solution.py:295
  (82 shorter events, 1.9 us)
Async XLA Ops:
  0.6 29.9 %copy-start = (bf16[384,1280]{1,0:T(8,128)(2,1)S(1)}, bf16[384,1280]{1,0:T(8,128)(2,1)}, u32[]{:S(2)}) copy-start(bf16[384,1280]{1,0:T(8,128)(2,1)} %g0_ref.1) | copy-start | bytes 2949124
  4.3 1.5 collective-permute-start
  6.8 7.0 %collective-permute-start.1 = (f32[3,128,128]{2,1,0:T(8,128)S(1)}, f32[3,128,128]{2,1,0:T(8,128)S(1)}, u32[]{:S(2)}, u32[]{:S(2)}) collective-permute-start(f32[3,128,128]{2,1,0:T(8,128)S(1)} %dynamic-slice_add_fusion), channel_id=1, source_target_pairs={{0,64},{32,96},{64,0},{96,32},{1,65},{33,97},{65,1},{97,33},{2,66}... | collective-permute-start | bytes 589832 | tf_op jit(solution)/shard_map/ppermute | solution.py:44
  13.8 23.3 %collective-permute-start.2 = (bf16[384,1280]{1,0:T(8,128)(2,1)}, bf16[384,1280]{1,0:T(8,128)(2,1)S(1)}, u32[]{:S(2)}, u32[]{:S(2)}) collective-permute-start(bf16[384,1280]{1,0:T(8,128)(2,1)} %g0_ref.1), channel_id=1, source_target_pairs={{0,64},{32,96},{64,0},{96,32},{1,65},{33,97},{65,1},{97,33},{2,66}... | collective-permute-start | bytes 2949128 | tf_op jit(solution)/shard_map/ppermute | solution.py:44
  20.8 6.4 %collective-permute-start.3 = (f32[3,128,128]{2,1,0:T(8,128)S(1)}, f32[3,128,128]{2,1,0:T(8,128)S(1)}, u32[]{:S(2)}, u32[]{:S(2)}) collective-permute-start(f32[3,128,128]{2,1,0:T(8,128)S(1)} %add.136), channel_id=1, source_target_pairs={{0,32},{32,0},{64,96},{96,64},{1,33},{33,1},{65,97},{97,65},{2,34}... | collective-permute-start | bytes 589832 | tf_op jit(solution)/shard_map/ppermute | solution.py:44
  23.0 14.1 %all-to-all-start = ((f32[4,20,1280]{2,1,0:T(8,128)}), f32[4,20,1280]{2,1,0:T(8,128)S(1)}, u32[]{:S(2)}, u32[]{:S(2)}) async-start(f32[4,20,1280]{2,1,0:T(8,128)} %base_rows.1), calls=%async_computation | async-start | bytes 983040 | tf_op jit(solution)/shard_map/all_to_all | solution.py:370
  30.2 6.9 %collective-permute-start.4 = (f32[8,128]{1,0:T(8,128)S(1)}, f32[8,128]{1,0:T(8,128)S(1)}, u32[]{:S(2)}, u32[]{:S(2)}) collective-permute-start(f32[8,128]{1,0:T(8,128)S(1)} %broadcast_in_dim.3), channel_id=1, source_target_pairs={{0,32},{32,0},{64,96},{96,64},{1,33},{33,1},{65,97},{97,65},{2,34}... | collective-permute-start | bytes 12296 | tf_op jit(solution)/shard_map/ppermute | solution.py:44
  30.5 11.6 %collective-permute-start.6 = (bf16[384,1280]{1,0:T(8,128)(2,1)S(1)}, bf16[384,1280]{1,0:T(8,128)(2,1)}, u32[]{:S(2)}, u32[]{:S(2)}) collective-permute-start(bf16[384,1280]{1,0:T(8,128)(2,1)S(1)} %copy-done), channel_id=1, source_target_pairs={{0,32},{32,0},{64,96},{96,64},{1,33},{33,1},{65,97},{97,65},{2,34}... | collective-permute-start | bytes 2949128 | tf_op jit(solution)/shard_map/ppermute | solution.py:44
  37.1 5.0 %copy-start.7 = (bf16[384,1280]{1,0:T(8,128)(2,1)}, bf16[384,1280]{1,0:T(8,128)(2,1)S(1)}, u32[]{:S(2)}) copy-start(bf16[384,1280]{1,0:T(8,128)(2,1)S(1)} %collective-permute-done.2.g2_ref) | copy-start | bytes 2949124
  37.2 5.0 %collective-permute-start.7 = (bf16[384,1280]{1,0:T(8,128)(2,1)S(1)}, bf16[384,1280]{1,0:T(8,128)(2,1)}, u32[]{:S(2)}, u32[]{:S(2)}) collective-permute-start(bf16[384,1280]{1,0:T(8,128)(2,1)S(1)} %collective-permute-done.2.g2_ref), channel_id=1, source_target_pairs={{0,32},{32,0},{64,96},{96,64},{1,33},{33,1},{65,97},{97,65},{2,34}... | collective-permute-start | bytes 2949128 | tf_op jit(solution)/shard_map/ppermute | solution.py:44
  37.2 3.7 %collective-permute-start.5 = (f32[8,128]{1,0:T(8,128)S(1)}, f32[8,128]{1,0:T(8,128)S(1)}, u32[]{:S(2)}, u32[]{:S(2)}) collective-permute-start(f32[8,128]{1,0:T(8,128)S(1)} %broadcast_add_fusion), channel_id=1, source_target_pairs={{0,64},{32,96},{64,0},{96,32},{1,65},{33,97},{65,1},{97,33},{2,66}... | collective-permute-start | bytes 12296 | tf_op jit(solution)/shard_map/ppermute | solution.py:44
  51.8 49.4 %copy-start.8 = (bf16[4,80,1280]{2,1,0:T(8,128)(2,1)S(1)}, bf16[4,80,1280]{2,1,0:T(8,128)(2,1)}, u32[]{:S(2)}) copy-start(bf16[4,80,1280]{2,1,0:T(8,128)(2,1)} %get-tuple-element.62) | copy-start | bytes 2457604
  51.8 20.3 %collective-permute-start.9 = (bf16[4,80,1280]{2,1,0:T(8,128)(2,1)}, bf16[4,80,1280]{2,1,0:T(8,128)(2,1)S(1)}, u32[]{:S(2)}, u32[]{:S(2)}) collective-permute-start(bf16[4,80,1280]{2,1,0:T(8,128)(2,1)} %get-tuple-element.57), channel_id=1, source_target_pairs={{0,12},{1,13},{2,14},{3,15},{4,0},{5,1},{6,2},{7,3},{8,4},{9,5},{1... | collective-permute-start | bytes 2457608 | tf_op jit(solution)/shard_map/ppermute | solution.py:40
  54.8 20.6 %collective-permute-start.8 = (bf16[4,80,1280]{2,1,0:T(8,128)(2,1)}, bf16[4,80,1280]{2,1,0:T(8,128)(2,1)S(1)}, u32[]{:S(2)}, u32[]{:S(2)}) collective-permute-start(bf16[4,80,1280]{2,1,0:T(8,128)(2,1)} %get-tuple-element.56), channel_id=1, source_target_pairs={{0,4},{1,5},{2,6},{3,7},{4,8},{5,9},{6,10},{7,11},{8,12},{9,13},{1... | collective-permute-start | bytes 2457608 | tf_op jit(solution)/shard_map/ppermute | solution.py:40
  54.8 25.0 %collective-permute-start.11 = (bf16[4,80,1280]{2,1,0:T(8,128)(2,1)}, bf16[4,80,1280]{2,1,0:T(8,128)(2,1)S(1)}, u32[]{:S(2)}, u32[]{:S(2)}) collective-permute-start(bf16[4,80,1280]{2,1,0:T(8,128)(2,1)} %get-tuple-element.63), channel_id=1, source_target_pairs={{0,3},{1,0},{2,1},{3,2},{4,7},{5,4},{6,5},{7,6},{8,11},{9,8},{10,9... | collective-permute-start | bytes 2457608 | tf_op jit(solution)/shard_map/ppermute | solution.py:40
  57.3 26.3 %collective-permute-start.12 = (bf16[4,80,1280]{2,1,0:T(8,128)(2,1)}, bf16[4,80,1280]{2,1,0:T(8,128)(2,1)S(1)}, u32[]{:S(2)}, u32[]{:S(2)}) collective-permute-start(bf16[4,80,1280]{2,1,0:T(8,128)(2,1)} %get-tuple-element.65), channel_id=1, source_target_pairs={{0,1},{1,2},{2,3},{3,0},{4,5},{5,6},{6,7},{7,4},{8,9},{9,10},{10,1... | collective-permute-start | bytes 2457608 | tf_op jit(solution)/shard_map/ppermute | solution.py:40
  76.5 11.3 %collective-permute-start.18 = (bf16[2,80,1280]{2,1,0:T(8,128)(2,1)S(1)}, bf16[2,80,1280]{2,1,0:T(8,128)(2,1)S(1)}, u32[]{:S(2)}, u32[]{:S(2)}) collective-permute-start(bf16[2,80,1280]{2,1,0:T(8,128)(2,1)S(1)} %add_convert_fusion.5), channel_id=1, source_target_pairs={{0,4},{1,5},{2,6},{3,7},{4,8},{5,9},{6,10},{7,11},{8,12},{9,13},{1... | collective-permute-start | bytes 1228808 | tf_op jit(solution)/shard_map/ppermute | solution.py:40
  76.6 11.2 %collective-permute-start.20 = (bf16[2,80,1280]{2,1,0:T(8,128)(2,1)S(1)}, bf16[2,80,1280]{2,1,0:T(8,128)(2,1)S(1)}, u32[]{:S(2)}, u32[]{:S(2)}) collective-permute-start(bf16[2,80,1280]{2,1,0:T(8,128)(2,1)S(1)} %add_convert_fusion.4), channel_id=1, source_target_pairs={{0,12},{1,13},{2,14},{3,15},{4,0},{5,1},{6,2},{7,3},{8,4},{9,5},{1... | collective-permute-start | bytes 1228808 | tf_op jit(solution)/shard_map/ppermute | solution.py:40
  80.9 11.9 %collective-permute-start.15 = (bf16[2,80,1280]{2,1,0:T(8,128)(2,1)S(1)}, bf16[2,80,1280]{2,1,0:T(8,128)(2,1)S(1)}, u32[]{:S(2)}, u32[]{:S(2)}) collective-permute-start(bf16[2,80,1280]{2,1,0:T(8,128)(2,1)S(1)} %add_convert_fusion.2), channel_id=1, source_target_pairs={{0,3},{1,0},{2,1},{3,2},{4,7},{5,4},{6,5},{7,6},{8,11},{9,8},{10,9... | collective-permute-start | bytes 1228808 | tf_op jit(solution)/shard_map/ppermute | solution.py:40
  84.6 16.5 %collective-permute-start.13 = (bf16[2,80,1280]{2,1,0:T(8,128)(2,1)S(1)}, bf16[2,80,1280]{2,1,0:T(8,128)(2,1)S(1)}, u32[]{:S(2)}, u32[]{:S(2)}) collective-permute-start(bf16[2,80,1280]{2,1,0:T(8,128)(2,1)S(1)} %add_convert_fusion.3), channel_id=1, source_target_pairs={{0,1},{1,2},{2,3},{3,0},{4,5},{5,6},{6,7},{7,4},{8,9},{9,10},{10,1... | collective-permute-start | bytes 1228808 | tf_op jit(solution)/shard_map/ppermute | solution.py:40
  84.7 29.5 %collective-permute-start.10 = (f32[80,1280]{1,0:T(8,128)S(1)}, f32[80,1280]{1,0:T(8,128)S(1)}, u32[]{:S(2)}, u32[]{:S(2)}) collective-permute-start(f32[80,1280]{1,0:T(8,128)S(1)} %reshape.28), channel_id=1, source_target_pairs={{0,16},{1,17},{2,18},{3,19},{4,20},{5,21},{6,22},{7,23},{8,24},{9,... | collective-permute-start | bytes 1228808 | tf_op jit(solution)/shard_map/ppermute | solution.py:40
  89.3 12.4 %collective-permute-start.21 = (bf16[80,1280]{1,0:T(8,128)(2,1)S(1)}, bf16[80,1280]{1,0:T(8,128)(2,1)S(1)}, u32[]{:S(2)}, u32[]{:S(2)}) collective-permute-start(bf16[80,1280]{1,0:T(8,128)(2,1)S(1)} %get-tuple-element.96), channel_id=1, source_target_pairs={{0,2},{1,3},{2,0},{3,1},{4,6},{5,7},{6,4},{7,5},{8,10},{9,11},{10,... | collective-permute-start | bytes 614408 | tf_op jit(solution)/shard_map/ppermute | solution.py:40
  91.6 11.8 %collective-permute-start.22 = (bf16[80,1280]{1,0:T(8,128)(2,1)S(1)}, bf16[80,1280]{1,0:T(8,128)(2,1)S(1)}, u32[]{:S(2)}, u32[]{:S(2)}) collective-permute-start(bf16[80,1280]{1,0:T(8,128)(2,1)S(1)} %get-tuple-element.97), channel_id=1, source_target_pairs={{0,3},{1,0},{2,1},{3,2},{4,7},{5,4},{6,5},{7,6},{8,11},{9,8},{10,9... | collective-permute-start | bytes 614408 | tf_op jit(solution)/shard_map/ppermute | solution.py:40
  92.8 10.9 %collective-permute-start.19 = (bf16[80,1280]{1,0:T(8,128)(2,1)S(1)}, bf16[80,1280]{1,0:T(8,128)(2,1)S(1)}, u32[]{:S(2)}, u32[]{:S(2)}) collective-permute-start(bf16[80,1280]{1,0:T(8,128)(2,1)S(1)} %fusion.12), channel_id=1, source_target_pairs={{0,1},{1,2},{2,3},{3,0},{4,5},{5,6},{6,7},{7,4},{8,9},{9,10},{10,1... | collective-permute-start | bytes 614408 | tf_op jit(solution)/shard_map/ppermute | solution.py:40
  101.5 7.4 %collective-permute-start.16 = (bf16[80,1280]{1,0:T(8,128)(2,1)S(1)}, bf16[80,1280]{1,0:T(8,128)(2,1)S(1)}, u32[]{:S(2)}, u32[]{:S(2)}) collective-permute-start(bf16[80,1280]{1,0:T(8,128)(2,1)S(1)} %get-tuple-element.98), channel_id=1, source_target_pairs={{0,8},{1,9},{2,10},{3,11},{4,12},{5,13},{6,14},{7,15},{8,0},{9,1},... | collective-permute-start | bytes 614408 | tf_op jit(solution)/shard_map/ppermute | solution.py:40
  101.6 7.3 %collective-permute-start.17 = (bf16[80,1280]{1,0:T(8,128)(2,1)S(1)}, bf16[80,1280]{1,0:T(8,128)(2,1)S(1)}, u32[]{:S(2)}, u32[]{:S(2)}) collective-permute-start(bf16[80,1280]{1,0:T(8,128)(2,1)S(1)} %get-tuple-element.99), channel_id=1, source_target_pairs={{0,12},{1,13},{2,14},{3,15},{4,0},{5,1},{6,2},{7,3},{8,4},{9,5},{1... | collective-permute-start | bytes 614408 | tf_op jit(solution)/shard_map/ppermute | solution.py:40
  103.4 7.6 %collective-permute-start.14 = (bf16[80,1280]{1,0:T(8,128)(2,1)S(1)}, bf16[80,1280]{1,0:T(8,128)(2,1)S(1)}, u32[]{:S(2)}, u32[]{:S(2)}) collective-permute-start(bf16[80,1280]{1,0:T(8,128)(2,1)S(1)} %fusion.11), channel_id=1, source_target_pairs={{0,4},{1,5},{2,6},{3,7},{4,8},{5,9},{6,10},{7,11},{8,12},{9,13},{1... | collective-permute-start | bytes 614408 | tf_op jit(solution)/shard_map/ppermute | solution.py:40
  111.2 9.5 %collective-permute-start.23 = (bf16[2,80,1280]{2,1,0:T(8,128)(2,1)S(1)}, bf16[2,80,1280]{2,1,0:T(8,128)(2,1)S(1)}, u32[]{:S(2)}, u32[]{:S(2)}) collective-permute-start(bf16[2,80,1280]{2,1,0:T(8,128)(2,1)S(1)} %pad_maximum_fusion.3), channel_id=1, source_target_pairs={{0,16},{1,17},{2,18},{3,19},{4,20},{5,21},{6,22},{7,23},{8,24},{9,... | collective-permute-start | bytes 1228808 | tf_op jit(solution)/shard_map/ppermute | solution.py:40
  120.9 6.5 %collective-permute-start.24 = (bf16[80,1280]{1,0:T(8,128)(2,1)S(1)}, bf16[80,1280]{1,0:T(8,128)(2,1)S(1)}, u32[]{:S(2)}, u32[]{:S(2)}) collective-permute-start(bf16[80,1280]{1,0:T(8,128)(2,1)S(1)} %get-tuple-element.90), channel_id=1, source_target_pairs={{0,12},{1,13},{2,14},{3,15},{4,0},{5,1},{6,2},{7,3},{8,4},{9,5},{1... | collective-permute-start | bytes 614408 | tf_op jit(solution)/shard_map/ppermute | solution.py:40
  121.6 9.6 %collective-permute-start.25 = (bf16[80,1280]{1,0:T(8,128)(2,1)S(1)}, bf16[80,1280]{1,0:T(8,128)(2,1)S(1)}, u32[]{:S(2)}, u32[]{:S(2)}) collective-permute-start(bf16[80,1280]{1,0:T(8,128)(2,1)S(1)} %get-tuple-element.90), channel_id=1, source_target_pairs={{0,8},{1,9},{2,10},{3,11},{4,12},{5,13},{6,14},{7,15},{8,0},{9,1},... | collective-permute-start | bytes 614408 | tf_op jit(solution)/shard_map/ppermute | solution.py:40
  122.2 9.0 %collective-permute-start.26 = (bf16[80,1280]{1,0:T(8,128)(2,1)S(1)}, bf16[80,1280]{1,0:T(8,128)(2,1)S(1)}, u32[]{:S(2)}, u32[]{:S(2)}) collective-permute-start(bf16[80,1280]{1,0:T(8,128)(2,1)S(1)} %get-tuple-element.90), channel_id=1, source_target_pairs={{0,4},{1,5},{2,6},{3,7},{4,8},{5,9},{6,10},{7,11},{8,12},{9,13},{1... | collective-permute-start | bytes 614408 | tf_op jit(solution)/shard_map/ppermute | solution.py:40
  123.2 10.5 %collective-permute-start.29 = (bf16[100,1280]{1,0:T(8,128)(2,1)S(1)}, bf16[100,1280]{1,0:T(8,128)(2,1)S(1)}, u32[]{:S(2)}, u32[]{:S(2)}) collective-permute-start(bf16[100,1280]{1,0:T(8,128)(2,1)S(1)} %get-tuple-element.102), channel_id=1, source_target_pairs={{0,1},{1,2},{2,3},{3,0},{4,5},{5,6},{6,7},{7,4},{8,9},{9,10},{10,1... | collective-permute-start | bytes 768008 | tf_op jit(solution)/shard_map/ppermute | solution.py:40
  123.3 13.8 %collective-permute-start.28 = (bf16[100,1280]{1,0:T(8,128)(2,1)S(1)}, bf16[100,1280]{1,0:T(8,128)(2,1)S(1)}, u32[]{:S(2)}, u32[]{:S(2)}) collective-permute-start(bf16[100,1280]{1,0:T(8,128)(2,1)S(1)} %get-tuple-element.101), channel_id=1, source_target_pairs={{0,2},{1,3},{2,0},{3,1},{4,6},{5,7},{6,4},{7,5},{8,10},{9,11},{10,... | collective-permute-start | bytes 768008 | tf_op jit(solution)/shard_map/ppermute | solution.py:40
  127.5 9.6 %collective-permute-start.27 = (bf16[100,1280]{1,0:T(8,128)(2,1)S(1)}, bf16[100,1280]{1,0:T(8,128)(2,1)S(1)}, u32[]{:S(2)}, u32[]{:S(2)}) collective-permute-start(bf16[100,1280]{1,0:T(8,128)(2,1)S(1)} %get-tuple-element.100), channel_id=1, source_target_pairs={{0,3},{1,0},{2,1},{3,2},{4,7},{5,4},{6,5},{7,6},{8,11},{9,8},{10,9... | collective-permute-start | bytes 768008 | tf_op jit(solution)/shard_map/ppermute | solution.py:40
  131.3 36.8 %copy-start.1 = (bf16[4,80,1280]{2,1,0:T(8,128)(2,1)}, bf16[4,80,1280]{2,1,0:T(8,128)(2,1)S(1)}, u32[]{:S(2)}) copy-start(bf16[4,80,1280]{2,1,0:T(8,128)(2,1)S(1)} %pad_maximum_fusion.rest_0_) | copy-start | bytes 2457604
  138.1 29.9 %copy-start.2 = (bf16[4,80,1280]{2,1,0:T(8,128)(2,1)}, bf16[4,80,1280]{2,1,0:T(8,128)(2,1)S(1)}, u32[]{:S(2)}) copy-start(bf16[4,80,1280]{2,1,0:T(8,128)(2,1)S(1)} %pad_maximum_fusion.1.rest_3_) | copy-start | bytes 2457604
  138.1 16.7 %collective-permute-start.30 = (bf16[4,80,1280]{2,1,0:T(8,128)(2,1)S(1)}, bf16[4,80,1280]{2,1,0:T(8,128)(2,1)S(1)}, u32[]{:S(2)}, u32[]{:S(2)}) collective-permute-start(bf16[4,80,1280]{2,1,0:T(8,128)(2,1)S(1)} %pad_maximum_fusion.rest_0_), channel_id=1, source_target_pairs={{0,3},{1,0},{2,1},{3,2},{4,7},{5,4},{6,5},{7,6},{8,11},{9,8},{10,9... | collective-permute-start | bytes 2457608 | tf_op jit(solution)/shard_map/ppermute | solution.py:40
  140.3 18.5 %collective-permute-start.32 = (bf16[4,80,1280]{2,1,0:T(8,128)(2,1)S(1)}, bf16[4,80,1280]{2,1,0:T(8,128)(2,1)S(1)}, u32[]{:S(2)}, u32[]{:S(2)}) collective-permute-start(bf16[4,80,1280]{2,1,0:T(8,128)(2,1)S(1)} %pad_maximum_fusion.rest_0_), channel_id=1, source_target_pairs={{0,1},{1,2},{2,3},{3,0},{4,5},{5,6},{6,7},{7,4},{8,9},{9,10},{10,1... | collective-permute-start | bytes 2457608 | tf_op jit(solution)/shard_map/ppermute | solution.py:40
  140.3 19.4 %collective-permute-start.34 = (bf16[4,80,1280]{2,1,0:T(8,128)(2,1)S(1)}, bf16[4,80,1280]{2,1,0:T(8,128)(2,1)S(1)}, u32[]{:S(2)}, u32[]{:S(2)}) collective-permute-start(bf16[4,80,1280]{2,1,0:T(8,128)(2,1)S(1)} %pad_maximum_fusion.1.rest_3_), channel_id=1, source_target_pairs={{0,12},{1,13},{2,14},{3,15},{4,0},{5,1},{6,2},{7,3},{8,4},{9,5},{1... | collective-permute-start | bytes 2457608 | tf_op jit(solution)/shard_map/ppermute | solution.py:40
  143.0 21.5 %collective-permute-start.36 = (bf16[4,80,1280]{2,1,0:T(8,128)(2,1)S(1)}, bf16[4,80,1280]{2,1,0:T(8,128)(2,1)S(1)}, u32[]{:S(2)}, u32[]{:S(2)}) collective-permute-start(bf16[4,80,1280]{2,1,0:T(8,128)(2,1)S(1)} %pad_maximum_fusion.1.rest_3_), channel_id=1, source_target_pairs={{0,4},{1,5},{2,6},{3,7},{4,8},{5,9},{6,10},{7,11},{8,12},{9,13},{1... | collective-permute-start | bytes 2457608 | tf_op jit(solution)/shard_map/ppermute | solution.py:40
  154.8 13.3 %copy-start.3 = (bf16[4,80,1280]{2,1,0:T(8,128)(2,1)}, bf16[4,80,1280]{2,1,0:T(8,128)(2,1)S(1)}, u32[]{:S(2)}) copy-start(bf16[4,80,1280]{2,1,0:T(8,128)(2,1)S(1)} %collective-permute-done.30.rest_1_) | copy-start | bytes 2457604
  155.6 17.6 %collective-permute-start.31 = (bf16[2,80,1280]{2,1,0:T(8,128)(2,1)}, bf16[2,80,1280]{2,1,0:T(8,128)(2,1)}, u32[]{:S(2)}, u32[]{:S(2)}) collective-permute-start(bf16[2,80,1280]{2,1,0:T(8,128)(2,1)} %slice.165), channel_id=1, source_target_pairs={{0,3},{1,0},{2,1},{3,2},{4,7},{5,4},{6,5},{7,6},{8,11},{9,8},{10,9... | collective-permute-start | bytes 1228808 | tf_op jit(solution)/shard_map/ppermute | solution.py:40
  158.9 9.2 %copy-start.4 = (bf16[4,80,1280]{2,1,0:T(8,128)(2,1)}, bf16[4,80,1280]{2,1,0:T(8,128)(2,1)S(1)}, u32[]{:S(2)}) copy-start(bf16[4,80,1280]{2,1,0:T(8,128)(2,1)S(1)} %collective-permute-done.32.rest_2_) | copy-start | bytes 2457604
  159.7 13.6 %collective-permute-start.33 = (bf16[2,80,1280]{2,1,0:T(8,128)(2,1)}, bf16[2,80,1280]{2,1,0:T(8,128)(2,1)}, u32[]{:S(2)}, u32[]{:S(2)}) collective-permute-start(bf16[2,80,1280]{2,1,0:T(8,128)(2,1)} %slice.166), channel_id=1, source_target_pairs={{0,1},{1,2},{2,3},{3,0},{4,5},{5,6},{6,7},{7,4},{8,9},{9,10},{10,1... | collective-permute-start | bytes 1228808 | tf_op jit(solution)/shard_map/ppermute | solution.py:40
  159.7 4.8 %copy-start.5 = (bf16[4,80,1280]{2,1,0:T(8,128)(2,1)}, bf16[4,80,1280]{2,1,0:T(8,128)(2,1)S(1)}, u32[]{:S(2)}) copy-start(bf16[4,80,1280]{2,1,0:T(8,128)(2,1)S(1)} %collective-permute-done.34.rest_4_) | copy-start | bytes 2457604
  160.6 12.7 %collective-permute-start.35 = (bf16[2,80,1280]{2,1,0:T(8,128)(2,1)}, bf16[2,80,1280]{2,1,0:T(8,128)(2,1)}, u32[]{:S(2)}, u32[]{:S(2)}) collective-permute-start(bf16[2,80,1280]{2,1,0:T(8,128)(2,1)} %slice.167), channel_id=1, source_target_pairs={{0,12},{1,13},{2,14},{3,15},{4,0},{5,1},{6,2},{7,3},{8,4},{9,5},{1... | collective-permute-start | bytes 1228808 | tf_op jit(solution)/shard_map/ppermute | solution.py:40
  164.5 1.1 copy-start.6
  165.6 9.6 %collective-permute-start.37 = (bf16[2,80,1280]{2,1,0:T(8,128)(2,1)}, bf16[2,80,1280]{2,1,0:T(8,128)(2,1)}, u32[]{:S(2)}, u32[]{:S(2)}) collective-permute-start(bf16[2,80,1280]{2,1,0:T(8,128)(2,1)} %slice.168), channel_id=1, source_target_pairs={{0,4},{1,5},{2,6},{3,7},{4,8},{5,9},{6,10},{7,11},{8,12},{9,13},{1... | collective-permute-start | bytes 1228808 | tf_op jit(solution)/shard_map/ppermute | solution.py:40

commit v4 on v3

--- a/solution.py
+++ b/solution.py
@@ -389,6 +389,7 @@
     there, base_tile = lax.optimization_barrier((there, base_tile))
     base_tiles = jnp.stack([base_tile, move(base_tile, "z", 1)])
     here, there = arrive(later[0], *here, "x"), arrive(later[3], *there, "y")
+    here, there = lax.optimization_barrier((here, there))
     here, there = reduce_tiles(here, "y"), reduce_tiles(there, "x")
     here, there = lax.reduce_precision(here, 8, 7), lax.reduce_precision(there, 8, 7)
     crossed = move(jnp.stack([there, here]).astype(bf16), "z", 1)
@@ -407,7 +408,6 @@
     there_got = [got[:TILE_R] for got in there_got]
     here = jnp.stack([tile] + here_got)
     there = jnp.stack([opposite] + there_got)
-    here, there, means = lax.optimization_barrier((here, there, means))
     here_1, here_3 = move(here, "x", -1), move(here, "x", 1)
     there_1, there_3 = move(there, "y", -1), move(there, "y", 1)
     last = [

time: 181 us -> 173 us (0.956); the launches traced: 178 us -> 172 us
  waiting for transfers between devices: 74.1 us -> 69.6 us
  other arithmetic: 11 us -> 7.29 us
  starting transfers between devices: 53.6 us -> 55.9 us
    ppermute x30, waiting for transfers between devices: 57.6 us -> 51.8 us  [move(): return lax.ppermute(value, 'worker', pairs)]
    ppermute x30, starting transfers between devices: 46.3 us -> 48.8 us  [move(): return lax.ppermute(value, 'worker', pairs)]
  transfers between devices with their start and end apart: 39 -> 39, of which waited for: 14 -> 21; matrix products, arithmetic and copies ran while one was open for 8% -> 6% of each run, Pallas kernels for 8% -> 8%
where the time goes in v4:
time: 173 us; the launch traced here: 172 us
  waiting for transfers between devices  69.6 us (40%)
  starting transfers between devices  55.9 us (32%)
  Pallas kernels  29.9 us (17%)
  other arithmetic  7.29 us (4%)
  local copies, waits for them, and re-layouts  6.51 us (4%)
  between operations  3.16 us (2%)
    ppermute x30, waiting for transfers between devices, move(): return lax.ppermute(value, 'worker', pairs)  51.8 us
    ppermute x30, starting transfers between devices, move(): return lax.ppermute(value, 'worker', pairs)  48.8 us
    ppermute x8, waiting for transfers between devices, swap_tp(): return lax.ppermute(value, 'tp', [(t, t ^ bit) for t in range(4)])  10.6 us
    pallas_call x1, Pallas kernels, pseudo_gradient(): pl.pallas_call(functools.partial(pseudo_body, outputs), out_shape=tuple((...  9.64 us
    pallas_call x2, Pallas kernels, place(): pl.pallas_call(functools.partial(place_body, where), out_shape=jax.ShapeD...  8.16 us
    all_to_all x1, waiting for transfers between devices, per_device(): base_tile = lax.all_to_all(base, 'worker', 0, 0, axis_index_groups=rings)  7.27 us
    pallas_call x1, Pallas kernels, attention(): pl.pallas_call(attention_body, out_shape=(jax.ShapeDtypeStruct((width, to...  4.93 us
    all_to_all x1, starting transfers between devices, per_device(): base_tile = lax.all_to_all(base, 'worker', 0, 0, axis_index_groups=rings)  4.3 us
  transfers between devices with their start and end apart: 39, of which 21 were waited for; matrix products, arithmetic and copies ran while one was open for 6% of the time, Pallas kernels for 8%

profile of v4, /device:TPU:32, one launch (start us, length us, event | category | flops | bytes accessed | tf_op | source)
XLA Modules:
  0.0 172.4 jit_solution(2705404850894580658)
XLA Ops:
  0.7 2.7 %cotangent_gram.1 = f32[6,128,128]{2,1,0:T(8,128)} custom-call(bf16[384,1280]{1,0:T(8,128)(2,1)} %g0_ref.1), custom_call_target="tpu_custom_call" | custom-call | tf_op jit(solution)/shard_map/cotangent_gram/pallas_call | solution.py:59
  3.4 0.9 constant_dynamic-slice_fusion.1
  4.4 1.4 collective-permute-done
  5.8 0.9 dynamic-slice_add_fusion
  6.9 6.9 %collective-permute-done.1 = f32[3,128,128]{2,1,0:T(8,128)S(1)} collective-permute-done((f32[3,128,128]{2,1,0:T(8,128)S(1)}, f32[3,128,128]{2,1,0:T(8,128)S(1)}, u32[]{:S(2)}, u32[]{:S(2)}) %collective-permute-start.1) | collective-permute-done | bytes 196640 | tf_op jit(solution)/shard_map/ppermute | solution.py:44
  14.1 0.6 reshape.27.seg_row_ref
  14.7 0.6 pad_add_fusion.at_ref
  15.2 4.9 %attention.1 = (bf16[640,384]{1,0:T(8,128)(2,1)}, f32[6,128,128]{2,1,0:T(8,128)}) custom-call(bf16[384,640]{1,0:T(8,128)(2,1)} %q_ref, bf16[384,640]{1,0:T(8,128)(2,1)} %k_ref.1, bf16[384,640]{1,0:T(8,128)(2,1)} %v_ref.1, s32[1,384]{1,0:T(1,128)} %reshape.27.seg_row_ref), custom_call_target="tpu_custom_call" | custom-call | tf_op jit(solution)/shard_map/attention/pallas_call | solution.py:102
  20.3 2.0 %base_rows.1 = f32[4,20,1280]{2,1,0:T(8,128)} custom-call(s32[4]{0:T(128)} %pad_add_fusion.at_ref, f32[20,5120]{1,0:T(8,128)} %master_ref.3, f32[20,5120]{1,0:T(8,128)} %momentum_ref.3), custom_call_target="tpu_custom_call" | custom-call | tf_op jit(solution)/shard_map/base_rows/pallas_call | solution.py:232
  22.3 4.3 %all-to-all-start = ((f32[4,20,1280]{2,1,0:T(8,128)}), f32[4,20,1280]{2,1,0:T(8,128)S(1)}, u32[]{:S(2)}, u32[]{:S(2)}) async-start(f32[4,20,1280]{2,1,0:T(8,128)} %base_rows.1), calls=%async_computation | async-start | bytes 983040 | tf_op jit(solution)/shard_map/all_to_all | solution.py:370
  26.6 0.7 multiply_reduce_fusion
  28.6 0.3 collective-permute-start.4
  28.8 0.3 collective-permute-start.6
  29.1 7.3 %all-to-all-done = f32[4,20,1280]{2,1,0:T(8,128)S(1)} async-done(((f32[4,20,1280]{2,1,0:T(8,128)}), f32[4,20,1280]{2,1,0:T(8,128)S(1)}, u32[]{:S(2)}, u32[]{:S(2)}) %all-to-all-start) | async-done | bytes 409632 | tf_op jit(solution)/shard_map/all_to_all | solution.py:370
  36.8 1.6 collective-permute-start.5
  38.4 2.0 %collective-permute-done.5 = f32[8,128]{1,0:T(8,128)S(1)} collective-permute-done((f32[8,128]{1,0:T(8,128)S(1)}, f32[8,128]{1,0:T(8,128)S(1)}, u32[]{:S(2)}, u32[]{:S(2)}) %collective-permute-start.5) | collective-permute-done | bytes 4128 | tf_op jit(solution)/shard_map/ppermute | solution.py:44
  40.4 0.5 slice.102
  41.6 9.6 %pseudo_gradient.1 = (bf16[4,80,1280]{2,1,0:T(8,128)(2,1)}, bf16[4,80,1280]{2,1,0:T(8,128)(2,1)}, bf16[4,80,1280]{2,1,0:T(8,128)(2,1)}, bf16[4,80,1280]{2,1,0:T(...) custom-call(s32[4]{0:T(128)} %pad_add_fusion.at_ref, ...), custom_call_target="tpu_custom_call" | custom-call | flops 2516582400 | bytes 18000000 | tf_op jit(solution)/shard_map/pseudo_gradient/pallas_call | solution.py:196
  51.3 2.8 %collective-permute-start.11 = (bf16[4,80,1280]{2,1,0:T(8,128)(2,1)}, bf16[4,80,1280]{2,1,0:T(8,128)(2,1)S(1)}, u32[]{:S(2)}, u32[]{:S(2)}) collective-permute-start(bf16[4,80,1280]{2,1,0:T(8,128)(2,1)} %get-tuple-element.62), channel_id=1, source_target_pairs={{0,3},{1,0},{2,1},{3,2},{4,7},{5,4},{6,5},{7,6},{8,11},{9,8},{10,9... | collective-permute-start | bytes 2457608 | tf_op jit(solution)/shard_map/ppermute | solution.py:40
  54.1 1.6 collective-permute-start.8
  55.7 1.7 collective-permute-start.9
  57.4 14.1 %collective-permute-done.11 = bf16[4,80,1280]{2,1,0:T(8,128)(2,1)S(1)} collective-permute-done((bf16[4,80,1280]{2,1,0:T(8,128)(2,1)}, bf16[4,80,1280]{2,1,0:T(8,128)(2,1)S(1)}, u32[]{:S(2)}, u32[]{:S(2)}) %collective-permute-start.11) | collective-permute-done | bytes 819232 | tf_op jit(solution)/shard_map/ppermute | solution.py:40
  71.5 1.2 add_convert_fusion
  72.6 3.7 %collective-permute-start.14 = (bf16[2,80,1280]{2,1,0:T(8,128)(2,1)S(1)}, bf16[2,80,1280]{2,1,0:T(8,128)(2,1)S(1)}, u32[]{:S(2)}, u32[]{:S(2)}) collective-permute-start(bf16[2,80,1280]{2,1,0:T(8,128)(2,1)S(1)} %add_convert_fusion), channel_id=1, source_target_pairs={{0,3},{1,0},{2,1},{3,2},{4,7},{5,4},{6,5},{7,6},{8,11},{9,8},{10,9... | collective-permute-start | bytes 1228808 | tf_op jit(solution)/shard_map/ppermute | solution.py:40
  76.3 1.2 add_convert_fusion.1
  78.0 1.7 collective-permute-start.15
  79.7 1.7 collective-permute-start.16
  81.3 3.0 %collective-permute-start.10 = (f32[80,1280]{1,0:T(8,128)S(1)}, f32[80,1280]{1,0:T(8,128)S(1)}, u32[]{:S(2)}, u32[]{:S(2)}) collective-permute-start(f32[80,1280]{1,0:T(8,128)S(1)} %reshape.28), channel_id=1, source_target_pairs={{0,16},{1,17},{2,18},{3,19},{4,20},{5,21},{6,22},{7,23},{8,24},{9,... | collective-permute-start | bytes 1228808 | tf_op jit(solution)/shard_map/ppermute | solution.py:40
  84.3 4.2 %collective-permute-done.13 = bf16[2,80,1280]{2,1,0:T(8,128)(2,1)S(1)} collective-permute-done((bf16[2,80,1280]{2,1,0:T(8,128)(2,1)S(1)}, bf16[2,80,1280]{2,1,0:T(8,128)(2,1)S(1)}, u32[]{:S(2)}, u32[]{:S(2)}) %collective-permute-start.13) | collective-permute-done | bytes 409632 | tf_op jit(solution)/shard_map/ppermute | solution.py:40
  88.9 0.7 copy-done.8
  90.3 1.7 collective-permute-start.17
  92.0 1.6 collective-permute-start.19
  93.6 2.0 %collective-permute-start.18 = (bf16[80,1280]{1,0:T(8,128)(2,1)S(1)}, bf16[80,1280]{1,0:T(8,128)(2,1)S(1)}, u32[]{:S(2)}, u32[]{:S(2)}) collective-permute-start(bf16[80,1280]{1,0:T(8,128)(2,1)S(1)} %get-tuple-element.88), channel_id=1, source_target_pairs={{0,8},{1,9},{2,10},{3,11},{4,12},{5,13},{6,14},{7,15},{8,0},{9,1},... | collective-permute-start | bytes 614408 | tf_op jit(solution)/shard_map/ppermute | solution.py:40
  95.8 3.4 %collective-permute-done.17 = bf16[80,1280]{1,0:T(8,128)(2,1)S(1)} collective-permute-done((bf16[80,1280]{1,0:T(8,128)(2,1)S(1)}, bf16[80,1280]{1,0:T(8,128)(2,1)S(1)}, u32[]{:S(2)}, u32[]{:S(2)}) %collective-permute-start.17) | collective-permute-done | bytes 204832 | tf_op jit(solution)/shard_map/ppermute | solution.py:40
  99.2 1.8 %collective-permute-start.22 = (bf16[80,1280]{1,0:T(8,128)(2,1)S(1)}, bf16[80,1280]{1,0:T(8,128)(2,1)S(1)}, u32[]{:S(2)}, u32[]{:S(2)}) collective-permute-start(bf16[80,1280]{1,0:T(8,128)(2,1)S(1)} %get-tuple-element.84), channel_id=1, source_target_pairs={{0,3},{1,0},{2,1},{3,2},{4,7},{5,4},{6,5},{7,6},{8,11},{9,8},{10,9... | collective-permute-start | bytes 614408 | tf_op jit(solution)/shard_map/ppermute | solution.py:40
  100.9 0.4 collective-permute-done.18
  101.5 2.0 %collective-permute-done.20 = bf16[80,1280]{1,0:T(8,128)(2,1)S(1)} collective-permute-done((bf16[80,1280]{1,0:T(8,128)(2,1)S(1)}, bf16[80,1280]{1,0:T(8,128)(2,1)S(1)}, u32[]{:S(2)}, u32[]{:S(2)}) %collective-permute-start.20) | collective-permute-done | bytes 204832 | tf_op jit(solution)/shard_map/ppermute | solution.py:40
  103.5 2.9 %collective-permute-done.22 = bf16[80,1280]{1,0:T(8,128)(2,1)S(1)} collective-permute-done((bf16[80,1280]{1,0:T(8,128)(2,1)S(1)}, bf16[80,1280]{1,0:T(8,128)(2,1)S(1)}, u32[]{:S(2)}, u32[]{:S(2)}) %collective-permute-start.22) | collective-permute-done | bytes 204832 | tf_op jit(solution)/shard_map/ppermute | solution.py:40
  106.4 1.8 %collective-permute-done.21 = bf16[80,1280]{1,0:T(8,128)(2,1)S(1)} collective-permute-done((bf16[80,1280]{1,0:T(8,128)(2,1)S(1)}, bf16[80,1280]{1,0:T(8,128)(2,1)S(1)}, u32[]{:S(2)}, u32[]{:S(2)}) %collective-permute-start.21) | collective-permute-done | bytes 204832 | tf_op jit(solution)/shard_map/ppermute | solution.py:40
  108.4 3.1 %collective-permute-start.23 = (bf16[2,80,1280]{2,1,0:T(8,128)(2,1)S(1)}, bf16[2,80,1280]{2,1,0:T(8,128)(2,1)S(1)}, u32[]{:S(2)}, u32[]{:S(2)}) collective-permute-start(bf16[2,80,1280]{2,1,0:T(8,128)(2,1)S(1)} %pad_maximum_fusion.5), channel_id=1, source_target_pairs={{0,16},{1,17},{2,18},{3,19},{4,20},{5,21},{6,22},{7,23},{8,24},{9,... | collective-permute-start | bytes 1228808 | tf_op jit(solution)/shard_map/ppermute | solution.py:40
  111.5 6.4 %collective-permute-done.23 = bf16[2,80,1280]{2,1,0:T(8,128)(2,1)S(1)} collective-permute-done((bf16[2,80,1280]{2,1,0:T(8,128)(2,1)S(1)}, bf16[2,80,1280]{2,1,0:T(8,128)(2,1)S(1)}, u32[]{:S(2)}, u32[]{:S(2)}) %collective-permute-start.23) | collective-permute-done | bytes 409632 | tf_op jit(solution)/shard_map/ppermute | solution.py:40
  118.2 3.7 %collective-permute-start.25 = (bf16[80,1280]{1,0:T(8,128)(2,1)S(1)}, bf16[80,1280]{1,0:T(8,128)(2,1)S(1)}, u32[]{:S(2)}, u32[]{:S(2)}) collective-permute-start(bf16[80,1280]{1,0:T(8,128)(2,1)S(1)} %get-tuple-element.94), channel_id=1, source_target_pairs={{0,8},{1,9},{2,10},{3,11},{4,12},{5,13},{6,14},{7,15},{8,0},{9,1},... | collective-permute-start | bytes 614408 | tf_op jit(solution)/shard_map/ppermute | solution.py:40
  122.1 2.2 %collective-permute-start.31 = (bf16[100,1280]{1,0:T(8,128)(2,1)S(1)}, bf16[100,1280]{1,0:T(8,128)(2,1)S(1)}, u32[]{:S(2)}, u32[]{:S(2)}) collective-permute-start(bf16[100,1280]{1,0:T(8,128)(2,1)S(1)} %get-tuple-element.100), channel_id=1, source_target_pairs={{0,3},{1,0},{2,1},{3,2},{4,7},{5,4},{6,5},{7,6},{8,11},{9,8},{10,9... | collective-permute-start | bytes 768008 | tf_op jit(solution)/shard_map/ppermute | solution.py:40
  124.3 0.7 collective-permute-start.32
  125.1 2.5 %collective-permute-start.33 = (bf16[100,1280]{1,0:T(8,128)(2,1)S(1)}, bf16[100,1280]{1,0:T(8,128)(2,1)S(1)}, u32[]{:S(2)}, u32[]{:S(2)}) collective-permute-start(bf16[100,1280]{1,0:T(8,128)(2,1)S(1)} %get-tuple-element.102), channel_id=1, source_target_pairs={{0,1},{1,2},{2,3},{3,0},{4,5},{5,6},{6,7},{7,4},{8,9},{9,10},{10,1... | collective-permute-start | bytes 768008 | tf_op jit(solution)/shard_map/ppermute | solution.py:40
  127.8 0.4 collective-permute-done.24
  128.3 0.3 collective-permute-start.29
  128.6 3.0 %collective-permute-start.27 = (bf16[4,80,1280]{2,1,0:T(8,128)(2,1)S(1)}, bf16[4,80,1280]{2,1,0:T(8,128)(2,1)S(1)}, u32[]{:S(2)}, u32[]{:S(2)}) collective-permute-start(bf16[4,80,1280]{2,1,0:T(8,128)(2,1)S(1)} %pad_maximum_fusion.2.rest_0_), channel_id=1, source_target_pairs={{0,3},{1,0},{2,1},{3,2},{4,7},{5,4},{6,5},{7,6},{8,11},{9,8},{10,9... | collective-permute-start | bytes 2457608 | tf_op jit(solution)/shard_map/ppermute | solution.py:40
  131.7 3.4 %collective-permute-done.32 = bf16[100,1280]{1,0:T(8,128)(2,1)S(1)} collective-permute-done((bf16[100,1280]{1,0:T(8,128)(2,1)S(1)}, bf16[100,1280]{1,0:T(8,128)(2,1)S(1)}, u32[]{:S(2)}, u32[]{:S(2)}) %collective-permute-start.32) | collective-permute-done | bytes 256032 | tf_op jit(solution)/shard_map/ppermute | solution.py:40
  135.1 3.2 %collective-permute-done.33 = bf16[100,1280]{1,0:T(8,128)(2,1)S(1)} collective-permute-done((bf16[100,1280]{1,0:T(8,128)(2,1)S(1)}, bf16[100,1280]{1,0:T(8,128)(2,1)S(1)}, u32[]{:S(2)}, u32[]{:S(2)}) %collective-permute-start.33) | collective-permute-done | bytes 256032 | tf_op jit(solution)/shard_map/ppermute | solution.py:40
  138.4 1.3 collective-permute-start.36
  139.7 2.0 %collective-permute-start.34 = (bf16[4,80,1280]{2,1,0:T(8,128)(2,1)S(1)}, bf16[4,80,1280]{2,1,0:T(8,128)(2,1)S(1)}, u32[]{:S(2)}, u32[]{:S(2)}) collective-permute-start(bf16[4,80,1280]{2,1,0:T(8,128)(2,1)S(1)} %pad_maximum_fusion.3.rest_3_), channel_id=1, source_target_pairs={{0,12},{1,13},{2,14},{3,15},{4,0},{5,1},{6,2},{7,3},{8,4},{9,5},{1... | collective-permute-start | bytes 2457608 | tf_op jit(solution)/shard_map/ppermute | solution.py:40
  141.7 9.0 %collective-permute-done.29.rest_2_ = bf16[4,80,1280]{2,1,0:T(8,128)(2,1)S(1)} collective-permute-done((bf16[4,80,1280]{2,1,0:T(8,128)(2,1)S(1)}, bf16[4,80,1280]{2,1,0:T(8,128)(2,1)S(1)}, u32[]{:S(2)}, u32[]{:S(2)}) %collective-permute-start.29) | collective-permute-done | bytes 819232 | tf_op jit(solution)/shard_map/ppermute | solution.py:40
  150.8 0.8 slice.150
  151.6 0.8 slice.149
  152.5 3.2 %collective-permute-start.28 = (bf16[2,80,1280]{2,1,0:T(8,128)(2,1)}, bf16[2,80,1280]{2,1,0:T(8,128)(2,1)}, u32[]{:S(2)}, u32[]{:S(2)}) collective-permute-start(bf16[2,80,1280]{2,1,0:T(8,128)(2,1)} %slice.149), channel_id=1, source_target_pairs={{0,3},{1,0},{2,1},{3,2},{4,7},{5,4},{6,5},{7,6},{8,11},{9,8},{10,9... | collective-permute-start | bytes 1228808 | tf_op jit(solution)/shard_map/ppermute | solution.py:40
  155.7 0.9 slice.157
  156.6 1.3 collective-permute-start.37
  157.9 0.9 slice.156
  158.8 1.9 %collective-permute-start.35 = (bf16[2,80,1280]{2,1,0:T(8,128)(2,1)}, bf16[2,80,1280]{2,1,0:T(8,128)(2,1)}, u32[]{:S(2)}, u32[]{:S(2)}) collective-permute-start(bf16[2,80,1280]{2,1,0:T(8,128)(2,1)} %slice.156), channel_id=1, source_target_pairs={{0,12},{1,13},{2,14},{3,15},{4,0},{5,1},{6,2},{7,3},{8,4},{9,5},{1... | collective-permute-start | bytes 1228808 | tf_op jit(solution)/shard_map/ppermute | solution.py:40
  160.8 0.8 pad_maximum_fusion.4.mean_ref
  161.6 2.4 %outer_rows.1 = (f32[20,5120]{1,0:T(8,128)}, f32[20,5120]{1,0:T(8,128)}) custom-call(s32[4]{0:T(128)} %pad_add_fusion.at_ref, f32[20,5120]{1,0:T(8,128)} %master_ref.3, f32[20,5120]{1,0:T(8,128)} %momentum_ref.3, f32[4,20,1280]{2,1,0:T(8,128)} %pad_maximum_fusion.4.mean_ref), custom_call_target="tpu_custom_call" | custom-call | tf_op jit(solution)/shard_map/outer_rows/pallas_call | solution.py:255
  164.0 5.2 %place_first.1.rest_4_ = bf16[640,5120]{1,0:T(8,128)(2,1)} custom-call(s32[4]{0:T(128)} %pad_add_fusion.at_ref, bf16[4,80,1280]{2,1,0:T(8,128)(2,1)} %copy-done.1, bf16[4,80,1280]{2,1,0:T(8,128)(2,1)} %copy-done.4, bf16[4,80,1280]{2,1,0:T(8,128)(2,1)} %copy-done.3, bf16[4,80,1280]{2,1,0:T(8,128)(2,1)} %copy-done.2, bf16[4,80,1280]{2,1,0:T(8,128)(2,1)} %copy-done.6, ...), custom_call_target="tpu_custom_call" | custom-call | bytes 9830400 | tf_op jit(solution)/shard_map/place_first/pallas_call | solution.py:295
  169.2 3.0 %place_last.1 = bf16[640,5120]{1,0:T(8,128)(2,1)} custom-call(s32[4]{0:T(128)} %pad_add_fusion.at_ref, bf16[2,80,1280]{2,1,0:T(8,128)(2,1)} %collective-permute-done.28.rest_0_, bf16[2,80,1280]{2,1,0:T(8,128)(2,1)} %collective-permute-done.30.rest_1_, bf16[2,80,1280]{2,1,0:T(8,128)(2,1)} %collective-permute-done.35.rest_2_, ...), custom_call_target="tpu_custom_call", output_to_operand_aliasing={{}: (5, {})} | custom-call | bytes 3276800 | tf_op jit(solution)/shard_map/place_last/pallas_call | solution.py:295
  (93 shorter events, 4.1 us)
Async XLA Ops:
  0.6 13.2 %copy-start = (bf16[384,1280]{1,0:T(8,128)(2,1)S(1)}, bf16[384,1280]{1,0:T(8,128)(2,1)}, u32[]{:S(2)}) copy-start(bf16[384,1280]{1,0:T(8,128)(2,1)} %g0_ref.1) | copy-start | bytes 2949124
  0.6 13.5 %copy-start.13 = (s32[384]{0:T(512)S(1)}, s32[384]{0:T(512)}, u32[]{:S(2)}) copy-start(s32[384]{0:T(512)} %param.12) | copy-start | bytes 4612
  4.3 1.5 collective-permute-start
  6.8 7.0 %collective-permute-start.1 = (f32[3,128,128]{2,1,0:T(8,128)S(1)}, f32[3,128,128]{2,1,0:T(8,128)S(1)}, u32[]{:S(2)}, u32[]{:S(2)}) collective-permute-start(f32[3,128,128]{2,1,0:T(8,128)S(1)} %dynamic-slice_add_fusion), channel_id=1, source_target_pairs={{0,64},{32,96},{64,0},{96,32},{1,65},{33,97},{65,1},{97,33},{2,66}... | collective-permute-start | bytes 589832 | tf_op jit(solution)/shard_map/ppermute | solution.py:44
  13.8 23.0 %collective-permute-start.2 = (bf16[384,1280]{1,0:T(8,128)(2,1)S(1)}, bf16[384,1280]{1,0:T(8,128)(2,1)S(1)}, u32[]{:S(2)}, u32[]{:S(2)}) collective-permute-start(bf16[384,1280]{1,0:T(8,128)(2,1)S(1)} %copy-done), channel_id=1, source_target_pairs={{0,64},{32,96},{64,0},{96,32},{1,65},{33,97},{65,1},{97,33},{2,66}... | collective-permute-start | bytes 2949128 | tf_op jit(solution)/shard_map/ppermute | solution.py:44
  20.2 6.5 %copy-start.12 = (f32[6,128,128]{2,1,0:T(8,128)S(1)}, f32[6,128,128]{2,1,0:T(8,128)}, u32[]{:S(2)}) copy-start(f32[6,128,128]{2,1,0:T(8,128)} %get-tuple-element.47) | copy-start | bytes 1179652
  20.2 6.4 %collective-permute-start.3 = (f32[3,128,128]{2,1,0:T(8,128)S(1)}, f32[3,128,128]{2,1,0:T(8,128)S(1)}, u32[]{:S(2)}, u32[]{:S(2)}) collective-permute-start(f32[3,128,128]{2,1,0:T(8,128)S(1)} %add.136), channel_id=1, source_target_pairs={{0,32},{32,0},{64,96},{96,64},{1,33},{33,1},{65,97},{97,65},{2,34}... | collective-permute-start | bytes 589832 | tf_op jit(solution)/shard_map/ppermute | solution.py:44
  22.3 14.1 %all-to-all-start = ((f32[4,20,1280]{2,1,0:T(8,128)}), f32[4,20,1280]{2,1,0:T(8,128)S(1)}, u32[]{:S(2)}, u32[]{:S(2)}) async-start(f32[4,20,1280]{2,1,0:T(8,128)} %base_rows.1), calls=%async_computation | async-start | bytes 983040 | tf_op jit(solution)/shard_map/all_to_all | solution.py:370
  28.6 7.9 %collective-permute-start.4 = (f32[8,128]{1,0:T(8,128)S(1)}, f32[8,128]{1,0:T(8,128)S(1)}, u32[]{:S(2)}, u32[]{:S(2)}) collective-permute-start(f32[8,128]{1,0:T(8,128)S(1)} %broadcast_in_dim.3), channel_id=1, source_target_pairs={{0,32},{32,0},{64,96},{96,64},{1,33},{33,1},{65,97},{97,65},{2,34}... | collective-permute-start | bytes 12296 | tf_op jit(solution)/shard_map/ppermute | solution.py:44
  28.8 12.8 %collective-permute-start.6 = (bf16[384,1280]{1,0:T(8,128)(2,1)S(1)}, bf16[384,1280]{1,0:T(8,128)(2,1)}, u32[]{:S(2)}, u32[]{:S(2)}) collective-permute-start(bf16[384,1280]{1,0:T(8,128)(2,1)S(1)} %copy-done), channel_id=1, source_target_pairs={{0,32},{32,0},{64,96},{96,64},{1,33},{33,1},{65,97},{97,65},{2,34}... | collective-permute-start | bytes 2949128 | tf_op jit(solution)/shard_map/ppermute | solution.py:44
  36.8 4.8 %copy-start.7 = (bf16[384,1280]{1,0:T(8,128)(2,1)}, bf16[384,1280]{1,0:T(8,128)(2,1)S(1)}, u32[]{:S(2)}) copy-start(bf16[384,1280]{1,0:T(8,128)(2,1)S(1)} %collective-permute-done.2.g2_ref) | copy-start | bytes 2949124
  36.8 4.8 %collective-permute-start.7 = (bf16[384,1280]{1,0:T(8,128)(2,1)S(1)}, bf16[384,1280]{1,0:T(8,128)(2,1)}, u32[]{:S(2)}, u32[]{:S(2)}) collective-permute-start(bf16[384,1280]{1,0:T(8,128)(2,1)S(1)} %collective-permute-done.2.g2_ref), channel_id=1, source_target_pairs={{0,32},{32,0},{64,96},{96,64},{1,33},{33,1},{65,97},{97,65},{2,34}... | collective-permute-start | bytes 2949128 | tf_op jit(solution)/shard_map/ppermute | solution.py:44
  36.8 3.6 %collective-permute-start.5 = (f32[8,128]{1,0:T(8,128)S(1)}, f32[8,128]{1,0:T(8,128)S(1)}, u32[]{:S(2)}, u32[]{:S(2)}) collective-permute-start(f32[8,128]{1,0:T(8,128)S(1)} %broadcast_add_fusion), channel_id=1, source_target_pairs={{0,64},{32,96},{64,0},{96,32},{1,65},{33,97},{65,1},{97,33},{2,66}... | collective-permute-start | bytes 12296 | tf_op jit(solution)/shard_map/ppermute | solution.py:44
  51.3 26.5 %copy-start.11 = (bf16[2,80,1280]{2,1,0:T(8,128)(2,1)S(1)}, bf16[2,80,1280]{2,1,0:T(8,128)(2,1)}, u32[]{:S(2)}) copy-start(bf16[2,80,1280]{2,1,0:T(8,128)(2,1)} %get-tuple-element.57) | copy-start | bytes 1228804
  51.3 20.2 %collective-permute-start.11 = (bf16[4,80,1280]{2,1,0:T(8,128)(2,1)}, bf16[4,80,1280]{2,1,0:T(8,128)(2,1)S(1)}, u32[]{:S(2)}, u32[]{:S(2)}) collective-permute-start(bf16[4,80,1280]{2,1,0:T(8,128)(2,1)} %get-tuple-element.62), channel_id=1, source_target_pairs={{0,3},{1,0},{2,1},{3,2},{4,7},{5,4},{6,5},{7,6},{8,11},{9,8},{10,9... | collective-permute-start | bytes 2457608 | tf_op jit(solution)/shard_map/ppermute | solution.py:40
  54.1 22.2 %collective-permute-start.12 = (bf16[4,80,1280]{2,1,0:T(8,128)(2,1)}, bf16[4,80,1280]{2,1,0:T(8,128)(2,1)S(1)}, u32[]{:S(2)}, u32[]{:S(2)}) collective-permute-start(bf16[4,80,1280]{2,1,0:T(8,128)(2,1)} %get-tuple-element.64), channel_id=1, source_target_pairs={{0,1},{1,2},{2,3},{3,0},{4,5},{5,6},{6,7},{7,4},{8,9},{9,10},{10,1... | collective-permute-start | bytes 2457608 | tf_op jit(solution)/shard_map/ppermute | solution.py:40
  54.1 23.6 %collective-permute-start.8 = (bf16[4,80,1280]{2,1,0:T(8,128)(2,1)}, bf16[4,80,1280]{2,1,0:T(8,128)(2,1)S(1)}, u32[]{:S(2)}, u32[]{:S(2)}) collective-permute-start(bf16[4,80,1280]{2,1,0:T(8,128)(2,1)} %get-tuple-element.55), channel_id=1, source_target_pairs={{0,4},{1,5},{2,6},{3,7},{4,8},{5,9},{6,10},{7,11},{8,12},{9,13},{1... | collective-permute-start | bytes 2457608 | tf_op jit(solution)/shard_map/ppermute | solution.py:40
  55.7 22.2 %collective-permute-start.9 = (bf16[4,80,1280]{2,1,0:T(8,128)(2,1)}, bf16[4,80,1280]{2,1,0:T(8,128)(2,1)S(1)}, u32[]{:S(2)}, u32[]{:S(2)}) collective-permute-start(bf16[4,80,1280]{2,1,0:T(8,128)(2,1)} %get-tuple-element.56), channel_id=1, source_target_pairs={{0,12},{1,13},{2,14},{3,15},{4,0},{5,1},{6,2},{7,3},{8,4},{9,5},{1... | collective-permute-start | bytes 2457608 | tf_op jit(solution)/shard_map/ppermute | solution.py:40
  71.5 6.4 %copy-start.10 = (bf16[2,80,1280]{2,1,0:T(8,128)(2,1)S(1)}, bf16[2,80,1280]{2,1,0:T(8,128)(2,1)}, u32[]{:S(2)}) copy-start(bf16[2,80,1280]{2,1,0:T(8,128)(2,1)} %get-tuple-element.58) | copy-start | bytes 1228804
  72.6 11.7 %collective-permute-start.14 = (bf16[2,80,1280]{2,1,0:T(8,128)(2,1)S(1)}, bf16[2,80,1280]{2,1,0:T(8,128)(2,1)S(1)}, u32[]{:S(2)}, u32[]{:S(2)}) collective-permute-start(bf16[2,80,1280]{2,1,0:T(8,128)(2,1)S(1)} %add_convert_fusion), channel_id=1, source_target_pairs={{0,3},{1,0},{2,1},{3,2},{4,7},{5,4},{6,5},{7,6},{8,11},{9,8},{10,9... | collective-permute-start | bytes 1228808 | tf_op jit(solution)/shard_map/ppermute | solution.py:40
  76.3 12.2 %copy-start.9 = (bf16[4,80,1280]{2,1,0:T(8,128)(2,1)S(1)}, bf16[4,80,1280]{2,1,0:T(8,128)(2,1)}, u32[]{:S(2)}) copy-start(bf16[4,80,1280]{2,1,0:T(8,128)(2,1)} %get-tuple-element.61) | copy-start | bytes 2457604
  77.5 11.0 %collective-permute-start.13 = (bf16[2,80,1280]{2,1,0:T(8,128)(2,1)S(1)}, bf16[2,80,1280]{2,1,0:T(8,128)(2,1)S(1)}, u32[]{:S(2)}, u32[]{:S(2)}) collective-permute-start(bf16[2,80,1280]{2,1,0:T(8,128)(2,1)S(1)} %add_convert_fusion.1), channel_id=1, source_target_pairs={{0,1},{1,2},{2,3},{3,0},{4,5},{5,6},{6,7},{7,4},{8,9},{9,10},{10,1... | collective-permute-start | bytes 1228808 | tf_op jit(solution)/shard_map/ppermute | solution.py:40
  78.0 10.8 %collective-permute-start.15 = (bf16[2,80,1280]{2,1,0:T(8,128)(2,1)S(1)}, bf16[2,80,1280]{2,1,0:T(8,128)(2,1)S(1)}, u32[]{:S(2)}, u32[]{:S(2)}) collective-permute-start(bf16[2,80,1280]{2,1,0:T(8,128)(2,1)S(1)} %add_convert_fusion.3), channel_id=1, source_target_pairs={{0,4},{1,5},{2,6},{3,7},{4,8},{5,9},{6,10},{7,11},{8,12},{9,13},{1... | collective-permute-start | bytes 1228808 | tf_op jit(solution)/shard_map/ppermute | solution.py:40
  79.7 9.3 %collective-permute-start.16 = (bf16[2,80,1280]{2,1,0:T(8,128)(2,1)S(1)}, bf16[2,80,1280]{2,1,0:T(8,128)(2,1)S(1)}, u32[]{:S(2)}, u32[]{:S(2)}) collective-permute-start(bf16[2,80,1280]{2,1,0:T(8,128)(2,1)S(1)} %add_convert_fusion.2), channel_id=1, source_target_pairs={{0,12},{1,13},{2,14},{3,15},{4,0},{5,1},{6,2},{7,3},{8,4},{9,5},{1... | collective-permute-start | bytes 1228808 | tf_op jit(solution)/shard_map/ppermute | solution.py:40
  81.3 30.2 %collective-permute-start.10 = (f32[80,1280]{1,0:T(8,128)S(1)}, f32[80,1280]{1,0:T(8,128)S(1)}, u32[]{:S(2)}, u32[]{:S(2)}) collective-permute-start(f32[80,1280]{1,0:T(8,128)S(1)} %reshape.28), channel_id=1, source_target_pairs={{0,16},{1,17},{2,18},{3,19},{4,20},{5,21},{6,22},{7,23},{8,24},{9,... | collective-permute-start | bytes 1228808 | tf_op jit(solution)/shard_map/ppermute | solution.py:40
  88.5 1.1 copy-start.8
  90.3 8.9 %collective-permute-start.17 = (bf16[80,1280]{1,0:T(8,128)(2,1)S(1)}, bf16[80,1280]{1,0:T(8,128)(2,1)S(1)}, u32[]{:S(2)}, u32[]{:S(2)}) collective-permute-start(bf16[80,1280]{1,0:T(8,128)(2,1)S(1)} %get-tuple-element.86), channel_id=1, source_target_pairs={{0,4},{1,5},{2,6},{3,7},{4,8},{5,9},{6,10},{7,11},{8,12},{9,13},{1... | collective-permute-start | bytes 614408 | tf_op jit(solution)/shard_map/ppermute | solution.py:40
  92.0 9.0 %collective-permute-start.19 = (bf16[80,1280]{1,0:T(8,128)(2,1)S(1)}, bf16[80,1280]{1,0:T(8,128)(2,1)S(1)}, u32[]{:S(2)}, u32[]{:S(2)}) collective-permute-start(bf16[80,1280]{1,0:T(8,128)(2,1)S(1)} %get-tuple-element.87), channel_id=1, source_target_pairs={{0,12},{1,13},{2,14},{3,15},{4,0},{5,1},{6,2},{7,3},{8,4},{9,5},{1... | collective-permute-start | bytes 614408 | tf_op jit(solution)/shard_map/ppermute | solution.py:40
  93.6 7.8 %collective-permute-start.18 = (bf16[80,1280]{1,0:T(8,128)(2,1)S(1)}, bf16[80,1280]{1,0:T(8,128)(2,1)S(1)}, u32[]{:S(2)}, u32[]{:S(2)}) collective-permute-start(bf16[80,1280]{1,0:T(8,128)(2,1)S(1)} %get-tuple-element.88), channel_id=1, source_target_pairs={{0,8},{1,9},{2,10},{3,11},{4,12},{5,13},{6,14},{7,15},{8,0},{9,1},... | collective-permute-start | bytes 614408 | tf_op jit(solution)/shard_map/ppermute | solution.py:40
  95.7 7.8 %collective-permute-start.20 = (bf16[80,1280]{1,0:T(8,128)(2,1)S(1)}, bf16[80,1280]{1,0:T(8,128)(2,1)S(1)}, u32[]{:S(2)}, u32[]{:S(2)}) collective-permute-start(bf16[80,1280]{1,0:T(8,128)(2,1)S(1)} %get-tuple-element.83), channel_id=1, source_target_pairs={{0,1},{1,2},{2,3},{3,0},{4,5},{5,6},{6,7},{7,4},{8,9},{9,10},{10,1... | collective-permute-start | bytes 614408 | tf_op jit(solution)/shard_map/ppermute | solution.py:40
  99.2 7.3 %collective-permute-start.22 = (bf16[80,1280]{1,0:T(8,128)(2,1)S(1)}, bf16[80,1280]{1,0:T(8,128)(2,1)S(1)}, u32[]{:S(2)}, u32[]{:S(2)}) collective-permute-start(bf16[80,1280]{1,0:T(8,128)(2,1)S(1)} %get-tuple-element.84), channel_id=1, source_target_pairs={{0,3},{1,0},{2,1},{3,2},{4,7},{5,4},{6,5},{7,6},{8,11},{9,8},{10,9... | collective-permute-start | bytes 614408 | tf_op jit(solution)/shard_map/ppermute | solution.py:40
  100.9 7.3 %collective-permute-start.21 = (bf16[80,1280]{1,0:T(8,128)(2,1)S(1)}, bf16[80,1280]{1,0:T(8,128)(2,1)S(1)}, u32[]{:S(2)}, u32[]{:S(2)}) collective-permute-start(bf16[80,1280]{1,0:T(8,128)(2,1)S(1)} %get-tuple-element.85), channel_id=1, source_target_pairs={{0,2},{1,3},{2,0},{3,1},{4,6},{5,7},{6,4},{7,5},{8,10},{9,11},{10,... | collective-permute-start | bytes 614408 | tf_op jit(solution)/shard_map/ppermute | solution.py:40
  108.4 9.5 %collective-permute-start.23 = (bf16[2,80,1280]{2,1,0:T(8,128)(2,1)S(1)}, bf16[2,80,1280]{2,1,0:T(8,128)(2,1)S(1)}, u32[]{:S(2)}, u32[]{:S(2)}) collective-permute-start(bf16[2,80,1280]{2,1,0:T(8,128)(2,1)S(1)} %pad_maximum_fusion.5), channel_id=1, source_target_pairs={{0,16},{1,17},{2,18},{3,19},{4,20},{5,21},{6,22},{7,23},{8,24},{9,... | collective-permute-start | bytes 1228808 | tf_op jit(solution)/shard_map/ppermute | solution.py:40
  118.1 7.0 %collective-permute-start.26 = (bf16[80,1280]{1,0:T(8,128)(2,1)S(1)}, bf16[80,1280]{1,0:T(8,128)(2,1)S(1)}, u32[]{:S(2)}, u32[]{:S(2)}) collective-permute-start(bf16[80,1280]{1,0:T(8,128)(2,1)S(1)} %get-tuple-element.94), channel_id=1, source_target_pairs={{0,4},{1,5},{2,6},{3,7},{4,8},{5,9},{6,10},{7,11},{8,12},{9,13},{1... | collective-permute-start | bytes 614408 | tf_op jit(solution)/shard_map/ppermute | solution.py:40
  118.2 9.7 %collective-permute-start.25 = (bf16[80,1280]{1,0:T(8,128)(2,1)S(1)}, bf16[80,1280]{1,0:T(8,128)(2,1)S(1)}, u32[]{:S(2)}, u32[]{:S(2)}) collective-permute-start(bf16[80,1280]{1,0:T(8,128)(2,1)S(1)} %get-tuple-element.94), channel_id=1, source_target_pairs={{0,8},{1,9},{2,10},{3,11},{4,12},{5,13},{6,14},{7,15},{8,0},{9,1},... | collective-permute-start | bytes 614408 | tf_op jit(solution)/shard_map/ppermute | solution.py:40
  121.9 6.3 %collective-permute-start.24 = (bf16[80,1280]{1,0:T(8,128)(2,1)S(1)}, bf16[80,1280]{1,0:T(8,128)(2,1)S(1)}, u32[]{:S(2)}, u32[]{:S(2)}) collective-permute-start(bf16[80,1280]{1,0:T(8,128)(2,1)S(1)} %get-tuple-element.94), channel_id=1, source_target_pairs={{0,12},{1,13},{2,14},{3,15},{4,0},{5,1},{6,2},{7,3},{8,4},{9,5},{1... | collective-permute-start | bytes 614408 | tf_op jit(solution)/shard_map/ppermute | solution.py:40
  122.1 9.6 %collective-permute-start.31 = (bf16[100,1280]{1,0:T(8,128)(2,1)S(1)}, bf16[100,1280]{1,0:T(8,128)(2,1)S(1)}, u32[]{:S(2)}, u32[]{:S(2)}) collective-permute-start(bf16[100,1280]{1,0:T(8,128)(2,1)S(1)} %get-tuple-element.100), channel_id=1, source_target_pairs={{0,3},{1,0},{2,1},{3,2},{4,7},{5,4},{6,5},{7,6},{8,11},{9,8},{10,9... | collective-permute-start | bytes 768008 | tf_op jit(solution)/shard_map/ppermute | solution.py:40
  124.3 10.8 %collective-permute-start.32 = (bf16[100,1280]{1,0:T(8,128)(2,1)S(1)}, bf16[100,1280]{1,0:T(8,128)(2,1)S(1)}, u32[]{:S(2)}, u32[]{:S(2)}) collective-permute-start(bf16[100,1280]{1,0:T(8,128)(2,1)S(1)} %get-tuple-element.101), channel_id=1, source_target_pairs={{0,2},{1,3},{2,0},{3,1},{4,6},{5,7},{6,4},{7,5},{8,10},{9,11},{10,... | collective-permute-start | bytes 768008 | tf_op jit(solution)/shard_map/ppermute | solution.py:40
  125.1 13.1 %collective-permute-start.33 = (bf16[100,1280]{1,0:T(8,128)(2,1)S(1)}, bf16[100,1280]{1,0:T(8,128)(2,1)S(1)}, u32[]{:S(2)}, u32[]{:S(2)}) collective-permute-start(bf16[100,1280]{1,0:T(8,128)(2,1)S(1)} %get-tuple-element.102), channel_id=1, source_target_pairs={{0,1},{1,2},{2,3},{3,0},{4,5},{5,6},{6,7},{7,4},{8,9},{9,10},{10,1... | collective-permute-start | bytes 768008 | tf_op jit(solution)/shard_map/ppermute | solution.py:40
  128.3 23.3 %copy-start.1 = (bf16[4,80,1280]{2,1,0:T(8,128)(2,1)}, bf16[4,80,1280]{2,1,0:T(8,128)(2,1)S(1)}, u32[]{:S(2)}) copy-start(bf16[4,80,1280]{2,1,0:T(8,128)(2,1)S(1)} %pad_maximum_fusion.2.rest_0_) | copy-start | bytes 2457604
  128.3 22.5 %collective-permute-start.29 = (bf16[4,80,1280]{2,1,0:T(8,128)(2,1)S(1)}, bf16[4,80,1280]{2,1,0:T(8,128)(2,1)S(1)}, u32[]{:S(2)}, u32[]{:S(2)}) collective-permute-start(bf16[4,80,1280]{2,1,0:T(8,128)(2,1)S(1)} %pad_maximum_fusion.2.rest_0_), channel_id=1, source_target_pairs={{0,1},{1,2},{2,3},{3,0},{4,5},{5,6},{6,7},{7,4},{8,9},{9,10},{10,1... | collective-permute-start | bytes 2457608 | tf_op jit(solution)/shard_map/ppermute | solution.py:40
  128.6 23.0 %collective-permute-start.27 = (bf16[4,80,1280]{2,1,0:T(8,128)(2,1)S(1)}, bf16[4,80,1280]{2,1,0:T(8,128)(2,1)S(1)}, u32[]{:S(2)}, u32[]{:S(2)}) collective-permute-start(bf16[4,80,1280]{2,1,0:T(8,128)(2,1)S(1)} %pad_maximum_fusion.2.rest_0_), channel_id=1, source_target_pairs={{0,3},{1,0},{2,1},{3,2},{4,7},{5,4},{6,5},{7,6},{8,11},{9,8},{10,9... | collective-permute-start | bytes 2457608 | tf_op jit(solution)/shard_map/ppermute | solution.py:40
  138.4 20.4 %copy-start.2 = (bf16[4,80,1280]{2,1,0:T(8,128)(2,1)}, bf16[4,80,1280]{2,1,0:T(8,128)(2,1)S(1)}, u32[]{:S(2)}) copy-start(bf16[4,80,1280]{2,1,0:T(8,128)(2,1)S(1)} %pad_maximum_fusion.3.rest_3_) | copy-start | bytes 2457604
  138.4 17.3 %collective-permute-start.36 = (bf16[4,80,1280]{2,1,0:T(8,128)(2,1)S(1)}, bf16[4,80,1280]{2,1,0:T(8,128)(2,1)S(1)}, u32[]{:S(2)}, u32[]{:S(2)}) collective-permute-start(bf16[4,80,1280]{2,1,0:T(8,128)(2,1)S(1)} %pad_maximum_fusion.3.rest_3_), channel_id=1, source_target_pairs={{0,4},{1,5},{2,6},{3,7},{4,8},{5,9},{6,10},{7,11},{8,12},{9,13},{1... | collective-permute-start | bytes 2457608 | tf_op jit(solution)/shard_map/ppermute | solution.py:40
  139.7 18.3 %collective-permute-start.34 = (bf16[4,80,1280]{2,1,0:T(8,128)(2,1)S(1)}, bf16[4,80,1280]{2,1,0:T(8,128)(2,1)S(1)}, u32[]{:S(2)}, u32[]{:S(2)}) collective-permute-start(bf16[4,80,1280]{2,1,0:T(8,128)(2,1)S(1)} %pad_maximum_fusion.3.rest_3_), channel_id=1, source_target_pairs={{0,12},{1,13},{2,14},{3,15},{4,0},{5,1},{6,2},{7,3},{8,4},{9,5},{1... | collective-permute-start | bytes 2457608 | tf_op jit(solution)/shard_map/ppermute | solution.py:40
  150.8 10.0 %copy-start.3 = (bf16[4,80,1280]{2,1,0:T(8,128)(2,1)}, bf16[4,80,1280]{2,1,0:T(8,128)(2,1)S(1)}, u32[]{:S(2)}) copy-start(bf16[4,80,1280]{2,1,0:T(8,128)(2,1)S(1)} %collective-permute-done.29.rest_2_) | copy-start | bytes 2457604
  151.6 17.6 %collective-permute-start.30 = (bf16[2,80,1280]{2,1,0:T(8,128)(2,1)}, bf16[2,80,1280]{2,1,0:T(8,128)(2,1)}, u32[]{:S(2)}, u32[]{:S(2)}) collective-permute-start(bf16[2,80,1280]{2,1,0:T(8,128)(2,1)} %slice.150), channel_id=1, source_target_pairs={{0,1},{1,2},{2,3},{3,0},{4,5},{5,6},{6,7},{7,4},{8,9},{9,10},{10,1... | collective-permute-start | bytes 1228808 | tf_op jit(solution)/shard_map/ppermute | solution.py:40
  151.6 9.9 %copy-start.4 = (bf16[4,80,1280]{2,1,0:T(8,128)(2,1)}, bf16[4,80,1280]{2,1,0:T(8,128)(2,1)S(1)}, u32[]{:S(2)}) copy-start(bf16[4,80,1280]{2,1,0:T(8,128)(2,1)S(1)} %collective-permute-done.27.rest_1_) | copy-start | bytes 2457604
  152.5 16.8 %collective-permute-start.28 = (bf16[2,80,1280]{2,1,0:T(8,128)(2,1)}, bf16[2,80,1280]{2,1,0:T(8,128)(2,1)}, u32[]{:S(2)}, u32[]{:S(2)}) collective-permute-start(bf16[2,80,1280]{2,1,0:T(8,128)(2,1)} %slice.149), channel_id=1, source_target_pairs={{0,3},{1,0},{2,1},{3,2},{4,7},{5,4},{6,5},{7,6},{8,11},{9,8},{10,9... | collective-permute-start | bytes 1228808 | tf_op jit(solution)/shard_map/ppermute | solution.py:40
  155.7 8.3 %copy-start.5 = (bf16[4,80,1280]{2,1,0:T(8,128)(2,1)}, bf16[4,80,1280]{2,1,0:T(8,128)(2,1)S(1)}, u32[]{:S(2)}) copy-start(bf16[4,80,1280]{2,1,0:T(8,128)(2,1)S(1)} %collective-permute-done.36.rest_5_) | copy-start | bytes 2457604
  156.6 12.6 %collective-permute-start.37 = (bf16[2,80,1280]{2,1,0:T(8,128)(2,1)}, bf16[2,80,1280]{2,1,0:T(8,128)(2,1)}, u32[]{:S(2)}, u32[]{:S(2)}) collective-permute-start(bf16[2,80,1280]{2,1,0:T(8,128)(2,1)} %slice.157), channel_id=1, source_target_pairs={{0,4},{1,5},{2,6},{3,7},{4,8},{5,9},{6,10},{7,11},{8,12},{9,13},{1... | collective-permute-start | bytes 1228808 | tf_op jit(solution)/shard_map/ppermute | solution.py:40
  157.9 6.1 %copy-start.6 = (bf16[4,80,1280]{2,1,0:T(8,128)(2,1)}, bf16[4,80,1280]{2,1,0:T(8,128)(2,1)S(1)}, u32[]{:S(2)}) copy-start(bf16[4,80,1280]{2,1,0:T(8,128)(2,1)S(1)} %collective-permute-done.34.rest_4_) | copy-start | bytes 2457604
  158.8 10.4 %collective-permute-start.35 = (bf16[2,80,1280]{2,1,0:T(8,128)(2,1)}, bf16[2,80,1280]{2,1,0:T(8,128)(2,1)}, u32[]{:S(2)}, u32[]{:S(2)}) collective-permute-start(bf16[2,80,1280]{2,1,0:T(8,128)(2,1)} %slice.156), channel_id=1, source_target_pairs={{0,12},{1,13},{2,14},{3,15},{4,0},{5,1},{6,2},{7,3},{8,4},{9,5},{1... | collective-permute-start | bytes 1228808 | tf_op jit(solution)/shard_map/ppermute | solution.py:40

commit v5 on v4

--- a/solution.py
+++ b/solution.py
@@ -354,26 +354,20 @@
 
     partner = swap_tp(out_grad, 1)
 
-    packed = cotangent_gram(out_grad)
-    side = (tp % 2) * 3
-    mine = lax.dynamic_slice_in_dim(packed, side, 3, 0)
-    mine = mine + swap_tp(lax.dynamic_slice_in_dim(packed, 3 - side, 3, 0), 1)
-    far = swap_tp(mine, 2)
-
-    mine, queries = lax.optimization_barrier((mine, queries))
+    gram = cotangent_gram(out_grad)
+    far = swap_tp(gram, 2)
+
+    gram, queries = lax.optimization_barrier((gram, queries))
     ct, own_gram = attention(queries, keys, values, segments)
-    far, crossing = lax.optimization_barrier((far, out_grad))
+    ct, early_at, crossing = lax.optimization_barrier((ct, at, out_grad))
     across = swap_tp(crossing, 2)
-    ct, early_at = lax.optimization_barrier((ct, at))
     base = base_rows(early_at, master, momentum)
     rings = [[first + n for n in range(NX)] for first in range(0, NX * NY * NZ, NX)]
     base_tile = lax.all_to_all(base, "worker", 0, 0, axis_index_groups=rings)
     base_tile = base_tile.reshape(TILE_R, 2 * HALF_C)
-    far, mine, ct, own_gram = lax.optimization_barrier((far, mine, ct, own_gram))
-    mine = mine + far
-    theirs = swap_tp(mine, 1)
-    squares = jnp.sum(lax.dynamic_slice_in_dim(own_gram, side, 3, 0) * mine)
-    squares = squares + jnp.sum(lax.dynamic_slice_in_dim(own_gram, 3 - side, 3, 0) * theirs)
+    far, gram, ct, own_gram = lax.optimization_barrier((far, gram, ct, own_gram))
+    gram = gram + far
+    squares = jnp.sum(own_gram * (gram + swap_tp(gram, 1)))
     squares = jnp.full((8, 128), squares, f32)
     squares = squares + swap_tp(squares, 1)
     across, base_tile, squares = lax.optimization_barrier((across, base_tile, squares))
@@ -400,10 +394,10 @@
     def mean_rows(k):
         return lax.dynamic_slice_in_dim(mean, ((x + k) % NX) * own_rows, own_rows, 0)
 
-    here_got = ring([tile] * 3, "y", -1)
     there_got = ring(
         [jnp.concatenate([opposite, mean_rows(NX - k).astype(bf16)]) for k in (1, 2, 3)], "x", -1
     )
+    here_got = ring([tile] * 3, "y", -1)
     means = jnp.stack([mean_rows(0)] + [got[TILE_R:].astype(f32) for got in there_got])
     there_got = [got[:TILE_R] for got in there_got]
     here = jnp.stack([tile] + here_got)

time: 173 us -> 171 us (0.988)
    ppermute x8 -> x7, waiting for transfers between devices: 10.6 us -> 9.58 us  [swap_tp(): return lax.ppermute(value, 'tp', [(t, t ^ bit) for t in range(4)])]
  transfers between devices with their start and end apart: 39 -> 38, of which waited for: 21 -> 20; matrix products, arithmetic and copies ran while one was open for 6% -> 7% of each run, Pallas kernels for 8% -> 9%
where the time goes in v5:
time: 171 us; the launch traced here: 170 us
  waiting for transfers between devices  69.1 us (40%)
  starting transfers between devices  56.2 us (33%)
  Pallas kernels  29.9 us (17%)
  other arithmetic  8.06 us (5%)
  local copies, waits for them, and re-layouts  5.26 us (3%)
  between operations  1.92 us (1%)
    ppermute x30, waiting for transfers between devices, move(): return lax.ppermute(value, 'worker', pairs)  52.8 us
    ppermute x30, starting transfers between devices, move(): return lax.ppermute(value, 'worker', pairs)  48.8 us
    pallas_call x1, Pallas kernels, pseudo_gradient(): pl.pallas_call(functools.partial(pseudo_body, outputs), out_shape=tuple((...  9.62 us
    ppermute x7, waiting for transfers between devices, swap_tp(): return lax.ppermute(value, 'tp', [(t, t ^ bit) for t in range(4)])  9.58 us
    pallas_call x2, Pallas kernels, place(): pl.pallas_call(functools.partial(place_body, where), out_shape=jax.ShapeD...  8.16 us
    all_to_all x1, waiting for transfers between devices, per_device(): base_tile = lax.all_to_all(base, 'worker', 0, 0, axis_index_groups=rings)  6.8 us
    pallas_call x1, Pallas kernels, attention(): pl.pallas_call(attention_body, out_shape=(jax.ShapeDtypeStruct((width, to...  4.92 us
    all_to_all x1, starting transfers between devices, per_device(): base_tile = lax.all_to_all(base, 'worker', 0, 0, axis_index_groups=rings)  4.3 us
  transfers between devices with their start and end apart: 38, of which 20 were waited for; matrix products, arithmetic and copies ran while one was open for 7% of the time, Pallas kernels for 9%

profile of v5, /device:TPU:32, one launch (start us, length us, event | category | flops | bytes accessed | tf_op | source)
XLA Modules:
  0.0 170.5 jit_solution(3040058494669984316)
XLA Ops:
  0.6 2.7 %cotangent_gram.1 = f32[6,128,128]{2,1,0:T(8,128)} custom-call(bf16[384,1280]{1,0:T(8,128)(2,1)} %g0_ref.1), custom_call_target="tpu_custom_call" | custom-call | tf_op jit(solution)/shard_map/cotangent_gram/pallas_call | solution.py:59
  3.4 1.3 reshape.27.seg_row_ref
  4.7 4.9 %attention.1 = (bf16[640,384]{1,0:T(8,128)(2,1)}, f32[6,128,128]{2,1,0:T(8,128)}) custom-call(bf16[384,640]{1,0:T(8,128)(2,1)} %q_ref, bf16[384,640]{1,0:T(8,128)(2,1)} %k_ref.1, bf16[384,640]{1,0:T(8,128)(2,1)} %v_ref.1, s32[1,384]{1,0:T(1,128)} %reshape.27.seg_row_ref), custom_call_target="tpu_custom_call" | custom-call | tf_op jit(solution)/shard_map/attention/pallas_call | solution.py:102
  9.6 0.6 pad_add_fusion.at_ref
  10.2 2.0 %collective-permute-start = (bf16[384,1280]{1,0:T(8,128)(2,1)S(1)}, bf16[384,1280]{1,0:T(8,128)(2,1)S(1)}, u32[]{:S(2)}, u32[]{:S(2)}) collective-permute-start(bf16[384,1280]{1,0:T(8,128)(2,1)S(1)} %copy-done), channel_id=1, source_target_pairs={{0,64},{32,96},{64,0},{96,32},{1,65},{33,97},{65,1},{97,33},{2,66}... | collective-permute-start | bytes 2949128 | tf_op jit(solution)/shard_map/ppermute | solution.py:44
  12.2 3.4 %collective-permute-done.1 = f32[6,128,128]{2,1,0:T(8,128)S(1)} collective-permute-done((f32[6,128,128]{2,1,0:T(8,128)}, f32[6,128,128]{2,1,0:T(8,128)S(1)}, u32[]{:S(2)}, u32[]{:S(2)}) %collective-permute-start.1) | collective-permute-done | bytes 393248 | tf_op jit(solution)/shard_map/ppermute | solution.py:44
  15.7 2.1 %base_rows.1 = f32[4,20,1280]{2,1,0:T(8,128)} custom-call(s32[4]{0:T(128)} %pad_add_fusion.at_ref, f32[20,5120]{1,0:T(8,128)} %master_ref.3, f32[20,5120]{1,0:T(8,128)} %momentum_ref.3), custom_call_target="tpu_custom_call" | custom-call | tf_op jit(solution)/shard_map/base_rows/pallas_call | solution.py:232
  17.8 4.3 %all-to-all-start = ((f32[4,20,1280]{2,1,0:T(8,128)}), f32[4,20,1280]{2,1,0:T(8,128)S(1)}, u32[]{:S(2)}, u32[]{:S(2)}) async-start(f32[4,20,1280]{2,1,0:T(8,128)} %base_rows.1), calls=%async_computation | async-start | bytes 983040 | tf_op jit(solution)/shard_map/all_to_all | solution.py:366
  22.1 1.7 multiply_reduce_fusion
  23.8 0.6 broadcast_in_dim.3
  24.7 0.3 collective-permute-start.5
  25.0 6.8 %all-to-all-done = f32[4,20,1280]{2,1,0:T(8,128)S(1)} async-done(((f32[4,20,1280]{2,1,0:T(8,128)}), f32[4,20,1280]{2,1,0:T(8,128)S(1)}, u32[]{:S(2)}, u32[]{:S(2)}) %all-to-all-start) | async-done | bytes 409632 | tf_op jit(solution)/shard_map/all_to_all | solution.py:366
  31.9 0.7 broadcast_add_fusion
  32.6 2.9 %collective-permute-done.g2_ref = bf16[384,1280]{1,0:T(8,128)(2,1)S(1)} collective-permute-done((bf16[384,1280]{1,0:T(8,128)(2,1)S(1)}, bf16[384,1280]{1,0:T(8,128)(2,1)S(1)}, u32[]{:S(2)}, u32[]{:S(2)}) %collective-permute-start) | collective-permute-done | bytes 983072 | tf_op jit(solution)/shard_map/ppermute | solution.py:44
  35.5 0.4 collective-permute-start.4
  35.8 3.3 %collective-permute-done.4 = f32[8,128]{1,0:T(8,128)S(1)} collective-permute-done((f32[8,128]{1,0:T(8,128)S(1)}, f32[8,128]{1,0:T(8,128)S(1)}, u32[]{:S(2)}, u32[]{:S(2)}) %collective-permute-start.4) | collective-permute-done | bytes 4128 | tf_op jit(solution)/shard_map/ppermute | solution.py:44
  39.1 0.5 slice.102
  40.3 9.6 %pseudo_gradient.1 = (bf16[4,80,1280]{2,1,0:T(8,128)(2,1)}, bf16[4,80,1280]{2,1,0:T(8,128)(2,1)}, bf16[4,80,1280]{2,1,0:T(8,128)(2,1)}, bf16[4,80,1280]{2,1,0:T(...) custom-call(s32[4]{0:T(128)} %pad_add_fusion.at_ref, ...), custom_call_target="tpu_custom_call" | custom-call | flops 2516582400 | bytes 18000000 | tf_op jit(solution)/shard_map/pseudo_gradient/pallas_call | solution.py:196
  50.0 2.8 %collective-permute-start.10 = (bf16[4,80,1280]{2,1,0:T(8,128)(2,1)}, bf16[4,80,1280]{2,1,0:T(8,128)(2,1)S(1)}, u32[]{:S(2)}, u32[]{:S(2)}) collective-permute-start(bf16[4,80,1280]{2,1,0:T(8,128)(2,1)} %get-tuple-element.60), channel_id=1, source_target_pairs={{0,3},{1,0},{2,1},{3,2},{4,7},{5,4},{6,5},{7,6},{8,11},{9,8},{10,9... | collective-permute-start | bytes 2457608 | tf_op jit(solution)/shard_map/ppermute | solution.py:40
  52.8 1.6 collective-permute-start.7
  54.4 1.7 collective-permute-start.8
  56.0 14.1 %collective-permute-done.10 = bf16[4,80,1280]{2,1,0:T(8,128)(2,1)S(1)} collective-permute-done((bf16[4,80,1280]{2,1,0:T(8,128)(2,1)}, bf16[4,80,1280]{2,1,0:T(8,128)(2,1)S(1)}, u32[]{:S(2)}, u32[]{:S(2)}) %collective-permute-start.10) | collective-permute-done | bytes 819232 | tf_op jit(solution)/shard_map/ppermute | solution.py:40
  70.1 1.2 add_convert_fusion
  71.3 3.7 %collective-permute-start.13 = (bf16[2,80,1280]{2,1,0:T(8,128)(2,1)S(1)}, bf16[2,80,1280]{2,1,0:T(8,128)(2,1)S(1)}, u32[]{:S(2)}, u32[]{:S(2)}) collective-permute-start(bf16[2,80,1280]{2,1,0:T(8,128)(2,1)S(1)} %add_convert_fusion), channel_id=1, source_target_pairs={{0,3},{1,0},{2,1},{3,2},{4,7},{5,4},{6,5},{7,6},{8,11},{9,8},{10,9... | collective-permute-start | bytes 1228808 | tf_op jit(solution)/shard_map/ppermute | solution.py:40
  75.0 1.2 add_convert_fusion.1
  76.7 1.7 collective-permute-start.14
  78.3 1.7 collective-permute-start.15
  80.0 3.0 %collective-permute-start.9 = (f32[80,1280]{1,0:T(8,128)S(1)}, f32[80,1280]{1,0:T(8,128)S(1)}, u32[]{:S(2)}, u32[]{:S(2)}) collective-permute-start(f32[80,1280]{1,0:T(8,128)S(1)} %reshape.28), channel_id=1, source_target_pairs={{0,16},{1,17},{2,18},{3,19},{4,20},{5,21},{6,22},{7,23},{8,24},{9,... | collective-permute-start | bytes 1228808 | tf_op jit(solution)/shard_map/ppermute | solution.py:40
  83.0 4.2 %collective-permute-done.12 = bf16[2,80,1280]{2,1,0:T(8,128)(2,1)S(1)} collective-permute-done((bf16[2,80,1280]{2,1,0:T(8,128)(2,1)S(1)}, bf16[2,80,1280]{2,1,0:T(8,128)(2,1)S(1)}, u32[]{:S(2)}, u32[]{:S(2)}) %collective-permute-start.12) | collective-permute-done | bytes 409632 | tf_op jit(solution)/shard_map/ppermute | solution.py:40
  87.6 0.7 copy-done.9
  88.3 0.3 convert_add_fusion.1
  88.6 0.3 pad_maximum_fusion
  89.0 1.7 collective-permute-start.16
  90.6 1.7 collective-permute-start.18
  92.3 2.0 %collective-permute-start.17 = (bf16[80,1280]{1,0:T(8,128)(2,1)S(1)}, bf16[80,1280]{1,0:T(8,128)(2,1)S(1)}, u32[]{:S(2)}, u32[]{:S(2)}) collective-permute-start(bf16[80,1280]{1,0:T(8,128)(2,1)S(1)} %get-tuple-element.84), channel_id=1, source_target_pairs={{0,8},{1,9},{2,10},{3,11},{4,12},{5,13},{6,14},{7,15},{8,0},{9,1},... | collective-permute-start | bytes 614408 | tf_op jit(solution)/shard_map/ppermute | solution.py:40
  94.5 3.4 %collective-permute-done.16 = bf16[80,1280]{1,0:T(8,128)(2,1)S(1)} collective-permute-done((bf16[80,1280]{1,0:T(8,128)(2,1)S(1)}, bf16[80,1280]{1,0:T(8,128)(2,1)S(1)}, u32[]{:S(2)}, u32[]{:S(2)}) %collective-permute-start.16) | collective-permute-done | bytes 204832 | tf_op jit(solution)/shard_map/ppermute | solution.py:40
  97.9 1.8 %collective-permute-start.21 = (bf16[80,1280]{1,0:T(8,128)(2,1)S(1)}, bf16[80,1280]{1,0:T(8,128)(2,1)S(1)}, u32[]{:S(2)}, u32[]{:S(2)}) collective-permute-start(bf16[80,1280]{1,0:T(8,128)(2,1)S(1)} %get-tuple-element.80), channel_id=1, source_target_pairs={{0,3},{1,0},{2,1},{3,2},{4,7},{5,4},{6,5},{7,6},{8,11},{9,8},{10,9... | collective-permute-start | bytes 614408 | tf_op jit(solution)/shard_map/ppermute | solution.py:40
  99.6 0.4 collective-permute-done.17
  100.2 2.0 %collective-permute-done.19 = bf16[80,1280]{1,0:T(8,128)(2,1)S(1)} collective-permute-done((bf16[80,1280]{1,0:T(8,128)(2,1)S(1)}, bf16[80,1280]{1,0:T(8,128)(2,1)S(1)}, u32[]{:S(2)}, u32[]{:S(2)}) %collective-permute-start.19) | collective-permute-done | bytes 204832 | tf_op jit(solution)/shard_map/ppermute | solution.py:40
  102.2 2.9 %collective-permute-done.21 = bf16[80,1280]{1,0:T(8,128)(2,1)S(1)} collective-permute-done((bf16[80,1280]{1,0:T(8,128)(2,1)S(1)}, bf16[80,1280]{1,0:T(8,128)(2,1)S(1)}, u32[]{:S(2)}, u32[]{:S(2)}) %collective-permute-start.21) | collective-permute-done | bytes 204832 | tf_op jit(solution)/shard_map/ppermute | solution.py:40
  105.1 1.8 %collective-permute-done.20 = bf16[80,1280]{1,0:T(8,128)(2,1)S(1)} collective-permute-done((bf16[80,1280]{1,0:T(8,128)(2,1)S(1)}, bf16[80,1280]{1,0:T(8,128)(2,1)S(1)}, u32[]{:S(2)}, u32[]{:S(2)}) %collective-permute-start.20) | collective-permute-done | bytes 204832 | tf_op jit(solution)/shard_map/ppermute | solution.py:40
  107.0 3.1 %collective-permute-start.22 = (bf16[2,80,1280]{2,1,0:T(8,128)(2,1)S(1)}, bf16[2,80,1280]{2,1,0:T(8,128)(2,1)S(1)}, u32[]{:S(2)}, u32[]{:S(2)}) collective-permute-start(bf16[2,80,1280]{2,1,0:T(8,128)(2,1)S(1)} %pad_maximum_fusion.5), channel_id=1, source_target_pairs={{0,16},{1,17},{2,18},{3,19},{4,20},{5,21},{6,22},{7,23},{8,24},{9,... | collective-permute-start | bytes 1228808 | tf_op jit(solution)/shard_map/ppermute | solution.py:40
  110.1 6.5 %collective-permute-done.22 = bf16[2,80,1280]{2,1,0:T(8,128)(2,1)S(1)} collective-permute-done((bf16[2,80,1280]{2,1,0:T(8,128)(2,1)S(1)}, bf16[2,80,1280]{2,1,0:T(8,128)(2,1)S(1)}, u32[]{:S(2)}, u32[]{:S(2)}) %collective-permute-start.22) | collective-permute-done | bytes 409632 | tf_op jit(solution)/shard_map/ppermute | solution.py:40
  116.9 3.7 %collective-permute-start.24 = (bf16[80,1280]{1,0:T(8,128)(2,1)S(1)}, bf16[80,1280]{1,0:T(8,128)(2,1)S(1)}, u32[]{:S(2)}, u32[]{:S(2)}) collective-permute-start(bf16[80,1280]{1,0:T(8,128)(2,1)S(1)} %get-tuple-element.90), channel_id=1, source_target_pairs={{0,8},{1,9},{2,10},{3,11},{4,12},{5,13},{6,14},{7,15},{8,0},{9,1},... | collective-permute-start | bytes 614408 | tf_op jit(solution)/shard_map/ppermute | solution.py:40
  120.7 2.2 %collective-permute-start.30 = (bf16[100,1280]{1,0:T(8,128)(2,1)S(1)}, bf16[100,1280]{1,0:T(8,128)(2,1)S(1)}, u32[]{:S(2)}, u32[]{:S(2)}) collective-permute-start(bf16[100,1280]{1,0:T(8,128)(2,1)S(1)} %get-tuple-element.96), channel_id=1, source_target_pairs={{0,3},{1,0},{2,1},{3,2},{4,7},{5,4},{6,5},{7,6},{8,11},{9,8},{10,9... | collective-permute-start | bytes 768008 | tf_op jit(solution)/shard_map/ppermute | solution.py:40
  122.9 0.7 collective-permute-start.31
  123.8 2.5 %collective-permute-start.32 = (bf16[100,1280]{1,0:T(8,128)(2,1)S(1)}, bf16[100,1280]{1,0:T(8,128)(2,1)S(1)}, u32[]{:S(2)}, u32[]{:S(2)}) collective-permute-start(bf16[100,1280]{1,0:T(8,128)(2,1)S(1)} %get-tuple-element.98), channel_id=1, source_target_pairs={{0,1},{1,2},{2,3},{3,0},{4,5},{5,6},{6,7},{7,4},{8,9},{9,10},{10,1... | collective-permute-start | bytes 768008 | tf_op jit(solution)/shard_map/ppermute | solution.py:40
  126.5 0.4 collective-permute-done.23
  127.0 0.3 collective-permute-start.28
  127.3 3.0 %collective-permute-start.26 = (bf16[4,80,1280]{2,1,0:T(8,128)(2,1)S(1)}, bf16[4,80,1280]{2,1,0:T(8,128)(2,1)S(1)}, u32[]{:S(2)}, u32[]{:S(2)}) collective-permute-start(bf16[4,80,1280]{2,1,0:T(8,128)(2,1)S(1)} %pad_maximum_fusion.2.rest_0_), channel_id=1, source_target_pairs={{0,3},{1,0},{2,1},{3,2},{4,7},{5,4},{6,5},{7,6},{8,11},{9,8},{10,9... | collective-permute-start | bytes 2457608 | tf_op jit(solution)/shard_map/ppermute | solution.py:40
  130.3 3.4 %collective-permute-done.31 = bf16[100,1280]{1,0:T(8,128)(2,1)S(1)} collective-permute-done((bf16[100,1280]{1,0:T(8,128)(2,1)S(1)}, bf16[100,1280]{1,0:T(8,128)(2,1)S(1)}, u32[]{:S(2)}, u32[]{:S(2)}) %collective-permute-start.31) | collective-permute-done | bytes 256032 | tf_op jit(solution)/shard_map/ppermute | solution.py:40
  133.8 3.2 %collective-permute-done.32 = bf16[100,1280]{1,0:T(8,128)(2,1)S(1)} collective-permute-done((bf16[100,1280]{1,0:T(8,128)(2,1)S(1)}, bf16[100,1280]{1,0:T(8,128)(2,1)S(1)}, u32[]{:S(2)}, u32[]{:S(2)}) %collective-permute-start.32) | collective-permute-done | bytes 256032 | tf_op jit(solution)/shard_map/ppermute | solution.py:40
  137.1 1.3 collective-permute-start.35
  138.4 2.0 %collective-permute-start.33 = (bf16[4,80,1280]{2,1,0:T(8,128)(2,1)S(1)}, bf16[4,80,1280]{2,1,0:T(8,128)(2,1)S(1)}, u32[]{:S(2)}, u32[]{:S(2)}) collective-permute-start(bf16[4,80,1280]{2,1,0:T(8,128)(2,1)S(1)} %pad_maximum_fusion.3.rest_3_), channel_id=1, source_target_pairs={{0,12},{1,13},{2,14},{3,15},{4,0},{5,1},{6,2},{7,3},{8,4},{9,5},{1... | collective-permute-start | bytes 2457608 | tf_op jit(solution)/shard_map/ppermute | solution.py:40
  140.4 10.0 %collective-permute-done.28.rest_2_ = bf16[4,80,1280]{2,1,0:T(8,128)(2,1)S(1)} collective-permute-done((bf16[4,80,1280]{2,1,0:T(8,128)(2,1)S(1)}, bf16[4,80,1280]{2,1,0:T(8,128)(2,1)S(1)}, u32[]{:S(2)}, u32[]{:S(2)}) %collective-permute-start.28) | collective-permute-done | bytes 819232 | tf_op jit(solution)/shard_map/ppermute | solution.py:40
  150.6 3.3 %collective-permute-start.27 = (bf16[2,80,1280]{2,1,0:T(8,128)(2,1)S(1)}, bf16[2,80,1280]{2,1,0:T(8,128)(2,1)}, u32[]{:S(2)}, u32[]{:S(2)}) collective-permute-start(bf16[2,80,1280]{2,1,0:T(8,128)(2,1)S(1)} %slice.149), channel_id=1, source_target_pairs={{0,3},{1,0},{2,1},{3,2},{4,7},{5,4},{6,5},{7,6},{8,11},{9,8},{10,9... | collective-permute-start | bytes 1228808 | tf_op jit(solution)/shard_map/ppermute | solution.py:40
  153.9 0.8 slice.157
  154.7 1.2 collective-permute-start.36
  155.9 0.8 slice.156
  156.7 2.0 %collective-permute-start.34 = (bf16[2,80,1280]{2,1,0:T(8,128)(2,1)}, bf16[2,80,1280]{2,1,0:T(8,128)(2,1)}, u32[]{:S(2)}, u32[]{:S(2)}) collective-permute-start(bf16[2,80,1280]{2,1,0:T(8,128)(2,1)} %slice.156), channel_id=1, source_target_pairs={{0,12},{1,13},{2,14},{3,15},{4,0},{5,1},{6,2},{7,3},{8,4},{9,5},{1... | collective-permute-start | bytes 1228808 | tf_op jit(solution)/shard_map/ppermute | solution.py:40
  158.8 0.8 pad_maximum_fusion.4.mean_ref
  159.6 2.4 %outer_rows.1 = (f32[20,5120]{1,0:T(8,128)}, f32[20,5120]{1,0:T(8,128)}) custom-call(s32[4]{0:T(128)} %pad_add_fusion.at_ref, f32[20,5120]{1,0:T(8,128)} %master_ref.3, f32[20,5120]{1,0:T(8,128)} %momentum_ref.3, f32[4,20,1280]{2,1,0:T(8,128)} %pad_maximum_fusion.4.mean_ref), custom_call_target="tpu_custom_call" | custom-call | tf_op jit(solution)/shard_map/outer_rows/pallas_call | solution.py:255
  162.1 5.2 %place_first.1.rest_4_ = bf16[640,5120]{1,0:T(8,128)(2,1)} custom-call(s32[4]{0:T(128)} %pad_add_fusion.at_ref, bf16[4,80,1280]{2,1,0:T(8,128)(2,1)} %copy-done.1, bf16[4,80,1280]{2,1,0:T(8,128)(2,1)} %copy-done.4, bf16[4,80,1280]{2,1,0:T(8,128)(2,1)} %copy-done.3, bf16[4,80,1280]{2,1,0:T(8,128)(2,1)} %copy-done.2, bf16[4,80,1280]{2,1,0:T(8,128)(2,1)} %copy-done.6, ...), custom_call_target="tpu_custom_call" | custom-call | bytes 9830400 | tf_op jit(solution)/shard_map/place_first/pallas_call | solution.py:295
  167.3 3.0 %place_last.1 = bf16[640,5120]{1,0:T(8,128)(2,1)} custom-call(s32[4]{0:T(128)} %pad_add_fusion.at_ref, bf16[2,80,1280]{2,1,0:T(8,128)(2,1)} %collective-permute-done.27.rest_0_, bf16[2,80,1280]{2,1,0:T(8,128)(2,1)} %collective-permute-done.29.rest_1_, bf16[2,80,1280]{2,1,0:T(8,128)(2,1)} %collective-permute-done.34.rest_2_, ...), custom_call_target="tpu_custom_call", output_to_operand_aliasing={{}: (5, {})} | custom-call | bytes 3276800 | tf_op jit(solution)/shard_map/place_last/pallas_call | solution.py:295
  (89 shorter events, 3.3 us)
Async XLA Ops:
  0.6 9.6 %copy-start = (bf16[384,1280]{1,0:T(8,128)(2,1)S(1)}, bf16[384,1280]{1,0:T(8,128)(2,1)}, u32[]{:S(2)}) copy-start(bf16[384,1280]{1,0:T(8,128)(2,1)} %g0_ref.1) | copy-start | bytes 2949124
  3.3 12.2 %copy-start.7 = (f32[6,128,128]{2,1,0:T(8,128)S(1)}, f32[6,128,128]{2,1,0:T(8,128)}, u32[]{:S(2)}) copy-start(f32[6,128,128]{2,1,0:T(8,128)} %cotangent_gram.1) | copy-start | bytes 1179652
  3.3 12.2 %collective-permute-start.1 = (f32[6,128,128]{2,1,0:T(8,128)}, f32[6,128,128]{2,1,0:T(8,128)S(1)}, u32[]{:S(2)}, u32[]{:S(2)}) collective-permute-start(f32[6,128,128]{2,1,0:T(8,128)} %cotangent_gram.1), channel_id=1, source_target_pairs={{0,64},{32,96},{64,0},{96,32},{1,65},{33,97},{65,1},{97,33},{2,66}... | collective-permute-start | bytes 1179656 | tf_op jit(solution)/shard_map/ppermute | solution.py:44
  10.2 25.3 %collective-permute-start = (bf16[384,1280]{1,0:T(8,128)(2,1)S(1)}, bf16[384,1280]{1,0:T(8,128)(2,1)S(1)}, u32[]{:S(2)}, u32[]{:S(2)}) collective-permute-start(bf16[384,1280]{1,0:T(8,128)(2,1)S(1)} %copy-done), channel_id=1, source_target_pairs={{0,64},{32,96},{64,0},{96,32},{1,65},{33,97},{65,1},{97,33},{2,66}... | collective-permute-start | bytes 2949128 | tf_op jit(solution)/shard_map/ppermute | solution.py:44
  15.6 6.5 %copy-start.13 = (f32[6,128,128]{2,1,0:T(8,128)S(1)}, f32[6,128,128]{2,1,0:T(8,128)}, u32[]{:S(2)}) copy-start(f32[6,128,128]{2,1,0:T(8,128)} %get-tuple-element.45) | copy-start | bytes 1179652
  15.6 6.5 %collective-permute-start.2 = (f32[6,128,128]{2,1,0:T(8,128)S(1)}, f32[6,128,128]{2,1,0:T(8,128)}, u32[]{:S(2)}, u32[]{:S(2)}) collective-permute-start(f32[6,128,128]{2,1,0:T(8,128)S(1)} %add.117), channel_id=1, source_target_pairs={{0,32},{32,0},{64,96},{96,64},{1,33},{33,1},{65,97},{97,65},{2,34}... | collective-permute-start | bytes 1179656 | tf_op jit(solution)/shard_map/ppermute | solution.py:44
  17.8 14.1 %all-to-all-start = ((f32[4,20,1280]{2,1,0:T(8,128)}), f32[4,20,1280]{2,1,0:T(8,128)S(1)}, u32[]{:S(2)}, u32[]{:S(2)}) async-start(f32[4,20,1280]{2,1,0:T(8,128)} %base_rows.1), calls=%async_computation | async-start | bytes 983040 | tf_op jit(solution)/shard_map/all_to_all | solution.py:366
  24.4 7.4 %collective-permute-start.3 = (f32[8,128]{1,0:T(8,128)S(1)}, f32[8,128]{1,0:T(8,128)S(1)}, u32[]{:S(2)}, u32[]{:S(2)}) collective-permute-start(f32[8,128]{1,0:T(8,128)S(1)} %broadcast_in_dim.3), channel_id=1, source_target_pairs={{0,32},{32,0},{64,96},{96,64},{1,33},{33,1},{65,97},{97,65},{2,34}... | collective-permute-start | bytes 12296 | tf_op jit(solution)/shard_map/ppermute | solution.py:44
  24.7 15.6 %collective-permute-start.5 = (bf16[384,1280]{1,0:T(8,128)(2,1)S(1)}, bf16[384,1280]{1,0:T(8,128)(2,1)}, u32[]{:S(2)}, u32[]{:S(2)}) collective-permute-start(bf16[384,1280]{1,0:T(8,128)(2,1)S(1)} %copy-done), channel_id=1, source_target_pairs={{0,32},{32,0},{64,96},{96,64},{1,33},{33,1},{65,97},{97,65},{2,34}... | collective-permute-start | bytes 2949128 | tf_op jit(solution)/shard_map/ppermute | solution.py:44
  35.5 4.8 %copy-start.8 = (bf16[384,1280]{1,0:T(8,128)(2,1)}, bf16[384,1280]{1,0:T(8,128)(2,1)S(1)}, u32[]{:S(2)}) copy-start(bf16[384,1280]{1,0:T(8,128)(2,1)S(1)} %collective-permute-done.g2_ref) | copy-start | bytes 2949124
  35.5 4.8 %collective-permute-start.6 = (bf16[384,1280]{1,0:T(8,128)(2,1)S(1)}, bf16[384,1280]{1,0:T(8,128)(2,1)}, u32[]{:S(2)}, u32[]{:S(2)}) collective-permute-start(bf16[384,1280]{1,0:T(8,128)(2,1)S(1)} %collective-permute-done.g2_ref), channel_id=1, source_target_pairs={{0,32},{32,0},{64,96},{96,64},{1,33},{33,1},{65,97},{97,65},{2,34}... | collective-permute-start | bytes 2949128 | tf_op jit(solution)/shard_map/ppermute | solution.py:44
  35.5 3.6 %collective-permute-start.4 = (f32[8,128]{1,0:T(8,128)S(1)}, f32[8,128]{1,0:T(8,128)S(1)}, u32[]{:S(2)}, u32[]{:S(2)}) collective-permute-start(f32[8,128]{1,0:T(8,128)S(1)} %broadcast_add_fusion), channel_id=1, source_target_pairs={{0,64},{32,96},{64,0},{96,32},{1,65},{33,97},{65,1},{97,33},{2,66}... | collective-permute-start | bytes 12296 | tf_op jit(solution)/shard_map/ppermute | solution.py:44
  50.0 26.5 %copy-start.12 = (bf16[2,80,1280]{2,1,0:T(8,128)(2,1)S(1)}, bf16[2,80,1280]{2,1,0:T(8,128)(2,1)}, u32[]{:S(2)}) copy-start(bf16[2,80,1280]{2,1,0:T(8,128)(2,1)} %get-tuple-element.55) | copy-start | bytes 1228804
  50.0 20.2 %collective-permute-start.10 = (bf16[4,80,1280]{2,1,0:T(8,128)(2,1)}, bf16[4,80,1280]{2,1,0:T(8,128)(2,1)S(1)}, u32[]{:S(2)}, u32[]{:S(2)}) collective-permute-start(bf16[4,80,1280]{2,1,0:T(8,128)(2,1)} %get-tuple-element.60), channel_id=1, source_target_pairs={{0,3},{1,0},{2,1},{3,2},{4,7},{5,4},{6,5},{7,6},{8,11},{9,8},{10,9... | collective-permute-start | bytes 2457608 | tf_op jit(solution)/shard_map/ppermute | solution.py:40
  52.8 22.2 %collective-permute-start.11 = (bf16[4,80,1280]{2,1,0:T(8,128)(2,1)}, bf16[4,80,1280]{2,1,0:T(8,128)(2,1)S(1)}, u32[]{:S(2)}, u32[]{:S(2)}) collective-permute-start(bf16[4,80,1280]{2,1,0:T(8,128)(2,1)} %get-tuple-element.62), channel_id=1, source_target_pairs={{0,1},{1,2},{2,3},{3,0},{4,5},{5,6},{6,7},{7,4},{8,9},{9,10},{10,1... | collective-permute-start | bytes 2457608 | tf_op jit(solution)/shard_map/ppermute | solution.py:40
  52.8 23.6 %collective-permute-start.7 = (bf16[4,80,1280]{2,1,0:T(8,128)(2,1)}, bf16[4,80,1280]{2,1,0:T(8,128)(2,1)S(1)}, u32[]{:S(2)}, u32[]{:S(2)}) collective-permute-start(bf16[4,80,1280]{2,1,0:T(8,128)(2,1)} %get-tuple-element.53), channel_id=1, source_target_pairs={{0,4},{1,5},{2,6},{3,7},{4,8},{5,9},{6,10},{7,11},{8,12},{9,13},{1... | collective-permute-start | bytes 2457608 | tf_op jit(solution)/shard_map/ppermute | solution.py:40
  54.4 22.2 %collective-permute-start.8 = (bf16[4,80,1280]{2,1,0:T(8,128)(2,1)}, bf16[4,80,1280]{2,1,0:T(8,128)(2,1)S(1)}, u32[]{:S(2)}, u32[]{:S(2)}) collective-permute-start(bf16[4,80,1280]{2,1,0:T(8,128)(2,1)} %get-tuple-element.54), channel_id=1, source_target_pairs={{0,12},{1,13},{2,14},{3,15},{4,0},{5,1},{6,2},{7,3},{8,4},{9,5},{1... | collective-permute-start | bytes 2457608 | tf_op jit(solution)/shard_map/ppermute | solution.py:40
  70.1 6.4 %copy-start.11 = (bf16[2,80,1280]{2,1,0:T(8,128)(2,1)S(1)}, bf16[2,80,1280]{2,1,0:T(8,128)(2,1)}, u32[]{:S(2)}) copy-start(bf16[2,80,1280]{2,1,0:T(8,128)(2,1)} %get-tuple-element.56) | copy-start | bytes 1228804
  71.3 11.7 %collective-permute-start.13 = (bf16[2,80,1280]{2,1,0:T(8,128)(2,1)S(1)}, bf16[2,80,1280]{2,1,0:T(8,128)(2,1)S(1)}, u32[]{:S(2)}, u32[]{:S(2)}) collective-permute-start(bf16[2,80,1280]{2,1,0:T(8,128)(2,1)S(1)} %add_convert_fusion), channel_id=1, source_target_pairs={{0,3},{1,0},{2,1},{3,2},{4,7},{5,4},{6,5},{7,6},{8,11},{9,8},{10,9... | collective-permute-start | bytes 1228808 | tf_op jit(solution)/shard_map/ppermute | solution.py:40
  75.0 12.2 %copy-start.10 = (bf16[4,80,1280]{2,1,0:T(8,128)(2,1)S(1)}, bf16[4,80,1280]{2,1,0:T(8,128)(2,1)}, u32[]{:S(2)}) copy-start(bf16[4,80,1280]{2,1,0:T(8,128)(2,1)} %get-tuple-element.59) | copy-start | bytes 2457604
  76.2 11.0 %collective-permute-start.12 = (bf16[2,80,1280]{2,1,0:T(8,128)(2,1)S(1)}, bf16[2,80,1280]{2,1,0:T(8,128)(2,1)S(1)}, u32[]{:S(2)}, u32[]{:S(2)}) collective-permute-start(bf16[2,80,1280]{2,1,0:T(8,128)(2,1)S(1)} %add_convert_fusion.1), channel_id=1, source_target_pairs={{0,1},{1,2},{2,3},{3,0},{4,5},{5,6},{6,7},{7,4},{8,9},{9,10},{10,1... | collective-permute-start | bytes 1228808 | tf_op jit(solution)/shard_map/ppermute | solution.py:40
  76.7 10.8 %collective-permute-start.14 = (bf16[2,80,1280]{2,1,0:T(8,128)(2,1)S(1)}, bf16[2,80,1280]{2,1,0:T(8,128)(2,1)S(1)}, u32[]{:S(2)}, u32[]{:S(2)}) collective-permute-start(bf16[2,80,1280]{2,1,0:T(8,128)(2,1)S(1)} %add_convert_fusion.3), channel_id=1, source_target_pairs={{0,4},{1,5},{2,6},{3,7},{4,8},{5,9},{6,10},{7,11},{8,12},{9,13},{1... | collective-permute-start | bytes 1228808 | tf_op jit(solution)/shard_map/ppermute | solution.py:40
  78.3 9.2 %collective-permute-start.15 = (bf16[2,80,1280]{2,1,0:T(8,128)(2,1)S(1)}, bf16[2,80,1280]{2,1,0:T(8,128)(2,1)S(1)}, u32[]{:S(2)}, u32[]{:S(2)}) collective-permute-start(bf16[2,80,1280]{2,1,0:T(8,128)(2,1)S(1)} %add_convert_fusion.2), channel_id=1, source_target_pairs={{0,12},{1,13},{2,14},{3,15},{4,0},{5,1},{6,2},{7,3},{8,4},{9,5},{1... | collective-permute-start | bytes 1228808 | tf_op jit(solution)/shard_map/ppermute | solution.py:40
  80.0 30.1 %collective-permute-start.9 = (f32[80,1280]{1,0:T(8,128)S(1)}, f32[80,1280]{1,0:T(8,128)S(1)}, u32[]{:S(2)}, u32[]{:S(2)}) collective-permute-start(f32[80,1280]{1,0:T(8,128)S(1)} %reshape.28), channel_id=1, source_target_pairs={{0,16},{1,17},{2,18},{3,19},{4,20},{5,21},{6,22},{7,23},{8,24},{9,... | collective-permute-start | bytes 1228808 | tf_op jit(solution)/shard_map/ppermute | solution.py:40
  87.1 1.1 copy-start.9
  89.0 8.9 %collective-permute-start.16 = (bf16[80,1280]{1,0:T(8,128)(2,1)S(1)}, bf16[80,1280]{1,0:T(8,128)(2,1)S(1)}, u32[]{:S(2)}, u32[]{:S(2)}) collective-permute-start(bf16[80,1280]{1,0:T(8,128)(2,1)S(1)} %get-tuple-element.82), channel_id=1, source_target_pairs={{0,4},{1,5},{2,6},{3,7},{4,8},{5,9},{6,10},{7,11},{8,12},{9,13},{1... | collective-permute-start | bytes 614408 | tf_op jit(solution)/shard_map/ppermute | solution.py:40
  90.6 9.0 %collective-permute-start.18 = (bf16[80,1280]{1,0:T(8,128)(2,1)S(1)}, bf16[80,1280]{1,0:T(8,128)(2,1)S(1)}, u32[]{:S(2)}, u32[]{:S(2)}) collective-permute-start(bf16[80,1280]{1,0:T(8,128)(2,1)S(1)} %get-tuple-element.83), channel_id=1, source_target_pairs={{0,12},{1,13},{2,14},{3,15},{4,0},{5,1},{6,2},{7,3},{8,4},{9,5},{1... | collective-permute-start | bytes 614408 | tf_op jit(solution)/shard_map/ppermute | solution.py:40
  92.3 7.8 %collective-permute-start.17 = (bf16[80,1280]{1,0:T(8,128)(2,1)S(1)}, bf16[80,1280]{1,0:T(8,128)(2,1)S(1)}, u32[]{:S(2)}, u32[]{:S(2)}) collective-permute-start(bf16[80,1280]{1,0:T(8,128)(2,1)S(1)} %get-tuple-element.84), channel_id=1, source_target_pairs={{0,8},{1,9},{2,10},{3,11},{4,12},{5,13},{6,14},{7,15},{8,0},{9,1},... | collective-permute-start | bytes 614408 | tf_op jit(solution)/shard_map/ppermute | solution.py:40
  94.4 7.8 %collective-permute-start.19 = (bf16[80,1280]{1,0:T(8,128)(2,1)S(1)}, bf16[80,1280]{1,0:T(8,128)(2,1)S(1)}, u32[]{:S(2)}, u32[]{:S(2)}) collective-permute-start(bf16[80,1280]{1,0:T(8,128)(2,1)S(1)} %get-tuple-element.79), channel_id=1, source_target_pairs={{0,1},{1,2},{2,3},{3,0},{4,5},{5,6},{6,7},{7,4},{8,9},{9,10},{10,1... | collective-permute-start | bytes 614408 | tf_op jit(solution)/shard_map/ppermute | solution.py:40
  97.9 7.3 %collective-permute-start.21 = (bf16[80,1280]{1,0:T(8,128)(2,1)S(1)}, bf16[80,1280]{1,0:T(8,128)(2,1)S(1)}, u32[]{:S(2)}, u32[]{:S(2)}) collective-permute-start(bf16[80,1280]{1,0:T(8,128)(2,1)S(1)} %get-tuple-element.80), channel_id=1, source_target_pairs={{0,3},{1,0},{2,1},{3,2},{4,7},{5,4},{6,5},{7,6},{8,11},{9,8},{10,9... | collective-permute-start | bytes 614408 | tf_op jit(solution)/shard_map/ppermute | solution.py:40
  99.6 7.3 %collective-permute-start.20 = (bf16[80,1280]{1,0:T(8,128)(2,1)S(1)}, bf16[80,1280]{1,0:T(8,128)(2,1)S(1)}, u32[]{:S(2)}, u32[]{:S(2)}) collective-permute-start(bf16[80,1280]{1,0:T(8,128)(2,1)S(1)} %get-tuple-element.81), channel_id=1, source_target_pairs={{0,2},{1,3},{2,0},{3,1},{4,6},{5,7},{6,4},{7,5},{8,10},{9,11},{10,... | collective-permute-start | bytes 614408 | tf_op jit(solution)/shard_map/ppermute | solution.py:40
  107.0 9.5 %collective-permute-start.22 = (bf16[2,80,1280]{2,1,0:T(8,128)(2,1)S(1)}, bf16[2,80,1280]{2,1,0:T(8,128)(2,1)S(1)}, u32[]{:S(2)}, u32[]{:S(2)}) collective-permute-start(bf16[2,80,1280]{2,1,0:T(8,128)(2,1)S(1)} %pad_maximum_fusion.5), channel_id=1, source_target_pairs={{0,16},{1,17},{2,18},{3,19},{4,20},{5,21},{6,22},{7,23},{8,24},{9,... | collective-permute-start | bytes 1228808 | tf_op jit(solution)/shard_map/ppermute | solution.py:40
  116.8 7.0 %collective-permute-start.25 = (bf16[80,1280]{1,0:T(8,128)(2,1)S(1)}, bf16[80,1280]{1,0:T(8,128)(2,1)S(1)}, u32[]{:S(2)}, u32[]{:S(2)}) collective-permute-start(bf16[80,1280]{1,0:T(8,128)(2,1)S(1)} %get-tuple-element.90), channel_id=1, source_target_pairs={{0,4},{1,5},{2,6},{3,7},{4,8},{5,9},{6,10},{7,11},{8,12},{9,13},{1... | collective-permute-start | bytes 614408 | tf_op jit(solution)/shard_map/ppermute | solution.py:40
  116.9 9.7 %collective-permute-start.24 = (bf16[80,1280]{1,0:T(8,128)(2,1)S(1)}, bf16[80,1280]{1,0:T(8,128)(2,1)S(1)}, u32[]{:S(2)}, u32[]{:S(2)}) collective-permute-start(bf16[80,1280]{1,0:T(8,128)(2,1)S(1)} %get-tuple-element.90), channel_id=1, source_target_pairs={{0,8},{1,9},{2,10},{3,11},{4,12},{5,13},{6,14},{7,15},{8,0},{9,1},... | collective-permute-start | bytes 614408 | tf_op jit(solution)/shard_map/ppermute | solution.py:40
  120.6 6.3 %collective-permute-start.23 = (bf16[80,1280]{1,0:T(8,128)(2,1)S(1)}, bf16[80,1280]{1,0:T(8,128)(2,1)S(1)}, u32[]{:S(2)}, u32[]{:S(2)}) collective-permute-start(bf16[80,1280]{1,0:T(8,128)(2,1)S(1)} %get-tuple-element.90), channel_id=1, source_target_pairs={{0,12},{1,13},{2,14},{3,15},{4,0},{5,1},{6,2},{7,3},{8,4},{9,5},{1... | collective-permute-start | bytes 614408 | tf_op jit(solution)/shard_map/ppermute | solution.py:40
  120.7 9.6 %collective-permute-start.30 = (bf16[100,1280]{1,0:T(8,128)(2,1)S(1)}, bf16[100,1280]{1,0:T(8,128)(2,1)S(1)}, u32[]{:S(2)}, u32[]{:S(2)}) collective-permute-start(bf16[100,1280]{1,0:T(8,128)(2,1)S(1)} %get-tuple-element.96), channel_id=1, source_target_pairs={{0,3},{1,0},{2,1},{3,2},{4,7},{5,4},{6,5},{7,6},{8,11},{9,8},{10,9... | collective-permute-start | bytes 768008 | tf_op jit(solution)/shard_map/ppermute | solution.py:40
  122.9 10.8 %collective-permute-start.31 = (bf16[100,1280]{1,0:T(8,128)(2,1)S(1)}, bf16[100,1280]{1,0:T(8,128)(2,1)S(1)}, u32[]{:S(2)}, u32[]{:S(2)}) collective-permute-start(bf16[100,1280]{1,0:T(8,128)(2,1)S(1)} %get-tuple-element.97), channel_id=1, source_target_pairs={{0,2},{1,3},{2,0},{3,1},{4,6},{5,7},{6,4},{7,5},{8,10},{9,11},{10,... | collective-permute-start | bytes 768008 | tf_op jit(solution)/shard_map/ppermute | solution.py:40
  123.8 13.1 %collective-permute-start.32 = (bf16[100,1280]{1,0:T(8,128)(2,1)S(1)}, bf16[100,1280]{1,0:T(8,128)(2,1)S(1)}, u32[]{:S(2)}, u32[]{:S(2)}) collective-permute-start(bf16[100,1280]{1,0:T(8,128)(2,1)S(1)} %get-tuple-element.98), channel_id=1, source_target_pairs={{0,1},{1,2},{2,3},{3,0},{4,5},{5,6},{6,7},{7,4},{8,9},{9,10},{10,1... | collective-permute-start | bytes 768008 | tf_op jit(solution)/shard_map/ppermute | solution.py:40
  127.0 23.4 %copy-start.1 = (bf16[4,80,1280]{2,1,0:T(8,128)(2,1)}, bf16[4,80,1280]{2,1,0:T(8,128)(2,1)S(1)}, u32[]{:S(2)}) copy-start(bf16[4,80,1280]{2,1,0:T(8,128)(2,1)S(1)} %pad_maximum_fusion.2.rest_0_) | copy-start | bytes 2457604
  127.0 23.4 %collective-permute-start.28 = (bf16[4,80,1280]{2,1,0:T(8,128)(2,1)S(1)}, bf16[4,80,1280]{2,1,0:T(8,128)(2,1)S(1)}, u32[]{:S(2)}, u32[]{:S(2)}) collective-permute-start(bf16[4,80,1280]{2,1,0:T(8,128)(2,1)S(1)} %pad_maximum_fusion.2.rest_0_), channel_id=1, source_target_pairs={{0,1},{1,2},{2,3},{3,0},{4,5},{5,6},{6,7},{7,4},{8,9},{9,10},{10,1... | collective-permute-start | bytes 2457608 | tf_op jit(solution)/shard_map/ppermute | solution.py:40
  127.3 23.2 %collective-permute-start.26 = (bf16[4,80,1280]{2,1,0:T(8,128)(2,1)S(1)}, bf16[4,80,1280]{2,1,0:T(8,128)(2,1)S(1)}, u32[]{:S(2)}, u32[]{:S(2)}) collective-permute-start(bf16[4,80,1280]{2,1,0:T(8,128)(2,1)S(1)} %pad_maximum_fusion.2.rest_0_), channel_id=1, source_target_pairs={{0,3},{1,0},{2,1},{3,2},{4,7},{5,4},{6,5},{7,6},{8,11},{9,8},{10,9... | collective-permute-start | bytes 2457608 | tf_op jit(solution)/shard_map/ppermute | solution.py:40
  137.1 19.7 %copy-start.2 = (bf16[4,80,1280]{2,1,0:T(8,128)(2,1)}, bf16[4,80,1280]{2,1,0:T(8,128)(2,1)S(1)}, u32[]{:S(2)}) copy-start(bf16[4,80,1280]{2,1,0:T(8,128)(2,1)S(1)} %pad_maximum_fusion.3.rest_3_) | copy-start | bytes 2457604
  137.1 16.8 %collective-permute-start.35 = (bf16[4,80,1280]{2,1,0:T(8,128)(2,1)S(1)}, bf16[4,80,1280]{2,1,0:T(8,128)(2,1)S(1)}, u32[]{:S(2)}, u32[]{:S(2)}) collective-permute-start(bf16[4,80,1280]{2,1,0:T(8,128)(2,1)S(1)} %pad_maximum_fusion.3.rest_3_), channel_id=1, source_target_pairs={{0,4},{1,5},{2,6},{3,7},{4,8},{5,9},{6,10},{7,11},{8,12},{9,13},{1... | collective-permute-start | bytes 2457608 | tf_op jit(solution)/shard_map/ppermute | solution.py:40
  138.4 17.5 %collective-permute-start.33 = (bf16[4,80,1280]{2,1,0:T(8,128)(2,1)S(1)}, bf16[4,80,1280]{2,1,0:T(8,128)(2,1)S(1)}, u32[]{:S(2)}, u32[]{:S(2)}) collective-permute-start(bf16[4,80,1280]{2,1,0:T(8,128)(2,1)S(1)} %pad_maximum_fusion.3.rest_3_), channel_id=1, source_target_pairs={{0,12},{1,13},{2,14},{3,15},{4,0},{5,1},{6,2},{7,3},{8,4},{9,5},{1... | collective-permute-start | bytes 2457608 | tf_op jit(solution)/shard_map/ppermute | solution.py:40
  150.4 8.4 %copy-start.3 = (bf16[4,80,1280]{2,1,0:T(8,128)(2,1)}, bf16[4,80,1280]{2,1,0:T(8,128)(2,1)S(1)}, u32[]{:S(2)}) copy-start(bf16[4,80,1280]{2,1,0:T(8,128)(2,1)S(1)} %collective-permute-done.28.rest_2_) | copy-start | bytes 2457604
  150.5 16.8 %collective-permute-start.29 = (bf16[2,80,1280]{2,1,0:T(8,128)(2,1)S(1)}, bf16[2,80,1280]{2,1,0:T(8,128)(2,1)}, u32[]{:S(2)}, u32[]{:S(2)}) collective-permute-start(bf16[2,80,1280]{2,1,0:T(8,128)(2,1)S(1)} %slice.150), channel_id=1, source_target_pairs={{0,1},{1,2},{2,3},{3,0},{4,5},{5,6},{6,7},{7,4},{8,9},{9,10},{10,1... | collective-permute-start | bytes 1228808 | tf_op jit(solution)/shard_map/ppermute | solution.py:40
  150.5 9.1 %copy-start.4 = (bf16[4,80,1280]{2,1,0:T(8,128)(2,1)}, bf16[4,80,1280]{2,1,0:T(8,128)(2,1)S(1)}, u32[]{:S(2)}) copy-start(bf16[4,80,1280]{2,1,0:T(8,128)(2,1)S(1)} %collective-permute-done.26.rest_1_) | copy-start | bytes 2457604
  150.6 16.7 %collective-permute-start.27 = (bf16[2,80,1280]{2,1,0:T(8,128)(2,1)S(1)}, bf16[2,80,1280]{2,1,0:T(8,128)(2,1)}, u32[]{:S(2)}, u32[]{:S(2)}) collective-permute-start(bf16[2,80,1280]{2,1,0:T(8,128)(2,1)S(1)} %slice.149), channel_id=1, source_target_pairs={{0,3},{1,0},{2,1},{3,2},{4,7},{5,4},{6,5},{7,6},{8,11},{9,8},{10,9... | collective-permute-start | bytes 1228808 | tf_op jit(solution)/shard_map/ppermute | solution.py:40
  153.9 8.2 %copy-start.5 = (bf16[4,80,1280]{2,1,0:T(8,128)(2,1)}, bf16[4,80,1280]{2,1,0:T(8,128)(2,1)S(1)}, u32[]{:S(2)}) copy-start(bf16[4,80,1280]{2,1,0:T(8,128)(2,1)S(1)} %collective-permute-done.35.rest_5_) | copy-start | bytes 2457604
  154.7 12.6 %collective-permute-start.36 = (bf16[2,80,1280]{2,1,0:T(8,128)(2,1)}, bf16[2,80,1280]{2,1,0:T(8,128)(2,1)}, u32[]{:S(2)}, u32[]{:S(2)}) collective-permute-start(bf16[2,80,1280]{2,1,0:T(8,128)(2,1)} %slice.157), channel_id=1, source_target_pairs={{0,4},{1,5},{2,6},{3,7},{4,8},{5,9},{6,10},{7,11},{8,12},{9,13},{1... | collective-permute-start | bytes 1228808 | tf_op jit(solution)/shard_map/ppermute | solution.py:40
  155.9 6.2 %copy-start.6 = (bf16[4,80,1280]{2,1,0:T(8,128)(2,1)}, bf16[4,80,1280]{2,1,0:T(8,128)(2,1)S(1)}, u32[]{:S(2)}) copy-start(bf16[4,80,1280]{2,1,0:T(8,128)(2,1)S(1)} %collective-permute-done.33.rest_4_) | copy-start | bytes 2457604
  156.7 10.5 %collective-permute-start.34 = (bf16[2,80,1280]{2,1,0:T(8,128)(2,1)}, bf16[2,80,1280]{2,1,0:T(8,128)(2,1)}, u32[]{:S(2)}, u32[]{:S(2)}) collective-permute-start(bf16[2,80,1280]{2,1,0:T(8,128)(2,1)} %slice.156), channel_id=1, source_target_pairs={{0,12},{1,13},{2,14},{3,15},{4,0},{5,1},{6,2},{7,3},{8,4},{9,5},{1... | collective-permute-start | bytes 1228808 | tf_op jit(solution)/shard_map/ppermute | solution.py:40

commit v6 on v5

--- a/solution.py
+++ b/solution.py
@@ -404,11 +404,12 @@
     there = jnp.stack([opposite] + there_got)
     here_1, here_3 = move(here, "x", -1), move(here, "x", 1)
     there_1, there_3 = move(there, "y", -1), move(there, "y", 1)
+    new_master, new_momentum = outer_rows(at, master, momentum, means)
+    here_1, new_master, new_momentum = lax.optimization_barrier((here_1, new_master, new_momentum))
     last = [
         move(here_1[:2], "x", -1), move(here_3[2:], "x", 1),
         move(there_1[:2], "y", -1), move(there_3[2:], "y", 1),
     ]
-    new_master, new_momentum = outer_rows(at, master, momentum, means)
     rows, width = drift.shape[1], drift.shape[2]
     so_far = place(
         "place_first",

time: 171 us -> 170 us (level)
  waiting for transfers between devices: 69.1 us -> 66.5 us
    ppermute x30, waiting for transfers between devices: 52.8 us -> 50.2 us  [move(): return lax.ppermute(value, 'worker', pairs)]
  transfers between devices with their start and end apart: 38 -> 38, of which waited for: 20 -> 21; matrix products, arithmetic and copies ran while one was open for 7% -> 8% of each run, Pallas kernels for 9% -> 9%
where the time goes in v6:
time: 170 us; the launch traced here: 169 us
  waiting for transfers between devices  66.5 us (39%)
  starting transfers between devices  56.3 us (33%)
  Pallas kernels  29.9 us (18%)
  other arithmetic  8.06 us (5%)
  local copies, waits for them, and re-layouts  6.4 us (4%)
  between operations  1.93 us (1%)
    ppermute x30, waiting for transfers between devices, move(): return lax.ppermute(value, 'worker', pairs)  50.2 us
    ppermute x30, starting transfers between devices, move(): return lax.ppermute(value, 'worker', pairs)  49 us
    pallas_call x1, Pallas kernels, pseudo_gradient(): pl.pallas_call(functools.partial(pseudo_body, outputs), out_shape=tuple((...  9.64 us
    ppermute x7, waiting for transfers between devices, swap_tp(): return lax.ppermute(value, 'tp', [(t, t ^ bit) for t in range(4)])  9.58 us
    pallas_call x2, Pallas kernels, place(): pl.pallas_call(functools.partial(place_body, where), out_shape=jax.ShapeD...  8.15 us
    all_to_all x1, waiting for transfers between devices, per_device(): base_tile = lax.all_to_all(base, 'worker', 0, 0, axis_index_groups=rings)  6.8 us
    pallas_call x1, Pallas kernels, attention(): pl.pallas_call(attention_body, out_shape=(jax.ShapeDtypeStruct((width, to...  4.93 us
    all_to_all x1, starting transfers between devices, per_device(): base_tile = lax.all_to_all(base, 'worker', 0, 0, axis_index_groups=rings)  4.3 us
  transfers between devices with their start and end apart: 38, of which 21 were waited for; matrix products, arithmetic and copies ran while one was open for 8% of the time, Pallas kernels for 9%

profile of v6, /device:TPU:32, one launch (start us, length us, event | category | flops | bytes accessed | tf_op | source)
XLA Modules:
  0.0 169.2 jit_solution(9395265450510679289)
XLA Ops:
  0.6 2.7 %cotangent_gram.1 = f32[6,128,128]{2,1,0:T(8,128)} custom-call(bf16[384,1280]{1,0:T(8,128)(2,1)} %g0_ref.1), custom_call_target="tpu_custom_call" | custom-call | tf_op jit(solution)/shard_map/cotangent_gram/pallas_call | solution.py:59
  3.4 1.3 reshape.27.seg_row_ref
  4.7 4.9 %attention.1 = (bf16[640,384]{1,0:T(8,128)(2,1)}, f32[6,128,128]{2,1,0:T(8,128)}) custom-call(bf16[384,640]{1,0:T(8,128)(2,1)} %q_ref, bf16[384,640]{1,0:T(8,128)(2,1)} %k_ref.1, bf16[384,640]{1,0:T(8,128)(2,1)} %v_ref.1, s32[1,384]{1,0:T(1,128)} %reshape.27.seg_row_ref), custom_call_target="tpu_custom_call" | custom-call | tf_op jit(solution)/shard_map/attention/pallas_call | solution.py:102
  9.6 0.6 pad_add_fusion.at_ref
  10.2 2.0 %collective-permute-start = (bf16[384,1280]{1,0:T(8,128)(2,1)S(1)}, bf16[384,1280]{1,0:T(8,128)(2,1)S(1)}, u32[]{:S(2)}, u32[]{:S(2)}) collective-permute-start(bf16[384,1280]{1,0:T(8,128)(2,1)S(1)} %copy-done), channel_id=1, source_target_pairs={{0,64},{32,96},{64,0},{96,32},{1,65},{33,97},{65,1},{97,33},{2,66}... | collective-permute-start | bytes 2949128 | tf_op jit(solution)/shard_map/ppermute | solution.py:44
  12.2 3.4 %collective-permute-done.1 = f32[6,128,128]{2,1,0:T(8,128)S(1)} collective-permute-done((f32[6,128,128]{2,1,0:T(8,128)}, f32[6,128,128]{2,1,0:T(8,128)S(1)}, u32[]{:S(2)}, u32[]{:S(2)}) %collective-permute-start.1) | collective-permute-done | bytes 393248 | tf_op jit(solution)/shard_map/ppermute | solution.py:44
  15.7 2.1 %base_rows.1 = f32[4,20,1280]{2,1,0:T(8,128)} custom-call(s32[4]{0:T(128)} %pad_add_fusion.at_ref, f32[20,5120]{1,0:T(8,128)} %master_ref.3, f32[20,5120]{1,0:T(8,128)} %momentum_ref.3), custom_call_target="tpu_custom_call" | custom-call | tf_op jit(solution)/shard_map/base_rows/pallas_call | solution.py:232
  17.8 4.3 %all-to-all-start = ((f32[4,20,1280]{2,1,0:T(8,128)}), f32[4,20,1280]{2,1,0:T(8,128)S(1)}, u32[]{:S(2)}, u32[]{:S(2)}) async-start(f32[4,20,1280]{2,1,0:T(8,128)} %base_rows.1), calls=%async_computation | async-start | bytes 983040 | tf_op jit(solution)/shard_map/all_to_all | solution.py:366
  22.1 1.7 %multiply_reduce_fusion = f32[]{:T(128)} fusion(f32[6,128,128]{2,1,0:T(8,128)S(1)} %copy-done.12, f32[6,128,128]{2,1,0:T(8,128)S(1)} %add.117, f32[6,128,128]{2,1,0:T(8,128)} %collective-permute-done.2), kind=kLoop, calls=%fused_computation.28 | loop fusion | flops 294911 | bytes 1179652 | tf_op jit(solution)/shard_map/reduce_sum | solution.py:370
  23.8 0.6 broadcast_in_dim.3
  24.7 0.3 collective-permute-start.5
  25.0 6.8 %all-to-all-done = f32[4,20,1280]{2,1,0:T(8,128)S(1)} async-done(((f32[4,20,1280]{2,1,0:T(8,128)}), f32[4,20,1280]{2,1,0:T(8,128)S(1)}, u32[]{:S(2)}, u32[]{:S(2)}) %all-to-all-start) | async-done | bytes 409632 | tf_op jit(solution)/shard_map/all_to_all | solution.py:366
  31.9 0.7 broadcast_add_fusion
  32.6 2.9 %collective-permute-done.g2_ref = bf16[384,1280]{1,0:T(8,128)(2,1)S(1)} collective-permute-done((bf16[384,1280]{1,0:T(8,128)(2,1)S(1)}, bf16[384,1280]{1,0:T(8,128)(2,1)S(1)}, u32[]{:S(2)}, u32[]{:S(2)}) %collective-permute-start) | collective-permute-done | bytes 983072 | tf_op jit(solution)/shard_map/ppermute | solution.py:44
  35.5 0.4 collective-permute-start.4
  35.8 3.3 %collective-permute-done.4 = f32[8,128]{1,0:T(8,128)S(1)} collective-permute-done((f32[8,128]{1,0:T(8,128)S(1)}, f32[8,128]{1,0:T(8,128)S(1)}, u32[]{:S(2)}, u32[]{:S(2)}) %collective-permute-start.4) | collective-permute-done | bytes 4128 | tf_op jit(solution)/shard_map/ppermute | solution.py:44
  39.1 0.5 slice.102
  40.3 9.6 %pseudo_gradient.1 = (bf16[4,80,1280]{2,1,0:T(8,128)(2,1)}, bf16[4,80,1280]{2,1,0:T(8,128)(2,1)}, bf16[4,80,1280]{2,1,0:T(8,128)(2,1)}, bf16[4,80,1280]{2,1,0:T(...) custom-call(s32[4]{0:T(128)} %pad_add_fusion.at_ref, ...), custom_call_target="tpu_custom_call" | custom-call | flops 2516582400 | bytes 18000000 | tf_op jit(solution)/shard_map/pseudo_gradient/pallas_call | solution.py:196
  50.0 2.8 %collective-permute-start.10 = (bf16[4,80,1280]{2,1,0:T(8,128)(2,1)}, bf16[4,80,1280]{2,1,0:T(8,128)(2,1)S(1)}, u32[]{:S(2)}, u32[]{:S(2)}) collective-permute-start(bf16[4,80,1280]{2,1,0:T(8,128)(2,1)} %get-tuple-element.63), channel_id=1, source_target_pairs={{0,3},{1,0},{2,1},{3,2},{4,7},{5,4},{6,5},{7,6},{8,11},{9,8},{10,9... | collective-permute-start | bytes 2457608 | tf_op jit(solution)/shard_map/ppermute | solution.py:40
  52.8 1.6 collective-permute-start.7
  54.4 1.7 collective-permute-start.8
  56.1 14.1 %collective-permute-done.10 = bf16[4,80,1280]{2,1,0:T(8,128)(2,1)S(1)} collective-permute-done((bf16[4,80,1280]{2,1,0:T(8,128)(2,1)}, bf16[4,80,1280]{2,1,0:T(8,128)(2,1)S(1)}, u32[]{:S(2)}, u32[]{:S(2)}) %collective-permute-start.10) | collective-permute-done | bytes 819232 | tf_op jit(solution)/shard_map/ppermute | solution.py:40
  70.2 1.2 add_convert_fusion
  71.3 3.7 %collective-permute-start.13 = (bf16[2,80,1280]{2,1,0:T(8,128)(2,1)S(1)}, bf16[2,80,1280]{2,1,0:T(8,128)(2,1)S(1)}, u32[]{:S(2)}, u32[]{:S(2)}) collective-permute-start(bf16[2,80,1280]{2,1,0:T(8,128)(2,1)S(1)} %add_convert_fusion), channel_id=1, source_target_pairs={{0,3},{1,0},{2,1},{3,2},{4,7},{5,4},{6,5},{7,6},{8,11},{9,8},{10,9... | collective-permute-start | bytes 1228808 | tf_op jit(solution)/shard_map/ppermute | solution.py:40
  75.0 1.2 add_convert_fusion.1
  76.7 1.7 collective-permute-start.14
  78.4 1.7 collective-permute-start.15
  80.0 3.0 %collective-permute-start.9 = (f32[80,1280]{1,0:T(8,128)S(1)}, f32[80,1280]{1,0:T(8,128)S(1)}, u32[]{:S(2)}, u32[]{:S(2)}) collective-permute-start(f32[80,1280]{1,0:T(8,128)S(1)} %reshape.28), channel_id=1, source_target_pairs={{0,16},{1,17},{2,18},{3,19},{4,20},{5,21},{6,22},{7,23},{8,24},{9,... | collective-permute-start | bytes 1228808 | tf_op jit(solution)/shard_map/ppermute | solution.py:40
  83.0 4.2 %collective-permute-done.12 = bf16[2,80,1280]{2,1,0:T(8,128)(2,1)S(1)} collective-permute-done((bf16[2,80,1280]{2,1,0:T(8,128)(2,1)S(1)}, bf16[2,80,1280]{2,1,0:T(8,128)(2,1)S(1)}, u32[]{:S(2)}, u32[]{:S(2)}) %collective-permute-start.12) | collective-permute-done | bytes 409632 | tf_op jit(solution)/shard_map/ppermute | solution.py:40
  87.6 0.7 copy-done.7
  89.0 1.7 collective-permute-start.16
  90.6 1.7 collective-permute-start.18
  92.3 2.0 %collective-permute-start.17 = (bf16[80,1280]{1,0:T(8,128)(2,1)S(1)}, bf16[80,1280]{1,0:T(8,128)(2,1)S(1)}, u32[]{:S(2)}, u32[]{:S(2)}) collective-permute-start(bf16[80,1280]{1,0:T(8,128)(2,1)S(1)} %get-tuple-element.90), channel_id=1, source_target_pairs={{0,8},{1,9},{2,10},{3,11},{4,12},{5,13},{6,14},{7,15},{8,0},{9,1},... | collective-permute-start | bytes 614408 | tf_op jit(solution)/shard_map/ppermute | solution.py:40
  94.5 3.4 %collective-permute-done.16 = bf16[80,1280]{1,0:T(8,128)(2,1)S(1)} collective-permute-done((bf16[80,1280]{1,0:T(8,128)(2,1)S(1)}, bf16[80,1280]{1,0:T(8,128)(2,1)S(1)}, u32[]{:S(2)}, u32[]{:S(2)}) %collective-permute-start.16) | collective-permute-done | bytes 204832 | tf_op jit(solution)/shard_map/ppermute | solution.py:40
  97.9 1.8 %collective-permute-start.21 = (bf16[80,1280]{1,0:T(8,128)(2,1)S(1)}, bf16[80,1280]{1,0:T(8,128)(2,1)S(1)}, u32[]{:S(2)}, u32[]{:S(2)}) collective-permute-start(bf16[80,1280]{1,0:T(8,128)(2,1)S(1)} %get-tuple-element.86), channel_id=1, source_target_pairs={{0,3},{1,0},{2,1},{3,2},{4,7},{5,4},{6,5},{7,6},{8,11},{9,8},{10,9... | collective-permute-start | bytes 614408 | tf_op jit(solution)/shard_map/ppermute | solution.py:40
  99.6 0.4 collective-permute-done.17
  100.2 2.0 %collective-permute-done.19 = bf16[80,1280]{1,0:T(8,128)(2,1)S(1)} collective-permute-done((bf16[80,1280]{1,0:T(8,128)(2,1)S(1)}, bf16[80,1280]{1,0:T(8,128)(2,1)S(1)}, u32[]{:S(2)}, u32[]{:S(2)}) %collective-permute-start.19) | collective-permute-done | bytes 204832 | tf_op jit(solution)/shard_map/ppermute | solution.py:40
  102.2 2.9 %collective-permute-done.21 = bf16[80,1280]{1,0:T(8,128)(2,1)S(1)} collective-permute-done((bf16[80,1280]{1,0:T(8,128)(2,1)S(1)}, bf16[80,1280]{1,0:T(8,128)(2,1)S(1)}, u32[]{:S(2)}, u32[]{:S(2)}) %collective-permute-start.21) | collective-permute-done | bytes 204832 | tf_op jit(solution)/shard_map/ppermute | solution.py:40
  105.1 1.8 %collective-permute-done.20 = bf16[80,1280]{1,0:T(8,128)(2,1)S(1)} collective-permute-done((bf16[80,1280]{1,0:T(8,128)(2,1)S(1)}, bf16[80,1280]{1,0:T(8,128)(2,1)S(1)}, u32[]{:S(2)}, u32[]{:S(2)}) %collective-permute-start.20) | collective-permute-done | bytes 204832 | tf_op jit(solution)/shard_map/ppermute | solution.py:40
  107.1 3.1 %collective-permute-start.22 = (bf16[2,80,1280]{2,1,0:T(8,128)(2,1)S(1)}, bf16[2,80,1280]{2,1,0:T(8,128)(2,1)S(1)}, u32[]{:S(2)}, u32[]{:S(2)}) collective-permute-start(bf16[2,80,1280]{2,1,0:T(8,128)(2,1)S(1)} %pad_maximum_fusion.5), channel_id=1, source_target_pairs={{0,16},{1,17},{2,18},{3,19},{4,20},{5,21},{6,22},{7,23},{8,24},{9,... | collective-permute-start | bytes 1228808 | tf_op jit(solution)/shard_map/ppermute | solution.py:40
  110.1 6.5 %collective-permute-done.22 = bf16[2,80,1280]{2,1,0:T(8,128)(2,1)S(1)} collective-permute-done((bf16[2,80,1280]{2,1,0:T(8,128)(2,1)S(1)}, bf16[2,80,1280]{2,1,0:T(8,128)(2,1)S(1)}, u32[]{:S(2)}, u32[]{:S(2)}) %collective-permute-start.22) | collective-permute-done | bytes 409632 | tf_op jit(solution)/shard_map/ppermute | solution.py:40
  116.9 3.7 %collective-permute-start.24 = (bf16[80,1280]{1,0:T(8,128)(2,1)S(1)}, bf16[80,1280]{1,0:T(8,128)(2,1)S(1)}, u32[]{:S(2)}, u32[]{:S(2)}) collective-permute-start(bf16[80,1280]{1,0:T(8,128)(2,1)S(1)} %get-tuple-element.96), channel_id=1, source_target_pairs={{0,8},{1,9},{2,10},{3,11},{4,12},{5,13},{6,14},{7,15},{8,0},{9,1},... | collective-permute-start | bytes 614408 | tf_op jit(solution)/shard_map/ppermute | solution.py:40
  120.8 2.2 %collective-permute-start.27 = (bf16[100,1280]{1,0:T(8,128)(2,1)S(1)}, bf16[100,1280]{1,0:T(8,128)(2,1)S(1)}, u32[]{:S(2)}, u32[]{:S(2)}) collective-permute-start(bf16[100,1280]{1,0:T(8,128)(2,1)S(1)} %get-tuple-element.102), channel_id=1, source_target_pairs={{0,3},{1,0},{2,1},{3,2},{4,7},{5,4},{6,5},{7,6},{8,11},{9,8},{10,9... | collective-permute-start | bytes 768008 | tf_op jit(solution)/shard_map/ppermute | solution.py:40
  123.0 0.7 collective-permute-start.28
  123.8 2.5 %collective-permute-start.29 = (bf16[100,1280]{1,0:T(8,128)(2,1)S(1)}, bf16[100,1280]{1,0:T(8,128)(2,1)S(1)}, u32[]{:S(2)}, u32[]{:S(2)}) collective-permute-start(bf16[100,1280]{1,0:T(8,128)(2,1)S(1)} %get-tuple-element.104), channel_id=1, source_target_pairs={{0,1},{1,2},{2,3},{3,0},{4,5},{5,6},{6,7},{7,4},{8,9},{9,10},{10,1... | collective-permute-start | bytes 768008 | tf_op jit(solution)/shard_map/ppermute | solution.py:40
  126.5 0.4 collective-permute-done.23
  127.0 0.3 collective-permute-start.31
  127.3 3.0 %collective-permute-start.26 = (bf16[4,80,1280]{2,1,0:T(8,128)(2,1)S(1)}, bf16[4,80,1280]{2,1,0:T(8,128)(2,1)S(1)}, u32[]{:S(2)}, u32[]{:S(2)}) collective-permute-start(bf16[4,80,1280]{2,1,0:T(8,128)(2,1)S(1)} %pad_maximum_fusion.2.rest_0_), channel_id=1, source_target_pairs={{0,3},{1,0},{2,1},{3,2},{4,7},{5,4},{6,5},{7,6},{8,11},{9,8},{10,9... | collective-permute-start | bytes 2457608 | tf_op jit(solution)/shard_map/ppermute | solution.py:40
  130.4 3.4 %collective-permute-done.28 = bf16[100,1280]{1,0:T(8,128)(2,1)S(1)} collective-permute-done((bf16[100,1280]{1,0:T(8,128)(2,1)S(1)}, bf16[100,1280]{1,0:T(8,128)(2,1)S(1)}, u32[]{:S(2)}, u32[]{:S(2)}) %collective-permute-start.28) | collective-permute-done | bytes 256032 | tf_op jit(solution)/shard_map/ppermute | solution.py:40
  133.8 3.2 %collective-permute-done.29 = bf16[100,1280]{1,0:T(8,128)(2,1)S(1)} collective-permute-done((bf16[100,1280]{1,0:T(8,128)(2,1)S(1)}, bf16[100,1280]{1,0:T(8,128)(2,1)S(1)}, u32[]{:S(2)}, u32[]{:S(2)}) %collective-permute-start.29) | collective-permute-done | bytes 256032 | tf_op jit(solution)/shard_map/ppermute | solution.py:40
  137.1 1.3 collective-permute-start.35
  138.4 2.0 %collective-permute-start.33 = (bf16[4,80,1280]{2,1,0:T(8,128)(2,1)S(1)}, bf16[4,80,1280]{2,1,0:T(8,128)(2,1)}, u32[]{:S(2)}, u32[]{:S(2)}) collective-permute-start(bf16[4,80,1280]{2,1,0:T(8,128)(2,1)S(1)} %pad_maximum_fusion.3.rest_3_), channel_id=1, source_target_pairs={{0,12},{1,13},{2,14},{3,15},{4,0},{5,1},{6,2},{7,3},{8,4},{9,5},{1... | collective-permute-start | bytes 2457608 | tf_op jit(solution)/shard_map/ppermute | solution.py:40
  140.5 0.8 pad_maximum_fusion.4.mean_ref
  141.3 2.4 %outer_rows.1 = (f32[20,5120]{1,0:T(8,128)}, f32[20,5120]{1,0:T(8,128)}) custom-call(s32[4]{0:T(128)} %pad_add_fusion.at_ref, f32[20,5120]{1,0:T(8,128)} %master_ref.3, f32[20,5120]{1,0:T(8,128)} %momentum_ref.3, f32[4,20,1280]{2,1,0:T(8,128)} %pad_maximum_fusion.4.mean_ref), custom_call_target="tpu_custom_call" | custom-call | tf_op jit(solution)/shard_map/outer_rows/pallas_call | solution.py:255
  143.7 6.6 %collective-permute-done.31.rest_2_ = bf16[4,80,1280]{2,1,0:T(8,128)(2,1)S(1)} collective-permute-done((bf16[4,80,1280]{2,1,0:T(8,128)(2,1)S(1)}, bf16[4,80,1280]{2,1,0:T(8,128)(2,1)S(1)}, u32[]{:S(2)}, u32[]{:S(2)}) %collective-permute-start.31) | collective-permute-done | bytes 819232 | tf_op jit(solution)/shard_map/ppermute | solution.py:40
  150.5 3.3 %collective-permute-start.30 = (bf16[2,80,1280]{2,1,0:T(8,128)(2,1)S(1)}, bf16[2,80,1280]{2,1,0:T(8,128)(2,1)}, u32[]{:S(2)}, u32[]{:S(2)}) collective-permute-start(bf16[2,80,1280]{2,1,0:T(8,128)(2,1)S(1)} %slice.129), channel_id=1, source_target_pairs={{0,3},{1,0},{2,1},{3,2},{4,7},{5,4},{6,5},{7,6},{8,11},{9,8},{10,9... | collective-permute-start | bytes 1228808 | tf_op jit(solution)/shard_map/ppermute | solution.py:40
  153.8 1.0 slice.159
  154.8 1.4 collective-permute-start.36
  156.2 1.0 slice.158
  157.2 2.0 %collective-permute-start.34 = (bf16[2,80,1280]{2,1,0:T(8,128)(2,1)S(1)}, bf16[2,80,1280]{2,1,0:T(8,128)(2,1)S(1)}, u32[]{:S(2)}, u32[]{:S(2)}) collective-permute-start(bf16[2,80,1280]{2,1,0:T(8,128)(2,1)S(1)} %slice.158), channel_id=1, source_target_pairs={{0,12},{1,13},{2,14},{3,15},{4,0},{5,1},{6,2},{7,3},{8,4},{9,5},{1... | collective-permute-start | bytes 1228808 | tf_op jit(solution)/shard_map/ppermute | solution.py:40
  159.2 5.2 %place_first.1.rest_4_ = bf16[640,5120]{1,0:T(8,128)(2,1)} custom-call(s32[4]{0:T(128)} %pad_add_fusion.at_ref, bf16[4,80,1280]{2,1,0:T(8,128)(2,1)} %copy-done.1, bf16[4,80,1280]{2,1,0:T(8,128)(2,1)} %copy-done.4, bf16[4,80,1280]{2,1,0:T(8,128)(2,1)} %copy-done.3, bf16[4,80,1280]{2,1,0:T(8,128)(2,1)} %copy-done.2, ...), custom_call_target="tpu_custom_call" | custom-call | bytes 9830400 | tf_op jit(solution)/shard_map/place_first/pallas_call | solution.py:295
  164.4 0.8 collective-permute-done.34.rest_2_
  165.3 0.8 copy-done.11
  166.0 3.0 %place_last.1 = bf16[640,5120]{1,0:T(8,128)(2,1)} custom-call(s32[4]{0:T(128)} %pad_add_fusion.at_ref, bf16[2,80,1280]{2,1,0:T(8,128)(2,1)} %collective-permute-done.30.rest_0_, bf16[2,80,1280]{2,1,0:T(8,128)(2,1)} %collective-permute-done.32.rest_1_, bf16[2,80,1280]{2,1,0:T(8,128)(2,1)} %copy-done.11, ...), custom_call_target="tpu_custom_call", output_to_operand_aliasing={{}: (5, {})} | custom-call | bytes 3276800 | tf_op jit(solution)/shard_map/place_last/pallas_call | solution.py:295
  (87 shorter events, 3.8 us)
Async XLA Ops:
  0.6 9.6 %copy-start = (bf16[384,1280]{1,0:T(8,128)(2,1)S(1)}, bf16[384,1280]{1,0:T(8,128)(2,1)}, u32[]{:S(2)}) copy-start(bf16[384,1280]{1,0:T(8,128)(2,1)} %g0_ref.1) | copy-start | bytes 2949124
  3.3 12.2 %copy-start.5 = (f32[6,128,128]{2,1,0:T(8,128)S(1)}, f32[6,128,128]{2,1,0:T(8,128)}, u32[]{:S(2)}) copy-start(f32[6,128,128]{2,1,0:T(8,128)} %cotangent_gram.1) | copy-start | bytes 1179652
  3.3 12.2 %collective-permute-start.1 = (f32[6,128,128]{2,1,0:T(8,128)}, f32[6,128,128]{2,1,0:T(8,128)S(1)}, u32[]{:S(2)}, u32[]{:S(2)}) collective-permute-start(f32[6,128,128]{2,1,0:T(8,128)} %cotangent_gram.1), channel_id=1, source_target_pairs={{0,64},{32,96},{64,0},{96,32},{1,65},{33,97},{65,1},{97,33},{2,66}... | collective-permute-start | bytes 1179656 | tf_op jit(solution)/shard_map/ppermute | solution.py:44
  10.2 25.3 %collective-permute-start = (bf16[384,1280]{1,0:T(8,128)(2,1)S(1)}, bf16[384,1280]{1,0:T(8,128)(2,1)S(1)}, u32[]{:S(2)}, u32[]{:S(2)}) collective-permute-start(bf16[384,1280]{1,0:T(8,128)(2,1)S(1)} %copy-done), channel_id=1, source_target_pairs={{0,64},{32,96},{64,0},{96,32},{1,65},{33,97},{65,1},{97,33},{2,66}... | collective-permute-start | bytes 2949128 | tf_op jit(solution)/shard_map/ppermute | solution.py:44
  15.6 6.5 %copy-start.12 = (f32[6,128,128]{2,1,0:T(8,128)S(1)}, f32[6,128,128]{2,1,0:T(8,128)}, u32[]{:S(2)}) copy-start(f32[6,128,128]{2,1,0:T(8,128)} %get-tuple-element.48) | copy-start | bytes 1179652
  15.6 6.5 %collective-permute-start.2 = (f32[6,128,128]{2,1,0:T(8,128)S(1)}, f32[6,128,128]{2,1,0:T(8,128)}, u32[]{:S(2)}, u32[]{:S(2)}) collective-permute-start(f32[6,128,128]{2,1,0:T(8,128)S(1)} %add.117), channel_id=1, source_target_pairs={{0,32},{32,0},{64,96},{96,64},{1,33},{33,1},{65,97},{97,65},{2,34}... | collective-permute-start | bytes 1179656 | tf_op jit(solution)/shard_map/ppermute | solution.py:44
  17.8 14.1 %all-to-all-start = ((f32[4,20,1280]{2,1,0:T(8,128)}), f32[4,20,1280]{2,1,0:T(8,128)S(1)}, u32[]{:S(2)}, u32[]{:S(2)}) async-start(f32[4,20,1280]{2,1,0:T(8,128)} %base_rows.1), calls=%async_computation | async-start | bytes 983040 | tf_op jit(solution)/shard_map/all_to_all | solution.py:366
  24.4 7.4 %collective-permute-start.3 = (f32[8,128]{1,0:T(8,128)S(1)}, f32[8,128]{1,0:T(8,128)S(1)}, u32[]{:S(2)}, u32[]{:S(2)}) collective-permute-start(f32[8,128]{1,0:T(8,128)S(1)} %broadcast_in_dim.3), channel_id=1, source_target_pairs={{0,32},{32,0},{64,96},{96,64},{1,33},{33,1},{65,97},{97,65},{2,34}... | collective-permute-start | bytes 12296 | tf_op jit(solution)/shard_map/ppermute | solution.py:44
  24.7 15.6 %collective-permute-start.5 = (bf16[384,1280]{1,0:T(8,128)(2,1)S(1)}, bf16[384,1280]{1,0:T(8,128)(2,1)}, u32[]{:S(2)}, u32[]{:S(2)}) collective-permute-start(bf16[384,1280]{1,0:T(8,128)(2,1)S(1)} %copy-done), channel_id=1, source_target_pairs={{0,32},{32,0},{64,96},{96,64},{1,33},{33,1},{65,97},{97,65},{2,34}... | collective-permute-start | bytes 2949128 | tf_op jit(solution)/shard_map/ppermute | solution.py:44
  35.5 4.8 %copy-start.6 = (bf16[384,1280]{1,0:T(8,128)(2,1)}, bf16[384,1280]{1,0:T(8,128)(2,1)S(1)}, u32[]{:S(2)}) copy-start(bf16[384,1280]{1,0:T(8,128)(2,1)S(1)} %collective-permute-done.g2_ref) | copy-start | bytes 2949124
  35.5 4.8 %collective-permute-start.6 = (bf16[384,1280]{1,0:T(8,128)(2,1)S(1)}, bf16[384,1280]{1,0:T(8,128)(2,1)}, u32[]{:S(2)}, u32[]{:S(2)}) collective-permute-start(bf16[384,1280]{1,0:T(8,128)(2,1)S(1)} %collective-permute-done.g2_ref), channel_id=1, source_target_pairs={{0,32},{32,0},{64,96},{96,64},{1,33},{33,1},{65,97},{97,65},{2,34}... | collective-permute-start | bytes 2949128 | tf_op jit(solution)/shard_map/ppermute | solution.py:44
  35.5 3.6 %collective-permute-start.4 = (f32[8,128]{1,0:T(8,128)S(1)}, f32[8,128]{1,0:T(8,128)S(1)}, u32[]{:S(2)}, u32[]{:S(2)}) collective-permute-start(f32[8,128]{1,0:T(8,128)S(1)} %broadcast_add_fusion), channel_id=1, source_target_pairs={{0,64},{32,96},{64,0},{96,32},{1,65},{33,97},{65,1},{97,33},{2,66}... | collective-permute-start | bytes 12296 | tf_op jit(solution)/shard_map/ppermute | solution.py:44
  50.0 26.5 %copy-start.10 = (bf16[2,80,1280]{2,1,0:T(8,128)(2,1)S(1)}, bf16[2,80,1280]{2,1,0:T(8,128)(2,1)}, u32[]{:S(2)}) copy-start(bf16[2,80,1280]{2,1,0:T(8,128)(2,1)} %get-tuple-element.58) | copy-start | bytes 1228804
  50.0 20.2 %collective-permute-start.10 = (bf16[4,80,1280]{2,1,0:T(8,128)(2,1)}, bf16[4,80,1280]{2,1,0:T(8,128)(2,1)S(1)}, u32[]{:S(2)}, u32[]{:S(2)}) collective-permute-start(bf16[4,80,1280]{2,1,0:T(8,128)(2,1)} %get-tuple-element.63), channel_id=1, source_target_pairs={{0,3},{1,0},{2,1},{3,2},{4,7},{5,4},{6,5},{7,6},{8,11},{9,8},{10,9... | collective-permute-start | bytes 2457608 | tf_op jit(solution)/shard_map/ppermute | solution.py:40
  52.8 22.2 %collective-permute-start.11 = (bf16[4,80,1280]{2,1,0:T(8,128)(2,1)}, bf16[4,80,1280]{2,1,0:T(8,128)(2,1)S(1)}, u32[]{:S(2)}, u32[]{:S(2)}) collective-permute-start(bf16[4,80,1280]{2,1,0:T(8,128)(2,1)} %get-tuple-element.65), channel_id=1, source_target_pairs={{0,1},{1,2},{2,3},{3,0},{4,5},{5,6},{6,7},{7,4},{8,9},{9,10},{10,1... | collective-permute-start | bytes 2457608 | tf_op jit(solution)/shard_map/ppermute | solution.py:40
  52.8 23.6 %collective-permute-start.7 = (bf16[4,80,1280]{2,1,0:T(8,128)(2,1)}, bf16[4,80,1280]{2,1,0:T(8,128)(2,1)S(1)}, u32[]{:S(2)}, u32[]{:S(2)}) collective-permute-start(bf16[4,80,1280]{2,1,0:T(8,128)(2,1)} %get-tuple-element.56), channel_id=1, source_target_pairs={{0,4},{1,5},{2,6},{3,7},{4,8},{5,9},{6,10},{7,11},{8,12},{9,13},{1... | collective-permute-start | bytes 2457608 | tf_op jit(solution)/shard_map/ppermute | solution.py:40
  54.4 22.2 %collective-permute-start.8 = (bf16[4,80,1280]{2,1,0:T(8,128)(2,1)}, bf16[4,80,1280]{2,1,0:T(8,128)(2,1)S(1)}, u32[]{:S(2)}, u32[]{:S(2)}) collective-permute-start(bf16[4,80,1280]{2,1,0:T(8,128)(2,1)} %get-tuple-element.57), channel_id=1, source_target_pairs={{0,12},{1,13},{2,14},{3,15},{4,0},{5,1},{6,2},{7,3},{8,4},{9,5},{1... | collective-permute-start | bytes 2457608 | tf_op jit(solution)/shard_map/ppermute | solution.py:40
  70.2 6.4 %copy-start.9 = (bf16[2,80,1280]{2,1,0:T(8,128)(2,1)S(1)}, bf16[2,80,1280]{2,1,0:T(8,128)(2,1)}, u32[]{:S(2)}) copy-start(bf16[2,80,1280]{2,1,0:T(8,128)(2,1)} %get-tuple-element.59) | copy-start | bytes 1228804
  71.3 11.7 %collective-permute-start.13 = (bf16[2,80,1280]{2,1,0:T(8,128)(2,1)S(1)}, bf16[2,80,1280]{2,1,0:T(8,128)(2,1)S(1)}, u32[]{:S(2)}, u32[]{:S(2)}) collective-permute-start(bf16[2,80,1280]{2,1,0:T(8,128)(2,1)S(1)} %add_convert_fusion), channel_id=1, source_target_pairs={{0,3},{1,0},{2,1},{3,2},{4,7},{5,4},{6,5},{7,6},{8,11},{9,8},{10,9... | collective-permute-start | bytes 1228808 | tf_op jit(solution)/shard_map/ppermute | solution.py:40
  75.0 12.2 %copy-start.8 = (bf16[4,80,1280]{2,1,0:T(8,128)(2,1)S(1)}, bf16[4,80,1280]{2,1,0:T(8,128)(2,1)}, u32[]{:S(2)}) copy-start(bf16[4,80,1280]{2,1,0:T(8,128)(2,1)} %get-tuple-element.62) | copy-start | bytes 2457604
  76.2 11.0 %collective-permute-start.12 = (bf16[2,80,1280]{2,1,0:T(8,128)(2,1)S(1)}, bf16[2,80,1280]{2,1,0:T(8,128)(2,1)S(1)}, u32[]{:S(2)}, u32[]{:S(2)}) collective-permute-start(bf16[2,80,1280]{2,1,0:T(8,128)(2,1)S(1)} %add_convert_fusion.1), channel_id=1, source_target_pairs={{0,1},{1,2},{2,3},{3,0},{4,5},{5,6},{6,7},{7,4},{8,9},{9,10},{10,1... | collective-permute-start | bytes 1228808 | tf_op jit(solution)/shard_map/ppermute | solution.py:40
  76.7 10.8 %collective-permute-start.14 = (bf16[2,80,1280]{2,1,0:T(8,128)(2,1)S(1)}, bf16[2,80,1280]{2,1,0:T(8,128)(2,1)S(1)}, u32[]{:S(2)}, u32[]{:S(2)}) collective-permute-start(bf16[2,80,1280]{2,1,0:T(8,128)(2,1)S(1)} %add_convert_fusion.3), channel_id=1, source_target_pairs={{0,4},{1,5},{2,6},{3,7},{4,8},{5,9},{6,10},{7,11},{8,12},{9,13},{1... | collective-permute-start | bytes 1228808 | tf_op jit(solution)/shard_map/ppermute | solution.py:40
  78.4 9.2 %collective-permute-start.15 = (bf16[2,80,1280]{2,1,0:T(8,128)(2,1)S(1)}, bf16[2,80,1280]{2,1,0:T(8,128)(2,1)S(1)}, u32[]{:S(2)}, u32[]{:S(2)}) collective-permute-start(bf16[2,80,1280]{2,1,0:T(8,128)(2,1)S(1)} %add_convert_fusion.2), channel_id=1, source_target_pairs={{0,12},{1,13},{2,14},{3,15},{4,0},{5,1},{6,2},{7,3},{8,4},{9,5},{1... | collective-permute-start | bytes 1228808 | tf_op jit(solution)/shard_map/ppermute | solution.py:40
  80.0 30.1 %collective-permute-start.9 = (f32[80,1280]{1,0:T(8,128)S(1)}, f32[80,1280]{1,0:T(8,128)S(1)}, u32[]{:S(2)}, u32[]{:S(2)}) collective-permute-start(f32[80,1280]{1,0:T(8,128)S(1)} %reshape.28), channel_id=1, source_target_pairs={{0,16},{1,17},{2,18},{3,19},{4,20},{5,21},{6,22},{7,23},{8,24},{9,... | collective-permute-start | bytes 1228808 | tf_op jit(solution)/shard_map/ppermute | solution.py:40
  87.2 1.1 copy-start.7
  89.0 8.9 %collective-permute-start.16 = (bf16[80,1280]{1,0:T(8,128)(2,1)S(1)}, bf16[80,1280]{1,0:T(8,128)(2,1)S(1)}, u32[]{:S(2)}, u32[]{:S(2)}) collective-permute-start(bf16[80,1280]{1,0:T(8,128)(2,1)S(1)} %get-tuple-element.88), channel_id=1, source_target_pairs={{0,4},{1,5},{2,6},{3,7},{4,8},{5,9},{6,10},{7,11},{8,12},{9,13},{1... | collective-permute-start | bytes 614408 | tf_op jit(solution)/shard_map/ppermute | solution.py:40
  90.6 9.0 %collective-permute-start.18 = (bf16[80,1280]{1,0:T(8,128)(2,1)S(1)}, bf16[80,1280]{1,0:T(8,128)(2,1)S(1)}, u32[]{:S(2)}, u32[]{:S(2)}) collective-permute-start(bf16[80,1280]{1,0:T(8,128)(2,1)S(1)} %get-tuple-element.89), channel_id=1, source_target_pairs={{0,12},{1,13},{2,14},{3,15},{4,0},{5,1},{6,2},{7,3},{8,4},{9,5},{1... | collective-permute-start | bytes 614408 | tf_op jit(solution)/shard_map/ppermute | solution.py:40
  92.3 7.8 %collective-permute-start.17 = (bf16[80,1280]{1,0:T(8,128)(2,1)S(1)}, bf16[80,1280]{1,0:T(8,128)(2,1)S(1)}, u32[]{:S(2)}, u32[]{:S(2)}) collective-permute-start(bf16[80,1280]{1,0:T(8,128)(2,1)S(1)} %get-tuple-element.90), channel_id=1, source_target_pairs={{0,8},{1,9},{2,10},{3,11},{4,12},{5,13},{6,14},{7,15},{8,0},{9,1},... | collective-permute-start | bytes 614408 | tf_op jit(solution)/shard_map/ppermute | solution.py:40
  94.4 7.8 %collective-permute-start.19 = (bf16[80,1280]{1,0:T(8,128)(2,1)S(1)}, bf16[80,1280]{1,0:T(8,128)(2,1)S(1)}, u32[]{:S(2)}, u32[]{:S(2)}) collective-permute-start(bf16[80,1280]{1,0:T(8,128)(2,1)S(1)} %get-tuple-element.85), channel_id=1, source_target_pairs={{0,1},{1,2},{2,3},{3,0},{4,5},{5,6},{6,7},{7,4},{8,9},{9,10},{10,1... | collective-permute-start | bytes 614408 | tf_op jit(solution)/shard_map/ppermute | solution.py:40
  97.9 7.3 %collective-permute-start.21 = (bf16[80,1280]{1,0:T(8,128)(2,1)S(1)}, bf16[80,1280]{1,0:T(8,128)(2,1)S(1)}, u32[]{:S(2)}, u32[]{:S(2)}) collective-permute-start(bf16[80,1280]{1,0:T(8,128)(2,1)S(1)} %get-tuple-element.86), channel_id=1, source_target_pairs={{0,3},{1,0},{2,1},{3,2},{4,7},{5,4},{6,5},{7,6},{8,11},{9,8},{10,9... | collective-permute-start | bytes 614408 | tf_op jit(solution)/shard_map/ppermute | solution.py:40
  99.6 7.3 %collective-permute-start.20 = (bf16[80,1280]{1,0:T(8,128)(2,1)S(1)}, bf16[80,1280]{1,0:T(8,128)(2,1)S(1)}, u32[]{:S(2)}, u32[]{:S(2)}) collective-permute-start(bf16[80,1280]{1,0:T(8,128)(2,1)S(1)} %get-tuple-element.87), channel_id=1, source_target_pairs={{0,2},{1,3},{2,0},{3,1},{4,6},{5,7},{6,4},{7,5},{8,10},{9,11},{10,... | collective-permute-start | bytes 614408 | tf_op jit(solution)/shard_map/ppermute | solution.py:40
  107.1 9.5 %collective-permute-start.22 = (bf16[2,80,1280]{2,1,0:T(8,128)(2,1)S(1)}, bf16[2,80,1280]{2,1,0:T(8,128)(2,1)S(1)}, u32[]{:S(2)}, u32[]{:S(2)}) collective-permute-start(bf16[2,80,1280]{2,1,0:T(8,128)(2,1)S(1)} %pad_maximum_fusion.5), channel_id=1, source_target_pairs={{0,16},{1,17},{2,18},{3,19},{4,20},{5,21},{6,22},{7,23},{8,24},{9,... | collective-permute-start | bytes 1228808 | tf_op jit(solution)/shard_map/ppermute | solution.py:40
  116.8 7.0 %collective-permute-start.25 = (bf16[80,1280]{1,0:T(8,128)(2,1)S(1)}, bf16[80,1280]{1,0:T(8,128)(2,1)S(1)}, u32[]{:S(2)}, u32[]{:S(2)}) collective-permute-start(bf16[80,1280]{1,0:T(8,128)(2,1)S(1)} %get-tuple-element.96), channel_id=1, source_target_pairs={{0,4},{1,5},{2,6},{3,7},{4,8},{5,9},{6,10},{7,11},{8,12},{9,13},{1... | collective-permute-start | bytes 614408 | tf_op jit(solution)/shard_map/ppermute | solution.py:40
  116.9 9.7 %collective-permute-start.24 = (bf16[80,1280]{1,0:T(8,128)(2,1)S(1)}, bf16[80,1280]{1,0:T(8,128)(2,1)S(1)}, u32[]{:S(2)}, u32[]{:S(2)}) collective-permute-start(bf16[80,1280]{1,0:T(8,128)(2,1)S(1)} %get-tuple-element.96), channel_id=1, source_target_pairs={{0,8},{1,9},{2,10},{3,11},{4,12},{5,13},{6,14},{7,15},{8,0},{9,1},... | collective-permute-start | bytes 614408 | tf_op jit(solution)/shard_map/ppermute | solution.py:40
  120.6 6.3 %collective-permute-start.23 = (bf16[80,1280]{1,0:T(8,128)(2,1)S(1)}, bf16[80,1280]{1,0:T(8,128)(2,1)S(1)}, u32[]{:S(2)}, u32[]{:S(2)}) collective-permute-start(bf16[80,1280]{1,0:T(8,128)(2,1)S(1)} %get-tuple-element.96), channel_id=1, source_target_pairs={{0,12},{1,13},{2,14},{3,15},{4,0},{5,1},{6,2},{7,3},{8,4},{9,5},{1... | collective-permute-start | bytes 614408 | tf_op jit(solution)/shard_map/ppermute | solution.py:40
  120.8 9.6 %collective-permute-start.27 = (bf16[100,1280]{1,0:T(8,128)(2,1)S(1)}, bf16[100,1280]{1,0:T(8,128)(2,1)S(1)}, u32[]{:S(2)}, u32[]{:S(2)}) collective-permute-start(bf16[100,1280]{1,0:T(8,128)(2,1)S(1)} %get-tuple-element.102), channel_id=1, source_target_pairs={{0,3},{1,0},{2,1},{3,2},{4,7},{5,4},{6,5},{7,6},{8,11},{9,8},{10,9... | collective-permute-start | bytes 768008 | tf_op jit(solution)/shard_map/ppermute | solution.py:40
  123.0 10.8 %collective-permute-start.28 = (bf16[100,1280]{1,0:T(8,128)(2,1)S(1)}, bf16[100,1280]{1,0:T(8,128)(2,1)S(1)}, u32[]{:S(2)}, u32[]{:S(2)}) collective-permute-start(bf16[100,1280]{1,0:T(8,128)(2,1)S(1)} %get-tuple-element.103), channel_id=1, source_target_pairs={{0,2},{1,3},{2,0},{3,1},{4,6},{5,7},{6,4},{7,5},{8,10},{9,11},{10,... | collective-permute-start | bytes 768008 | tf_op jit(solution)/shard_map/ppermute | solution.py:40
  123.8 13.1 %collective-permute-start.29 = (bf16[100,1280]{1,0:T(8,128)(2,1)S(1)}, bf16[100,1280]{1,0:T(8,128)(2,1)S(1)}, u32[]{:S(2)}, u32[]{:S(2)}) collective-permute-start(bf16[100,1280]{1,0:T(8,128)(2,1)S(1)} %get-tuple-element.104), channel_id=1, source_target_pairs={{0,1},{1,2},{2,3},{3,0},{4,5},{5,6},{6,7},{7,4},{8,9},{9,10},{10,1... | collective-permute-start | bytes 768008 | tf_op jit(solution)/shard_map/ppermute | solution.py:40
  127.0 13.4 %copy-start.1 = (bf16[4,80,1280]{2,1,0:T(8,128)(2,1)}, bf16[4,80,1280]{2,1,0:T(8,128)(2,1)S(1)}, u32[]{:S(2)}) copy-start(bf16[4,80,1280]{2,1,0:T(8,128)(2,1)S(1)} %pad_maximum_fusion.2.rest_0_) | copy-start | bytes 2457604
  127.0 23.3 %collective-permute-start.31 = (bf16[4,80,1280]{2,1,0:T(8,128)(2,1)S(1)}, bf16[4,80,1280]{2,1,0:T(8,128)(2,1)S(1)}, u32[]{:S(2)}, u32[]{:S(2)}) collective-permute-start(bf16[4,80,1280]{2,1,0:T(8,128)(2,1)S(1)} %pad_maximum_fusion.2.rest_0_), channel_id=1, source_target_pairs={{0,1},{1,2},{2,3},{3,0},{4,5},{5,6},{6,7},{7,4},{8,9},{9,10},{10,1... | collective-permute-start | bytes 2457608 | tf_op jit(solution)/shard_map/ppermute | solution.py:40
  127.3 23.1 %collective-permute-start.26 = (bf16[4,80,1280]{2,1,0:T(8,128)(2,1)S(1)}, bf16[4,80,1280]{2,1,0:T(8,128)(2,1)S(1)}, u32[]{:S(2)}, u32[]{:S(2)}) collective-permute-start(bf16[4,80,1280]{2,1,0:T(8,128)(2,1)S(1)} %pad_maximum_fusion.2.rest_0_), channel_id=1, source_target_pairs={{0,3},{1,0},{2,1},{3,2},{4,7},{5,4},{6,5},{7,6},{8,11},{9,8},{10,9... | collective-permute-start | bytes 2457608 | tf_op jit(solution)/shard_map/ppermute | solution.py:40
  137.1 13.3 %copy-start.2 = (bf16[4,80,1280]{2,1,0:T(8,128)(2,1)}, bf16[4,80,1280]{2,1,0:T(8,128)(2,1)S(1)}, u32[]{:S(2)}) copy-start(bf16[4,80,1280]{2,1,0:T(8,128)(2,1)S(1)} %pad_maximum_fusion.3.rest_3_) | copy-start | bytes 2457604
  137.1 16.7 %collective-permute-start.35 = (bf16[4,80,1280]{2,1,0:T(8,128)(2,1)S(1)}, bf16[4,80,1280]{2,1,0:T(8,128)(2,1)}, u32[]{:S(2)}, u32[]{:S(2)}) collective-permute-start(bf16[4,80,1280]{2,1,0:T(8,128)(2,1)S(1)} %pad_maximum_fusion.3.rest_3_), channel_id=1, source_target_pairs={{0,4},{1,5},{2,6},{3,7},{4,8},{5,9},{6,10},{7,11},{8,12},{9,13},{1... | collective-permute-start | bytes 2457608 | tf_op jit(solution)/shard_map/ppermute | solution.py:40
  138.4 17.8 %collective-permute-start.33 = (bf16[4,80,1280]{2,1,0:T(8,128)(2,1)S(1)}, bf16[4,80,1280]{2,1,0:T(8,128)(2,1)}, u32[]{:S(2)}, u32[]{:S(2)}) collective-permute-start(bf16[4,80,1280]{2,1,0:T(8,128)(2,1)S(1)} %pad_maximum_fusion.3.rest_3_), channel_id=1, source_target_pairs={{0,12},{1,13},{2,14},{3,15},{4,0},{5,1},{6,2},{7,3},{8,4},{9,5},{1... | collective-permute-start | bytes 2457608 | tf_op jit(solution)/shard_map/ppermute | solution.py:40
  150.3 6.9 %copy-start.3 = (bf16[4,80,1280]{2,1,0:T(8,128)(2,1)}, bf16[4,80,1280]{2,1,0:T(8,128)(2,1)S(1)}, u32[]{:S(2)}) copy-start(bf16[4,80,1280]{2,1,0:T(8,128)(2,1)S(1)} %collective-permute-done.31.rest_2_) | copy-start | bytes 2457604
  150.4 14.0 %collective-permute-start.32 = (bf16[2,80,1280]{2,1,0:T(8,128)(2,1)S(1)}, bf16[2,80,1280]{2,1,0:T(8,128)(2,1)}, u32[]{:S(2)}, u32[]{:S(2)}) collective-permute-start(bf16[2,80,1280]{2,1,0:T(8,128)(2,1)S(1)} %slice.154), channel_id=1, source_target_pairs={{0,1},{1,2},{2,3},{3,0},{4,5},{5,6},{6,7},{7,4},{8,9},{9,10},{10,1... | collective-permute-start | bytes 1228808 | tf_op jit(solution)/shard_map/ppermute | solution.py:40
  150.5 8.8 %copy-start.4 = (bf16[4,80,1280]{2,1,0:T(8,128)(2,1)}, bf16[4,80,1280]{2,1,0:T(8,128)(2,1)S(1)}, u32[]{:S(2)}) copy-start(bf16[4,80,1280]{2,1,0:T(8,128)(2,1)S(1)} %collective-permute-done.26.rest_1_) | copy-start | bytes 2457604
  150.5 13.9 %collective-permute-start.30 = (bf16[2,80,1280]{2,1,0:T(8,128)(2,1)S(1)}, bf16[2,80,1280]{2,1,0:T(8,128)(2,1)}, u32[]{:S(2)}, u32[]{:S(2)}) collective-permute-start(bf16[2,80,1280]{2,1,0:T(8,128)(2,1)S(1)} %slice.129), channel_id=1, source_target_pairs={{0,3},{1,0},{2,1},{3,2},{4,7},{5,4},{6,5},{7,6},{8,11},{9,8},{10,9... | collective-permute-start | bytes 1228808 | tf_op jit(solution)/shard_map/ppermute | solution.py:40
  154.8 9.6 %collective-permute-start.36 = (bf16[2,80,1280]{2,1,0:T(8,128)(2,1)S(1)}, bf16[2,80,1280]{2,1,0:T(8,128)(2,1)}, u32[]{:S(2)}, u32[]{:S(2)}) collective-permute-start(bf16[2,80,1280]{2,1,0:T(8,128)(2,1)S(1)} %slice.159), channel_id=1, source_target_pairs={{0,4},{1,5},{2,6},{3,7},{4,8},{5,9},{6,10},{7,11},{8,12},{9,13},{1... | collective-permute-start | bytes 1228808 | tf_op jit(solution)/shard_map/ppermute | solution.py:40
  157.2 8.0 %collective-permute-start.34 = (bf16[2,80,1280]{2,1,0:T(8,128)(2,1)S(1)}, bf16[2,80,1280]{2,1,0:T(8,128)(2,1)S(1)}, u32[]{:S(2)}, u32[]{:S(2)}) collective-permute-start(bf16[2,80,1280]{2,1,0:T(8,128)(2,1)S(1)} %slice.158), channel_id=1, source_target_pairs={{0,12},{1,13},{2,14},{3,15},{4,0},{5,1},{6,2},{7,3},{8,4},{9,5},{1... | collective-permute-start | bytes 1228808 | tf_op jit(solution)/shard_map/ppermute | solution.py:40
  165.3 0.8 copy-start.11

commit v7 on v6

--- a/solution.py
+++ b/solution.py
@@ -130,11 +130,12 @@
 ]
 
 
-def pseudo_body(outputs, at_ref, scale_ref, ct_ref, g0_ref, g1_ref, g2_ref, g3_ref, drift_ref, *rest):
+def pseudo_body(outputs, entries, at_ref, near_ref, far_ref, ct_ref, g0_ref, g1_ref, g2_ref, g3_ref, drift_ref, *rest):
     outs = rest[:len(outputs)]
     drift_buf, g_buf, rows_buf, out_buf, drift_sems, g_sems, out_sems = rest[len(outputs):]
     x, y, zh, tp = at_ref[0], at_ref[1], at_ref[2], at_ref[3]
-    scale = scale_ref[0]
+    squares = near_ref[:1, :1] + far_ref[:1, :1]
+    scale = inner_rate / jnp.sqrt(squares / entries + 1e-06)
     pieces = ((g0_ref, g1_ref), (g2_ref, g3_ref))
 
     def g_copy(slot, ref, k):
@@ -188,17 +189,17 @@
         one.wait()
 
 
-def pseudo_gradient(outputs, name, at, scale, ct, pieces, drift):
+def pseudo_gradient(outputs, name, entries, at, squares, ct, pieces, drift):
     smem = pl.BlockSpec(memory_space=pltpu.SMEM)
     hbm = pl.BlockSpec(memory_space=pl.ANY)
     tokens, rows = ct.shape[1], ct.shape[0]
     count = sum(len(tiles) for tiles in outputs)
     return pl.pallas_call(
-        functools.partial(pseudo_body, outputs),
+        functools.partial(pseudo_body, outputs, entries),
         out_shape=tuple(
             jax.ShapeDtypeStruct((len(tiles), TILE_R, 2 * HALF_C), bf16) for tiles in outputs
         ),
-        in_specs=[smem, smem, pl.BlockSpec(memory_space=pltpu.VMEM)] + [hbm] * 5,
+        in_specs=[smem] + [pl.BlockSpec(memory_space=pltpu.VMEM)] * 3 + [hbm] * 5,
         out_specs=(hbm,) * len(outputs),
         scratch_shapes=[
             pltpu.VMEM((8, rows, HALF_C), bf16),
@@ -214,7 +215,7 @@
             flops=2 * rows * tokens * 5120, bytes_accessed=18_000_000, transcendentals=0
         ),
         name=name,
-    )(at, scale, ct, *pieces, drift)
+    )(at, *squares, ct, *pieces, drift)
 
 
 def base_body(at_ref, master_ref, momentum_ref, base_ref):
@@ -372,12 +373,11 @@
     squares = squares + swap_tp(squares, 1)
     across, base_tile, squares = lax.optimization_barrier((across, base_tile, squares))
     across_partner = swap_tp(across, 1)
-    squares = squares + swap_tp(squares, 2)
-    scale = (inner_rate / jnp.sqrt(squares[0, :1] / entries + 1e-06))
+    squares = (squares, swap_tp(squares, 2))
 
     pieces = (out_grad, partner, across, across_partner)
-    scale, base_tile = lax.optimization_barrier((scale, base_tile))
-    sends = pseudo_gradient(FIRST + LATER, "pseudo_gradient", at, scale, ct, pieces, drift)
+    squares, base_tile = lax.optimization_barrier((squares, base_tile))
+    sends = pseudo_gradient(FIRST + LATER, "pseudo_gradient", entries, at, squares, ct, pieces, drift)
     waves, later = sends[:4], sends[4:]
     here, there = pass_on(waves[:2], later[:3], "x"), pass_on(waves[2:], later[3:], "y")
     there, base_tile = lax.optimization_barrier((there, base_tile))

time: 170 us -> 170 us (level)
  transfers between devices with their start and end apart: 38 -> 38, of which waited for: 21 -> 20; matrix products, arithmetic and copies ran while one was open for 8% -> 7% of each run, Pallas kernels for 9% -> 9%
where the time goes in v7:
time: 170 us; the launch traced here: 169 us
  waiting for transfers between devices  66.6 us (39%)
  starting transfers between devices  56.3 us (33%)
  Pallas kernels  29.9 us (18%)
  other arithmetic  8.05 us (5%)
  local copies, waits for them, and re-layouts  6.45 us (4%)
    ppermute x30, waiting for transfers between devices, move(): return lax.ppermute(value, 'worker', pairs)  50.2 us
    ppermute x30, starting transfers between devices, move(): return lax.ppermute(value, 'worker', pairs)  49 us
    pallas_call x1, Pallas kernels, pseudo_gradient(): pl.pallas_call(functools.partial(pseudo_body, outputs, entries), out_shap...  9.64 us
    ppermute x7, waiting for transfers between devices, swap_tp(): return lax.ppermute(value, 'tp', [(t, t ^ bit) for t in range(4)])  9.6 us
    pallas_call x2, Pallas kernels, place(): pl.pallas_call(functools.partial(place_body, where), out_shape=jax.ShapeD...  8.15 us
    all_to_all x1, waiting for transfers between devices, per_device(): base_tile = lax.all_to_all(base, 'worker', 0, 0, axis_index_groups=rings)  6.8 us
    pallas_call x1, Pallas kernels, attention(): pl.pallas_call(attention_body, out_shape=(jax.ShapeDtypeStruct((width, to...  4.93 us
    all_to_all x1, starting transfers between devices, per_device(): base_tile = lax.all_to_all(base, 'worker', 0, 0, axis_index_groups=rings)  4.3 us
  transfers between devices with their start and end apart: 38, of which 20 were waited for; matrix products, arithmetic and copies ran while one was open for 7% of the time, Pallas kernels for 9%

profile of v7, /device:TPU:32, one launch (start us, length us, event | category | flops | bytes accessed | tf_op | source)
XLA Modules:
  0.0 168.6 jit_solution(10561213780879727588)
XLA Ops:
  0.6 2.7 %cotangent_gram.1 = f32[6,128,128]{2,1,0:T(8,128)} custom-call(bf16[384,1280]{1,0:T(8,128)(2,1)} %g0_ref.1), custom_call_target="tpu_custom_call" | custom-call | tf_op jit(solution)/shard_map/cotangent_gram/pallas_call | solution.py:59
  3.4 1.3 reshape.20.seg_row_ref
  4.7 4.9 %attention.1 = (bf16[640,384]{1,0:T(8,128)(2,1)}, f32[6,128,128]{2,1,0:T(8,128)}) custom-call(bf16[384,640]{1,0:T(8,128)(2,1)} %q_ref, bf16[384,640]{1,0:T(8,128)(2,1)} %k_ref.1, bf16[384,640]{1,0:T(8,128)(2,1)} %v_ref.1, s32[1,384]{1,0:T(1,128)} %reshape.20.seg_row_ref), custom_call_target="tpu_custom_call" | custom-call | tf_op jit(solution)/shard_map/attention/pallas_call | solution.py:102
  9.6 0.6 pad_add_fusion.at_ref
  10.2 2.0 %collective-permute-start = (bf16[384,1280]{1,0:T(8,128)(2,1)S(1)}, bf16[384,1280]{1,0:T(8,128)(2,1)S(1)}, u32[]{:S(2)}, u32[]{:S(2)}) collective-permute-start(bf16[384,1280]{1,0:T(8,128)(2,1)S(1)} %copy-done), channel_id=1, source_target_pairs={{0,64},{32,96},{64,0},{96,32},{1,65},{33,97},{65,1},{97,33},{2,66}... | collective-permute-start | bytes 2949128 | tf_op jit(solution)/shard_map/ppermute | solution.py:44
  12.1 3.4 %collective-permute-done.1 = f32[6,128,128]{2,1,0:T(8,128)S(1)} collective-permute-done((f32[6,128,128]{2,1,0:T(8,128)}, f32[6,128,128]{2,1,0:T(8,128)S(1)}, u32[]{:S(2)}, u32[]{:S(2)}) %collective-permute-start.1) | collective-permute-done | bytes 393248 | tf_op jit(solution)/shard_map/ppermute | solution.py:44
  15.7 2.1 %base_rows.1 = f32[4,20,1280]{2,1,0:T(8,128)} custom-call(s32[4]{0:T(128)} %pad_add_fusion.at_ref, f32[20,5120]{1,0:T(8,128)} %master_ref.3, f32[20,5120]{1,0:T(8,128)} %momentum_ref.3), custom_call_target="tpu_custom_call" | custom-call | tf_op jit(solution)/shard_map/base_rows/pallas_call | solution.py:233
  17.8 4.3 %all-to-all-start = ((f32[4,20,1280]{2,1,0:T(8,128)}), f32[4,20,1280]{2,1,0:T(8,128)S(1)}, u32[]{:S(2)}, u32[]{:S(2)}) async-start(f32[4,20,1280]{2,1,0:T(8,128)} %base_rows.1), calls=%async_computation | async-start | bytes 983040 | tf_op jit(solution)/shard_map/all_to_all | solution.py:367
  22.1 1.7 %multiply_reduce_fusion = f32[]{:T(128)} fusion(f32[6,128,128]{2,1,0:T(8,128)S(1)} %copy-done.12, f32[6,128,128]{2,1,0:T(8,128)S(1)} %add.110, f32[6,128,128]{2,1,0:T(8,128)} %collective-permute-done.2), kind=kLoop, calls=%fused_computation.28 | loop fusion | flops 294911 | bytes 1179652 | tf_op jit(solution)/shard_map/reduce_sum | solution.py:371
  23.8 0.6 broadcast_in_dim.3
  24.7 0.3 collective-permute-start.5
  25.0 6.8 %all-to-all-done = f32[4,20,1280]{2,1,0:T(8,128)S(1)} async-done(((f32[4,20,1280]{2,1,0:T(8,128)}), f32[4,20,1280]{2,1,0:T(8,128)S(1)}, u32[]{:S(2)}, u32[]{:S(2)}) %all-to-all-start) | async-done | bytes 409632 | tf_op jit(solution)/shard_map/all_to_all | solution.py:367
  31.9 0.7 broadcast_add_fusion.near_ref
  32.6 2.9 %collective-permute-done.g2_ref = bf16[384,1280]{1,0:T(8,128)(2,1)S(1)} collective-permute-done((bf16[384,1280]{1,0:T(8,128)(2,1)S(1)}, bf16[384,1280]{1,0:T(8,128)(2,1)S(1)}, u32[]{:S(2)}, u32[]{:S(2)}) %collective-permute-start) | collective-permute-done | bytes 983072 | tf_op jit(solution)/shard_map/ppermute | solution.py:44
  35.5 0.4 collective-permute-start.4
  35.8 3.3 %collective-permute-done.4.far_ref = f32[8,128]{1,0:T(8,128)S(1)} collective-permute-done((f32[8,128]{1,0:T(8,128)S(1)}, f32[8,128]{1,0:T(8,128)S(1)}, u32[]{:S(2)}, u32[]{:S(2)}) %collective-permute-start.4) | collective-permute-done | bytes 4128 | tf_op jit(solution)/shard_map/ppermute | solution.py:44
  39.1 0.6 copy-done.14
  39.7 9.6 %pseudo_gradient.1 = (bf16[4,80,1280]{2,1,0:T(8,128)(2,1)}, bf16[4,80,1280]{2,1,0:T(8,128)(2,1)}, bf16[4,80,1280]{2,1,0:T(8,128)(2,1)}, bf16[4,80,1280]{2,1,0:T(...) custom-call(s32[4]{0:T(128)} %pad_add_fusion.at_ref, ...), custom_call_target="tpu_custom_call" | custom-call | flops 2516582400 | bytes 18000000 | tf_op jit(solution)/shard_map/pseudo_gradient/pallas_call | solution.py:197
  49.3 2.8 %collective-permute-start.10 = (bf16[4,80,1280]{2,1,0:T(8,128)(2,1)}, bf16[4,80,1280]{2,1,0:T(8,128)(2,1)S(1)}, u32[]{:S(2)}, u32[]{:S(2)}) collective-permute-start(bf16[4,80,1280]{2,1,0:T(8,128)(2,1)} %get-tuple-element.65), channel_id=1, source_target_pairs={{0,3},{1,0},{2,1},{3,2},{4,7},{5,4},{6,5},{7,6},{8,11},{9,8},{10,9... | collective-permute-start | bytes 2457608 | tf_op jit(solution)/shard_map/ppermute | solution.py:40
  52.2 1.6 collective-permute-start.7
  53.7 1.7 collective-permute-start.8
  55.4 14.1 %collective-permute-done.10 = bf16[4,80,1280]{2,1,0:T(8,128)(2,1)S(1)} collective-permute-done((bf16[4,80,1280]{2,1,0:T(8,128)(2,1)}, bf16[4,80,1280]{2,1,0:T(8,128)(2,1)S(1)}, u32[]{:S(2)}, u32[]{:S(2)}) %collective-permute-start.10) | collective-permute-done | bytes 819232 | tf_op jit(solution)/shard_map/ppermute | solution.py:40
  69.5 1.2 add_convert_fusion
  70.7 3.7 %collective-permute-start.13 = (bf16[2,80,1280]{2,1,0:T(8,128)(2,1)S(1)}, bf16[2,80,1280]{2,1,0:T(8,128)(2,1)S(1)}, u32[]{:S(2)}, u32[]{:S(2)}) collective-permute-start(bf16[2,80,1280]{2,1,0:T(8,128)(2,1)S(1)} %add_convert_fusion), channel_id=1, source_target_pairs={{0,3},{1,0},{2,1},{3,2},{4,7},{5,4},{6,5},{7,6},{8,11},{9,8},{10,9... | collective-permute-start | bytes 1228808 | tf_op jit(solution)/shard_map/ppermute | solution.py:40
  74.3 1.2 add_convert_fusion.1
  76.1 1.6 collective-permute-start.14
  77.7 1.7 collective-permute-start.15
  79.4 3.0 %collective-permute-start.9 = (f32[80,1280]{1,0:T(8,128)S(1)}, f32[80,1280]{1,0:T(8,128)S(1)}, u32[]{:S(2)}, u32[]{:S(2)}) collective-permute-start(f32[80,1280]{1,0:T(8,128)S(1)} %reshape.21), channel_id=1, source_target_pairs={{0,16},{1,17},{2,18},{3,19},{4,20},{5,21},{6,22},{7,23},{8,24},{9,... | collective-permute-start | bytes 1228808 | tf_op jit(solution)/shard_map/ppermute | solution.py:40
  82.3 4.2 %collective-permute-done.12 = bf16[2,80,1280]{2,1,0:T(8,128)(2,1)S(1)} collective-permute-done((bf16[2,80,1280]{2,1,0:T(8,128)(2,1)S(1)}, bf16[2,80,1280]{2,1,0:T(8,128)(2,1)S(1)}, u32[]{:S(2)}, u32[]{:S(2)}) %collective-permute-start.12) | collective-permute-done | bytes 409632 | tf_op jit(solution)/shard_map/ppermute | solution.py:40
  86.9 0.7 copy-done.7
  88.4 1.6 collective-permute-start.16
  90.0 1.7 collective-permute-start.18
  91.7 2.0 %collective-permute-start.17 = (bf16[80,1280]{1,0:T(8,128)(2,1)S(1)}, bf16[80,1280]{1,0:T(8,128)(2,1)S(1)}, u32[]{:S(2)}, u32[]{:S(2)}) collective-permute-start(bf16[80,1280]{1,0:T(8,128)(2,1)S(1)} %get-tuple-element.92), channel_id=1, source_target_pairs={{0,8},{1,9},{2,10},{3,11},{4,12},{5,13},{6,14},{7,15},{8,0},{9,1},... | collective-permute-start | bytes 614408 | tf_op jit(solution)/shard_map/ppermute | solution.py:40
  93.9 3.4 %collective-permute-done.16 = bf16[80,1280]{1,0:T(8,128)(2,1)S(1)} collective-permute-done((bf16[80,1280]{1,0:T(8,128)(2,1)S(1)}, bf16[80,1280]{1,0:T(8,128)(2,1)S(1)}, u32[]{:S(2)}, u32[]{:S(2)}) %collective-permute-start.16) | collective-permute-done | bytes 204832 | tf_op jit(solution)/shard_map/ppermute | solution.py:40
  97.2 1.8 %collective-permute-start.21 = (bf16[80,1280]{1,0:T(8,128)(2,1)S(1)}, bf16[80,1280]{1,0:T(8,128)(2,1)S(1)}, u32[]{:S(2)}, u32[]{:S(2)}) collective-permute-start(bf16[80,1280]{1,0:T(8,128)(2,1)S(1)} %get-tuple-element.88), channel_id=1, source_target_pairs={{0,3},{1,0},{2,1},{3,2},{4,7},{5,4},{6,5},{7,6},{8,11},{9,8},{10,9... | collective-permute-start | bytes 614408 | tf_op jit(solution)/shard_map/ppermute | solution.py:40
  99.0 0.4 collective-permute-done.17
  99.6 2.0 %collective-permute-done.19 = bf16[80,1280]{1,0:T(8,128)(2,1)S(1)} collective-permute-done((bf16[80,1280]{1,0:T(8,128)(2,1)S(1)}, bf16[80,1280]{1,0:T(8,128)(2,1)S(1)}, u32[]{:S(2)}, u32[]{:S(2)}) %collective-permute-start.19) | collective-permute-done | bytes 204832 | tf_op jit(solution)/shard_map/ppermute | solution.py:40
  101.6 2.9 %collective-permute-done.21 = bf16[80,1280]{1,0:T(8,128)(2,1)S(1)} collective-permute-done((bf16[80,1280]{1,0:T(8,128)(2,1)S(1)}, bf16[80,1280]{1,0:T(8,128)(2,1)S(1)}, u32[]{:S(2)}, u32[]{:S(2)}) %collective-permute-start.21) | collective-permute-done | bytes 204832 | tf_op jit(solution)/shard_map/ppermute | solution.py:40
  104.5 1.8 %collective-permute-done.20 = bf16[80,1280]{1,0:T(8,128)(2,1)S(1)} collective-permute-done((bf16[80,1280]{1,0:T(8,128)(2,1)S(1)}, bf16[80,1280]{1,0:T(8,128)(2,1)S(1)}, u32[]{:S(2)}, u32[]{:S(2)}) %collective-permute-start.20) | collective-permute-done | bytes 204832 | tf_op jit(solution)/shard_map/ppermute | solution.py:40
  106.4 3.1 %collective-permute-start.22 = (bf16[2,80,1280]{2,1,0:T(8,128)(2,1)S(1)}, bf16[2,80,1280]{2,1,0:T(8,128)(2,1)S(1)}, u32[]{:S(2)}, u32[]{:S(2)}) collective-permute-start(bf16[2,80,1280]{2,1,0:T(8,128)(2,1)S(1)} %pad_maximum_fusion.5), channel_id=1, source_target_pairs={{0,16},{1,17},{2,18},{3,19},{4,20},{5,21},{6,22},{7,23},{8,24},{9,... | collective-permute-start | bytes 1228808 | tf_op jit(solution)/shard_map/ppermute | solution.py:40
  109.5 6.5 %collective-permute-done.22 = bf16[2,80,1280]{2,1,0:T(8,128)(2,1)S(1)} collective-permute-done((bf16[2,80,1280]{2,1,0:T(8,128)(2,1)S(1)}, bf16[2,80,1280]{2,1,0:T(8,128)(2,1)S(1)}, u32[]{:S(2)}, u32[]{:S(2)}) %collective-permute-start.22) | collective-permute-done | bytes 409632 | tf_op jit(solution)/shard_map/ppermute | solution.py:40
  116.2 3.7 %collective-permute-start.24 = (bf16[80,1280]{1,0:T(8,128)(2,1)S(1)}, bf16[80,1280]{1,0:T(8,128)(2,1)S(1)}, u32[]{:S(2)}, u32[]{:S(2)}) collective-permute-start(bf16[80,1280]{1,0:T(8,128)(2,1)S(1)} %get-tuple-element.98), channel_id=1, source_target_pairs={{0,8},{1,9},{2,10},{3,11},{4,12},{5,13},{6,14},{7,15},{8,0},{9,1},... | collective-permute-start | bytes 614408 | tf_op jit(solution)/shard_map/ppermute | solution.py:40
  120.1 2.2 %collective-permute-start.27 = (bf16[100,1280]{1,0:T(8,128)(2,1)S(1)}, bf16[100,1280]{1,0:T(8,128)(2,1)S(1)}, u32[]{:S(2)}, u32[]{:S(2)}) collective-permute-start(bf16[100,1280]{1,0:T(8,128)(2,1)S(1)} %get-tuple-element.104), channel_id=1, source_target_pairs={{0,3},{1,0},{2,1},{3,2},{4,7},{5,4},{6,5},{7,6},{8,11},{9,8},{10,9... | collective-permute-start | bytes 768008 | tf_op jit(solution)/shard_map/ppermute | solution.py:40
  122.3 0.7 collective-permute-start.28
  123.2 2.5 %collective-permute-start.29 = (bf16[100,1280]{1,0:T(8,128)(2,1)S(1)}, bf16[100,1280]{1,0:T(8,128)(2,1)S(1)}, u32[]{:S(2)}, u32[]{:S(2)}) collective-permute-start(bf16[100,1280]{1,0:T(8,128)(2,1)S(1)} %get-tuple-element.106), channel_id=1, source_target_pairs={{0,1},{1,2},{2,3},{3,0},{4,5},{5,6},{6,7},{7,4},{8,9},{9,10},{10,1... | collective-permute-start | bytes 768008 | tf_op jit(solution)/shard_map/ppermute | solution.py:40
  125.9 0.4 collective-permute-done.23
  126.4 0.3 collective-permute-start.31
  126.7 3.0 %collective-permute-start.26 = (bf16[4,80,1280]{2,1,0:T(8,128)(2,1)S(1)}, bf16[4,80,1280]{2,1,0:T(8,128)(2,1)S(1)}, u32[]{:S(2)}, u32[]{:S(2)}) collective-permute-start(bf16[4,80,1280]{2,1,0:T(8,128)(2,1)S(1)} %pad_maximum_fusion.2.rest_0_), channel_id=1, source_target_pairs={{0,3},{1,0},{2,1},{3,2},{4,7},{5,4},{6,5},{7,6},{8,11},{9,8},{10,9... | collective-permute-start | bytes 2457608 | tf_op jit(solution)/shard_map/ppermute | solution.py:40
  129.7 3.4 %collective-permute-done.28 = bf16[100,1280]{1,0:T(8,128)(2,1)S(1)} collective-permute-done((bf16[100,1280]{1,0:T(8,128)(2,1)S(1)}, bf16[100,1280]{1,0:T(8,128)(2,1)S(1)}, u32[]{:S(2)}, u32[]{:S(2)}) %collective-permute-start.28) | collective-permute-done | bytes 256032 | tf_op jit(solution)/shard_map/ppermute | solution.py:40
  133.2 3.2 %collective-permute-done.29 = bf16[100,1280]{1,0:T(8,128)(2,1)S(1)} collective-permute-done((bf16[100,1280]{1,0:T(8,128)(2,1)S(1)}, bf16[100,1280]{1,0:T(8,128)(2,1)S(1)}, u32[]{:S(2)}, u32[]{:S(2)}) %collective-permute-start.29) | collective-permute-done | bytes 256032 | tf_op jit(solution)/shard_map/ppermute | solution.py:40
  136.5 1.3 collective-permute-start.35
  137.7 2.0 %collective-permute-start.33 = (bf16[4,80,1280]{2,1,0:T(8,128)(2,1)S(1)}, bf16[4,80,1280]{2,1,0:T(8,128)(2,1)}, u32[]{:S(2)}, u32[]{:S(2)}) collective-permute-start(bf16[4,80,1280]{2,1,0:T(8,128)(2,1)S(1)} %pad_maximum_fusion.3.rest_3_), channel_id=1, source_target_pairs={{0,12},{1,13},{2,14},{3,15},{4,0},{5,1},{6,2},{7,3},{8,4},{9,5},{1... | collective-permute-start | bytes 2457608 | tf_op jit(solution)/shard_map/ppermute | solution.py:40
  139.8 0.8 pad_maximum_fusion.4.mean_ref
  140.6 2.4 %outer_rows.1 = (f32[20,5120]{1,0:T(8,128)}, f32[20,5120]{1,0:T(8,128)}) custom-call(s32[4]{0:T(128)} %pad_add_fusion.at_ref, f32[20,5120]{1,0:T(8,128)} %master_ref.3, f32[20,5120]{1,0:T(8,128)} %momentum_ref.3, f32[4,20,1280]{2,1,0:T(8,128)} %pad_maximum_fusion.4.mean_ref), custom_call_target="tpu_custom_call" | custom-call | tf_op jit(solution)/shard_map/outer_rows/pallas_call | solution.py:256
  143.1 6.6 %collective-permute-done.31.rest_2_ = bf16[4,80,1280]{2,1,0:T(8,128)(2,1)S(1)} collective-permute-done((bf16[4,80,1280]{2,1,0:T(8,128)(2,1)S(1)}, bf16[4,80,1280]{2,1,0:T(8,128)(2,1)S(1)}, u32[]{:S(2)}, u32[]{:S(2)}) %collective-permute-start.31) | collective-permute-done | bytes 819232 | tf_op jit(solution)/shard_map/ppermute | solution.py:40
  149.9 3.3 %collective-permute-start.30 = (bf16[2,80,1280]{2,1,0:T(8,128)(2,1)S(1)}, bf16[2,80,1280]{2,1,0:T(8,128)(2,1)}, u32[]{:S(2)}, u32[]{:S(2)}) collective-permute-start(bf16[2,80,1280]{2,1,0:T(8,128)(2,1)S(1)} %slice.125), channel_id=1, source_target_pairs={{0,3},{1,0},{2,1},{3,2},{4,7},{5,4},{6,5},{7,6},{8,11},{9,8},{10,9... | collective-permute-start | bytes 1228808 | tf_op jit(solution)/shard_map/ppermute | solution.py:40
  153.1 1.0 slice.155
  154.2 1.4 collective-permute-start.36
  155.6 1.0 slice.154
  156.7 1.9 %collective-permute-start.34 = (bf16[2,80,1280]{2,1,0:T(8,128)(2,1)S(1)}, bf16[2,80,1280]{2,1,0:T(8,128)(2,1)S(1)}, u32[]{:S(2)}, u32[]{:S(2)}) collective-permute-start(bf16[2,80,1280]{2,1,0:T(8,128)(2,1)S(1)} %slice.154), channel_id=1, source_target_pairs={{0,12},{1,13},{2,14},{3,15},{4,0},{5,1},{6,2},{7,3},{8,4},{9,5},{1... | collective-permute-start | bytes 1228808 | tf_op jit(solution)/shard_map/ppermute | solution.py:40
  158.6 5.2 %place_first.1.rest_4_ = bf16[640,5120]{1,0:T(8,128)(2,1)} custom-call(s32[4]{0:T(128)} %pad_add_fusion.at_ref, bf16[4,80,1280]{2,1,0:T(8,128)(2,1)} %copy-done.1, bf16[4,80,1280]{2,1,0:T(8,128)(2,1)} %copy-done.4, bf16[4,80,1280]{2,1,0:T(8,128)(2,1)} %copy-done.3, bf16[4,80,1280]{2,1,0:T(8,128)(2,1)} %copy-done.2, ...), custom_call_target="tpu_custom_call" | custom-call | bytes 9830400 | tf_op jit(solution)/shard_map/place_first/pallas_call | solution.py:296
  163.8 0.9 collective-permute-done.34.rest_2_
  164.7 0.8 copy-done.11
  165.4 3.0 %place_last.1 = bf16[640,5120]{1,0:T(8,128)(2,1)} custom-call(s32[4]{0:T(128)} %pad_add_fusion.at_ref, bf16[2,80,1280]{2,1,0:T(8,128)(2,1)} %collective-permute-done.30.rest_0_, bf16[2,80,1280]{2,1,0:T(8,128)(2,1)} %collective-permute-done.32.rest_1_, bf16[2,80,1280]{2,1,0:T(8,128)(2,1)} %copy-done.11, ...), custom_call_target="tpu_custom_call", output_to_operand_aliasing={{}: (5, {})} | custom-call | bytes 3276800 | tf_op jit(solution)/shard_map/place_last/pallas_call | solution.py:296
  (89 shorter events, 3.8 us)
Async XLA Ops:
  0.6 9.6 %copy-start = (bf16[384,1280]{1,0:T(8,128)(2,1)S(1)}, bf16[384,1280]{1,0:T(8,128)(2,1)}, u32[]{:S(2)}) copy-start(bf16[384,1280]{1,0:T(8,128)(2,1)} %g0_ref.1) | copy-start | bytes 2949124
  3.3 12.2 %copy-start.5 = (f32[6,128,128]{2,1,0:T(8,128)S(1)}, f32[6,128,128]{2,1,0:T(8,128)}, u32[]{:S(2)}) copy-start(f32[6,128,128]{2,1,0:T(8,128)} %cotangent_gram.1) | copy-start | bytes 1179652
  3.3 12.2 %collective-permute-start.1 = (f32[6,128,128]{2,1,0:T(8,128)}, f32[6,128,128]{2,1,0:T(8,128)S(1)}, u32[]{:S(2)}, u32[]{:S(2)}) collective-permute-start(f32[6,128,128]{2,1,0:T(8,128)} %cotangent_gram.1), channel_id=1, source_target_pairs={{0,64},{32,96},{64,0},{96,32},{1,65},{33,97},{65,1},{97,33},{2,66}... | collective-permute-start | bytes 1179656 | tf_op jit(solution)/shard_map/ppermute | solution.py:44
  10.2 25.3 %collective-permute-start = (bf16[384,1280]{1,0:T(8,128)(2,1)S(1)}, bf16[384,1280]{1,0:T(8,128)(2,1)S(1)}, u32[]{:S(2)}, u32[]{:S(2)}) collective-permute-start(bf16[384,1280]{1,0:T(8,128)(2,1)S(1)} %copy-done), channel_id=1, source_target_pairs={{0,64},{32,96},{64,0},{96,32},{1,65},{33,97},{65,1},{97,33},{2,66}... | collective-permute-start | bytes 2949128 | tf_op jit(solution)/shard_map/ppermute | solution.py:44
  15.6 6.5 %copy-start.12 = (f32[6,128,128]{2,1,0:T(8,128)S(1)}, f32[6,128,128]{2,1,0:T(8,128)}, u32[]{:S(2)}) copy-start(f32[6,128,128]{2,1,0:T(8,128)} %get-tuple-element.49) | copy-start | bytes 1179652
  15.6 6.5 %collective-permute-start.2 = (f32[6,128,128]{2,1,0:T(8,128)S(1)}, f32[6,128,128]{2,1,0:T(8,128)}, u32[]{:S(2)}, u32[]{:S(2)}) collective-permute-start(f32[6,128,128]{2,1,0:T(8,128)S(1)} %add.110), channel_id=1, source_target_pairs={{0,32},{32,0},{64,96},{96,64},{1,33},{33,1},{65,97},{97,65},{2,34}... | collective-permute-start | bytes 1179656 | tf_op jit(solution)/shard_map/ppermute | solution.py:44
  17.8 14.1 %all-to-all-start = ((f32[4,20,1280]{2,1,0:T(8,128)}), f32[4,20,1280]{2,1,0:T(8,128)S(1)}, u32[]{:S(2)}, u32[]{:S(2)}) async-start(f32[4,20,1280]{2,1,0:T(8,128)} %base_rows.1), calls=%async_computation | async-start | bytes 983040 | tf_op jit(solution)/shard_map/all_to_all | solution.py:367
  24.4 7.4 %collective-permute-start.3 = (f32[8,128]{1,0:T(8,128)S(1)}, f32[8,128]{1,0:T(8,128)S(1)}, u32[]{:S(2)}, u32[]{:S(2)}) collective-permute-start(f32[8,128]{1,0:T(8,128)S(1)} %broadcast_in_dim.3), channel_id=1, source_target_pairs={{0,32},{32,0},{64,96},{96,64},{1,33},{33,1},{65,97},{97,65},{2,34}... | collective-permute-start | bytes 12296 | tf_op jit(solution)/shard_map/ppermute | solution.py:44
  24.7 14.4 %collective-permute-start.5 = (bf16[384,1280]{1,0:T(8,128)(2,1)S(1)}, bf16[384,1280]{1,0:T(8,128)(2,1)}, u32[]{:S(2)}, u32[]{:S(2)}) collective-permute-start(bf16[384,1280]{1,0:T(8,128)(2,1)S(1)} %copy-done), channel_id=1, source_target_pairs={{0,32},{32,0},{64,96},{96,64},{1,33},{33,1},{65,97},{97,65},{2,34}... | collective-permute-start | bytes 2949128 | tf_op jit(solution)/shard_map/ppermute | solution.py:44
  32.6 6.6 %copy-start.13 = (f32[8,128]{1,0:T(8,128)}, f32[8,128]{1,0:T(8,128)S(1)}, u32[]{:S(2)}) copy-start(f32[8,128]{1,0:T(8,128)S(1)} %broadcast_add_fusion.near_ref) | copy-start | bytes 12292
  35.5 3.6 %copy-start.6 = (bf16[384,1280]{1,0:T(8,128)(2,1)}, bf16[384,1280]{1,0:T(8,128)(2,1)S(1)}, u32[]{:S(2)}) copy-start(bf16[384,1280]{1,0:T(8,128)(2,1)S(1)} %collective-permute-done.g2_ref) | copy-start | bytes 2949124
  35.5 3.6 %collective-permute-start.6 = (bf16[384,1280]{1,0:T(8,128)(2,1)S(1)}, bf16[384,1280]{1,0:T(8,128)(2,1)}, u32[]{:S(2)}, u32[]{:S(2)}) collective-permute-start(bf16[384,1280]{1,0:T(8,128)(2,1)S(1)} %collective-permute-done.g2_ref), channel_id=1, source_target_pairs={{0,32},{32,0},{64,96},{96,64},{1,33},{33,1},{65,97},{97,65},{2,34}... | collective-permute-start | bytes 2949128 | tf_op jit(solution)/shard_map/ppermute | solution.py:44
  35.5 3.6 %collective-permute-start.4 = (f32[8,128]{1,0:T(8,128)S(1)}, f32[8,128]{1,0:T(8,128)S(1)}, u32[]{:S(2)}, u32[]{:S(2)}) collective-permute-start(f32[8,128]{1,0:T(8,128)S(1)} %broadcast_add_fusion.near_ref), channel_id=1, source_target_pairs={{0,64},{32,96},{64,0},{96,32},{1,65},{33,97},{65,1},{97,33},{2,66}... | collective-permute-start | bytes 12296 | tf_op jit(solution)/shard_map/ppermute | solution.py:44
  39.1 0.6 copy-start.14
  49.3 26.5 %copy-start.10 = (bf16[2,80,1280]{2,1,0:T(8,128)(2,1)S(1)}, bf16[2,80,1280]{2,1,0:T(8,128)(2,1)}, u32[]{:S(2)}) copy-start(bf16[2,80,1280]{2,1,0:T(8,128)(2,1)} %get-tuple-element.60) | copy-start | bytes 1228804
  49.3 20.2 %collective-permute-start.10 = (bf16[4,80,1280]{2,1,0:T(8,128)(2,1)}, bf16[4,80,1280]{2,1,0:T(8,128)(2,1)S(1)}, u32[]{:S(2)}, u32[]{:S(2)}) collective-permute-start(bf16[4,80,1280]{2,1,0:T(8,128)(2,1)} %get-tuple-element.65), channel_id=1, source_target_pairs={{0,3},{1,0},{2,1},{3,2},{4,7},{5,4},{6,5},{7,6},{8,11},{9,8},{10,9... | collective-permute-start | bytes 2457608 | tf_op jit(solution)/shard_map/ppermute | solution.py:40
  52.2 22.2 %collective-permute-start.11 = (bf16[4,80,1280]{2,1,0:T(8,128)(2,1)}, bf16[4,80,1280]{2,1,0:T(8,128)(2,1)S(1)}, u32[]{:S(2)}, u32[]{:S(2)}) collective-permute-start(bf16[4,80,1280]{2,1,0:T(8,128)(2,1)} %get-tuple-element.67), channel_id=1, source_target_pairs={{0,1},{1,2},{2,3},{3,0},{4,5},{5,6},{6,7},{7,4},{8,9},{9,10},{10,1... | collective-permute-start | bytes 2457608 | tf_op jit(solution)/shard_map/ppermute | solution.py:40
  52.2 23.6 %collective-permute-start.7 = (bf16[4,80,1280]{2,1,0:T(8,128)(2,1)}, bf16[4,80,1280]{2,1,0:T(8,128)(2,1)S(1)}, u32[]{:S(2)}, u32[]{:S(2)}) collective-permute-start(bf16[4,80,1280]{2,1,0:T(8,128)(2,1)} %get-tuple-element.58), channel_id=1, source_target_pairs={{0,4},{1,5},{2,6},{3,7},{4,8},{5,9},{6,10},{7,11},{8,12},{9,13},{1... | collective-permute-start | bytes 2457608 | tf_op jit(solution)/shard_map/ppermute | solution.py:40
  53.7 22.2 %collective-permute-start.8 = (bf16[4,80,1280]{2,1,0:T(8,128)(2,1)}, bf16[4,80,1280]{2,1,0:T(8,128)(2,1)S(1)}, u32[]{:S(2)}, u32[]{:S(2)}) collective-permute-start(bf16[4,80,1280]{2,1,0:T(8,128)(2,1)} %get-tuple-element.59), channel_id=1, source_target_pairs={{0,12},{1,13},{2,14},{3,15},{4,0},{5,1},{6,2},{7,3},{8,4},{9,5},{1... | collective-permute-start | bytes 2457608 | tf_op jit(solution)/shard_map/ppermute | solution.py:40
  69.5 6.4 %copy-start.9 = (bf16[2,80,1280]{2,1,0:T(8,128)(2,1)S(1)}, bf16[2,80,1280]{2,1,0:T(8,128)(2,1)}, u32[]{:S(2)}) copy-start(bf16[2,80,1280]{2,1,0:T(8,128)(2,1)} %get-tuple-element.61) | copy-start | bytes 1228804
  70.7 11.7 %collective-permute-start.13 = (bf16[2,80,1280]{2,1,0:T(8,128)(2,1)S(1)}, bf16[2,80,1280]{2,1,0:T(8,128)(2,1)S(1)}, u32[]{:S(2)}, u32[]{:S(2)}) collective-permute-start(bf16[2,80,1280]{2,1,0:T(8,128)(2,1)S(1)} %add_convert_fusion), channel_id=1, source_target_pairs={{0,3},{1,0},{2,1},{3,2},{4,7},{5,4},{6,5},{7,6},{8,11},{9,8},{10,9... | collective-permute-start | bytes 1228808 | tf_op jit(solution)/shard_map/ppermute | solution.py:40
  74.3 12.2 %copy-start.8 = (bf16[4,80,1280]{2,1,0:T(8,128)(2,1)S(1)}, bf16[4,80,1280]{2,1,0:T(8,128)(2,1)}, u32[]{:S(2)}) copy-start(bf16[4,80,1280]{2,1,0:T(8,128)(2,1)} %get-tuple-element.64) | copy-start | bytes 2457604
  75.5 11.0 %collective-permute-start.12 = (bf16[2,80,1280]{2,1,0:T(8,128)(2,1)S(1)}, bf16[2,80,1280]{2,1,0:T(8,128)(2,1)S(1)}, u32[]{:S(2)}, u32[]{:S(2)}) collective-permute-start(bf16[2,80,1280]{2,1,0:T(8,128)(2,1)S(1)} %add_convert_fusion.1), channel_id=1, source_target_pairs={{0,1},{1,2},{2,3},{3,0},{4,5},{5,6},{6,7},{7,4},{8,9},{9,10},{10,1... | collective-permute-start | bytes 1228808 | tf_op jit(solution)/shard_map/ppermute | solution.py:40
  76.1 10.8 %collective-permute-start.14 = (bf16[2,80,1280]{2,1,0:T(8,128)(2,1)S(1)}, bf16[2,80,1280]{2,1,0:T(8,128)(2,1)S(1)}, u32[]{:S(2)}, u32[]{:S(2)}) collective-permute-start(bf16[2,80,1280]{2,1,0:T(8,128)(2,1)S(1)} %add_convert_fusion.3), channel_id=1, source_target_pairs={{0,4},{1,5},{2,6},{3,7},{4,8},{5,9},{6,10},{7,11},{8,12},{9,13},{1... | collective-permute-start | bytes 1228808 | tf_op jit(solution)/shard_map/ppermute | solution.py:40
  77.7 9.2 %collective-permute-start.15 = (bf16[2,80,1280]{2,1,0:T(8,128)(2,1)S(1)}, bf16[2,80,1280]{2,1,0:T(8,128)(2,1)S(1)}, u32[]{:S(2)}, u32[]{:S(2)}) collective-permute-start(bf16[2,80,1280]{2,1,0:T(8,128)(2,1)S(1)} %add_convert_fusion.2), channel_id=1, source_target_pairs={{0,12},{1,13},{2,14},{3,15},{4,0},{5,1},{6,2},{7,3},{8,4},{9,5},{1... | collective-permute-start | bytes 1228808 | tf_op jit(solution)/shard_map/ppermute | solution.py:40
  79.4 30.1 %collective-permute-start.9 = (f32[80,1280]{1,0:T(8,128)S(1)}, f32[80,1280]{1,0:T(8,128)S(1)}, u32[]{:S(2)}, u32[]{:S(2)}) collective-permute-start(f32[80,1280]{1,0:T(8,128)S(1)} %reshape.21), channel_id=1, source_target_pairs={{0,16},{1,17},{2,18},{3,19},{4,20},{5,21},{6,22},{7,23},{8,24},{9,... | collective-permute-start | bytes 1228808 | tf_op jit(solution)/shard_map/ppermute | solution.py:40
  86.5 1.1 copy-start.7
  88.4 8.9 %collective-permute-start.16 = (bf16[80,1280]{1,0:T(8,128)(2,1)S(1)}, bf16[80,1280]{1,0:T(8,128)(2,1)S(1)}, u32[]{:S(2)}, u32[]{:S(2)}) collective-permute-start(bf16[80,1280]{1,0:T(8,128)(2,1)S(1)} %get-tuple-element.90), channel_id=1, source_target_pairs={{0,4},{1,5},{2,6},{3,7},{4,8},{5,9},{6,10},{7,11},{8,12},{9,13},{1... | collective-permute-start | bytes 614408 | tf_op jit(solution)/shard_map/ppermute | solution.py:40
  90.0 9.0 %collective-permute-start.18 = (bf16[80,1280]{1,0:T(8,128)(2,1)S(1)}, bf16[80,1280]{1,0:T(8,128)(2,1)S(1)}, u32[]{:S(2)}, u32[]{:S(2)}) collective-permute-start(bf16[80,1280]{1,0:T(8,128)(2,1)S(1)} %get-tuple-element.91), channel_id=1, source_target_pairs={{0,12},{1,13},{2,14},{3,15},{4,0},{5,1},{6,2},{7,3},{8,4},{9,5},{1... | collective-permute-start | bytes 614408 | tf_op jit(solution)/shard_map/ppermute | solution.py:40
  91.7 7.8 %collective-permute-start.17 = (bf16[80,1280]{1,0:T(8,128)(2,1)S(1)}, bf16[80,1280]{1,0:T(8,128)(2,1)S(1)}, u32[]{:S(2)}, u32[]{:S(2)}) collective-permute-start(bf16[80,1280]{1,0:T(8,128)(2,1)S(1)} %get-tuple-element.92), channel_id=1, source_target_pairs={{0,8},{1,9},{2,10},{3,11},{4,12},{5,13},{6,14},{7,15},{8,0},{9,1},... | collective-permute-start | bytes 614408 | tf_op jit(solution)/shard_map/ppermute | solution.py:40
  93.8 7.8 %collective-permute-start.19 = (bf16[80,1280]{1,0:T(8,128)(2,1)S(1)}, bf16[80,1280]{1,0:T(8,128)(2,1)S(1)}, u32[]{:S(2)}, u32[]{:S(2)}) collective-permute-start(bf16[80,1280]{1,0:T(8,128)(2,1)S(1)} %get-tuple-element.87), channel_id=1, source_target_pairs={{0,1},{1,2},{2,3},{3,0},{4,5},{5,6},{6,7},{7,4},{8,9},{9,10},{10,1... | collective-permute-start | bytes 614408 | tf_op jit(solution)/shard_map/ppermute | solution.py:40
  97.2 7.3 %collective-permute-start.21 = (bf16[80,1280]{1,0:T(8,128)(2,1)S(1)}, bf16[80,1280]{1,0:T(8,128)(2,1)S(1)}, u32[]{:S(2)}, u32[]{:S(2)}) collective-permute-start(bf16[80,1280]{1,0:T(8,128)(2,1)S(1)} %get-tuple-element.88), channel_id=1, source_target_pairs={{0,3},{1,0},{2,1},{3,2},{4,7},{5,4},{6,5},{7,6},{8,11},{9,8},{10,9... | collective-permute-start | bytes 614408 | tf_op jit(solution)/shard_map/ppermute | solution.py:40
  99.0 7.3 %collective-permute-start.20 = (bf16[80,1280]{1,0:T(8,128)(2,1)S(1)}, bf16[80,1280]{1,0:T(8,128)(2,1)S(1)}, u32[]{:S(2)}, u32[]{:S(2)}) collective-permute-start(bf16[80,1280]{1,0:T(8,128)(2,1)S(1)} %get-tuple-element.89), channel_id=1, source_target_pairs={{0,2},{1,3},{2,0},{3,1},{4,6},{5,7},{6,4},{7,5},{8,10},{9,11},{10,... | collective-permute-start | bytes 614408 | tf_op jit(solution)/shard_map/ppermute | solution.py:40
  106.4 9.5 %collective-permute-start.22 = (bf16[2,80,1280]{2,1,0:T(8,128)(2,1)S(1)}, bf16[2,80,1280]{2,1,0:T(8,128)(2,1)S(1)}, u32[]{:S(2)}, u32[]{:S(2)}) collective-permute-start(bf16[2,80,1280]{2,1,0:T(8,128)(2,1)S(1)} %pad_maximum_fusion.5), channel_id=1, source_target_pairs={{0,16},{1,17},{2,18},{3,19},{4,20},{5,21},{6,22},{7,23},{8,24},{9,... | collective-permute-start | bytes 1228808 | tf_op jit(solution)/shard_map/ppermute | solution.py:40
  116.1 7.0 %collective-permute-start.25 = (bf16[80,1280]{1,0:T(8,128)(2,1)S(1)}, bf16[80,1280]{1,0:T(8,128)(2,1)S(1)}, u32[]{:S(2)}, u32[]{:S(2)}) collective-permute-start(bf16[80,1280]{1,0:T(8,128)(2,1)S(1)} %get-tuple-element.98), channel_id=1, source_target_pairs={{0,4},{1,5},{2,6},{3,7},{4,8},{5,9},{6,10},{7,11},{8,12},{9,13},{1... | collective-permute-start | bytes 614408 | tf_op jit(solution)/shard_map/ppermute | solution.py:40
  116.2 9.7 %collective-permute-start.24 = (bf16[80,1280]{1,0:T(8,128)(2,1)S(1)}, bf16[80,1280]{1,0:T(8,128)(2,1)S(1)}, u32[]{:S(2)}, u32[]{:S(2)}) collective-permute-start(bf16[80,1280]{1,0:T(8,128)(2,1)S(1)} %get-tuple-element.98), channel_id=1, source_target_pairs={{0,8},{1,9},{2,10},{3,11},{4,12},{5,13},{6,14},{7,15},{8,0},{9,1},... | collective-permute-start | bytes 614408 | tf_op jit(solution)/shard_map/ppermute | solution.py:40
  120.0 6.3 %collective-permute-start.23 = (bf16[80,1280]{1,0:T(8,128)(2,1)S(1)}, bf16[80,1280]{1,0:T(8,128)(2,1)S(1)}, u32[]{:S(2)}, u32[]{:S(2)}) collective-permute-start(bf16[80,1280]{1,0:T(8,128)(2,1)S(1)} %get-tuple-element.98), channel_id=1, source_target_pairs={{0,12},{1,13},{2,14},{3,15},{4,0},{5,1},{6,2},{7,3},{8,4},{9,5},{1... | collective-permute-start | bytes 614408 | tf_op jit(solution)/shard_map/ppermute | solution.py:40
  120.1 9.6 %collective-permute-start.27 = (bf16[100,1280]{1,0:T(8,128)(2,1)S(1)}, bf16[100,1280]{1,0:T(8,128)(2,1)S(1)}, u32[]{:S(2)}, u32[]{:S(2)}) collective-permute-start(bf16[100,1280]{1,0:T(8,128)(2,1)S(1)} %get-tuple-element.104), channel_id=1, source_target_pairs={{0,3},{1,0},{2,1},{3,2},{4,7},{5,4},{6,5},{7,6},{8,11},{9,8},{10,9... | collective-permute-start | bytes 768008 | tf_op jit(solution)/shard_map/ppermute | solution.py:40
  122.3 10.8 %collective-permute-start.28 = (bf16[100,1280]{1,0:T(8,128)(2,1)S(1)}, bf16[100,1280]{1,0:T(8,128)(2,1)S(1)}, u32[]{:S(2)}, u32[]{:S(2)}) collective-permute-start(bf16[100,1280]{1,0:T(8,128)(2,1)S(1)} %get-tuple-element.105), channel_id=1, source_target_pairs={{0,2},{1,3},{2,0},{3,1},{4,6},{5,7},{6,4},{7,5},{8,10},{9,11},{10,... | collective-permute-start | bytes 768008 | tf_op jit(solution)/shard_map/ppermute | solution.py:40
  123.2 13.1 %collective-permute-start.29 = (bf16[100,1280]{1,0:T(8,128)(2,1)S(1)}, bf16[100,1280]{1,0:T(8,128)(2,1)S(1)}, u32[]{:S(2)}, u32[]{:S(2)}) collective-permute-start(bf16[100,1280]{1,0:T(8,128)(2,1)S(1)} %get-tuple-element.106), channel_id=1, source_target_pairs={{0,1},{1,2},{2,3},{3,0},{4,5},{5,6},{6,7},{7,4},{8,9},{9,10},{10,1... | collective-permute-start | bytes 768008 | tf_op jit(solution)/shard_map/ppermute | solution.py:40
  126.4 13.4 %copy-start.1 = (bf16[4,80,1280]{2,1,0:T(8,128)(2,1)}, bf16[4,80,1280]{2,1,0:T(8,128)(2,1)S(1)}, u32[]{:S(2)}) copy-start(bf16[4,80,1280]{2,1,0:T(8,128)(2,1)S(1)} %pad_maximum_fusion.2.rest_0_) | copy-start | bytes 2457604
  126.4 23.3 %collective-permute-start.31 = (bf16[4,80,1280]{2,1,0:T(8,128)(2,1)S(1)}, bf16[4,80,1280]{2,1,0:T(8,128)(2,1)S(1)}, u32[]{:S(2)}, u32[]{:S(2)}) collective-permute-start(bf16[4,80,1280]{2,1,0:T(8,128)(2,1)S(1)} %pad_maximum_fusion.2.rest_0_), channel_id=1, source_target_pairs={{0,1},{1,2},{2,3},{3,0},{4,5},{5,6},{6,7},{7,4},{8,9},{9,10},{10,1... | collective-permute-start | bytes 2457608 | tf_op jit(solution)/shard_map/ppermute | solution.py:40
  126.7 23.1 %collective-permute-start.26 = (bf16[4,80,1280]{2,1,0:T(8,128)(2,1)S(1)}, bf16[4,80,1280]{2,1,0:T(8,128)(2,1)S(1)}, u32[]{:S(2)}, u32[]{:S(2)}) collective-permute-start(bf16[4,80,1280]{2,1,0:T(8,128)(2,1)S(1)} %pad_maximum_fusion.2.rest_0_), channel_id=1, source_target_pairs={{0,3},{1,0},{2,1},{3,2},{4,7},{5,4},{6,5},{7,6},{8,11},{9,8},{10,9... | collective-permute-start | bytes 2457608 | tf_op jit(solution)/shard_map/ppermute | solution.py:40
  136.5 13.3 %copy-start.2 = (bf16[4,80,1280]{2,1,0:T(8,128)(2,1)}, bf16[4,80,1280]{2,1,0:T(8,128)(2,1)S(1)}, u32[]{:S(2)}) copy-start(bf16[4,80,1280]{2,1,0:T(8,128)(2,1)S(1)} %pad_maximum_fusion.3.rest_3_) | copy-start | bytes 2457604
  136.5 16.7 %collective-permute-start.35 = (bf16[4,80,1280]{2,1,0:T(8,128)(2,1)S(1)}, bf16[4,80,1280]{2,1,0:T(8,128)(2,1)}, u32[]{:S(2)}, u32[]{:S(2)}) collective-permute-start(bf16[4,80,1280]{2,1,0:T(8,128)(2,1)S(1)} %pad_maximum_fusion.3.rest_3_), channel_id=1, source_target_pairs={{0,4},{1,5},{2,6},{3,7},{4,8},{5,9},{6,10},{7,11},{8,12},{9,13},{1... | collective-permute-start | bytes 2457608 | tf_op jit(solution)/shard_map/ppermute | solution.py:40
  137.7 17.9 %collective-permute-start.33 = (bf16[4,80,1280]{2,1,0:T(8,128)(2,1)S(1)}, bf16[4,80,1280]{2,1,0:T(8,128)(2,1)}, u32[]{:S(2)}, u32[]{:S(2)}) collective-permute-start(bf16[4,80,1280]{2,1,0:T(8,128)(2,1)S(1)} %pad_maximum_fusion.3.rest_3_), channel_id=1, source_target_pairs={{0,12},{1,13},{2,14},{3,15},{4,0},{5,1},{6,2},{7,3},{8,4},{9,5},{1... | collective-permute-start | bytes 2457608 | tf_op jit(solution)/shard_map/ppermute | solution.py:40
  149.7 7.0 %copy-start.3 = (bf16[4,80,1280]{2,1,0:T(8,128)(2,1)}, bf16[4,80,1280]{2,1,0:T(8,128)(2,1)S(1)}, u32[]{:S(2)}) copy-start(bf16[4,80,1280]{2,1,0:T(8,128)(2,1)S(1)} %collective-permute-done.31.rest_2_) | copy-start | bytes 2457604
  149.7 14.0 %collective-permute-start.32 = (bf16[2,80,1280]{2,1,0:T(8,128)(2,1)S(1)}, bf16[2,80,1280]{2,1,0:T(8,128)(2,1)}, u32[]{:S(2)}, u32[]{:S(2)}) collective-permute-start(bf16[2,80,1280]{2,1,0:T(8,128)(2,1)S(1)} %slice.150), channel_id=1, source_target_pairs={{0,1},{1,2},{2,3},{3,0},{4,5},{5,6},{6,7},{7,4},{8,9},{9,10},{10,1... | collective-permute-start | bytes 1228808 | tf_op jit(solution)/shard_map/ppermute | solution.py:40
  149.8 8.8 %copy-start.4 = (bf16[4,80,1280]{2,1,0:T(8,128)(2,1)}, bf16[4,80,1280]{2,1,0:T(8,128)(2,1)S(1)}, u32[]{:S(2)}) copy-start(bf16[4,80,1280]{2,1,0:T(8,128)(2,1)S(1)} %collective-permute-done.26.rest_1_) | copy-start | bytes 2457604
  149.9 13.9 %collective-permute-start.30 = (bf16[2,80,1280]{2,1,0:T(8,128)(2,1)S(1)}, bf16[2,80,1280]{2,1,0:T(8,128)(2,1)}, u32[]{:S(2)}, u32[]{:S(2)}) collective-permute-start(bf16[2,80,1280]{2,1,0:T(8,128)(2,1)S(1)} %slice.125), channel_id=1, source_target_pairs={{0,3},{1,0},{2,1},{3,2},{4,7},{5,4},{6,5},{7,6},{8,11},{9,8},{10,9... | collective-permute-start | bytes 1228808 | tf_op jit(solution)/shard_map/ppermute | solution.py:40
  154.2 9.6 %collective-permute-start.36 = (bf16[2,80,1280]{2,1,0:T(8,128)(2,1)S(1)}, bf16[2,80,1280]{2,1,0:T(8,128)(2,1)}, u32[]{:S(2)}, u32[]{:S(2)}) collective-permute-start(bf16[2,80,1280]{2,1,0:T(8,128)(2,1)S(1)} %slice.155), channel_id=1, source_target_pairs={{0,4},{1,5},{2,6},{3,7},{4,8},{5,9},{6,10},{7,11},{8,12},{9,13},{1... | collective-permute-start | bytes 1228808 | tf_op jit(solution)/shard_map/ppermute | solution.py:40
  156.7 8.0 %collective-permute-start.34 = (bf16[2,80,1280]{2,1,0:T(8,128)(2,1)S(1)}, bf16[2,80,1280]{2,1,0:T(8,128)(2,1)S(1)}, u32[]{:S(2)}, u32[]{:S(2)}) collective-permute-start(bf16[2,80,1280]{2,1,0:T(8,128)(2,1)S(1)} %slice.154), channel_id=1, source_target_pairs={{0,12},{1,13},{2,14},{3,15},{4,0},{5,1},{6,2},{7,3},{8,4},{9,5},{1... | collective-permute-start | bytes 1228808 | tf_op jit(solution)/shard_map/ppermute | solution.py:40
  164.7 0.8 copy-start.11
